TPU v7x, 32 devices: a whole 2x2x4 slice. The times are simulated.
32 devices in a mesh: fsdp: 32 (over z, y, x, core).
Axes of the slice: x: 2, y: 2, z: 4, core: 2. Of those that a mesh axis runs over, the one named last changes fastest.
Arguments:
- tokens: float32 [23328, 1152], P('fsdp'), may hold values from -6 to 6
- image_valid: int32 [32], P('fsdp'), may hold values 0 or 1
- attn_gain: float32 [1152], P('fsdp'), may hold values from 0.1 to 1.9
- attn_shift: float32 [1152], P('fsdp'), may hold values from -1.8 to 1.8
- query_weight: float32 [1327104], P('fsdp'), may hold values from -0.25 to 0.25
- query_bias: float32 [1152], P('fsdp'), may hold values from -3 to 3
- key_weight: float32 [1327104], P('fsdp'), may hold values from -0.25 to 0.25
- value_weight: float32 [1327104], P('fsdp'), may hold values from -0.1875 to 0.1875
- value_bias: float32 [1152], P('fsdp'), may hold values from -0.6 to 0.6
- output_weight: float32 [1327104], P('fsdp'), may hold values from -1 to 1
- output_bias: float32 [1152], P('fsdp'), may hold values from -1.8 to 1.8
- mlp_gain: float32 [1152], P('fsdp'), may hold values from 0.1 to 1.9
- mlp_shift: float32 [1152], P('fsdp'), may hold values from -1.8 to 1.8
- expand_weight: float32 [4958208], P('fsdp'), may hold values from -0.1875 to 0.1875
- expand_bias: float32 [4320], P('fsdp'), may hold values from -3 to 3
- reduce_weight: float32 [4958208], P('fsdp'), may hold values from -0.09375 to 0.09375
- reduce_bias: float32 [1152], P('fsdp'), may hold values from -1.8 to 1.8
- cotangent: float32 [23328, 1152], P('fsdp'), may hold values from -6 to 6
Outputs:
- layer_out: float32 [23328, 1152], P('fsdp')
- tokens_grad: float32 [23328, 1152], P('fsdp')
- attn_gain_grad: float32 [1152], P('fsdp')
- attn_shift_grad: float32 [1152], P('fsdp')
- query_weight_grad: float32 [1327104], P('fsdp')
- query_bias_grad: float32 [1152], P('fsdp')
- key_weight_grad: float32 [1327104], P('fsdp')
- value_weight_grad: float32 [1327104], P('fsdp')
- value_bias_grad: float32 [1152], P('fsdp')
- output_weight_grad: float32 [1327104], P('fsdp')
- output_bias_grad: float32 [1152], P('fsdp')
- mlp_gain_grad: float32 [1152], P('fsdp')
- mlp_shift_grad: float32 [1152], P('fsdp')
- expand_weight_grad: float32 [4958208], P('fsdp')
- expand_bias_grad: float32 [4320], P('fsdp')
- reduce_weight_grad: float32 [4958208], P('fsdp')
- reduce_bias_grad: float32 [1152], P('fsdp')
All inputs are finite; a program needn't handle non-finite values. No bound on the sum of `image_valid` on one device may be relied on, other than what follows from the above.
Results may differ from a plain program's by a relative error of at most 0.013.
The roundings to bfloat16 on the way count: a program that leaves them out, or rounds other values in their place, can miss the bound.
Values may be sent and summed in bfloat16 or wider, within the bound.
No kernel may reach another device: no remote copies, remote signals or barrier semaphores. Data moves between devices by JAX's collectives and lax.ppermute only.
A program may use at most 384 MiB of HBM per device.

v0:
```python
import jax
import jax.numpy as jnp
from jax import lax
from jax.sharding import PartitionSpec as P

D = 1152
HEADS = 16
HEAD_DIM = 72
FF = 4304


def layer_norm(values, gain, shift):
    centre = jnp.mean(values, axis=-1, keepdims=True)
    centered = values - centre
    spread = jnp.mean(centered * centered, axis=-1, keepdims=True)
    return centered * lax.rsqrt(spread + 1e-06) * gain + shift


def gelu_tanh(values):
    return jax.nn.gelu(values, approximate=True)


def product(left, right):
    return jnp.dot(left, right, preferred_element_type=jnp.float32)


def layout_dims():
    return (
        (D,),
        (D,),
        (D, D),
        (D,),
        (D, D),
        (D, D),
        (D,),
        (D, D),
        (D,),
        (D,),
        (D,),
        (D, FF),
        (FF,),
        (FF, D),
        (D,),
    )


def unpack_flat(flat, shape_dims):
    length = 1
    for extent in shape_dims:
        length = length * extent
    return flat[:length].reshape(shape_dims)


def matrix_slice(left, right, offset, length):
    out_cols = right.shape[1]
    row_count = length // out_cols + 2
    padded = jnp.pad(left, ((0, 0), (0, row_count)))
    first_row = offset // out_cols
    block = lax.dynamic_slice_in_dim(padded, first_row, row_count, 1)
    term = jnp.einsum("tr,tc->rc", block, right, preferred_element_type=jnp.float32).reshape(-1)
    return lax.dynamic_slice_in_dim(term, offset, length)


def vector_slice(vector, offset, length, full_length):
    padded = jnp.pad(vector, (0, full_length + length - vector.shape[0]))
    return lax.dynamic_slice_in_dim(padded, offset, length)


def owned_sums(entries, devices, start, count):
    pieces = []
    for entry in entries:
        width = entry[-1]
        offset = start * width
        length = count * width
        if entry[0] == "matrix":
            piece = matrix_slice(entry[1], entry[2], offset, length)
        else:
            piece = vector_slice(entry[1], offset, length, width * devices)
        pieces.append(piece.reshape(count, width))
    return jnp.concatenate(pieces, axis=1)


def split_owned(joined, entries):
    results = []
    position = 0
    for entry in entries:
        width = entry[-1]
        results.append(joined[0, position : position + width])
        position = position + width
    return results


def on_device(
    tokens,
    image_valid,
    attn_gain,
    attn_shift,
    query_weight,
    query_bias,
    key_weight,
    value_weight,
    value_bias,
    output_weight,
    output_bias,
    mlp_gain,
    mlp_shift,
    expand_weight,
    expand_bias,
    reduce_weight,
    reduce_bias,
    cotangent,
):
    devices = lax.axis_size("fsdp")
    shards = (
        attn_gain,
        attn_shift,
        query_weight,
        query_bias,
        key_weight,
        value_weight,
        value_bias,
        output_weight,
        output_bias,
        mlp_gain,
        mlp_shift,
        expand_weight,
        expand_bias,
        reduce_weight,
        reduce_bias,
    )
    widths = [piece.shape[0] for piece in shards]
    narrow = [piece.astype(jnp.bfloat16) for piece in shards]
    dims_all = layout_dims()
    fetched = (
        lax.all_gather(narrow[0], "fsdp", axis=0, tiled=True),
        lax.all_gather(narrow[1], "fsdp", axis=0, tiled=True),
        lax.all_gather(narrow[2], "fsdp", axis=0, tiled=True),
        lax.all_gather(narrow[3], "fsdp", axis=0, tiled=True),
        lax.all_gather(narrow[4], "fsdp", axis=0, tiled=True),
        lax.all_gather(narrow[5], "fsdp", axis=0, tiled=True),
        lax.all_gather(narrow[6], "fsdp", axis=0, tiled=True),
        lax.all_gather(narrow[7], "fsdp", axis=0, tiled=True),
        lax.all_gather(narrow[8], "fsdp", axis=0, tiled=True),
        lax.all_gather(narrow[9], "fsdp", axis=0, tiled=True),
        lax.all_gather(narrow[10], "fsdp", axis=0, tiled=True),
        lax.all_gather(narrow[11], "fsdp", axis=0, tiled=True),
        lax.all_gather(narrow[12], "fsdp", axis=0, tiled=True),
        lax.all_gather(narrow[13], "fsdp", axis=0, tiled=True),
        lax.all_gather(narrow[14], "fsdp", axis=0, tiled=True),
    )
    params = [unpack_flat(flat, shape_dims) for flat, shape_dims in zip(fetched, dims_all)]
    image_count = image_valid.shape[0]
    seq_len = tokens.shape[0] // image_count
    scale = HEAD_DIM ** (-0.5)
    weight_img = jnp.repeat(image_valid.astype(jnp.float32), seq_len)[:, None]
    gain_one = params[0].astype(jnp.float32)
    shift_one = params[1].astype(jnp.float32)
    normed, norm_back_one = jax.vjp(layer_norm, tokens, gain_one, shift_one)
    normed_low = normed.astype(jnp.bfloat16)
    query = (product(normed_low, params[2]) + params[3].astype(jnp.float32)).astype(jnp.bfloat16)
    keys = product(normed_low, params[4]).astype(jnp.bfloat16)
    values = (product(normed_low, params[5]) + params[6].astype(jnp.float32)).astype(jnp.bfloat16)
    query_heads = query.reshape(image_count, seq_len, HEADS, HEAD_DIM)
    key_heads = keys.reshape(image_count, seq_len, HEADS, HEAD_DIM)
    value_heads = values.reshape(image_count, seq_len, HEADS, HEAD_DIM)
    scores = (
        jnp.einsum("bqhd,bkhd->bhqk", query_heads, key_heads, preferred_element_type=jnp.float32)
        * scale
    )
    highest = jnp.max(scores, axis=-1, keepdims=True)
    expd = jnp.exp(scores - highest)
    totals = jnp.sum(expd, axis=-1, keepdims=True)
    log_total = highest + jnp.log(totals)
    probs_low = (expd / totals).astype(jnp.bfloat16)
    mixed = jnp.einsum(
        "bhqk,bkhd->bqhd", probs_low, value_heads, preferred_element_type=jnp.float32
    )
    mixed_low = mixed.reshape(image_count * seq_len, D).astype(jnp.bfloat16)
    resid = tokens + product(mixed_low, params[7]) + params[8].astype(jnp.float32)
    gain_two = params[9].astype(jnp.float32)
    shift_two = params[10].astype(jnp.float32)
    normed_two, norm_back_two = jax.vjp(layer_norm, resid, gain_two, shift_two)
    normed_two_low = normed_two.astype(jnp.bfloat16)
    pre_act = product(normed_two_low, params[11]) + params[12].astype(jnp.float32)
    hidden, gelu_back = jax.vjp(gelu_tanh, pre_act)
    hidden_low = hidden.astype(jnp.bfloat16)
    layer_out = weight_img * (
        resid + product(hidden_low, params[13]) + params[14].astype(jnp.float32)
    )
    refetched = (
        lax.all_gather(narrow[2], "fsdp", axis=0, tiled=True),
        lax.all_gather(narrow[4], "fsdp", axis=0, tiled=True),
        lax.all_gather(narrow[5], "fsdp", axis=0, tiled=True),
        lax.all_gather(narrow[7], "fsdp", axis=0, tiled=True),
        lax.all_gather(narrow[11], "fsdp", axis=0, tiled=True),
        lax.all_gather(narrow[13], "fsdp", axis=0, tiled=True),
    )
    again = tuple(
        (
            unpack_flat(flat, shape_dims)
            for flat, shape_dims in zip(
                refetched,
                (dims_all[2], dims_all[4], dims_all[5], dims_all[7], dims_all[11], dims_all[13]),
            )
        )
    )
    back_query, back_key, back_value, back_output, back_expand, back_reduce = again
    grad_out = weight_img * cotangent
    grad_branch = grad_out.astype(jnp.bfloat16)
    reduce_b_grad = jnp.sum(grad_branch.astype(jnp.float32), axis=0)
    grad_hidden = jnp.einsum(
        "td,fd->tf", grad_branch, back_reduce, preferred_element_type=jnp.float32
    )
    grad_pre = gelu_back(grad_hidden)[0].astype(jnp.bfloat16)
    expand_b_grad = jnp.sum(grad_pre.astype(jnp.float32), axis=0)
    grad_normed_two = jnp.einsum(
        "tf,df->td", grad_pre, back_expand, preferred_element_type=jnp.float32
    )
    resid_part, gain_two_grad, shift_two_grad = norm_back_two(grad_normed_two)
    grad_resid = grad_out + resid_part
    grad_attn = grad_resid.astype(jnp.bfloat16)
    output_b_grad = jnp.sum(grad_attn.astype(jnp.float32), axis=0)
    outer_entries = [
        ("vector", gain_two_grad, widths[9]),
        ("vector", shift_two_grad, widths[10]),
        ("matrix", normed_two_low, grad_pre, widths[11]),
        ("vector", expand_b_grad, widths[12]),
        ("matrix", hidden_low, grad_branch, widths[13]),
        ("vector", reduce_b_grad, widths[14]),
        ("matrix", mixed_low, grad_attn, widths[7]),
        ("vector", output_b_grad, widths[8]),
    ]
    grad_mixed = jnp.einsum(
        "te,de->td", grad_attn, back_output, preferred_element_type=jnp.float32
    ).astype(jnp.bfloat16)
    grad_mixed_heads = grad_mixed.reshape(image_count, seq_len, HEADS, HEAD_DIM)
    scores_again = (
        jnp.einsum("bqhd,bkhd->bhqk", query_heads, key_heads, preferred_element_type=jnp.float32)
        * scale
    )
    probs_again = jnp.exp(scores_again - log_total)
    probs_again_low = probs_again.astype(jnp.bfloat16)
    grad_value = jnp.einsum(
        "bhqk,bqhd->bkhd", probs_again_low, grad_mixed_heads, preferred_element_type=jnp.float32
    ).astype(jnp.bfloat16)
    grad_probs = jnp.einsum(
        "bqhd,bkhd->bhqk", grad_mixed_heads, value_heads, preferred_element_type=jnp.float32
    )
    grad_scores = (
        probs_again * (grad_probs - jnp.sum(grad_probs * probs_again, axis=-1, keepdims=True))
    ).astype(jnp.bfloat16)
    grad_query = (
        jnp.einsum("bhqk,bkhd->bqhd", grad_scores, key_heads, preferred_element_type=jnp.float32)
        * scale
    ).astype(jnp.bfloat16)
    grad_key = (
        jnp.einsum("bhqk,bqhd->bkhd", grad_scores, query_heads, preferred_element_type=jnp.float32)
        * scale
    ).astype(jnp.bfloat16)
    rows = image_count * seq_len
    grad_query = grad_query.reshape(rows, D)
    grad_key = grad_key.reshape(rows, D)
    grad_value = grad_value.reshape(rows, D)
    query_b_grad = jnp.sum(grad_query.astype(jnp.float32), axis=0)
    value_b_grad = jnp.sum(grad_value.astype(jnp.float32), axis=0)
    grad_normed = jnp.einsum(
        "te,de->td", grad_query, back_query, preferred_element_type=jnp.float32
    )
    grad_normed = grad_normed + jnp.einsum(
        "te,de->td", grad_key, back_key, preferred_element_type=jnp.float32
    )
    grad_normed = grad_normed + jnp.einsum(
        "te,de->td", grad_value, back_value, preferred_element_type=jnp.float32
    )
    tokens_part, gain_one_grad, shift_one_grad = norm_back_one(grad_normed)
    tokens_grad = grad_resid + tokens_part
    inner_entries = [
        ("vector", gain_one_grad, widths[0]),
        ("vector", shift_one_grad, widths[1]),
        ("matrix", normed_low, grad_query, widths[2]),
        ("vector", query_b_grad, widths[3]),
        ("matrix", normed_low, grad_key, widths[4]),
        ("matrix", normed_low, grad_value, widths[5]),
        ("vector", value_b_grad, widths[6]),
    ]
    all_entries = inner_entries + [
        outer_entries[6],
        outer_entries[7],
        outer_entries[0],
        outer_entries[1],
        outer_entries[2],
        outer_entries[3],
        outer_entries[4],
        outer_entries[5],
    ]
    all_joined = lax.psum_scatter(
        owned_sums(all_entries, devices, jnp.int32(0), 1 * lax.axis_size("fsdp")),
        "fsdp",
        scatter_dimension=0,
        tiled=True,
    )
    ordered = split_owned(all_joined, all_entries)
    return (
        layer_out,
        tokens_grad,
        ordered[0],
        ordered[1],
        ordered[2],
        ordered[3],
        ordered[4],
        ordered[5],
        ordered[6],
        ordered[7],
        ordered[8],
        ordered[9],
        ordered[10],
        ordered[11],
        ordered[12],
        ordered[13],
        ordered[14],
    )


def solution(mesh):
    in_specs = (
        P("fsdp", None),
        P("fsdp"),
        P("fsdp"),
        P("fsdp"),
        P("fsdp"),
        P("fsdp"),
        P("fsdp"),
        P("fsdp"),
        P("fsdp"),
        P("fsdp"),
        P("fsdp"),
        P("fsdp"),
        P("fsdp"),
        P("fsdp"),
        P("fsdp"),
        P("fsdp"),
        P("fsdp"),
        P("fsdp", None),
    )
    out_specs = (
        P("fsdp", None),
        P("fsdp", None),
        P("fsdp"),
        P("fsdp"),
        P("fsdp"),
        P("fsdp"),
        P("fsdp"),
        P("fsdp"),
        P("fsdp"),
        P("fsdp"),
        P("fsdp"),
        P("fsdp"),
        P("fsdp"),
        P("fsdp"),
        P("fsdp"),
        P("fsdp"),
        P("fsdp"),
    )
    return jax.shard_map(
        on_device, mesh=mesh, in_specs=in_specs, out_specs=out_specs, check_vma=False
    )
```

profile of v0, /device:TPU:8, one launch (start us, length us, event | category | flops | bytes accessed | tf_op | source)
XLA Modules:
  0.0 2034.7 jit_solution(10942745007842772498)
XLA Ops:
  38.6 42.9 %all-reduce.17 = (bf16[1152]{0:T(1024)(128)(2,1)S(1)}, bf16[1152]{0:T(1024)(128)(2,1)S(1)}, bf16[1152]{0:T(1024)(128)(2,1)S(1)}, bf16[1152]{0:T(1024)(128)(2,1)S...) all-reduce(bf16[1152]{0:T(1024)(128)(2,1)S(1)} %dynamic-update-slic, ...), channel_id=1, replica_groups=mesh['fsdp'=32] {'fsdp'}, use_global_device_ids=true, to_apply=%add.6 | all-reduce | flops 13536 | bytes 54144
  87.9 48.6 %reduce.8 = bf16[32,41472]{1,0:T(8,128)(2,1)} reduce(bf16[32,1,41472]{2,1,0:T(2,128)(2,1)} %all-gather.9.cloned.1.call-done, bf16[]{:T(256)} %constant.151), dimensions={1}, to_apply=%all-gather.reduce_sub_computation | reduce | bytes 5308418 | tf_op jit(solution)/shard_map/all_gather | solution.py:140
  147.2 48.8 %reduce.9 = bf16[32,41472]{1,0:T(8,128)(2,1)} reduce(bf16[32,1,41472]{2,1,0:T(2,128)(2,1)} %all-gather.11.cloned.1.call-done, bf16[]{:T(256)} %constant.151), dimensions={1}, to_apply=%all-gather.1.reduce_sub_computation | reduce | bytes 5308418 | tf_op jit(solution)/shard_map/all_gather | solution.py:137
  215.1 48.6 %reduce.10 = bf16[32,41472]{1,0:T(8,128)(2,1)} reduce(bf16[32,1,41472]{2,1,0:T(2,128)(2,1)} %all-gather.13.cloned.1.call-done, bf16[]{:T(256)} %constant.151), dimensions={1}, to_apply=%all-gather.2.reduce_sub_computation | reduce | bytes 5308418 | tf_op jit(solution)/shard_map/all_gather | solution.py:139
  295.7 48.6 %reduce.11 = bf16[32,41472]{1,0:T(8,128)(2,1)} reduce(bf16[32,1,41472]{2,1,0:T(2,128)(2,1)} %all-gather.15.cloned.1.call-done, bf16[]{:T(256)} %constant.151), dimensions={1}, to_apply=%all-gather.3.reduce_sub_computation | reduce | bytes 5308418 | tf_op jit(solution)/shard_map/all_gather | solution.py:142
  350.9 19.6 multiply_reduce_fusion.1
  386.3 18.5 fusion.19
  412.3 191.8 %all-reduce.24.cloned.1.call-done = (bf16[4958208]{0:T(1024)(128)(2,1)}, bf16[4958208]{0:T(1024)(128)(2,1)}) async-done(((bf16[4958208]{0:T(1024)(128)(2,1)}, bf16[4958208]{0:T(1024)(128)(2,1)}), (bf16[4958208]{0:T(1024)(128)(2,1)}, bf16[4958208]{0:T(1024)(128)(2,1)})) %all-reduce.24.cloned.1.call-update) | async-done | bytes 19832848
  604.2 19.2 reshape.319
  623.4 20.2 reshape.318
  658.3 20.4 %convert_reduce_fusion = (f32[4304]{0:T(1024)}, bf16[729,4304]{1,0:T(8,128)(2,1)}) fusion(f32[729,4304]{1,0:T(8,128)} %fusion.29, f32[4304]{0:T(1024)S(1)} %slice_convert_fusion, bf16[729,1152]{1,0:T(8,128)(2,1)S(1)} %copy-done.21, bf16[4304,1152]{1,0:T(8,128)(2,1)} %reshape.319), kind=kOutput, calls=%fused_computation.21 | convolution fusion | flops 7301226496 | bytes 30456160 | tf_op jit(solution)/shard_map/td,fd->tf/dot_general | solution.py:211
  709.6 29.0 %multiply_reduce_fusion = (f32[16,729]{1,0:T(8,128)S(1)}, f32[16,729,729]{1,2,0:T(8,128)}) fusion(f32[16,729,729]{1,2,0:T(8,128)} %get-tuple-element.59, f32[16,729]{1,0:T(8,128)S(1)} %log_add_fusion, bf16[729,16,72]{0,2,1:T(8,128)(2,1)} %bitcast.90, bf16[729,16,72]{0,2,1:T(8,128)(2,1)} %bitcast.93), kind=kOutput, calls=%fused_computation.1 | convolution fusion | flops 1258440576 | bytes 71476992 | tf_op jit(solution)/shard_map/bqhd,bkhd->bhqk/dot_general | solution.py:246
  738.6 30.2 %multiply_convert_fusion = bf16[16,729,729]{1,2,0:T(8,128)(2,1)} fusion(f32[16,729,729]{1,2,0:T(8,128)} %get-tuple-element.64, f32[16,729,729]{1,2,0:T(8,128)} %get-tuple-element.59, f32[16,729]{1,0:T(8,128)S(1)} %get-tuple-element.63, f32[16,729]{1,0:T(8,128)S(1)} %log_add_fusion), kind=kLoop, calls=%fused_computation | loop fusion | flops 42515280 | bytes 85123872 | tf_op jit(solution)/shard_map/convert_element_type | solution.py:251
  833.5 18.1 fusion.30
  895.2 36.9 %reshape.335 = f32[32,154944]{1,0:T(8,128)} reshape(f32[1152,4304]{1,0:T(8,128)} %fusion.28) | data formatting | bytes 39665664 | tf_op jit(solution)/shard_map/reshape | solution.py:79
  932.3 28.1 %reshape.337 = f32[32,154944]{1,0:T(8,128)} reshape(f32[4304,1152]{1,0:T(8,128)} %fusion.30) | data formatting | bytes 39665664 | tf_op jit(solution)/shard_map/reshape | solution.py:79
  963.2 17.7 dynamic-update-slice.13
  982.4 17.9 dynamic-update-slice.15
  1000.3 17.7 dynamic-update-slice.16
  1019.5 17.7 dynamic-update-slice.18
  1041.7 53.9 %dynamic-update-slice.22 = f32[32,476199]{1,0:T(8,128)} dynamic-update-slice(f32[32,476199]{1,0:T(8,128)} %dynamic-update-slice.21, f32[32,154944]{1,0:T(8,128)} %reshape.335, s32[]{} %constant.161, s32[]{} %constant.172) | dynamic-update-slice | bytes 39665668
  1097.1 53.8 %dynamic-update-slice.24 = f32[32,476199]{1,0:T(8,128)} dynamic-update-slice(f32[32,476199]{1,0:T(8,128)} %dynamic-update-slice.23, f32[32,154944]{1,0:T(8,128)} %reshape.337, s32[]{} %constant.161, s32[]{} %constant.174) | dynamic-update-slice | bytes 39665668
  1160.5 17.0 fusion.16
  1177.5 831.9 %all-reduce.22.cloned.1.call-done = f32[32,476199]{1,0:T(8,128)} async-done(((f32[32,476199]{1,0:T(8,128)}), f32[32,476199]{1,0:T(8,128)}) %all-reduce.22.cloned.1.call-update) | async-done | bytes 60953488
  (266 shorter events, 321.3 us)
Async XLA Ops:
  7.2 8.3 copy-start.25
  7.2 80.7 %all-gather.9.cloned.1.call-start = ((), (), s32[]{:S(2)}) async-start(), calls=%async_computation | async-start | bytes 5474304 | tf_op jit(solution)/shard_map/all_gather | solution.py:140
  9.0 138.2 %all-gather.11.cloned.1.call-start = ((), (), s32[]{:S(2)}) async-start(), calls=%async_computation.1 | async-start | bytes 5474304 | tf_op jit(solution)/shard_map/all_gather | solution.py:137
  10.8 204.4 %all-gather.13.cloned.1.call-start = ((), (), s32[]{:S(2)}) async-start(), calls=%async_computation.2 | async-start | bytes 5474304 | tf_op jit(solution)/shard_map/all_gather | solution.py:139
  12.5 283.2 %all-gather.15.cloned.1.call-start = ((), (), s32[]{:S(2)}) async-start(), calls=%async_computation.3 | async-start | bytes 5474304 | tf_op jit(solution)/shard_map/all_gather | solution.py:142
  14.3 589.9 %all-reduce.24.cloned.1.call-start = ((), (), s32[]{:S(2)}) async-start(), calls=%async_computation.5 | async-start | bytes 39665664
  35.8 45.7 %copy-start = (f32[729,1152]{1,0:T(8,128)S(1)}, f32[729,1152]{1,0:T(8,128)}, u32[]{:S(2)}) copy-start(f32[729,1152]{1,0:T(8,128)} %param.18) | copy-start | bytes 10077700
  35.9 1973.6 %all-reduce.22.cloned.1.call-start = ((), (), s32[]{:S(2)}) async-start(), calls=%async_computation.4 | async-start | bytes 121929728
  83.3 560.3 %copy-start.26 = (f32[1152]{0:T(1024)}, f32[1152]{0:T(1024)S(1)}, u32[]{:S(2)}) copy-start(f32[1152]{0:T(1024)S(1)} %convert_element_type.225) | copy-start | bytes 13828
  83.3 750.1 %copy-start.45 = (f32[4304]{0:T(1024)}, f32[4304]{0:T(1024)S(1)}, u32[]{:S(2)}) copy-start(f32[4304]{0:T(1024)S(1)} %slice_convert_fusion) | copy-start | bytes 51652
  270.5 6.2 copy-start.16
  270.5 6.2 copy-start.19
  386.3 18.6 copy-start.28
  623.4 20.2 copy-start.9
  643.6 14.7 copy-start.21
  768.7 11.2 copy-start.2
  811.7 9.8 slice-start
  821.5 12.0 copy-start.22
  833.5 18.1 copy-start.11
  888.8 6.2 copy-start.48
  888.8 6.3 copy-start.47
  895.2 36.9 %copy-start.44 = (f32[4304]{0:T(1024)S(1)}, f32[4304]{0:T(1024)}, u32[]{:S(2)}) copy-start(f32[4304]{0:T(1024)} %get-tuple-element.42) | copy-start | bytes 51652
  932.2 29.5 %copy-start.35 = (f32[32,36]{1,0:T(8,128)S(1)}, f32[32,36]{1,0:T(8,128)}, u32[]{:S(2)}) copy-start(f32[32,36]{1,0:T(8,128)} %reshape.325) | copy-start | bytes 13828
  1097.1 53.8 %copy-start.34 = (f32[32,36]{1,0:T(8,128)S(1)}, f32[32,36]{1,0:T(8,128)}, u32[]{:S(2)}) copy-start(f32[32,36]{1,0:T(8,128)} %reshape.338) | copy-start | bytes 13828
  (45 other events, 132.2 us)
Sparse Core Ops, SparseCore 0:
  11.5 67.6 all-gather.8
  82.7 64.4 all-gather.10
  150.7 64.4 all-gather.12
  218.5 64.4 all-gather.14
  289.2 314.9 all-reduce.23
  1152.5 856.9 all-reduce.21
where the time goes:
time: 2050 us; the launch traced here: 2030 us
  waiting for transfers between devices  1040 us (51%)
  local copies, waits for them, and re-layouts  415 us (20%)
  other arithmetic  260 us (13%)
  matrix products  260 us (13%)
  blocking collectives  42.9 us (2%)
    unnamed x8, waiting for transfers between devices  1020 us
    unnamed x166, local copies, waits for them, and re-layouts  224 us
    reshape x15, local copies, waits for them, and re-layouts, owned_sums(): pieces.append(piece.reshape(count, width))  90.7 us
    reshape x6, local copies, waits for them, and re-layouts, unpack_flat(): return flat[:length].reshape(shape_dims)  65.5 us
    dot_general x6, matrix products, product(): return jnp.dot(left, right, preferred_element_type=jnp.float32)  50.5 us
    all_gather x1, other arithmetic, on_device(): lax.all_gather(narrow[2], 'fsdp', axis=0, tiled=True)  48.8 us
    all_gather x1, other arithmetic, on_device(): lax.all_gather(narrow[5], 'fsdp', axis=0, tiled=True)  48.6 us
    all_gather x1, other arithmetic, on_device(): lax.all_gather(narrow[7], 'fsdp', axis=0, tiled=True)  48.6 us
  transfers between devices with their start and end apart: 6, of which 4 were waited for; matrix products, arithmetic and copies ran while one was open for 18% of the time, Pallas kernels for 0%

commit v1 on v0

v1 whole, which is shorter than its diff:
```python
import functools
import itertools
import jax
import jax.numpy as jnp
from jax import lax
from jax.sharding import PartitionSpec as P
from jax.experimental import pallas as pl
from jax.experimental.pallas import tpu as pltpu
D=1152; HEADS=16; HEAD_DIM=72; LANES=128
NEG=-1e30
LOG2E=1.4426950408889634
def nt(a,b): return lax.dot_general(a,b,(((1,),(1,)),((),())),preferred_element_type=jnp.float32)
def nn(a,b): return lax.dot_general(a,b,(((1,),(0,)),((),())),preferred_element_type=jnp.float32)

def fill_heads(dst, src, col, tokens, fill):
    rows=dst.shape[1]
    for h in range(HEADS):
        if fill is not None:
            dst[h]=fill
        dst[h,0:tokens,0:HEAD_DIM]=src[:,col+h*HEAD_DIM:col+(h+1)*HEAD_DIM]

def pad_values(rows, tokens, kind):
    lane=lax.broadcasted_iota(jnp.int32,(rows,LANES),1)
    row=lax.broadcasted_iota(jnp.int32,(rows,LANES),0)
    if kind=="query":
        v=jnp.where(lane==HEAD_DIM,1.0,0.0)
    elif kind=="key":
        v=jnp.where((lane==HEAD_DIM)&(row>=tokens),NEG,0.0)
    else:
        v=jnp.zeros((rows,LANES),jnp.float32)
    return v.astype(jnp.bfloat16)

def fwd_kernel(tokens, krows, qrows, per, qkv_ref, mixed_ref, lse_ref, qs, ks, vs, os):
    step=pl.program_id(0)
    @pl.when(step==0)
    def _():
        fill_heads(qs,qkv_ref,0,tokens,pad_values(qrows,tokens,"query"))
        fill_heads(ks,qkv_ref,D,tokens,pad_values(krows,tokens,"key"))
        zero=pad_values(krows,tokens,"value")
        for h in range(HEADS):
            vs[h]=zero
            vs[h,0:tokens,0:HEAD_DIM]=qkv_ref[:,2*D+h*HEAD_DIM:2*D+(h+1)*HEAD_DIM]
    c=HEAD_DIM**-0.5*LOG2E
    for j in range(per):
        h=step*per+j
        s=nt(ks[h],qs[h])
        m=jnp.max(s,axis=0,keepdims=True)
        e=jnp.exp2((s-m)*c)
        l=jnp.sum(e,axis=0,keepdims=True)
        p=(e*(1.0/l)).astype(jnp.bfloat16)
        vt=vs[h].T
        ot=nn(vt,p)
        os[h]=ot.T.astype(jnp.bfloat16)
        lse_ref[j]=m*c+jnp.log2(l)
    @pl.when(step==pl.num_programs(0)-1)
    def _():
        for h in range(HEADS):
            mixed_ref[:,h*HEAD_DIM:(h+1)*HEAD_DIM]=os[h,0:tokens,0:HEAD_DIM]

def attn_fwd(qkv, per=1):
    tokens=qkv.shape[0]
    krows=-(-tokens//16)*16; qrows=-(-tokens//128)*128
    return pl.pallas_call(functools.partial(fwd_kernel,tokens,krows,qrows,per),
        grid=(HEADS//per,),
        in_specs=[pl.BlockSpec(qkv.shape,lambda i:(0,0),pipeline_mode=pl.Buffered(1))],
        out_specs=[pl.BlockSpec((tokens,D),lambda i:(0,0),pipeline_mode=pl.Buffered(1)),pl.BlockSpec((per,1,qrows),lambda i:(i,0,0))],
        out_shape=[jax.ShapeDtypeStruct((tokens,D),jnp.bfloat16),jax.ShapeDtypeStruct((HEADS,1,qrows),jnp.float32)],
        scratch_shapes=[pltpu.VMEM((HEADS,qrows,LANES),jnp.bfloat16),pltpu.VMEM((HEADS,krows,LANES),jnp.bfloat16),
                        pltpu.VMEM((HEADS,krows,LANES),jnp.bfloat16),pltpu.VMEM((HEADS,qrows,LANES),jnp.bfloat16)],
        compiler_params=pltpu.CompilerParams(vmem_limit_bytes=56<<20,dimension_semantics=("arbitrary",)),
        cost_estimate=pl.CostEstimate(flops=4*HEADS*qrows*krows*LANES,bytes_accessed=4*tokens*D*2,transcendentals=HEADS*qrows*krows),
        name="attention_forward")(qkv)

def bwd_kernel(tokens, krows, qrows, per, qkv_ref, go_ref, lse_ref, dqkv_ref, qs, ks, vs, gs):
    step=pl.program_id(0)
    @pl.when(step==0)
    def _():
        fill_heads(qs,qkv_ref,0,tokens,pad_values(qrows,tokens,"query"))
        fill_heads(ks,qkv_ref,D,tokens,pad_values(krows,tokens,"key"))
        fill_heads(vs,qkv_ref,2*D,tokens,pad_values(krows,tokens,"value"))
        fill_heads(gs,go_ref,0,tokens,pad_values(qrows,tokens,"value"))
    scale=HEAD_DIM**-0.5
    c=scale*LOG2E
    for j in range(per):
        h=step*per+j
        q=qs[h]; k=ks[h]; v=vs[h]; g=gs[h]
        s=nt(k,q)
        p=jnp.exp2(s*c-lse_ref[j])
        dp=nt(v,g)
        dv=nn(p.astype(jnp.bfloat16),g)
        delta=jnp.sum(p*dp,axis=0,keepdims=True)
        ds=(p*(dp-delta)).astype(jnp.bfloat16)
        dk=nn(ds,q)*scale
        dqt=nn(k.T,ds)*scale
        qs[h]=dqt.T.astype(jnp.bfloat16)
        ks[h]=dk.astype(jnp.bfloat16)
        vs[h]=dv.astype(jnp.bfloat16)
    @pl.when(step==pl.num_programs(0)-1)
    def _():
        for i,r in enumerate((qs,ks,vs)):
            for h in range(HEADS):
                dqkv_ref[:,i*D+h*HEAD_DIM:i*D+(h+1)*HEAD_DIM]=r[h,0:tokens,0:HEAD_DIM]

def attn_bwd(qkv, gmixed, lse, per=1):
    tokens=qkv.shape[0]
    krows=-(-tokens//16)*16; qrows=-(-tokens//128)*128
    return pl.pallas_call(functools.partial(bwd_kernel,tokens,krows,qrows,per),
        grid=(HEADS//per,),
        in_specs=[pl.BlockSpec(qkv.shape,lambda i:(0,0),pipeline_mode=pl.Buffered(1)),pl.BlockSpec(gmixed.shape,lambda i:(0,0),pipeline_mode=pl.Buffered(1)),
                  pl.BlockSpec((per,1,qrows),lambda i:(i,0,0))],
        out_specs=pl.BlockSpec((tokens,3*D),lambda i:(0,0),pipeline_mode=pl.Buffered(1)),
        out_shape=jax.ShapeDtypeStruct((tokens,3*D),jnp.bfloat16),
        scratch_shapes=[pltpu.VMEM((HEADS,qrows,LANES),jnp.bfloat16),pltpu.VMEM((HEADS,krows,LANES),jnp.bfloat16),
                        pltpu.VMEM((HEADS,krows,LANES),jnp.bfloat16),pltpu.VMEM((HEADS,qrows,LANES),jnp.bfloat16)],
        compiler_params=pltpu.CompilerParams(vmem_limit_bytes=56<<20,dimension_semantics=("arbitrary",)),
        cost_estimate=pl.CostEstimate(flops=10*HEADS*qrows*krows*LANES,bytes_accessed=7*tokens*D*2,transcendentals=HEADS*qrows*krows),
        name="attention_backward")(qkv,gmixed,lse)


FF = 4304
GROUPS = 16
FF_GROUP = FF // GROUPS
FF_ROWS = 272
FF_PAD = GROUPS * FF_ROWS
PAIR_ROWS = D // GROUPS
HALF_UP = FF_PAD // 2
HALF_DOWN = FF_ROWS // 2
SQUARE_HALF = 2 * D
EXTRA = 128
VECTORS = (0, 1, 3, 6, 8, 9, 10, 12, 14)
bf16 = jnp.bfloat16
f32 = jnp.float32


def product(left, right):
    return jnp.dot(left, right, preferred_element_type=f32)


def product_t(left, right):
    return lax.dot_general(left, right, (((0,), (0,)), ((), ())), preferred_element_type=f32)


def product_bt(left, right):
    return lax.dot_general(left, right, (((1,), (1,)), ((), ())), preferred_element_type=f32)


def swap(value, mask):
    devices = lax.axis_size("fsdp")
    return lax.ppermute(value, "fsdp", [(i, i ^ mask) for i in range(devices)])


def pad_hidden(columns):
    rows = columns.shape[0]
    grouped = columns.reshape(rows, GROUPS, FF_GROUP)
    return jnp.pad(grouped, ((0, 0), (0, 0), (0, FF_ROWS - FF_GROUP))).reshape(rows, FF_PAD)


def trim_hidden(columns):
    rows = columns.shape[0]
    return columns.reshape(rows, GROUPS, FF_ROWS)[:, :, :FF_GROUP].reshape(rows, FF)


def place_kernel(kind, coords, *refs):
    sources, targets, sems = refs[:8], refs[8:-1], refs[-1]
    core, x, y, z = coords[0], coords[1], coords[2], coords[3]
    copies = []
    for stream, part, near, dz in itertools.product(range(2), range(4), range(2), range(4)):
        src = sources[4 * stream + part].at[near * 4 + dz]
        owner = core if part < 2 else 1 - core
        far = part % 2
        dx, dy = (near, far) if stream == 0 else (far, near)
        chip = ((z ^ dz) * 2 + (y ^ dy)) * 2 + (x ^ dx)
        sem = sems.at[len(copies)]
        cols = src.shape[-1]
        if kind == "down":
            groups = src.shape[0]
            first = PAIR_ROWS // 8 if stream else 0
            dst = targets[0].at[chip * 2 + owner, first : first + groups]
        elif kind == "up":
            col = owner * HALF_UP + (D if stream else 0)
            dst = targets[0].at[chip, :, pl.ds(pl.multiple_of(col, 128), cols)]
        elif stream == 0:
            col = owner * SQUARE_HALF
            dst = targets[0].at[chip, :, pl.ds(pl.multiple_of(col, 128), cols)]
        else:
            dst = targets[0].at[chip, :, pl.ds(D, cols)]
            copies.append(pltpu.make_async_copy(src, dst, sem))
            last = pltpu.make_async_copy(src, targets[1].at[chip], sem)
            pl.when(owner == 0)(copies[-1].start)
            pl.when(owner == 1)(last.start)
            continue
        copies.append(pltpu.make_async_copy(src, dst, sem))
        copies[-1].start()
    for copy in copies:
        copy.wait()


def place(streams, coords, kind, shapes):
    sources = list(streams[0]) + list(streams[1])
    if kind == "down":
        sources = [s.reshape(8, -1, 8, D) for s in sources]
    size = sum(s.size for s in sources) * 2
    return pl.pallas_call(
        functools.partial(place_kernel, kind),
        in_specs=[pl.BlockSpec(memory_space=pltpu.SMEM)]
        + [pl.BlockSpec(memory_space=pltpu.HBM)] * 8,
        out_specs=[pl.BlockSpec(memory_space=pltpu.HBM)] * len(shapes),
        out_shape=[jax.ShapeDtypeStruct(s, bf16) for s in shapes],
        scratch_shapes=[pltpu.SemaphoreType.DMA((64,))],
        cost_estimate=pl.CostEstimate(flops=0, bytes_accessed=2 * size, transcendentals=0),
        name="place_" + kind,
    )(coords, *sources)


def spread(block, cut, axis):
    parts = [block] + [swap(block, 8 * step) for step in (1, 2, 3)]
    streams = []
    for stream in range(2):
        if axis == 1:
            own = jnp.stack([p[:, :cut] if stream == 0 else p[:, cut:] for p in parts])
        else:
            own = jnp.stack([p[:cut] if stream == 0 else p[cut:] for p in parts])
        near, far = (2, 4) if stream == 0 else (4, 2)
        first = jnp.concatenate([own, swap(own, near)])
        second = swap(first, far)
        streams.append((first, second, swap(first, 1), swap(second, 1)))
    return streams


def pick(value, index, axis):
    return lax.dynamic_index_in_dim(value, index, axis, keepdims=False)


def collect(keep, send, coords, cut, axis):
    core, x, y, z = coords
    other = swap(send, 1)
    rows, cols = keep.shape[1:]
    whole = (keep.astype(f32) + other.astype(f32)).reshape(4, 2, 2, rows, cols)
    results = []
    for stream in range(2):
        if axis == 1:
            value = whole[..., :cut] if stream == 0 else whole[..., cut:]
        else:
            value = whole[..., :cut, :] if stream == 0 else whole[..., cut:, :]
        if stream == 0:
            got = swap(pick(value, 1 - y, 1).astype(bf16), 4)
            value = pick(value, y, 1) + got.astype(f32)
            got = swap(pick(value, 1 - x, 1).astype(bf16), 2)
            value = pick(value, x, 1) + got.astype(f32)
        else:
            got = swap(pick(value, 1 - x, 2).astype(bf16), 2)
            value = pick(value, x, 2) + got.astype(f32)
            got = swap(pick(value, 1 - y, 1).astype(bf16), 4)
            value = pick(value, y, 1) + got.astype(f32)
        results.append(value)
    value = jnp.concatenate(results, axis=2 if axis == 1 else 1)
    total = pick(value, z, 0)
    for step in (1, 2, 3):
        total = total + swap(pick(value, z ^ step, 0).astype(bf16), 8 * step).astype(f32)
    return total


def fetch_pairs(narrow, core):
    q, k, v, o = (narrow[i].reshape(PAIR_ROWS // 2, D) for i in (2, 4, 5, 7))
    up = pad_hidden(narrow[11].reshape(PAIR_ROWS // 2, FF))
    down = narrow[13]
    first = jnp.concatenate([q, k, up[:, :HALF_UP]], axis=1)
    second = jnp.concatenate([v, o, up[:, HALF_UP:]], axis=1)
    lead = D * HALF_DOWN - down.shape[0]
    rows = PAIR_ROWS // 2
    tail = jnp.pad(down[:lead], (0, rows * EXTRA - lead)).reshape(rows, EXTRA)
    is_first = core == 0
    mine = jnp.where(is_first, first, second)
    theirs = jnp.where(is_first, second, first)
    got = swap(jnp.concatenate([theirs, tail], axis=1), 1)
    other = got[:, : mine.shape[1]]
    block = jnp.where(is_first, jnp.concatenate([mine, other]), jnp.concatenate([other, mine]))
    extra = got[:, mine.shape[1] :].reshape(-1)[:lead]
    end = jnp.zeros((D * HALF_DOWN - (down.shape[0] - lead),), bf16)
    down_block = jnp.where(
        is_first, jnp.concatenate([down, extra]), jnp.concatenate([down[lead:], end])
    ).reshape(HALF_DOWN, D)
    return block[:, :SQUARE_HALF], block[:, SQUARE_HALF:], down_block


def unpair(total, core):
    rows = total.shape[0] // 2
    keep = lax.dynamic_slice_in_dim(total, core * rows, rows, 0)
    got = swap(lax.dynamic_slice_in_dim(total, (1 - core) * rows, rows, 0), 1)
    is_first = core == 0
    return jnp.where(is_first, keep, got), jnp.where(is_first, got, keep)


def normalize(values):
    centre = jnp.mean(values, axis=-1, keepdims=True)
    centered = values - centre
    spread_sq = jnp.mean(centered * centered, axis=-1, keepdims=True)
    inverse = lax.rsqrt(spread_sq + 1e-06)
    return centered * inverse, inverse


def normalize_back(grad, gain, xhat, inverse):
    scaled = grad * gain
    first = jnp.mean(scaled, axis=-1, keepdims=True)
    second = jnp.mean(scaled * xhat, axis=-1, keepdims=True)
    return inverse * (scaled - first - xhat * second)


def gather_vectors(narrow):
    widths = [narrow[i].shape[0] for i in VECTORS]
    joined = jnp.concatenate([narrow[i] for i in VECTORS])
    joined = jnp.pad(joined, (0, 2048 - joined.shape[0])).reshape(16, 128)
    whole = lax.all_gather(joined, "fsdp", axis=0, tiled=True).reshape(-1, 2048)
    found = {}
    position = 0
    for i, width in zip(VECTORS, widths):
        found[i] = whole[:, position : position + width].reshape(-1).astype(f32)
        position += width
    return found


def on_device(*args):
    devices = lax.axis_size("fsdp")
    tokens, image_valid = args[0], args[1]
    shards = args[2:17]
    cotangent = args[17]
    staged = devices == 32
    widths = [piece.shape[0] for piece in shards]
    narrow = [piece.astype(bf16) for piece in shards]
    index = lax.axis_index("fsdp")
    core, x, y, z = index % 2, (index // 2) % 2, (index // 4) % 2, index // 8
    coords = (core, x, y, z)
    image_count = image_valid.shape[0]
    seq_len = tokens.shape[0] // image_count
    weight_img = jnp.repeat(image_valid.astype(f32), seq_len)[:, None]

    vectors = gather_vectors(narrow)
    if staged:
        where = jnp.stack(coords).astype(jnp.int32)
        square_block, up_block, down_block = fetch_pairs(narrow, core)
        blocks = (GROUPS, PAIR_ROWS)
        weight_qkv, weight_o = place(
            spread(square_block, D, 1), where, "square", [blocks + (3 * D,), blocks + (D,)]
        )
        weight_qkv, weight_o = weight_qkv.reshape(D, 3 * D), weight_o.reshape(D, D)
        (weight_up,) = place(spread(up_block, D, 1), where, "up", [blocks + (FF_PAD,)])
        weight_up = weight_up.reshape(D, FF_PAD)
        (weight_down,) = place(
            spread(down_block, PAIR_ROWS, 0), where, "down", [(2 * GROUPS, HALF_DOWN // 8, 8, D)]
        )
        weight_down = weight_down.reshape(FF_PAD, D)
    else:
        whole = {
            i: lax.all_gather(narrow[i], "fsdp", axis=0, tiled=True) for i in (2, 4, 5, 7, 11, 13)
        }
        square = [whole[i][: D * D].reshape(D, D) for i in (2, 4, 5, 7)]
        weight_qkv = jnp.concatenate(square[:3], axis=1)
        weight_o = square[3]
        weight_up = pad_hidden(whole[11][: D * FF].reshape(D, FF))
        weight_down = pad_hidden(whole[13][: D * FF].reshape(FF, D).T).T

    vec = lambda i: vectors[i][:D]
    gain_one, shift_one, gain_two, shift_two = vec(0), vec(1), vec(9), vec(10)
    bias_qkv = jnp.concatenate([vec(3), jnp.zeros((D,), f32), vec(6)])
    bias_o, bias_down = vec(8), vec(14)
    bias_up = pad_hidden(vectors[12][:FF].reshape(1, FF))

    xhat_one, inverse_one = normalize(tokens)
    normed = (xhat_one * gain_one + shift_one).astype(bf16)
    qkv = (product(normed, weight_qkv) + bias_qkv).astype(bf16)
    mixed, lse = attn_fwd(qkv, 2)
    resid = tokens + product(mixed, weight_o) + bias_o
    xhat_two, inverse_two = normalize(resid)
    normed_two = (xhat_two * gain_two + shift_two).astype(bf16)
    pre = product(normed_two, weight_up) + bias_up
    hidden, gelu_back = jax.vjp(lambda t: jax.nn.gelu(t, approximate=True), pre)
    hidden = hidden.astype(bf16)
    layer_out = weight_img * (resid + product(hidden, weight_down) + bias_down)

    grad_out = weight_img * cotangent
    grad_branch = grad_out.astype(bf16)
    grads = {14: jnp.sum(grad_branch.astype(f32), axis=0)}
    down_grad = product_t(hidden, grad_branch).astype(bf16)
    grad_pre = gelu_back(product_bt(grad_branch, weight_down))[0].astype(bf16)
    up_bias_grad = jnp.sum(grad_pre.astype(f32), axis=0)
    up_grad = product_t(normed_two, grad_pre).astype(bf16)
    grad_normed_two = product_bt(grad_pre, weight_up)
    grads[9] = jnp.sum(grad_normed_two * xhat_two, axis=0)
    grads[10] = jnp.sum(grad_normed_two, axis=0)
    grad_resid = grad_out + normalize_back(grad_normed_two, gain_two, xhat_two, inverse_two)
    grad_attn = grad_resid.astype(bf16)
    grads[8] = jnp.sum(grad_attn.astype(f32), axis=0)
    o_grad = product_t(mixed, grad_attn).astype(bf16)
    grad_mixed = product_bt(grad_attn, weight_o).astype(bf16)
    grad_qkv = attn_bwd(qkv, grad_mixed, lse, 2)
    qkv_bias_grad = jnp.sum(grad_qkv.astype(f32), axis=0)
    grads[3], grads[6] = qkv_bias_grad[:D], qkv_bias_grad[2 * D :]
    qkv_grad = product_t(normed, grad_qkv).astype(bf16)
    grad_normed = product_bt(grad_qkv, weight_qkv)
    grads[0] = jnp.sum(grad_normed * xhat_one, axis=0)
    grads[1] = jnp.sum(grad_normed, axis=0)
    tokens_grad = grad_resid + normalize_back(grad_normed, gain_one, xhat_one, inverse_one)
    grads[12] = trim_hidden(up_bias_grad.reshape(1, FF_PAD)).reshape(FF)

    rows = []
    for i in VECTORS:
        row = grads[i]
        row = jnp.pad(row, (0, widths[i] * devices - row.shape[0]))
        rows.append(row.reshape(devices, widths[i]))
    rows = jnp.concatenate(rows, axis=1)
    owned = [None] * 15
    if staged:
        down_halves = down_grad.reshape(GROUPS, 2, HALF_DOWN, D)
        down_total = collect(
            pick(down_halves, core, 1), pick(down_halves, 1 - core, 1), coords, PAIR_ROWS, 0
        )
        flat = down_total.reshape(-1)
        size = widths[13]
        lead = flat.shape[0] - size
        got = swap(flat[size:], 1)
        owned[13] = jnp.where(core == 0, flat[:size], jnp.concatenate([got, flat[: size - lead]]))

        up_grad = up_grad.reshape(GROUPS, PAIR_ROWS, FF_PAD)
        up_total = collect(
            lax.dynamic_slice_in_dim(up_grad, core * HALF_UP, HALF_UP, 2),
            lax.dynamic_slice_in_dim(up_grad, (1 - core) * HALF_UP, HALF_UP, 2),
            coords,
            D,
            1,
        )
        owned[11] = trim_hidden(jnp.concatenate(unpair(up_total, core), axis=1)).reshape(-1)

        rows = jnp.pad(rows, ((0, 0), (0, PAIR_ROWS // 2 * EXTRA - rows.shape[1])))
        rows = rows.reshape(D, EXTRA).astype(bf16)
        first = jnp.concatenate([qkv_grad[:, :SQUARE_HALF], rows], axis=1)
        second = jnp.concatenate([qkv_grad[:, SQUARE_HALF:], o_grad, jnp.zeros_like(rows)], axis=1)
        shape = (GROUPS, PAIR_ROWS, SQUARE_HALF + EXTRA)
        square_total = collect(
            jnp.where(core == 0, first, second).reshape(shape),
            jnp.where(core == 0, second, first).reshape(shape),
            coords,
            D + EXTRA,
            1,
        )
        left, right = unpair(square_total, core)
        owned[2] = left[:, :D].reshape(-1)
        owned[4] = left[:, D : 2 * D].reshape(-1)
        owned[5] = right[:, :D].reshape(-1)
        owned[7] = right[:, D : 2 * D].reshape(-1)
        small = left[:, 2 * D :].reshape(-1)
    else:
        scatter = lambda value: lax.psum_scatter(
            value.astype(f32).reshape(-1), "fsdp", scatter_dimension=0, tiled=True
        )
        fill = lambda value, i: jnp.pad(
            value.reshape(-1), (0, widths[i] * devices - value.size)
        )
        for position, i in enumerate((2, 4, 5)):
            owned[i] = scatter(fill(qkv_grad[:, position * D : (position + 1) * D], i))
        owned[7] = scatter(fill(o_grad, 7))
        owned[11] = scatter(fill(trim_hidden(up_grad), 11))
        owned[13] = scatter(fill(trim_hidden(down_grad.T).T, 13))
        small = scatter(rows)
    position = 0
    for i in VECTORS:
        owned[i] = small[position : position + widths[i]]
        position += widths[i]
    return (layer_out, tokens_grad, *owned)


def solution(mesh):
    row, flat = P("fsdp", None), P("fsdp")
    in_specs = (row, flat) + (flat,) * 15 + (row,)
    out_specs = (row, row) + (flat,) * 15
    return jax.shard_map(
        on_device, mesh=mesh, in_specs=in_specs, out_specs=out_specs, check_vma=False
    )
```

time: 2050 us -> 1820 us (0.89)
  Pallas kernels: 0 us -> 1010 us
  waiting for transfers between devices: 1040 us -> 371 us
  local copies, waits for them, and re-layouts: 415 us -> 127 us
  other arithmetic: 260 us -> 73.4 us
  matrix products: 260 us -> 141 us
  starting transfers between devices: 0.25 us -> 53.7 us
    unnamed x8 -> x0, waiting for transfers between devices: 1020 us -> none
    pallas_call x0 -> x5, Pallas kernels: none -> 1010 us  [the longest x3 936 us: place(): pl.pallas_call(functools.partial(place_kernel, kind), in_specs=[pl.BlockS...]
    ppermute x0 -> x61, waiting for transfers between devices: none -> 371 us  [swap(): return lax.ppermute(value, 'fsdp', [(i, i ^ mask) for i in range(devices)])]
    unnamed x166 -> x207, local copies, waits for them, and re-layouts: 224 us -> 28.1 us
    all_gather x4 -> x0, other arithmetic: 195 us -> none  [the longest x1 48.8 us: on_device(): lax.all_gather(narrow[2], 'fsdp', axis=0, tiled=True)]
    reshape x21 -> x25, local copies, waits for them, and re-layouts: 156 us -> 16.8 us  [the longest x4 5.96 us: fetch_pairs(): q, k, v, o = (narrow[i].reshape(PAIR_ROWS // 2, D) for i in (2, 4, 5, 7))]
    dot_general x23 -> x12, matrix products: 248 us -> 141 us  [the longest x4 54.1 us: product_bt(): lax.dot_general(left, right, (((1,), (1,)), ((), ())), preferred_element_...]
    ppermute x0 -> x61, starting transfers between devices: none -> 53.7 us  [swap(): return lax.ppermute(value, 'fsdp', [(i, i ^ mask) for i in range(devices)])]
  transfers between devices with their start and end apart: 6 -> 61, of which waited for: 4 -> 22; matrix products, arithmetic and copies ran while one was open for 18% -> 9% of each run, Pallas kernels for 0% -> 34%
where the time goes in v1:
time: 1820 us; the launch traced here: 1810 us
  Pallas kernels  1010 us (55%)
  waiting for transfers between devices  371 us (20%)
  matrix products  141 us (8%)
  local copies, waits for them, and re-layouts  127 us (7%)
  other arithmetic  73.4 us (4%)
  starting transfers between devices  53.7 us (3%)
  blocking collectives  35.9 us (2%)
    pallas_call x3, Pallas kernels, place(): pl.pallas_call(functools.partial(place_kernel, kind), in_specs=[pl.BlockS...  936 us
    ppermute x61, waiting for transfers between devices, swap(): return lax.ppermute(value, 'fsdp', [(i, i ^ mask) for i in range(devices)])  371 us
    dot_general x4, matrix products, product_bt(): lax.dot_general(left, right, (((1,), (1,)), ((), ())), preferred_element_...  54.1 us
    ppermute x61, starting transfers between devices, swap(): return lax.ppermute(value, 'fsdp', [(i, i ^ mask) for i in range(devices)])  53.7 us
    dot_general x4, matrix products, product(): return jnp.dot(left, right, preferred_element_type=f32)  44.1 us
    pallas_call x1, Pallas kernels, attn_bwd(): pl.pallas_call(functools.partial(bwd_kernel, tokens, krows, qrows, per),...  44 us
    dot_general x4, matrix products, product_t(): lax.dot_general(left, right, (((0,), (0,)), ((), ())), preferred_element_...  43.1 us
  transfers between devices with their start and end apart: 61, of which 22 were waited for; matrix products, arithmetic and copies ran while one was open for 9% of the time, Pallas kernels for 34%

profile of v1, /device:TPU:8, one launch (start us, length us, event | category | flops | bytes accessed | tf_op | source)
XLA Modules:
  0.0 1812.5 jit_solution(6147465912940277715)
XLA Ops:
  27.5 35.9 %all_gather.3 = bf16[512,128]{1,0:T(8,128)(2,1)S(1)} all-gather(bf16[16,128]{1,0:T(8,128)(2,1)S(1)} %pad_bitcast_fusion), channel_id=1, replica_groups=mesh['fsdp'=32] {'fsdp'}, dimensions={0}, use_global_device_ids=true | all-gather | bytes 135168 | tf_op jit(solution)/shard_map/all_gather | solution.py:313
  114.6 19.0 %collective-permute-done.25 = bf16[136,1152]{1,0:T(8,128)(2,1)} collective-permute-done((bf16[136,1152]{1,0:T(8,128)(2,1)}, bf16[136,1152]{1,0:T(8,128)(2,1)}, u32[]{:S(2)}, u32[]{:S(2)}) %collective-permute-start.25) | collective-permute-done | bytes 313376 | tf_op jit(solution)/shard_map/ppermute | solution.py:149
  135.5 11.8 collective-permute-done.24
  210.9 61.9 %collective-permute-done.4 = bf16[4,72,1152]{2,1,0:T(8,128)(2,1)S(1)} collective-permute-done((bf16[4,72,1152]{2,1,0:T(8,128)(2,1)S(1)}, bf16[4,72,1152]{2,1,0:T(8,128)(2,1)S(1)}, u32[]{:S(2)}, u32[]{:S(2)}) %collective-permute-start.4) | collective-permute-done | bytes 663584 | tf_op jit(solution)/shard_map/ppermute | solution.py:149
  281.2 23.6 %collective-permute-done.27 = bf16[8,72,1152]{2,1,0:T(8,128)(2,1)S(1)} collective-permute-done((bf16[8,72,1152]{2,1,0:T(8,128)(2,1)S(1)}, bf16[8,72,1152]{2,1,0:T(8,128)(2,1)S(1)}, u32[]{:S(2)}, u32[]{:S(2)}) %collective-permute-start.27) | collective-permute-done | bytes 1327136 | tf_op jit(solution)/shard_map/ppermute | solution.py:149
  305.1 28.2 %collective-permute-done.16.refs_1_ = bf16[8,72,1152]{2,1,0:T(8,128)(2,1)} collective-permute-done((bf16[8,72,1152]{2,1,0:T(8,128)(2,1)S(1)}, bf16[8,72,1152]{2,1,0:T(8,128)(2,1)}, u32[]{:S(2)}, u32[]{:S(2)}) %collective-permute-start.16) | collective-permute-done | bytes 1327136 | tf_op jit(solution)/shard_map/ppermute | solution.py:149
  334.9 26.5 %collective-permute-done.5.refs_1_ = bf16[8,72,1152]{2,1,0:T(8,128)(2,1)} collective-permute-done((bf16[8,72,1152]{2,1,0:T(8,128)(2,1)}, bf16[8,72,1152]{2,1,0:T(8,128)(2,1)}, u32[]{:S(2)}, u32[]{:S(2)}) %collective-permute-start.5) | collective-permute-done | bytes 1327136 | tf_op jit(solution)/shard_map/ppermute | solution.py:149
  365.2 306.1 %place_down.1 = bf16[32,17,8,1152]{3,2,1,0:T(8,128)(2,1)} custom-call(s32[4]{0:T(128)} %pad_add_fusion.coords, bf16[8,9,8,1152]{3,2,1,0:T(8,128)(2,1)} %copy-done.25, bf16[8,9,8,1152]{3,2,1,0:T(8,128)(2,1)} %bitcast.286, bf16[8,9,8,1152]{3,2,1,0:T(8,128)(2,1)} %bitcast.287, bf16[8,9,8,1152]{3,2,1,0:T(8,128)(2,1)} %bitcast.288, ...), custom_call_target="tpu_custom_call" | custom-call | bytes 20054016 | tf_op jit(solution)/shard_map/place_down/pallas_call | solution.py:203
  671.3 306.1 %place_up.1 = bf16[16,72,4352]{2,1,0:T(8,128)(2,1)} custom-call(s32[4]{0:T(128)} %pad_add_fusion.coords, bf16[8,72,1152]{2,1,0:T(8,128)(2,1)} %copy-done.27, bf16[8,72,1152]{2,1,0:T(8,128)(2,1)} %collective-permute-done.16.refs_1_, bf16[8,72,1152]{2,1,0:T(8,128)(2,1)} %copy-done.36, bf16[8,72,1152]{2,1,0:T(8,128)(2,1)} %collective-permute-done.18.refs_3_, ...), custom_call_target="tpu_custom_call" | custom-call | bytes 20054016 | tf_op jit(solution)/shard_map/place_up/pallas_call | solution.py:203
  977.5 324.0 %place_square.1 = (bf16[16,72,3456]{2,1,0:T(8,128)(2,1)}, bf16[16,72,1152]{2,1,0:T(8,128)(2,1)}) custom-call(s32[4]{0:T(128)} %pad_add_fusion.coords, bf16[8,72,1152]{2,1,0:T(8,128)(2,1)} %constant_dynamic-update-slice_fusion.refs_0_, bf16[8,72,1152]{2,1,0:T(8,128)(2,1)} %collective-permute-done.5.refs_1_, ...), custom_call_target="tpu_custom_call" | custom-call | bytes 21233664 | tf_op jit(solution)/shard_map/place_square/pallas_call | solution.py:203
  1301.5 13.0 add_convert_fusion.qkv_ref
  1314.4 27.5 %attention_forward.1 = (bf16[729,1152]{1,0:T(8,128)(2,1)}, f32[16,1,768]{2,1,0:T(1,128)}) custom-call(bf16[729,3456]{1,0:T(8,128)(2,1)} %add_convert_fusion.qkv_ref), custom_call_target="tpu_custom_call" | custom-call | flops 4630511616 | bytes 6718464 | tf_op jit(solution)/shard_map/attention_forward/pallas_call | solution.py:63
  1359.6 20.3 %fusion.69 = (bf16[4352]{0:T(1024)(128)(2,1)S(1)}, bf16[729,4352]{1,0:T(8,128)(2,1)}) fusion(f32[729,4352]{1,0:T(8,128)} %fusion.67, f32[4352]{0:T(1024)S(1)} %copy-done.52, bf16[729,1152]{1,0:T(8,128)(2,1)} %get-tuple-element.34, bf16[4352,1152]{1,0:T(8,128)(2,1)} %bitcast.276), kind=kOutput, calls=%fused_computation.258 | convolution fusion | flops 7379476480 | bytes 30768384 | tf_op jit(solution)/shard_map/dot_general | solution.py:144
  1379.9 16.3 multiply_reduce_fusion
  1403.8 44.0 %attention_backward.1 = bf16[729,3456]{1,0:T(8,128)(2,1)} custom-call(bf16[729,3456]{1,0:T(8,128)(2,1)} %add_convert_fusion.qkv_ref, bf16[729,1152]{1,0:T(8,128)(2,1)} %convolution_convert_fusion.4.go_ref, f32[16,1,768]{2,1,0:T(1,128)} %get-tuple-element.24.lse_ref), custom_call_target="tpu_custom_call" | custom-call | flops 11576279040 | bytes 11757312 | tf_op jit(solution)/shard_map/attention_backward/pallas_call | solution.py:107
  1447.8 13.7 multiply_reduce_fusion.1
  1480.4 13.6 convolution_convert_fusion.1
  1494.0 13.9 convolution_convert_fusion
  1545.9 14.3 fusion.9
  1599.1 16.4 collective-permute-done.46
  1617.7 23.0 %collective-permute-done.55 = bf16[4,2,64,1152]{3,2,1,0:T(8,128)(2,1)} collective-permute-done((bf16[4,2,64,1152]{3,2,1,0:T(8,128)(2,1)}, bf16[4,2,64,1152]{3,2,1,0:T(8,128)(2,1)}, u32[]{:S(2)}, u32[]{:S(2)}) %collective-permute-start.55) | collective-permute-done | bytes 1179680 | tf_op jit(solution)/shard_map/ppermute | solution.py:149
  1648.5 39.4 %collective-permute-done.47 = bf16[4,72,1024]{2,1,0:T(8,128)(2,1)S(1)} collective-permute-done((bf16[4,72,1024]{2,1,0:T(8,128)(2,1)S(1)}, bf16[4,72,1024]{2,1,0:T(8,128)(2,1)S(1)}, u32[]{:S(2)}, u32[]{:S(2)}) %collective-permute-start.47) | collective-permute-done | bytes 589856 | tf_op jit(solution)/shard_map/ppermute | solution.py:149
  1714.6 27.1 %collective-permute-done.59 = bf16[136,1152]{1,0:T(8,128)(2,1)S(1)} collective-permute-done((bf16[136,1152]{1,0:T(8,128)(2,1)S(1)}, bf16[136,1152]{1,0:T(8,128)(2,1)S(1)}, u32[]{:S(2)}, u32[]{:S(2)}) %collective-permute-start.59) | collective-permute-done | bytes 313376 | tf_op jit(solution)/shard_map/ppermute | solution.py:149
  1778.9 20.9 %collective-permute-done.41 = bf16[72,2432]{1,0:T(8,128)(2,1)S(1)} collective-permute-done((bf16[72,2432]{1,0:T(8,128)(2,1)S(1)}, bf16[72,2432]{1,0:T(8,128)(2,1)S(1)}, u32[]{:S(2)}, u32[]{:S(2)}) %collective-permute-start.41) | collective-permute-done | bytes 350240 | tf_op jit(solution)/shard_map/ppermute | solution.py:149
  (518 shorter events, 362.8 us)
Async XLA Ops:
  82.2 107.5 %collective-permute-start.1 = (bf16[72,2304]{1,0:T(8,128)(2,1)}, bf16[72,2304]{1,0:T(8,128)(2,1)}, u32[]{:S(2)}, u32[]{:S(2)}) collective-permute-start(bf16[72,2304]{1,0:T(8,128)(2,1)} %slice.326), channel_id=1, source_target_pairs={{0,8},{1,9},{2,10},{3,11},{4,12},{5,13},{6,14},{7,15},{8,0},{9,1},... | collective-permute-start | bytes 995336 | tf_op jit(solution)/shard_map/ppermute | solution.py:149
  89.0 97.5 %collective-permute-start.2 = (bf16[72,2304]{1,0:T(8,128)(2,1)}, bf16[72,2304]{1,0:T(8,128)(2,1)}, u32[]{:S(2)}, u32[]{:S(2)}) collective-permute-start(bf16[72,2304]{1,0:T(8,128)(2,1)} %slice.326), channel_id=1, source_target_pairs={{0,16},{1,17},{2,18},{3,19},{4,20},{5,21},{6,22},{7,23},{8,24},{9,... | collective-permute-start | bytes 995336 | tf_op jit(solution)/shard_map/ppermute | solution.py:149
  89.0 94.4 %collective-permute-start.3 = (bf16[72,2304]{1,0:T(8,128)(2,1)}, bf16[72,2304]{1,0:T(8,128)(2,1)}, u32[]{:S(2)}, u32[]{:S(2)}) collective-permute-start(bf16[72,2304]{1,0:T(8,128)(2,1)} %slice.326), channel_id=1, source_target_pairs={{0,24},{1,25},{2,26},{3,27},{4,28},{5,29},{6,30},{7,31},{8,16},{9,... | collective-permute-start | bytes 995336 | tf_op jit(solution)/shard_map/ppermute | solution.py:149
  193.5 79.4 %collective-permute-start.31 = (bf16[8,64,1152]{2,1,0:T(8,128)(2,1)S(1)}, bf16[8,64,1152]{2,1,0:T(8,128)(2,1)S(1)}, u32[]{:S(2)}, u32[]{:S(2)}) collective-permute-start(bf16[8,64,1152]{2,1,0:T(8,128)(2,1)S(1)} %constant_dynamic-update-slice_fusion.27), channel_id=1, source_target_pairs={{0,2},{1,3},{2,0},{3,1},{4,6},{5,7},{6,4},{7,5},{8,10},{9,11},{10,... | collective-permute-start | bytes 3538952 | tf_op jit(solution)/shard_map/ppermute | solution.py:149
  195.6 77.8 %collective-permute-start.32 = (bf16[8,64,1152]{2,1,0:T(8,128)(2,1)S(1)}, bf16[8,64,1152]{2,1,0:T(8,128)(2,1)S(1)}, u32[]{:S(2)}, u32[]{:S(2)}) collective-permute-start(bf16[8,64,1152]{2,1,0:T(8,128)(2,1)S(1)} %constant_dynamic-update-slice_fusion.27), channel_id=1, source_target_pairs={{0,1},{1,0},{2,3},{3,2},{4,5},{5,4},{6,7},{7,6},{8,9},{9,8},{10,11... | collective-permute-start | bytes 3538952 | tf_op jit(solution)/shard_map/ppermute | solution.py:149
  205.2 69.9 %collective-permute-start.20 = (bf16[8,72,1024]{2,1,0:T(8,128)(2,1)S(1)}, bf16[8,72,1024]{2,1,0:T(8,128)(2,1)S(1)}, u32[]{:S(2)}, u32[]{:S(2)}) collective-permute-start(bf16[8,72,1024]{2,1,0:T(8,128)(2,1)S(1)} %constant_dynamic-update-slice_fusion.15.refs_4_), channel_id=1, source_target_pairs={{0,2},{1,3},{2,0},{3,1},{4,6},{5,7},{6,4},{7,5},{8,10},{9,11},{10,... | collective-permute-start | bytes 3538952 | tf_op jit(solution)/shard_map/ppermute | solution.py:149
  207.1 65.7 %collective-permute-start.4 = (bf16[4,72,1152]{2,1,0:T(8,128)(2,1)S(1)}, bf16[4,72,1152]{2,1,0:T(8,128)(2,1)S(1)}, u32[]{:S(2)}, u32[]{:S(2)}) collective-permute-start(bf16[4,72,1152]{2,1,0:T(8,128)(2,1)S(1)} %pad_maximum_fusion.2), channel_id=1, source_target_pairs={{0,2},{1,3},{2,0},{3,1},{4,6},{5,7},{6,4},{7,5},{8,10},{9,11},{10,... | collective-permute-start | bytes 1990664 | tf_op jit(solution)/shard_map/ppermute | solution.py:149
  209.0 63.9 %collective-permute-start.8 = (bf16[4,72,1152]{2,1,0:T(8,128)(2,1)S(1)}, bf16[4,72,1152]{2,1,0:T(8,128)(2,1)S(1)}, u32[]{:S(2)}, u32[]{:S(2)}) collective-permute-start(bf16[4,72,1152]{2,1,0:T(8,128)(2,1)S(1)} %pad_maximum_fusion.3), channel_id=1, source_target_pairs={{0,4},{1,5},{2,6},{3,7},{4,0},{5,1},{6,2},{7,3},{8,12},{9,13},{10,... | collective-permute-start | bytes 1990664 | tf_op jit(solution)/shard_map/ppermute | solution.py:149
  273.4 59.9 %collective-permute-start.16 = (bf16[8,72,1152]{2,1,0:T(8,128)(2,1)S(1)}, bf16[8,72,1152]{2,1,0:T(8,128)(2,1)}, u32[]{:S(2)}, u32[]{:S(2)}) collective-permute-start(bf16[8,72,1152]{2,1,0:T(8,128)(2,1)S(1)} %constant_dynamic-update-slice_fusion.10.refs_0_), channel_id=1, source_target_pairs={{0,4},{1,5},{2,6},{3,7},{4,0},{5,1},{6,2},{7,3},{8,12},{9,13},{10,... | collective-permute-start | bytes 3981320 | tf_op jit(solution)/shard_map/ppermute | solution.py:149
  275.1 58.2 %collective-permute-start.17 = (bf16[8,72,1152]{2,1,0:T(8,128)(2,1)S(1)}, bf16[8,72,1152]{2,1,0:T(8,128)(2,1)S(1)}, u32[]{:S(2)}, u32[]{:S(2)}) collective-permute-start(bf16[8,72,1152]{2,1,0:T(8,128)(2,1)S(1)} %constant_dynamic-update-slice_fusion.10.refs_0_), channel_id=1, source_target_pairs={{0,1},{1,0},{2,3},{3,2},{4,5},{5,4},{6,7},{7,6},{8,9},{9,8},{10,11... | collective-permute-start | bytes 3981320 | tf_op jit(solution)/shard_map/ppermute | solution.py:149
  280.8 80.6 %collective-permute-start.5 = (bf16[8,72,1152]{2,1,0:T(8,128)(2,1)}, bf16[8,72,1152]{2,1,0:T(8,128)(2,1)}, u32[]{:S(2)}, u32[]{:S(2)}) collective-permute-start(bf16[8,72,1152]{2,1,0:T(8,128)(2,1)} %constant_dynamic-update-slice_fusion.refs_0_), channel_id=1, source_target_pairs={{0,4},{1,5},{2,6},{3,7},{4,0},{5,1},{6,2},{7,3},{8,12},{9,13},{10,... | collective-permute-start | bytes 3981320 | tf_op jit(solution)/shard_map/ppermute | solution.py:149
  304.8 56.6 %collective-permute-start.9 = (bf16[8,72,1152]{2,1,0:T(8,128)(2,1)}, bf16[8,72,1152]{2,1,0:T(8,128)(2,1)}, u32[]{:S(2)}, u32[]{:S(2)}) collective-permute-start(bf16[8,72,1152]{2,1,0:T(8,128)(2,1)} %constant_dynamic-update-slice_fusion.5.refs_4_), channel_id=1, source_target_pairs={{0,2},{1,3},{2,0},{3,1},{4,6},{5,7},{6,4},{7,5},{8,10},{9,11},{10,... | collective-permute-start | bytes 3981320 | tf_op jit(solution)/shard_map/ppermute | solution.py:149
  305.0 56.8 %collective-permute-start.33 = (bf16[8,64,1152]{2,1,0:T(8,128)(2,1)S(1)}, bf16[8,64,1152]{2,1,0:T(8,128)(2,1)S(1)}, u32[]{:S(2)}, u32[]{:S(2)}) collective-permute-start(bf16[8,64,1152]{2,1,0:T(8,128)(2,1)S(1)} %collective-permute-done.31), channel_id=1, source_target_pairs={{0,1},{1,0},{2,3},{3,2},{4,5},{5,4},{6,7},{7,6},{8,9},{9,8},{10,11... | collective-permute-start | bytes 3538952 | tf_op jit(solution)/shard_map/ppermute | solution.py:149
  361.4 616.1 %collective-permute-start.6 = (bf16[8,72,1152]{2,1,0:T(8,128)(2,1)}, bf16[8,72,1152]{2,1,0:T(8,128)(2,1)}, u32[]{:S(2)}, u32[]{:S(2)}) collective-permute-start(bf16[8,72,1152]{2,1,0:T(8,128)(2,1)} %constant_dynamic-update-slice_fusion.refs_0_), channel_id=1, source_target_pairs={{0,1},{1,0},{2,3},{3,2},{4,5},{5,4},{6,7},{7,6},{8,9},{9,8},{10,11... | collective-permute-start | bytes 3981320 | tf_op jit(solution)/shard_map/ppermute | solution.py:149
  361.4 616.1 %collective-permute-start.10 = (bf16[8,72,1152]{2,1,0:T(8,128)(2,1)}, bf16[8,72,1152]{2,1,0:T(8,128)(2,1)}, u32[]{:S(2)}, u32[]{:S(2)}) collective-permute-start(bf16[8,72,1152]{2,1,0:T(8,128)(2,1)} %constant_dynamic-update-slice_fusion.5.refs_4_), channel_id=1, source_target_pairs={{0,1},{1,0},{2,3},{3,2},{4,5},{5,4},{6,7},{7,6},{8,9},{9,8},{10,11... | collective-permute-start | bytes 3981320 | tf_op jit(solution)/shard_map/ppermute | solution.py:149
  361.9 309.4 %collective-permute-start.18 = (bf16[8,72,1152]{2,1,0:T(8,128)(2,1)}, bf16[8,72,1152]{2,1,0:T(8,128)(2,1)}, u32[]{:S(2)}, u32[]{:S(2)}) collective-permute-start(bf16[8,72,1152]{2,1,0:T(8,128)(2,1)} %collective-permute-done.16.refs_1_), channel_id=1, source_target_pairs={{0,1},{1,0},{2,3},{3,2},{4,5},{5,4},{6,7},{7,6},{8,9},{9,8},{10,11... | collective-permute-start | bytes 3981320 | tf_op jit(solution)/shard_map/ppermute | solution.py:149
  362.0 615.5 %collective-permute-start.7 = (bf16[8,72,1152]{2,1,0:T(8,128)(2,1)}, bf16[8,72,1152]{2,1,0:T(8,128)(2,1)}, u32[]{:S(2)}, u32[]{:S(2)}) collective-permute-start(bf16[8,72,1152]{2,1,0:T(8,128)(2,1)} %collective-permute-done.5.refs_1_), channel_id=1, source_target_pairs={{0,1},{1,0},{2,3},{3,2},{4,5},{5,4},{6,7},{7,6},{8,9},{9,8},{10,11... | collective-permute-start | bytes 3981320 | tf_op jit(solution)/shard_map/ppermute | solution.py:149
  362.4 615.1 %collective-permute-start.11 = (bf16[8,72,1152]{2,1,0:T(8,128)(2,1)}, bf16[8,72,1152]{2,1,0:T(8,128)(2,1)}, u32[]{:S(2)}, u32[]{:S(2)}) collective-permute-start(bf16[8,72,1152]{2,1,0:T(8,128)(2,1)} %collective-permute-done.9.refs_5_), channel_id=1, source_target_pairs={{0,1},{1,0},{2,3},{3,2},{4,5},{5,4},{6,7},{7,6},{8,9},{9,8},{10,11... | collective-permute-start | bytes 3981320 | tf_op jit(solution)/shard_map/ppermute | solution.py:149
  1583.0 61.1 %collective-permute-start.44 = (bf16[4,2,72,1152]{3,2,1,0:T(8,128)(2,1)}, bf16[4,2,72,1152]{3,2,1,0:T(8,128)(2,1)}, u32[]{:S(2)}, u32[]{:S(2)}) collective-permute-start(bf16[4,2,72,1152]{3,2,1,0:T(8,128)(2,1)} %fusion.12), channel_id=1, source_target_pairs={{0,4},{1,5},{2,6},{3,7},{4,0},{5,1},{6,2},{7,3},{8,12},{9,13},{10,... | collective-permute-start | bytes 3981320 | tf_op jit(solution)/shard_map/ppermute | solution.py:149
  1587.9 58.5 %collective-permute-start.53 = (bf16[4,2,72,1152]{3,2,1,0:T(8,128)(2,1)}, bf16[4,2,72,1152]{3,2,1,0:T(8,128)(2,1)}, u32[]{:S(2)}, u32[]{:S(2)}) collective-permute-start(bf16[4,2,72,1152]{3,2,1,0:T(8,128)(2,1)} %fusion.13), channel_id=1, source_target_pairs={{0,4},{1,5},{2,6},{3,7},{4,0},{5,1},{6,2},{7,3},{8,12},{9,13},{10,... | collective-permute-start | bytes 3981320 | tf_op jit(solution)/shard_map/ppermute | solution.py:149
  1598.5 113.3 %collective-permute-start.35 = (bf16[4,2,72,1280]{3,2,1,0:T(8,128)(2,1)S(1)}, bf16[4,2,72,1280]{3,2,1,0:T(8,128)(2,1)S(1)}, u32[]{:S(2)}, u32[]{:S(2)}) collective-permute-start(bf16[4,2,72,1280]{3,2,1,0:T(8,128)(2,1)S(1)} %fusion.10), channel_id=1, source_target_pairs={{0,4},{1,5},{2,6},{3,7},{4,0},{5,1},{6,2},{7,3},{8,12},{9,13},{10,... | collective-permute-start | bytes 4423688 | tf_op jit(solution)/shard_map/ppermute | solution.py:149
  1615.5 84.6 %collective-permute-start.37 = (bf16[4,2,72,1152]{3,2,1,0:T(8,128)(2,1)S(1)}, bf16[4,2,72,1152]{3,2,1,0:T(8,128)(2,1)}, u32[]{:S(2)}, u32[]{:S(2)}) collective-permute-start(bf16[4,2,72,1152]{3,2,1,0:T(8,128)(2,1)S(1)} %fusion.11), channel_id=1, source_target_pairs={{0,2},{1,3},{2,0},{3,1},{4,6},{5,7},{6,4},{7,5},{8,10},{9,11},{10,... | collective-permute-start | bytes 3981320 | tf_op jit(solution)/shard_map/ppermute | solution.py:149
  1646.4 56.7 %collective-permute-start.45 = (bf16[4,72,1152]{2,1,0:T(8,128)(2,1)S(1)}, bf16[4,72,1152]{2,1,0:T(8,128)(2,1)S(1)}, u32[]{:S(2)}, u32[]{:S(2)}) collective-permute-start(bf16[4,72,1152]{2,1,0:T(8,128)(2,1)S(1)} %fusion.29), channel_id=1, source_target_pairs={{0,2},{1,3},{2,0},{3,1},{4,6},{5,7},{6,4},{7,5},{8,10},{9,11},{10,... | collective-permute-start | bytes 1990664 | tf_op jit(solution)/shard_map/ppermute | solution.py:149
  1702.8 66.6 %collective-permute-start.38 = (bf16[4,72,1152]{2,1,0:T(8,128)(2,1)}, bf16[4,72,1152]{2,1,0:T(8,128)(2,1)}, u32[]{:S(2)}, u32[]{:S(2)}) collective-permute-start(bf16[4,72,1152]{2,1,0:T(8,128)(2,1)} %fusion.28), channel_id=1, source_target_pairs={{0,4},{1,5},{2,6},{3,7},{4,0},{5,1},{6,2},{7,3},{8,12},{9,13},{10,... | collective-permute-start | bytes 1990664 | tf_op jit(solution)/shard_map/ppermute | solution.py:149
  (127 other events, 3660.1 us)

commit v2 on v1

--- a/solution.py
+++ b/solution.py
@@ -161,36 +161,46 @@
 
 
 def place_kernel(kind, coords, *refs):
-    sources, targets, sems = refs[:8], refs[8:-1], refs[-1]
+    sources, targets = refs[:8], refs[8:-10]
+    held, in_sems, out_sems = refs[-10:-2], refs[-2], refs[-1]
     core, x, y, z = coords[0], coords[1], coords[2], coords[3]
+    arrivals = [
+        pltpu.make_async_copy(sources[i], held[i], in_sems.at[i]) for i in range(8)
+    ]
+    for arrival in arrivals:
+        arrival.start()
     copies = []
-    for stream, part, near, dz in itertools.product(range(2), range(4), range(2), range(4)):
-        src = sources[4 * stream + part].at[near * 4 + dz]
-        owner = core if part < 2 else 1 - core
-        far = part % 2
-        dx, dy = (near, far) if stream == 0 else (far, near)
-        chip = ((z ^ dz) * 2 + (y ^ dy)) * 2 + (x ^ dx)
-        sem = sems.at[len(copies)]
-        cols = src.shape[-1]
-        if kind == "down":
-            groups = src.shape[0]
-            first = PAIR_ROWS // 8 if stream else 0
-            dst = targets[0].at[chip * 2 + owner, first : first + groups]
-        elif kind == "up":
-            col = owner * HALF_UP + (D if stream else 0)
-            dst = targets[0].at[chip, :, pl.ds(pl.multiple_of(col, 128), cols)]
-        elif stream == 0:
-            col = owner * SQUARE_HALF
-            dst = targets[0].at[chip, :, pl.ds(pl.multiple_of(col, 128), cols)]
-        else:
-            dst = targets[0].at[chip, :, pl.ds(D, cols)]
-            copies.append(pltpu.make_async_copy(src, dst, sem))
-            last = pltpu.make_async_copy(src, targets[1].at[chip], sem)
-            pl.when(owner == 0)(copies[-1].start)
-            pl.when(owner == 1)(last.start)
-            continue
-        copies.append(pltpu.make_async_copy(src, dst, sem))
-        copies[-1].start()
+
+    def move(src, dst):
+        copies.append(pltpu.make_async_copy(src, dst, out_sems.at[len(copies)]))
+        return copies[-1]
+
+    for part, stream in itertools.product(range(4), range(2)):
+        arrivals[4 * stream + part].wait()
+        for near, dz in itertools.product(range(2), range(4)):
+            src = held[4 * stream + part].at[near * 4 + dz]
+            owner = core if part < 2 else 1 - core
+            far = part % 2
+            dx, dy = (near, far) if stream == 0 else (far, near)
+            chip = ((z ^ dz) * 2 + (y ^ dy)) * 2 + (x ^ dx)
+            cols = src.shape[-1]
+            if kind == "down":
+                groups = src.shape[0]
+                first = PAIR_ROWS // 8 if stream else 0
+                row = (chip ^ (core * 8)) * 2 + owner
+                move(src, targets[0].at[row, first : first + groups]).start()
+            elif kind == "up":
+                col = (HALF_UP if part >= 2 else 0) + (D if stream else 0)
+                move(src, targets[0].at[chip, :, col : col + cols]).start()
+            elif stream == 0:
+                col = pl.multiple_of(owner * SQUARE_HALF, 128)
+                move(src.at[:, EXTRA:], targets[0].at[chip, :, pl.ds(col, D)]).start()
+                move(src.at[:, :EXTRA], targets[2].at[owner * GROUPS + chip]).start()
+            else:
+                copy = move(src, targets[0].at[chip, :, D : 2 * D])
+                last = pltpu.make_async_copy(src, targets[1].at[chip], out_sems.at[len(copies) - 1])
+                pl.when(owner == 0)(copy.start)
+                pl.when(owner == 1)(last.start)
     for copy in copies:
         copy.wait()
 
@@ -206,66 +216,123 @@
         + [pl.BlockSpec(memory_space=pltpu.HBM)] * 8,
         out_specs=[pl.BlockSpec(memory_space=pltpu.HBM)] * len(shapes),
         out_shape=[jax.ShapeDtypeStruct(s, bf16) for s in shapes],
-        scratch_shapes=[pltpu.SemaphoreType.DMA((64,))],
+        scratch_shapes=[pltpu.VMEM(s.shape, bf16) for s in sources]
+        + [pltpu.SemaphoreType.DMA((8,)), pltpu.SemaphoreType.DMA((96,))],
+        compiler_params=pltpu.CompilerParams(vmem_limit_bytes=24 << 20),
         cost_estimate=pl.CostEstimate(flops=0, bytes_accessed=2 * size, transcendentals=0),
         name="place_" + kind,
     )(coords, *sources)
 
 
-def spread(block, cut, axis):
-    parts = [block] + [swap(block, 8 * step) for step in (1, 2, 3)]
+def tie(*values):
+    leaves, form = jax.tree.flatten(values)
+    return form.unflatten(lax.optimization_barrier(leaves))
+
+
+def gather_z(block):
+    return [block] + [swap(block, 8 * step) for step in (1, 2, 3)]
+
+
+def gather_near(parts, cut, axis):
     streams = []
     for stream in range(2):
         if axis == 1:
             own = jnp.stack([p[:, :cut] if stream == 0 else p[:, cut:] for p in parts])
         else:
             own = jnp.stack([p[:cut] if stream == 0 else p[cut:] for p in parts])
-        near, far = (2, 4) if stream == 0 else (4, 2)
-        first = jnp.concatenate([own, swap(own, near)])
-        second = swap(first, far)
-        streams.append((first, second, swap(first, 1), swap(second, 1)))
+        streams.append((own, swap(own, 4 if stream else 2)))
     return streams
+
+
+def gather_far(streams):
+    results = []
+    for stream in range(2):
+        first = jnp.concatenate(streams[stream])
+        results.append((first, swap(first, 2 if stream else 4), swap(first, 1)))
+    return results
+
+
+def gather_core(streams):
+    return [(first, second, third, swap(second, 1)) for first, second, third in streams]
 
 
 def pick(value, index, axis):
     return lax.dynamic_index_in_dim(value, index, axis, keepdims=False)
 
 
-def collect(keep, send, coords, cut, axis):
+def take(value, where):
+    for axis in reversed(range(len(where))):
+        if where[axis] is not None:
+            value = pick(value, where[axis], axis)
+    return value
+
+
+def cut_streams(value, cut, axis):
+    if axis == 1:
+        return value[..., :cut], value[..., cut:]
+    return value[..., :cut, :], value[..., cut:, :]
+
+
+def total_of(terms):
+    total = terms[0].astype(f32)
+    for term in terms[1:]:
+        total = total + term.astype(f32)
+    return total
+
+
+def sum_far(keep, other, coords, cut, axis):
     core, x, y, z = coords
-    other = swap(send, 1)
-    rows, cols = keep.shape[1:]
-    whole = (keep.astype(f32) + other.astype(f32)).reshape(4, 2, 2, rows, cols)
-    results = []
+    keeps, others = cut_streams(keep, cut, axis), cut_streams(other, cut, axis)
+    got = []
     for stream in range(2):
-        if axis == 1:
-            value = whole[..., :cut] if stream == 0 else whole[..., cut:]
-        else:
-            value = whole[..., :cut, :] if stream == 0 else whole[..., cut:, :]
-        if stream == 0:
-            got = swap(pick(value, 1 - y, 1).astype(bf16), 4)
-            value = pick(value, y, 1) + got.astype(f32)
-            got = swap(pick(value, 1 - x, 1).astype(bf16), 2)
-            value = pick(value, x, 1) + got.astype(f32)
-        else:
-            got = swap(pick(value, 1 - x, 2).astype(bf16), 2)
-            value = pick(value, x, 2) + got.astype(f32)
-            got = swap(pick(value, 1 - y, 1).astype(bf16), 4)
-            value = pick(value, y, 1) + got.astype(f32)
-        results.append(value)
-    value = jnp.concatenate(results, axis=2 if axis == 1 else 1)
-    total = pick(value, z, 0)
-    for step in (1, 2, 3):
-        total = total + swap(pick(value, z ^ step, 0).astype(bf16), 8 * step).astype(f32)
-    return total
+        to = (None, None, 1 - x) if stream else (None, 1 - y)
+        send = total_of([take(keeps[stream], to), take(others[stream], to)]).astype(bf16)
+        got.append(swap(send, 2 if stream else 4))
+    return got
+
+
+def sum_near(keep, other, far, coords, cut, axis):
+    core, x, y, z = coords
+    keeps, others = cut_streams(keep, cut, axis), cut_streams(other, cut, axis)
+    got = []
+    for stream in range(2):
+        to = (None, 1 - y, x) if stream else (None, y, 1 - x)
+        after = (None, 1 - y) if stream else (None, 1 - x)
+        terms = [take(keeps[stream], to), take(others[stream], to), take(far[stream], after)]
+        got.append(swap(total_of(terms).astype(bf16), 4 if stream else 2))
+    return got
+
+
+def sum_z(keep, other, far, near, coords, cut, axis):
+    core, x, y, z = coords
+    keeps, others = cut_streams(keep, cut, axis), cut_streams(other, cut, axis)
+
+    def at(plane):
+        pieces = []
+        for stream in range(2):
+            after = (plane, y) if stream else (plane, x)
+            terms = [
+                take(keeps[stream], (plane, y, x)),
+                take(others[stream], (plane, y, x)),
+                take(far[stream], after),
+                take(near[stream], (plane,)),
+            ]
+            pieces.append(total_of(terms))
+        return jnp.concatenate(pieces, axis=axis)
+
+    got = [swap(at(z ^ step).astype(bf16), 8 * step) for step in (1, 2, 3)]
+    return lambda arrived: total_of([at(z)] + arrived), got
 
 
 def fetch_pairs(narrow, core):
     q, k, v, o = (narrow[i].reshape(PAIR_ROWS // 2, D) for i in (2, 4, 5, 7))
     up = pad_hidden(narrow[11].reshape(PAIR_ROWS // 2, FF))
     down = narrow[13]
-    first = jnp.concatenate([q, k, up[:, :HALF_UP]], axis=1)
-    second = jnp.concatenate([v, o, up[:, HALF_UP:]], axis=1)
+    small = jnp.concatenate([narrow[i] for i in VECTORS])
+    small = jnp.pad(small, (0, PAIR_ROWS // 2 * EXTRA - small.shape[0]))
+    small = small.reshape(PAIR_ROWS // 2, EXTRA)
+    first = jnp.concatenate([small, q, k, up[:, :HALF_UP]], axis=1)
+    second = jnp.concatenate([small, v, o, up[:, HALF_UP:]], axis=1)
     lead = D * HALF_DOWN - down.shape[0]
     rows = PAIR_ROWS // 2
     tail = jnp.pad(down[:lead], (0, rows * EXTRA - lead)).reshape(rows, EXTRA)
@@ -280,7 +347,8 @@
     down_block = jnp.where(
         is_first, jnp.concatenate([down, extra]), jnp.concatenate([down[lead:], end])
     ).reshape(HALF_DOWN, D)
-    return block[:, :SQUARE_HALF], block[:, SQUARE_HALF:], down_block
+    square = SQUARE_HALF + EXTRA
+    return block[:, :square], block[:, square:], down_block
 
 
 def unpair(total, core):
@@ -306,17 +374,27 @@
     return inverse * (scaled - first - xhat * second)
 
 
-def gather_vectors(narrow):
-    widths = [narrow[i].shape[0] for i in VECTORS]
-    joined = jnp.concatenate([narrow[i] for i in VECTORS])
-    joined = jnp.pad(joined, (0, 2048 - joined.shape[0])).reshape(16, 128)
-    whole = lax.all_gather(joined, "fsdp", axis=0, tiled=True).reshape(-1, 2048)
+def name_vectors(whole, widths):
     found = {}
     position = 0
-    for i, width in zip(VECTORS, widths):
-        found[i] = whole[:, position : position + width].reshape(-1).astype(f32)
-        position += width
+    for i in VECTORS:
+        found[i] = whole[:, position : position + widths[i]].reshape(-1).astype(f32)
+        position += widths[i]
     return found
+
+
+def gather_plain(narrow, widths):
+    whole = {
+        i: lax.all_gather(narrow[i], "fsdp", axis=0, tiled=True) for i in (2, 4, 5, 7, 11, 13)
+    }
+    square = [whole[i][: D * D].reshape(D, D) for i in (2, 4, 5, 7)]
+    up = pad_hidden(whole[11][: D * FF].reshape(D, FF))
+    down = pad_hidden(whole[13][: D * FF].reshape(FF, D).T).T
+    joined = jnp.concatenate([narrow[i] for i in VECTORS])
+    length = joined.shape[0]
+    joined = jnp.pad(joined, (0, 2048 - length)).reshape(16, 128)
+    joined = lax.all_gather(joined, "fsdp", axis=0, tiled=True).reshape(-1, 2048)
+    return jnp.concatenate(square[:3], axis=1), square[3], up, down, name_vectors(joined, widths)
 
 
 def on_device(*args):
@@ -334,65 +412,112 @@
     seq_len = tokens.shape[0] // image_count
     weight_img = jnp.repeat(image_valid.astype(f32), seq_len)[:, None]
 
-    vectors = gather_vectors(narrow)
+    grad_out = weight_img * cotangent
+    grad_branch = grad_out.astype(bf16)
+    grads = {14: jnp.sum(grad_branch.astype(f32), axis=0)}
+    xhat_one, inverse_one = normalize(tokens)
     if staged:
         where = jnp.stack(coords).astype(jnp.int32)
-        square_block, up_block, down_block = fetch_pairs(narrow, core)
+        sq, up, down = fetch_pairs(narrow, core)
+        square_cut = D + EXTRA
+        sq = gather_z(sq)
+        sq, up, down, xhat_one, inverse_one, grad_branch = tie(
+            sq, up, down, xhat_one, inverse_one, grad_branch
+        )
+        sq = gather_near(sq, square_cut, 1)
+        up = gather_z(up)
+        (sq,) = tie(sq)
+        sq = gather_far(sq)
+        sq, up, down = tie(sq, up, down)
+        sq = gather_core(sq)
+        up = gather_near(up, D, 1)
+        down = gather_z(down)
         blocks = (GROUPS, PAIR_ROWS)
-        weight_qkv, weight_o = place(
-            spread(square_block, D, 1), where, "square", [blocks + (3 * D,), blocks + (D,)]
+        weight_qkv, weight_o, small = place(
+            sq, where, "square", [blocks + (3 * D,), blocks + (D,), (2 * GROUPS, PAIR_ROWS, EXTRA)]
         )
         weight_qkv, weight_o = weight_qkv.reshape(D, 3 * D), weight_o.reshape(D, D)
-        (weight_up,) = place(spread(up_block, D, 1), where, "up", [blocks + (FF_PAD,)])
-        weight_up = weight_up.reshape(D, FF_PAD)
-        (weight_down,) = place(
-            spread(down_block, PAIR_ROWS, 0), where, "down", [(2 * GROUPS, HALF_DOWN // 8, 8, D)]
-        )
-        weight_down = weight_down.reshape(FF_PAD, D)
+        small = small[:GROUPS].reshape(devices, PAIR_ROWS // 2 * EXTRA)
+        vectors = name_vectors(small, widths)
     else:
-        whole = {
-            i: lax.all_gather(narrow[i], "fsdp", axis=0, tiled=True) for i in (2, 4, 5, 7, 11, 13)
-        }
-        square = [whole[i][: D * D].reshape(D, D) for i in (2, 4, 5, 7)]
-        weight_qkv = jnp.concatenate(square[:3], axis=1)
-        weight_o = square[3]
-        weight_up = pad_hidden(whole[11][: D * FF].reshape(D, FF))
-        weight_down = pad_hidden(whole[13][: D * FF].reshape(FF, D).T).T
+        weight_qkv, weight_o, weight_up, weight_down, vectors = gather_plain(narrow, widths)
 
     vec = lambda i: vectors[i][:D]
     gain_one, shift_one, gain_two, shift_two = vec(0), vec(1), vec(9), vec(10)
     bias_qkv = jnp.concatenate([vec(3), jnp.zeros((D,), f32), vec(6)])
     bias_o, bias_down = vec(8), vec(14)
     bias_up = pad_hidden(vectors[12][:FF].reshape(1, FF))
-
-    xhat_one, inverse_one = normalize(tokens)
+    if staged:
+        bias_up = jnp.where(core == 0, bias_up, jnp.roll(bias_up, HALF_UP, axis=1))
+
     normed = (xhat_one * gain_one + shift_one).astype(bf16)
     qkv = (product(normed, weight_qkv) + bias_qkv).astype(bf16)
+    if staged:
+        qkv, up = tie(qkv, up)
+        up = gather_far(up)
     mixed, lse = attn_fwd(qkv, 2)
+    if staged:
+        mixed, lse, up, down = tie(mixed, lse, up, down)
+        up = gather_core(up)
+        down = gather_near(down, PAIR_ROWS, 0)
     resid = tokens + product(mixed, weight_o) + bias_o
     xhat_two, inverse_two = normalize(resid)
     normed_two = (xhat_two * gain_two + shift_two).astype(bf16)
+    if staged:
+        normed_two, up, down = tie(normed_two, up, down)
+        down = gather_far(down)
+        (weight_up,) = place(up, where, "up", [blocks + (FF_PAD,)])
+        weight_up = weight_up.reshape(D, FF_PAD)
     pre = product(normed_two, weight_up) + bias_up
     hidden, gelu_back = jax.vjp(lambda t: jax.nn.gelu(t, approximate=True), pre)
     hidden = hidden.astype(bf16)
-    layer_out = weight_img * (resid + product(hidden, weight_down) + bias_down)
-
-    grad_out = weight_img * cotangent
-    grad_branch = grad_out.astype(bf16)
-    grads = {14: jnp.sum(grad_branch.astype(f32), axis=0)}
+    if staged:
+        hidden, down = tie(hidden, down)
+        down = gather_core(down)
     down_grad = product_t(hidden, grad_branch).astype(bf16)
+    if staged:
+        down_grad, down = tie(down_grad, down)
+        down_grad = down_grad.reshape(4, 2, 2, 2, HALF_DOWN, D)
+        down_keep, down_send = pick(down_grad, core, 3), pick(down_grad, 1 - core, 3)
+        down_send = jnp.concatenate([down_send[2:], down_send[:2]])
+        down_other = swap(down_send, 1)
+        (weight_down,) = place(down, where, "down", [(2 * GROUPS, HALF_DOWN // 8, 8, D)])
+        weight_down = weight_down.reshape(FF_PAD, D)
+    branch = resid + product(hidden, weight_down) + bias_down
+    layer_out = weight_img * branch
+    if staged:
+        down_at = (core, x, y, z ^ (2 * core))
+        down_keep, down_other, weight_down, layer_out = tie(
+            down_keep, down_other, weight_down, layer_out
+        )
+        down_far = sum_far(down_keep, down_other, down_at, PAIR_ROWS, 0)
     grad_pre = gelu_back(product_bt(grad_branch, weight_down))[0].astype(bf16)
     up_bias_grad = jnp.sum(grad_pre.astype(f32), axis=0)
     up_grad = product_t(normed_two, grad_pre).astype(bf16)
+    if staged:
+        down_far, up_grad, grad_pre = tie(down_far, up_grad, grad_pre)
+        down_near = sum_near(down_keep, down_other, down_far, down_at, PAIR_ROWS, 0)
+        up_grad = up_grad.reshape(4, 2, 2, PAIR_ROWS, FF_PAD)
+        up_keep, up_send = up_grad[..., :HALF_UP], up_grad[..., HALF_UP:]
+        up_other = swap(up_send, 1)
     grad_normed_two = product_bt(grad_pre, weight_up)
     grads[9] = jnp.sum(grad_normed_two * xhat_two, axis=0)
     grads[10] = jnp.sum(grad_normed_two, axis=0)
     grad_resid = grad_out + normalize_back(grad_normed_two, gain_two, xhat_two, inverse_two)
     grad_attn = grad_resid.astype(bf16)
     grads[8] = jnp.sum(grad_attn.astype(f32), axis=0)
+    if staged:
+        down_near, up_other, grad_attn = tie(down_near, up_other, grad_attn)
+        down_sum, down_z = sum_z(
+            down_keep, down_other, down_far, down_near, down_at, PAIR_ROWS, 0
+        )
+        up_far = sum_far(up_keep, up_other, coords, D, 1)
     o_grad = product_t(mixed, grad_attn).astype(bf16)
     grad_mixed = product_bt(grad_attn, weight_o).astype(bf16)
     grad_qkv = attn_bwd(qkv, grad_mixed, lse, 2)
+    if staged:
+        grad_qkv, o_grad, down_z, up_far = tie(grad_qkv, o_grad, down_z, up_far)
+        up_near = sum_near(up_keep, up_other, up_far, coords, D, 1)
     qkv_bias_grad = jnp.sum(grad_qkv.astype(f32), axis=0)
     grads[3], grads[6] = qkv_bias_grad[:D], qkv_bias_grad[2 * D :]
     qkv_grad = product_t(normed, grad_qkv).astype(bf16)
@@ -400,6 +525,8 @@
     grads[0] = jnp.sum(grad_normed * xhat_one, axis=0)
     grads[1] = jnp.sum(grad_normed, axis=0)
     tokens_grad = grad_resid + normalize_back(grad_normed, gain_one, xhat_one, inverse_one)
+    if staged:
+        up_bias_grad = jnp.where(core == 0, up_bias_grad, jnp.roll(up_bias_grad, HALF_UP))
     grads[12] = trim_hidden(up_bias_grad.reshape(1, FF_PAD)).reshape(FF)
 
     rows = []
@@ -410,44 +537,38 @@
     rows = jnp.concatenate(rows, axis=1)
     owned = [None] * 15
     if staged:
-        down_halves = down_grad.reshape(GROUPS, 2, HALF_DOWN, D)
-        down_total = collect(
-            pick(down_halves, core, 1), pick(down_halves, 1 - core, 1), coords, PAIR_ROWS, 0
-        )
+        rows = jnp.pad(rows, ((0, 0), (0, PAIR_ROWS // 2 * EXTRA - rows.shape[1])))
+        rows = rows.reshape(D, EXTRA).astype(bf16)
+        first = jnp.concatenate([rows, qkv_grad[:, :SQUARE_HALF]], axis=1)
+        second = jnp.concatenate([jnp.zeros_like(rows), qkv_grad[:, SQUARE_HALF:], o_grad], axis=1)
+        shape = (4, 2, 2, PAIR_ROWS, SQUARE_HALF + EXTRA)
+        keep = jnp.where(core == 0, first, second).reshape(shape)
+        send = jnp.where(core == 0, second, first).reshape(shape)
+        keep, send, up_near = tie(keep, send, up_near)
+        up_sum, up_z = sum_z(up_keep, up_other, up_far, up_near, coords, D, 1)
+        other = swap(send, 1)
+        (other,) = tie(other)
+        far = sum_far(keep, other, coords, square_cut, 1)
+        far, up_z = tie(far, up_z)
+        near = sum_near(keep, other, far, coords, square_cut, 1)
+
+        down_total = down_sum(down_z)
         flat = down_total.reshape(-1)
         size = widths[13]
         lead = flat.shape[0] - size
         got = swap(flat[size:], 1)
         owned[13] = jnp.where(core == 0, flat[:size], jnp.concatenate([got, flat[: size - lead]]))
-
-        up_grad = up_grad.reshape(GROUPS, PAIR_ROWS, FF_PAD)
-        up_total = collect(
-            lax.dynamic_slice_in_dim(up_grad, core * HALF_UP, HALF_UP, 2),
-            lax.dynamic_slice_in_dim(up_grad, (1 - core) * HALF_UP, HALF_UP, 2),
-            coords,
-            D,
-            1,
-        )
+        up_total = up_sum(up_z)
         owned[11] = trim_hidden(jnp.concatenate(unpair(up_total, core), axis=1)).reshape(-1)
-
-        rows = jnp.pad(rows, ((0, 0), (0, PAIR_ROWS // 2 * EXTRA - rows.shape[1])))
-        rows = rows.reshape(D, EXTRA).astype(bf16)
-        first = jnp.concatenate([qkv_grad[:, :SQUARE_HALF], rows], axis=1)
-        second = jnp.concatenate([qkv_grad[:, SQUARE_HALF:], o_grad, jnp.zeros_like(rows)], axis=1)
-        shape = (GROUPS, PAIR_ROWS, SQUARE_HALF + EXTRA)
-        square_total = collect(
-            jnp.where(core == 0, first, second).reshape(shape),
-            jnp.where(core == 0, second, first).reshape(shape),
-            coords,
-            D + EXTRA,
-            1,
-        )
-        left, right = unpair(square_total, core)
-        owned[2] = left[:, :D].reshape(-1)
-        owned[4] = left[:, D : 2 * D].reshape(-1)
-        owned[5] = right[:, :D].reshape(-1)
-        owned[7] = right[:, D : 2 * D].reshape(-1)
-        small = left[:, 2 * D :].reshape(-1)
+        near, owned[13], owned[11] = tie(near, owned[13], owned[11])
+
+        square_sum, got = sum_z(keep, other, far, near, coords, square_cut, 1)
+        left, right = unpair(square_sum(got), core)
+        owned[2] = left[:, EXTRA:square_cut].reshape(-1)
+        owned[4] = left[:, square_cut:].reshape(-1)
+        owned[5] = right[:, EXTRA:square_cut].reshape(-1)
+        owned[7] = right[:, square_cut:].reshape(-1)
+        small = left[:, :EXTRA].reshape(-1)
     else:
         scatter = lambda value: lax.psum_scatter(
             value.astype(f32).reshape(-1), "fsdp", scatter_dimension=0, tiled=True

time: 1820 us -> 689 us (0.38)
  Pallas kernels: 1010 us -> 101 us
  waiting for transfers between devices: 371 us -> 197 us
  blocking collectives: 35.9 us -> 0 us
    pallas_call x3, Pallas kernels: 936 us -> 29.1 us  [place(): pl.pallas_call(functools.partial(place_kernel, kind), in_specs=[pl.BlockS...]
    ppermute x61, waiting for transfers between devices: 371 us -> 197 us  [swap(): return lax.ppermute(value, 'fsdp', [(i, i ^ mask) for i in range(devices)])]
    all_gather x1 -> x0, blocking collectives: 35.9 us -> none  [gather_vectors(): whole = lax.all_gather(joined, 'fsdp', axis=0, tiled=True).reshape(-1, 2048)]
  transfers between devices with their start and end apart: 61 -> 61, of which waited for: 22 -> 25; matrix products, arithmetic and copies ran while one was open for 9% -> 31% of each run, Pallas kernels for 34% -> 15%
where the time goes in v2:
time: 689 us; the launch traced here: 679 us
  waiting for transfers between devices  197 us (29%)
  matrix products  135 us (20%)
  local copies, waits for them, and re-layouts  112 us (16%)
  Pallas kernels  101 us (15%)
  other arithmetic  84.3 us (12%)
  starting transfers between devices  46.2 us (7%)
    ppermute x61, waiting for transfers between devices, swap(): return lax.ppermute(value, 'fsdp', [(i, i ^ mask) for i in range(devices)])  197 us
    dot_general x4, matrix products, product_bt(): lax.dot_general(left, right, (((1,), (1,)), ((), ())), preferred_element_...  48.7 us
    dot_general x4, matrix products, product(): return jnp.dot(left, right, preferred_element_type=f32)  47.2 us
    ppermute x61, starting transfers between devices, swap(): return lax.ppermute(value, 'fsdp', [(i, i ^ mask) for i in range(devices)])  46.2 us
    pallas_call x1, Pallas kernels, attn_bwd(): pl.pallas_call(functools.partial(bwd_kernel, tokens, krows, qrows, per),...  43.8 us
    dot_general x4, matrix products, product_t(): lax.dot_general(left, right, (((0,), (0,)), ((), ())), preferred_element_...  38.9 us
    pallas_call x3, Pallas kernels, place(): pl.pallas_call(functools.partial(place_kernel, kind), in_specs=[pl.BlockS...  29.1 us
    pallas_call x1, Pallas kernels, attn_fwd(): pl.pallas_call(functools.partial(fwd_kernel, tokens, krows, qrows, per),...  28 us
  transfers between devices with their start and end apart: 61, of which 25 were waited for; matrix products, arithmetic and copies ran while one was open for 31% of the time, Pallas kernels for 15%

profile of v2, /device:TPU:8, one launch (start us, length us, event | category | flops | bytes accessed | tf_op | source)
XLA Modules:
  0.0 678.7 jit_solution(4809437964442488973)
XLA Ops:
  34.9 10.1 %collective-permute-done.1 = bf16[72,2432]{1,0:T(8,128)(2,1)S(1)} collective-permute-done((bf16[72,2432]{1,0:T(8,128)(2,1)S(1)}, bf16[72,2432]{1,0:T(8,128)(2,1)S(1)}, u32[]{:S(2)}, u32[]{:S(2)}) %collective-permute-start.1) | collective-permute-done | bytes 350240 | tf_op jit(solution)/shard_map/ppermute | solution.py:149
  44.9 11.1 %collective-permute-done.2 = bf16[72,2432]{1,0:T(8,128)(2,1)S(1)} collective-permute-done((bf16[72,2432]{1,0:T(8,128)(2,1)S(1)}, bf16[72,2432]{1,0:T(8,128)(2,1)S(1)}, u32[]{:S(2)}, u32[]{:S(2)}) %collective-permute-start.2) | collective-permute-done | bytes 350240 | tf_op jit(solution)/shard_map/ppermute | solution.py:149
  67.3 14.4 %collective-permute-done.5 = bf16[4,72,1152]{2,1,0:T(8,128)(2,1)S(1)} collective-permute-done((bf16[4,72,1152]{2,1,0:T(8,128)(2,1)S(1)}, bf16[4,72,1152]{2,1,0:T(8,128)(2,1)S(1)}, u32[]{:S(2)}, u32[]{:S(2)}) %collective-permute-start.5) | collective-permute-done | bytes 663584 | tf_op jit(solution)/shard_map/ppermute | solution.py:149
  85.5 9.6 %collective-permute-done.10 = bf16[72,2176]{1,0:T(8,128)(2,1)S(1)} collective-permute-done((bf16[72,2176]{1,0:T(8,128)(2,1)S(1)}, bf16[72,2176]{1,0:T(8,128)(2,1)S(1)}, u32[]{:S(2)}, u32[]{:S(2)}) %collective-permute-start.10) | collective-permute-done | bytes 313376 | tf_op jit(solution)/shard_map/ppermute | solution.py:149
  96.4 13.4 %collective-permute-done.11 = bf16[72,2176]{1,0:T(8,128)(2,1)S(1)} collective-permute-done((bf16[72,2176]{1,0:T(8,128)(2,1)S(1)}, bf16[72,2176]{1,0:T(8,128)(2,1)S(1)}, u32[]{:S(2)}, u32[]{:S(2)}) %collective-permute-start.11) | collective-permute-done | bytes 313376 | tf_op jit(solution)/shard_map/ppermute | solution.py:149
  111.1 14.6 %collective-permute-done.12 = bf16[72,2176]{1,0:T(8,128)(2,1)S(1)} collective-permute-done((bf16[72,2176]{1,0:T(8,128)(2,1)S(1)}, bf16[72,2176]{1,0:T(8,128)(2,1)S(1)}, u32[]{:S(2)}, u32[]{:S(2)}) %collective-permute-start.12) | collective-permute-done | bytes 313376 | tf_op jit(solution)/shard_map/ppermute | solution.py:149
  149.0 12.7 %add_convert_fusion.qkv_ref = bf16[729,3456]{1,0:T(8,128)(2,1)} fusion(bf16[1152,3456]{1,0:T(8,128)(2,1)} %bitcast.357, f32[3456]{0:T(1024)S(1)} %pad_maximum_fusion.23, f32[729,1152]{1,0:T(8,128)} %subtract_multiply_fusion.1, f32[1152]{0:T(1024)S(1)} %reshape.840, f32[1152]{0:T(1024)S(1)} %reshape.839), kind=kOutput, calls=%fused_computation.14 | convolution fusion | flops 5812311552 | bytes 16383744 | tf_op jit(solution)/shard_map/dot_general | solution.py:136
  176.5 28.0 %attention_forward.1 = (bf16[729,1152]{1,0:T(8,128)(2,1)}, f32[16,1,768]{2,1,0:T(1,128)}) custom-call(bf16[729,3456]{1,0:T(8,128)(2,1)} %add_convert_fusion.qkv_ref), custom_call_target="tpu_custom_call" | custom-call | flops 4630511616 | bytes 6718464 | tf_op jit(solution)/shard_map/attention_forward/pallas_call | solution.py:63
  206.3 14.2 %collective-permute-done.23 = bf16[136,1152]{1,0:T(8,128)(2,1)S(1)} collective-permute-done((bf16[136,1152]{1,0:T(8,128)(2,1)}, bf16[136,1152]{1,0:T(8,128)(2,1)S(1)}, u32[]{:S(2)}, u32[]{:S(2)}) %collective-permute-start.23) | collective-permute-done | bytes 313376 | tf_op jit(solution)/shard_map/ppermute | solution.py:149
  247.1 17.1 %multiply_convert_fusion = (bf16[729,4352]{1,0:T(8,128)(2,1)}, f32[729,4352]{1,0:T(8,128)}) fusion(f32[4352]{0:T(1024)S(1)} %maximum_select_fusion.2, bf16[729,1152]{1,0:T(8,128)(2,1)} %add_convert_fusion.1, bf16[1152,4352]{1,0:T(8,128)(2,1)S(1)} %bitcast.345), kind=kOutput, calls=%fused_computation.13 | convolution fusion | flops 7341412352 | bytes 30759680 | tf_op jit(solution)/shard_map/dot_general | solution.py:136
  273.7 11.9 %convolution_convert_fusion.1 = bf16[4352,1152]{1,0:T(8,128)(2,1)S(1)} fusion(bf16[729,4352]{1,0:T(8,128)(2,1)} %get-tuple-element.180, bf16[729,1152]{1,0:T(8,128)(2,1)} %get-tuple-element.181), kind=kOutput, calls=%fused_computation.1 | convolution fusion | flops 7314702336 | bytes 18051840 | tf_op jit(solution)/shard_map/dot_general | solution.py:140
  311.4 15.9 %place_down.1 = bf16[32,17,8,1152]{3,2,1,0:T(8,128)(2,1)S(1)} custom-call(s32[4]{0:T(128)S(1)} %pad_add_fusion.coords, bf16[8,9,8,1152]{3,2,1,0:T(8,128)(2,1)S(1)} %bitcast.349, bf16[8,9,8,1152]{3,2,1,0:T(8,128)(2,1)S(1)} %bitcast.351, bf16[8,9,8,1152]{3,2,1,0:T(8,128)(2,1)S(1)} %bitcast.352, bf16[8,9,8,1152]{3,2,1,0:T(8,128)(2,1)S(1)} %bitcast.353, ...), custom_call_target="tpu_custom_call" | custom-call | bytes 20054016 | tf_op jit(solution)/shard_map/place_down/pallas_call | solution.py:213
  327.3 14.7 %fusion.9 = f32[729,1152]{1,0:T(8,128)} fusion(f32[729,1152]{1,0:T(8,128)S(1)} %copy-done.25, bf16[729,4352]{1,0:T(8,128)(2,1)} %get-tuple-element.180, bf16[4352,1152]{1,0:T(8,128)(2,1)S(1)} %bitcast.347, f32[1152]{0:T(1024)S(1)} %reshape.846, f32[]{:T(128)} %bitcast.3), kind=kOutput, calls=%fused_computation.27 | convolution fusion | flops 7312207872 | bytes 23095300 | tf_op jit(solution)/shard_map/dot_general | solution.py:136
  351.4 19.7 %convert_reduce_fusion = (bf16[4352]{0:T(1024)(128)(2,1)S(1)}, bf16[729,4352]{1,0:T(8,128)(2,1)}) fusion(f32[729,4352]{1,0:T(8,128)} %get-tuple-element.311, f32[4352]{0:T(1024)S(1)} %maximum_select_fusion.2, bf16[729,1152]{1,0:T(8,128)(2,1)S(1)} %copy-done.54, bf16[4352,1152]{1,0:T(8,128)(2,1)} %bitcast.348), kind=kOutput, calls=%fused_computation.12 | convolution fusion | flops 7382648832 | bytes 30768384 | tf_op jit(solution)/shard_map/dot_general | solution.py:144
  371.1 11.3 %convolution_convert_fusion = bf16[1152,4352]{1,0:T(8,128)(2,1)S(1)} fusion(bf16[729,1152]{1,0:T(8,128)(2,1)S(1)} %copy-done.53, bf16[729,4352]{1,0:T(8,128)(2,1)} %get-tuple-element.201), kind=kOutput, calls=%fused_computation | convolution fusion | flops 7314702336 | bytes 18051840 | tf_op jit(solution)/shard_map/dot_general | solution.py:140
  403.2 15.7 %multiply_reduce_fusion = (bf16[1152]{0:T(1024)(128)(2,1)S(1)}, f32[729]{0:T(1024)S(1)}, f32[729]{0:T(1024)S(1)}, bf16[1152]{0:T(1024)(128)(2,1)S(1)}, f32[729,1152]{1,0:T(8,128)}) fusion(f32[729,1152]{1,0:T(8,128)S(1)} %copy-done.26, f32[729]{0:T(1024)S(1)} %add_rsqrt_fusion, f32[729]{0:T(1024)S(1)} %broadcast_multiply_fusion.4, f32[1152]{0:T(1024)S(1)} %reshape.844, ...), kind=kOutput, calls=%fused_computation.28 | convolution fusion | flops 7317242880 | bytes 23111568 | tf_op jit(solution)/shard_map/dot_general | solution.py:144
  450.6 43.8 %attention_backward.1 = bf16[729,3456]{1,0:T(8,128)(2,1)} custom-call(bf16[729,3456]{1,0:T(8,128)(2,1)} %add_convert_fusion.qkv_ref, bf16[729,1152]{1,0:T(8,128)(2,1)} %convolution_convert_fusion.4.go_ref, f32[16,1,768]{2,1,0:T(1,128)} %get-tuple-element.207.lse_ref), custom_call_target="tpu_custom_call" | custom-call | flops 11576279040 | bytes 11757312 | tf_op jit(solution)/shard_map/attention_backward/pallas_call | solution.py:107
  501.3 9.5 %multiply_reduce_fusion.1 = (bf16[1152]{0:T(1024)(128)(2,1)}, f32[729]{0:T(1024)}, f32[729]{0:T(1024)}, bf16[1152]{0:T(1024)(128)(2,1)S(1)}, f32[729,1152]{1,0:T(8,128)}) fusion(f32[729,1152]{1,0:T(8,128)S(1)} %copy-done.28, f32[1152]{0:T(1024)S(1)} %copy-done.67, bf16[729,3456]{1,0:T(8,128)(2,1)S(1)} %copy-done.46, bf16[1152,3456]{1,0:T(8,128)(2,1)S(1)} %bitcast.360), kind=kOutput, calls=%fused_computation.29 | convolution fusion | flops 5810627584 | bytes 19734984 | tf_op jit(solution)/shard_map/dot_general | solution.py:144
  514.3 9.6 %convolution_convert_fusion.2 = bf16[1152,3456]{1,0:T(8,128)(2,1)S(1)} fusion(bf16[729,3456]{1,0:T(8,128)(2,1)} %attention_backward.1, f32[729,1152]{1,0:T(8,128)S(1)} %copy-done.29, f32[1152]{0:T(1024)S(1)} %copy-done.74, f32[1152]{0:T(1024)S(1)} %copy-done.67), kind=kOutput, calls=%fused_computation.4 | convolution fusion | flops 5811253760 | bytes 16369920 | tf_op jit(solution)/shard_map/dot_general | solution.py:140
  538.8 10.3 %broadcast_select_fusion = (bf16[4,2,2,72,2432]{4,3,2,1,0:T(8,128)(2,1)}, bf16[4,2,2,72,2432]{4,3,2,1,0:T(8,128)(2,1)}) fusion(pred[]{:T(512)S(6)} %eq.6, bf16[4,2,2,72,2304]{4,3,2,1,0:T(8,128)(2,1)} %bitcast.363, bf16[4,2,2,72,128]{4,3,2,1,0:T(8,128)(2,1)} %convert_element_type.1004, bf16[4,2,2,72,1152]{4,3,2,1,0:T(8,128)(2,1)} %bitcast.374, ...), kind=kLoop, calls=%fused_computation.18 | loop fusion | flops 33619968 | bytes 22123264 | tf_op jit(solution)/shard_map/jit(_where)/select_n | solution.py:546
  580.0 11.1 %collective-permute-done.52 = bf16[72,2176]{1,0:T(8,128)(2,1)S(1)} collective-permute-done((bf16[72,2176]{1,0:T(8,128)(2,1)S(1)}, bf16[72,2176]{1,0:T(8,128)(2,1)S(1)}, u32[]{:S(2)}, u32[]{:S(2)}) %collective-permute-start.52) | collective-permute-done | bytes 313376 | tf_op jit(solution)/shard_map/ppermute | solution.py:149
  596.1 10.7 %collective-permute-done.49 = bf16[4,2,72,1152]{3,2,1,0:T(8,128)(2,1)S(1)} collective-permute-done((bf16[4,2,72,1152]{3,2,1,0:T(8,128)(2,1)S(1)}, bf16[4,2,72,1152]{3,2,1,0:T(8,128)(2,1)S(1)}, u32[]{:S(2)}, u32[]{:S(2)}) %collective-permute-start.49) | collective-permute-done | bytes 1327136 | tf_op jit(solution)/shard_map/ppermute | solution.py:149
  641.7 11.1 %collective-permute-done.57 = bf16[72,2432]{1,0:T(8,128)(2,1)S(1)} collective-permute-done((bf16[72,2432]{1,0:T(8,128)(2,1)S(1)}, bf16[72,2432]{1,0:T(8,128)(2,1)S(1)}, u32[]{:S(2)}, u32[]{:S(2)}) %collective-permute-start.57) | collective-permute-done | bytes 350240 | tf_op jit(solution)/shard_map/ppermute | solution.py:149
  652.7 12.1 %collective-permute-done.58 = bf16[72,2432]{1,0:T(8,128)(2,1)S(1)} collective-permute-done((bf16[72,2432]{1,0:T(8,128)(2,1)S(1)}, bf16[72,2432]{1,0:T(8,128)(2,1)S(1)}, u32[]{:S(2)}, u32[]{:S(2)}) %collective-permute-start.58) | collective-permute-done | bytes 350240 | tf_op jit(solution)/shard_map/ppermute | solution.py:149
  (511 shorter events, 322.5 us)
Async XLA Ops:
  32.5 31.3 %collective-permute-start.3 = (bf16[72,2432]{1,0:T(8,128)(2,1)S(1)}, bf16[72,2432]{1,0:T(8,128)(2,1)S(1)}, u32[]{:S(2)}, u32[]{:S(2)}) collective-permute-start(bf16[72,2432]{1,0:T(8,128)(2,1)S(1)} %slice.422), channel_id=1, source_target_pairs={{0,24},{1,25},{2,26},{3,27},{4,28},{5,29},{6,30},{7,31},{8,16},{9,... | collective-permute-start | bytes 1050632 | tf_op jit(solution)/shard_map/ppermute | solution.py:149
  82.0 43.7 %collective-permute-start.6 = (bf16[8,72,1280]{2,1,0:T(8,128)(2,1)S(1)}, bf16[8,72,1280]{2,1,0:T(8,128)(2,1)}, u32[]{:S(2)}, u32[]{:S(2)}) collective-permute-start(bf16[8,72,1280]{2,1,0:T(8,128)(2,1)S(1)} %constant_dynamic-update-slice_fusion.refs_0_), channel_id=1, source_target_pairs={{0,4},{1,5},{2,6},{3,7},{4,0},{5,1},{6,2},{7,3},{8,12},{9,13},{10,... | collective-permute-start | bytes 4423688 | tf_op jit(solution)/shard_map/ppermute | solution.py:149
  83.6 42.2 %collective-permute-start.7 = (bf16[8,72,1280]{2,1,0:T(8,128)(2,1)S(1)}, bf16[8,72,1280]{2,1,0:T(8,128)(2,1)}, u32[]{:S(2)}, u32[]{:S(2)}) collective-permute-start(bf16[8,72,1280]{2,1,0:T(8,128)(2,1)S(1)} %constant_dynamic-update-slice_fusion.refs_0_), channel_id=1, source_target_pairs={{0,1},{1,0},{2,3},{3,2},{4,5},{5,4},{6,7},{7,6},{8,9},{9,8},{10,11... | collective-permute-start | bytes 4423688 | tf_op jit(solution)/shard_map/ppermute | solution.py:149
  83.8 42.0 %collective-permute-start.8 = (bf16[8,72,1152]{2,1,0:T(8,128)(2,1)S(1)}, bf16[8,72,1152]{2,1,0:T(8,128)(2,1)}, u32[]{:S(2)}, u32[]{:S(2)}) collective-permute-start(bf16[8,72,1152]{2,1,0:T(8,128)(2,1)S(1)} %constant_dynamic-update-slice_fusion.2.refs_4_), channel_id=1, source_target_pairs={{0,2},{1,3},{2,0},{3,1},{4,6},{5,7},{6,4},{7,5},{8,10},{9,11},{10,... | collective-permute-start | bytes 3981320 | tf_op jit(solution)/shard_map/ppermute | solution.py:149
  85.3 40.5 %collective-permute-start.9 = (bf16[8,72,1152]{2,1,0:T(8,128)(2,1)S(1)}, bf16[8,72,1152]{2,1,0:T(8,128)(2,1)}, u32[]{:S(2)}, u32[]{:S(2)}) collective-permute-start(bf16[8,72,1152]{2,1,0:T(8,128)(2,1)S(1)} %constant_dynamic-update-slice_fusion.2.refs_4_), channel_id=1, source_target_pairs={{0,1},{1,0},{2,3},{3,2},{4,5},{5,4},{6,7},{7,6},{8,9},{9,8},{10,11... | collective-permute-start | bytes 3981320 | tf_op jit(solution)/shard_map/ppermute | solution.py:149
  131.0 30.7 %collective-permute-start.16 = (bf16[4,72,1024]{2,1,0:T(8,128)(2,1)}, bf16[4,72,1024]{2,1,0:T(8,128)(2,1)}, u32[]{:S(2)}, u32[]{:S(2)}) collective-permute-start(bf16[4,72,1024]{2,1,0:T(8,128)(2,1)} %pad_maximum_fusion.8), channel_id=1, source_target_pairs={{0,4},{1,5},{2,6},{3,7},{4,0},{5,1},{6,2},{7,3},{8,12},{9,13},{10,... | collective-permute-start | bytes 1769480 | tf_op jit(solution)/shard_map/ppermute | solution.py:149
  162.9 57.6 %collective-permute-start.17 = (bf16[8,72,1152]{2,1,0:T(8,128)(2,1)S(1)}, bf16[8,72,1152]{2,1,0:T(8,128)(2,1)}, u32[]{:S(2)}, u32[]{:S(2)}) collective-permute-start(bf16[8,72,1152]{2,1,0:T(8,128)(2,1)S(1)} %constant_dynamic-update-slice_fusion.4.refs_0_), channel_id=1, source_target_pairs={{0,4},{1,5},{2,6},{3,7},{4,0},{5,1},{6,2},{7,3},{8,12},{9,13},{10,... | collective-permute-start | bytes 3981320 | tf_op jit(solution)/shard_map/ppermute | solution.py:149
  163.5 57.0 %collective-permute-start.18 = (bf16[8,72,1152]{2,1,0:T(8,128)(2,1)S(1)}, bf16[8,72,1152]{2,1,0:T(8,128)(2,1)}, u32[]{:S(2)}, u32[]{:S(2)}) collective-permute-start(bf16[8,72,1152]{2,1,0:T(8,128)(2,1)S(1)} %constant_dynamic-update-slice_fusion.4.refs_0_), channel_id=1, source_target_pairs={{0,1},{1,0},{2,3},{3,2},{4,5},{5,4},{6,7},{7,6},{8,9},{9,8},{10,11... | collective-permute-start | bytes 3981320 | tf_op jit(solution)/shard_map/ppermute | solution.py:149
  165.7 54.8 %collective-permute-start.19 = (bf16[8,72,1024]{2,1,0:T(8,128)(2,1)S(1)}, bf16[8,72,1024]{2,1,0:T(8,128)(2,1)}, u32[]{:S(2)}, u32[]{:S(2)}) collective-permute-start(bf16[8,72,1024]{2,1,0:T(8,128)(2,1)S(1)} %constant_dynamic-update-slice_fusion.6.refs_4_), channel_id=1, source_target_pairs={{0,2},{1,3},{2,0},{3,1},{4,6},{5,7},{6,4},{7,5},{8,10},{9,11},{10,... | collective-permute-start | bytes 3538952 | tf_op jit(solution)/shard_map/ppermute | solution.py:149
  166.3 54.2 %collective-permute-start.20 = (bf16[8,72,1024]{2,1,0:T(8,128)(2,1)S(1)}, bf16[8,72,1024]{2,1,0:T(8,128)(2,1)}, u32[]{:S(2)}, u32[]{:S(2)}) collective-permute-start(bf16[8,72,1024]{2,1,0:T(8,128)(2,1)S(1)} %constant_dynamic-update-slice_fusion.6.refs_4_), channel_id=1, source_target_pairs={{0,1},{1,0},{2,3},{3,2},{4,5},{5,4},{6,7},{7,6},{8,9},{9,8},{10,11... | collective-permute-start | bytes 3538952 | tf_op jit(solution)/shard_map/ppermute | solution.py:149
  241.5 31.6 %collective-permute-start.28 = (bf16[8,72,1152]{2,1,0:T(8,128)(2,1)S(1)}, bf16[8,72,1152]{2,1,0:T(8,128)(2,1)S(1)}, u32[]{:S(2)}, u32[]{:S(2)}) collective-permute-start(bf16[8,72,1152]{2,1,0:T(8,128)(2,1)S(1)} %constant_dynamic-update-slice_fusion.8), channel_id=1, source_target_pairs={{0,4},{1,5},{2,6},{3,7},{4,0},{5,1},{6,2},{7,3},{8,12},{9,13},{10,... | collective-permute-start | bytes 3981320 | tf_op jit(solution)/shard_map/ppermute | solution.py:149
  242.1 31.0 %collective-permute-start.29 = (bf16[8,72,1152]{2,1,0:T(8,128)(2,1)S(1)}, bf16[8,72,1152]{2,1,0:T(8,128)(2,1)S(1)}, u32[]{:S(2)}, u32[]{:S(2)}) collective-permute-start(bf16[8,72,1152]{2,1,0:T(8,128)(2,1)S(1)} %constant_dynamic-update-slice_fusion.8), channel_id=1, source_target_pairs={{0,1},{1,0},{2,3},{3,2},{4,5},{5,4},{6,7},{7,6},{8,9},{9,8},{10,11... | collective-permute-start | bytes 3981320 | tf_op jit(solution)/shard_map/ppermute | solution.py:149
  303.5 38.6 %collective-permute-start.34 = (bf16[4,2,2,136,1152]{4,3,2,1,0:T(8,128)(2,1)}, bf16[4,2,2,136,1152]{4,3,2,1,0:T(8,128)(2,1)}, u32[]{:S(2)}, u32[]{:S(2)}) collective-permute-start(bf16[4,2,2,136,1152]{4,3,2,1,0:T(8,128)(2,1)} %pad_maximum_fusion.2), channel_id=1, source_target_pairs={{0,1},{1,0},{2,3},{3,2},{4,5},{5,4},{6,7},{7,6},{8,9},{9,8},{10,11... | collective-permute-start | bytes 15040520 | tf_op jit(solution)/shard_map/ppermute | solution.py:149
  349.3 33.2 %collective-permute-start.36 = (bf16[4,2,64,1152]{3,2,1,0:T(8,128)(2,1)S(1)}, bf16[4,2,64,1152]{3,2,1,0:T(8,128)(2,1)S(1)}, u32[]{:S(2)}, u32[]{:S(2)}) collective-permute-start(bf16[4,2,64,1152]{3,2,1,0:T(8,128)(2,1)S(1)} %fusion.18), channel_id=1, source_target_pairs={{0,2},{1,3},{2,0},{3,1},{4,6},{5,7},{6,4},{7,5},{8,10},{9,11},{10,... | collective-permute-start | bytes 3538952 | tf_op jit(solution)/shard_map/ppermute | solution.py:149
  350.5 32.0 %collective-permute-start.35 = (bf16[4,2,72,1152]{3,2,1,0:T(8,128)(2,1)S(1)}, bf16[4,2,72,1152]{3,2,1,0:T(8,128)(2,1)}, u32[]{:S(2)}, u32[]{:S(2)}) collective-permute-start(bf16[4,2,72,1152]{3,2,1,0:T(8,128)(2,1)S(1)} %fusion.12), channel_id=1, source_target_pairs={{0,4},{1,5},{2,6},{3,7},{4,0},{5,1},{6,2},{7,3},{8,12},{9,13},{10,... | collective-permute-start | bytes 3981320 | tf_op jit(solution)/shard_map/ppermute | solution.py:149
  388.1 36.9 %collective-permute-start.39 = (bf16[4,2,2,72,2176]{4,3,2,1,0:T(8,128)(2,1)}, bf16[4,2,2,72,2176]{4,3,2,1,0:T(8,128)(2,1)}, u32[]{:S(2)}, u32[]{:S(2)}) collective-permute-start(bf16[4,2,2,72,2176]{4,3,2,1,0:T(8,128)(2,1)} %slice.440), channel_id=1, source_target_pairs={{0,1},{1,0},{2,3},{3,2},{4,5},{5,4},{6,7},{7,6},{8,9},{9,8},{10,11... | collective-permute-start | bytes 15040520 | tf_op jit(solution)/shard_map/ppermute | solution.py:149
  432.1 68.5 %collective-permute-start.44 = (bf16[4,2,72,1024]{3,2,1,0:T(8,128)(2,1)}, bf16[4,2,72,1024]{3,2,1,0:T(8,128)(2,1)}, u32[]{:S(2)}, u32[]{:S(2)}) collective-permute-start(bf16[4,2,72,1024]{3,2,1,0:T(8,128)(2,1)} %fusion.19), channel_id=1, source_target_pairs={{0,2},{1,3},{2,0},{3,1},{4,6},{5,7},{6,4},{7,5},{8,10},{9,11},{10,... | collective-permute-start | bytes 3538952 | tf_op jit(solution)/shard_map/ppermute | solution.py:149
  434.6 66.0 %collective-permute-start.43 = (bf16[4,2,72,1152]{3,2,1,0:T(8,128)(2,1)}, bf16[4,2,72,1152]{3,2,1,0:T(8,128)(2,1)}, u32[]{:S(2)}, u32[]{:S(2)}) collective-permute-start(bf16[4,2,72,1152]{3,2,1,0:T(8,128)(2,1)} %fusion.13), channel_id=1, source_target_pairs={{0,4},{1,5},{2,6},{3,7},{4,0},{5,1},{6,2},{7,3},{8,12},{9,13},{10,... | collective-permute-start | bytes 3981320 | tf_op jit(solution)/shard_map/ppermute | solution.py:149
  441.8 58.8 %collective-permute-start.42 = (bf16[136,1152]{1,0:T(8,128)(2,1)}, bf16[136,1152]{1,0:T(8,128)(2,1)S(1)}, u32[]{:S(2)}, u32[]{:S(2)}) collective-permute-start(bf16[136,1152]{1,0:T(8,128)(2,1)} %pad_maximum_fusion.18), channel_id=1, source_target_pairs={{0,24},{1,25},{2,26},{3,27},{4,28},{5,29},{6,30},{7,31},{8,16},{9,... | collective-permute-start | bytes 940040 | tf_op jit(solution)/shard_map/ppermute | solution.py:149
  444.1 56.5 %collective-permute-start.41 = (bf16[136,1152]{1,0:T(8,128)(2,1)}, bf16[136,1152]{1,0:T(8,128)(2,1)}, u32[]{:S(2)}, u32[]{:S(2)}) collective-permute-start(bf16[136,1152]{1,0:T(8,128)(2,1)} %pad_maximum_fusion.17), channel_id=1, source_target_pairs={{0,16},{1,17},{2,18},{3,19},{4,20},{5,21},{6,22},{7,23},{8,24},{9,... | collective-permute-start | bytes 940040 | tf_op jit(solution)/shard_map/ppermute | solution.py:149
  444.8 55.7 %collective-permute-start.40 = (bf16[136,1152]{1,0:T(8,128)(2,1)}, bf16[136,1152]{1,0:T(8,128)(2,1)}, u32[]{:S(2)}, u32[]{:S(2)}) collective-permute-start(bf16[136,1152]{1,0:T(8,128)(2,1)} %pad_maximum_fusion.16), channel_id=1, source_target_pairs={{0,8},{1,9},{2,10},{3,11},{4,12},{5,13},{6,14},{7,15},{8,0},{9,1},... | collective-permute-start | bytes 940040 | tf_op jit(solution)/shard_map/ppermute | solution.py:149
  576.5 30.3 %collective-permute-start.49 = (bf16[4,2,72,1152]{3,2,1,0:T(8,128)(2,1)S(1)}, bf16[4,2,72,1152]{3,2,1,0:T(8,128)(2,1)S(1)}, u32[]{:S(2)}, u32[]{:S(2)}) collective-permute-start(bf16[4,2,72,1152]{3,2,1,0:T(8,128)(2,1)S(1)} %fusion.14), channel_id=1, source_target_pairs={{0,2},{1,3},{2,0},{3,1},{4,6},{5,7},{6,4},{7,5},{8,10},{9,11},{10,... | collective-permute-start | bytes 3981320 | tf_op jit(solution)/shard_map/ppermute | solution.py:149
  578.1 33.1 %collective-permute-start.48 = (bf16[4,2,72,1280]{3,2,1,0:T(8,128)(2,1)S(1)}, bf16[4,2,72,1280]{3,2,1,0:T(8,128)(2,1)S(1)}, u32[]{:S(2)}, u32[]{:S(2)}) collective-permute-start(bf16[4,2,72,1280]{3,2,1,0:T(8,128)(2,1)S(1)} %fusion.10), channel_id=1, source_target_pairs={{0,4},{1,5},{2,6},{3,7},{4,0},{5,1},{6,2},{7,3},{8,12},{9,13},{10,... | collective-permute-start | bytes 4423688 | tf_op jit(solution)/shard_map/ppermute | solution.py:149
  641.2 30.1 %collective-permute-start.59 = (bf16[72,2432]{1,0:T(8,128)(2,1)S(1)}, bf16[72,2432]{1,0:T(8,128)(2,1)S(1)}, u32[]{:S(2)}, u32[]{:S(2)}) collective-permute-start(bf16[72,2432]{1,0:T(8,128)(2,1)S(1)} %pad_maximum_fusion.15), channel_id=1, source_target_pairs={{0,24},{1,25},{2,26},{3,27},{4,28},{5,29},{6,30},{7,31},{8,16},{9,... | collective-permute-start | bytes 1050632 | tf_op jit(solution)/shard_map/ppermute | solution.py:149
  (130 other events, 1836.2 us)

commit v3 on v2

v3 whole, which is shorter than its diff:
```python
import functools
import itertools
import jax
import jax.numpy as jnp
from jax import lax
from jax.sharding import PartitionSpec as P
from jax.experimental import pallas as pl
from jax.experimental.pallas import tpu as pltpu
D=1152; HEADS=16; HEAD_DIM=72; LANES=128
NEG=-1e30
LOG2E=1.4426950408889634
def nt(a,b): return lax.dot_general(a,b,(((1,),(1,)),((),())),preferred_element_type=jnp.float32)
def nn(a,b): return lax.dot_general(a,b,(((1,),(0,)),((),())),preferred_element_type=jnp.float32)

def fill_heads(dst, src, col, tokens, fill):
    rows=dst.shape[1]
    for h in range(HEADS):
        if fill is not None:
            dst[h]=fill
        dst[h,0:tokens,0:HEAD_DIM]=src[:,col+h*HEAD_DIM:col+(h+1)*HEAD_DIM]

def pad_values(rows, tokens, kind):
    lane=lax.broadcasted_iota(jnp.int32,(rows,LANES),1)
    row=lax.broadcasted_iota(jnp.int32,(rows,LANES),0)
    if kind=="query":
        v=jnp.where(lane==HEAD_DIM,1.0,0.0)
    elif kind=="key":
        v=jnp.where((lane==HEAD_DIM)&(row>=tokens),NEG,0.0)
    else:
        v=jnp.zeros((rows,LANES),jnp.float32)
    return v.astype(jnp.bfloat16)

def fwd_kernel(tokens, krows, qrows, per, qkv_ref, mixed_ref, lse_ref, qs, ks, vs, os):
    step=pl.program_id(0)
    @pl.when(step==0)
    def _():
        fill_heads(qs,qkv_ref,0,tokens,pad_values(qrows,tokens,"query"))
        fill_heads(ks,qkv_ref,D,tokens,pad_values(krows,tokens,"key"))
        zero=pad_values(krows,tokens,"value")
        for h in range(HEADS):
            vs[h]=zero
            vs[h,0:tokens,0:HEAD_DIM]=qkv_ref[:,2*D+h*HEAD_DIM:2*D+(h+1)*HEAD_DIM]
    c=HEAD_DIM**-0.5*LOG2E
    for j in range(per):
        h=step*per+j
        s=nt(ks[h],qs[h])
        m=jnp.max(s,axis=0,keepdims=True)
        e=jnp.exp2((s-m)*c)
        l=jnp.sum(e,axis=0,keepdims=True)
        p=(e*(1.0/l)).astype(jnp.bfloat16)
        vt=vs[h].T
        ot=nn(vt,p)
        os[h]=ot.T.astype(jnp.bfloat16)
        lse_ref[j]=m*c+jnp.log2(l)
    @pl.when(step==pl.num_programs(0)-1)
    def _():
        for h in range(HEADS):
            mixed_ref[:,h*HEAD_DIM:(h+1)*HEAD_DIM]=os[h,0:tokens,0:HEAD_DIM]

def attn_fwd(qkv, per=1):
    tokens=qkv.shape[0]
    krows=-(-tokens//16)*16; qrows=-(-tokens//128)*128
    return pl.pallas_call(functools.partial(fwd_kernel,tokens,krows,qrows,per),
        grid=(HEADS//per,),
        in_specs=[pl.BlockSpec(qkv.shape,lambda i:(0,0),pipeline_mode=pl.Buffered(1))],
        out_specs=[pl.BlockSpec((tokens,D),lambda i:(0,0),pipeline_mode=pl.Buffered(1)),pl.BlockSpec((per,1,qrows),lambda i:(i,0,0))],
        out_shape=[jax.ShapeDtypeStruct((tokens,D),jnp.bfloat16),jax.ShapeDtypeStruct((HEADS,1,qrows),jnp.float32)],
        scratch_shapes=[pltpu.VMEM((HEADS,qrows,LANES),jnp.bfloat16),pltpu.VMEM((HEADS,krows,LANES),jnp.bfloat16),
                        pltpu.VMEM((HEADS,krows,LANES),jnp.bfloat16),pltpu.VMEM((HEADS,qrows,LANES),jnp.bfloat16)],
        compiler_params=pltpu.CompilerParams(vmem_limit_bytes=56<<20,dimension_semantics=("arbitrary",)),
        cost_estimate=pl.CostEstimate(flops=4*HEADS*qrows*krows*LANES,bytes_accessed=4*tokens*D*2,transcendentals=HEADS*qrows*krows),
        name="attention_forward")(qkv)

def bwd_kernel(tokens, krows, qrows, per, qkv_ref, go_ref, lse_ref, dqkv_ref, qs, ks, vs, gs):
    step=pl.program_id(0)
    @pl.when(step==0)
    def _():
        fill_heads(qs,qkv_ref,0,tokens,pad_values(qrows,tokens,"query"))
        fill_heads(ks,qkv_ref,D,tokens,pad_values(krows,tokens,"key"))
        fill_heads(vs,qkv_ref,2*D,tokens,pad_values(krows,tokens,"value"))
        fill_heads(gs,go_ref,0,tokens,pad_values(qrows,tokens,"value"))
    scale=HEAD_DIM**-0.5
    c=scale*LOG2E
    for j in range(per):
        h=step*per+j
        q=qs[h]; k=ks[h]; v=vs[h]; g=gs[h]
        s=nt(k,q)
        p=jnp.exp2(s*c-lse_ref[j])
        dp=nt(v,g)
        dv=nn(p.astype(jnp.bfloat16),g)
        delta=jnp.sum(p*dp,axis=0,keepdims=True)
        ds=(p*(dp-delta)).astype(jnp.bfloat16)
        dk=nn(ds,q)*scale
        dqt=nn(k.T,ds)*scale
        qs[h]=dqt.T.astype(jnp.bfloat16)
        ks[h]=dk.astype(jnp.bfloat16)
        vs[h]=dv.astype(jnp.bfloat16)
    @pl.when(step==pl.num_programs(0)-1)
    def _():
        for i,r in enumerate((qs,ks,vs)):
            for h in range(HEADS):
                dqkv_ref[:,i*D+h*HEAD_DIM:i*D+(h+1)*HEAD_DIM]=r[h,0:tokens,0:HEAD_DIM]

def attn_bwd(qkv, gmixed, lse, per=1):
    tokens=qkv.shape[0]
    krows=-(-tokens//16)*16; qrows=-(-tokens//128)*128
    return pl.pallas_call(functools.partial(bwd_kernel,tokens,krows,qrows,per),
        grid=(HEADS//per,),
        in_specs=[pl.BlockSpec(qkv.shape,lambda i:(0,0),pipeline_mode=pl.Buffered(1)),pl.BlockSpec(gmixed.shape,lambda i:(0,0),pipeline_mode=pl.Buffered(1)),
                  pl.BlockSpec((per,1,qrows),lambda i:(i,0,0))],
        out_specs=pl.BlockSpec((tokens,3*D),lambda i:(0,0),pipeline_mode=pl.Buffered(1)),
        out_shape=jax.ShapeDtypeStruct((tokens,3*D),jnp.bfloat16),
        scratch_shapes=[pltpu.VMEM((HEADS,qrows,LANES),jnp.bfloat16),pltpu.VMEM((HEADS,krows,LANES),jnp.bfloat16),
                        pltpu.VMEM((HEADS,krows,LANES),jnp.bfloat16),pltpu.VMEM((HEADS,qrows,LANES),jnp.bfloat16)],
        compiler_params=pltpu.CompilerParams(vmem_limit_bytes=56<<20,dimension_semantics=("arbitrary",)),
        cost_estimate=pl.CostEstimate(flops=10*HEADS*qrows*krows*LANES,bytes_accessed=7*tokens*D*2,transcendentals=HEADS*qrows*krows),
        name="attention_backward")(qkv,gmixed,lse)


FF = 4304
GROUPS = 16
FF_GROUP = FF // GROUPS
FF_ROWS = 272
FF_PAD = GROUPS * FF_ROWS
PAIR_ROWS = D // GROUPS
HALF_DOWN = FF_ROWS // 2
OWN_ROWS = PAIR_ROWS // 2
TILE = 8
BLOCK_TILES = 5
PAIR_TILES = PAIR_ROWS // TILE
EXTRA = 128
QKV_CUT = 14 * 128
UP_CUT = 22 * 128
UP_PIECES = 4
REST_ROWS = UP_PIECES * BLOCK_TILES * TILE + BLOCK_TILES * TILE + HALF_DOWN
VECTORS = (0, 1, 3, 6, 8, 9, 10, 12, 14)
bf16 = jnp.bfloat16
f32 = jnp.float32


def product(left, right):
    return jnp.dot(left, right, preferred_element_type=f32)


def product_t(left, right):
    return lax.dot_general(left, right, (((0,), (0,)), ((), ())), preferred_element_type=f32)


def product_bt(left, right):
    return lax.dot_general(left, right, (((1,), (1,)), ((), ())), preferred_element_type=f32)


def swap(value, mask):
    devices = lax.axis_size("fsdp")
    return lax.ppermute(value, "fsdp", [(i, i ^ mask) for i in range(devices)])


def pad_hidden(columns):
    rows = columns.shape[0]
    grouped = columns.reshape(rows, GROUPS, FF_GROUP)
    return jnp.pad(grouped, ((0, 0), (0, 0), (0, FF_ROWS - FF_GROUP))).reshape(rows, FF_PAD)


def trim_hidden(columns):
    rows = columns.shape[0]
    return columns.reshape(rows, GROUPS, FF_ROWS)[:, :, :FF_GROUP].reshape(rows, FF)


def place_square_kernel(coords, *refs):
    sources, (whole, small) = refs[:8], refs[8:10]
    held, in_sems, out_sems = refs[10:18], refs[18], refs[19]
    core, x, y, z = coords[0], coords[1], coords[2], coords[3]
    arrivals = [pltpu.make_async_copy(sources[i], held[i], in_sems.at[i]) for i in range(8)]
    for arrival in arrivals:
        arrival.start()
    copies, extras = [], []
    for part, stream in itertools.product(range(4), range(2)):
        arrivals[4 * stream + part].wait()
        for near, dz in itertools.product(range(2), range(4)):
            src = held[4 * stream + part].at[near * 4 + dz]
            owner = core if part < 2 else 1 - core
            far = part % 2
            dx, dy = (near, far) if stream == 0 else (far, near)
            chip = ((z ^ dz) * 2 + (y ^ dy)) * 2 + (x ^ dx)
            cols = src.shape[-1] - (0 if stream else EXTRA)
            col = QKV_CUT - EXTRA if stream else 0
            src_cols = pl.ds(0 if stream else EXTRA, cols)
            first = PAIR_TILES * chip + BLOCK_TILES * owner
            copies.append(
                pltpu.make_async_copy(
                    src.at[pl.ds(owner, BLOCK_TILES - 1), :, src_cols],
                    whole.at[pl.ds(first, BLOCK_TILES - 1), :, pl.ds(col, cols)],
                    out_sems.at[len(copies)],
                )
            )
            copies[-1].start()
            extra = pltpu.make_async_copy(
                src.at[BLOCK_TILES - 1, :, src_cols],
                whole.at[PAIR_TILES * chip + BLOCK_TILES - 1, :, pl.ds(col, cols)],
                out_sems.at[96 + len(extras)],
            )
            pl.when(owner == 0)(extra.start)
            extras.append((owner, extra))
            if stream == 0:
                copies.append(
                    pltpu.make_async_copy(
                        src.at[:, :, :EXTRA], small.at[chip * 2 + owner], out_sems.at[len(copies)]
                    )
                )
                copies[-1].start()
    for copy in copies:
        copy.wait()
    for owner, extra in extras:
        pl.when(owner == 0)(extra.wait)


def place_square(streams, coords):
    sources = [s.reshape(8, BLOCK_TILES, TILE, -1) for s in (*streams[0], *streams[1])]
    size = sum(s.size for s in sources) * 2
    whole, small = pl.pallas_call(
        place_square_kernel,
        in_specs=[pl.BlockSpec(memory_space=pltpu.SMEM)]
        + [pl.BlockSpec(memory_space=pltpu.HBM)] * 8,
        out_specs=[pl.BlockSpec(memory_space=pltpu.HBM)] * 2,
        out_shape=[
            jax.ShapeDtypeStruct((GROUPS * PAIR_TILES, TILE, 3 * D), bf16),
            jax.ShapeDtypeStruct((2 * GROUPS, BLOCK_TILES, TILE, EXTRA), bf16),
        ],
        scratch_shapes=[pltpu.VMEM(s.shape, bf16) for s in sources]
        + [pltpu.SemaphoreType.DMA((8,)), pltpu.SemaphoreType.DMA((160,))],
        compiler_params=pltpu.CompilerParams(vmem_limit_bytes=40 << 20),
        cost_estimate=pl.CostEstimate(flops=0, bytes_accessed=2 * size, transcendentals=0),
        name="place_square",
    )(coords, *sources)
    return whole.reshape(D, 3 * D), small.reshape(2 * GROUPS, -1)


def place_rest_kernel(source, up, out, down, held, in_sems, out_sems):
    arrivals = [
        pltpu.make_async_copy(source.at[i], held.at[i], in_sems.at[i]) for i in range(2 * GROUPS)
    ]
    for arrival in arrivals:
        arrival.start()
    copies = []
    for device in range(2 * GROUPS):
        chip, owner = device // 2, device % 2
        src = held.at[device]
        arrivals[device].wait()
        jobs = []
        count = BLOCK_TILES - owner
        first = PAIR_TILES * chip + BLOCK_TILES * owner
        for piece in range(UP_PIECES):
            cols = min(D, FF_PAD - piece * D)
            jobs.append(
                (
                    src.at[pl.ds(piece * BLOCK_TILES + owner, count), :, pl.ds(0, cols)],
                    up.at[pl.ds(first, count), :, pl.ds(piece * D, cols)],
                )
            )
        base = UP_PIECES * BLOCK_TILES
        jobs.append((src.at[pl.ds(base + owner, count)], out.at[pl.ds(first, count)]))
        rows = HALF_DOWN // TILE
        jobs.append((src.at[pl.ds(base + BLOCK_TILES, rows)], down.at[pl.ds(device * rows, rows)]))
        for one, other in jobs:
            copies.append(pltpu.make_async_copy(one, other, out_sems.at[len(copies)]))
            copies[-1].start()
    for copy in copies:
        copy.wait()


def place_rest(gathered):
    source = gathered.reshape(2 * GROUPS, REST_ROWS // TILE, TILE, D)
    up, out, down = pl.pallas_call(
        place_rest_kernel,
        in_specs=[pl.BlockSpec(memory_space=pltpu.HBM)],
        out_specs=[pl.BlockSpec(memory_space=pltpu.HBM)] * 3,
        out_shape=[
            jax.ShapeDtypeStruct((D // TILE, TILE, FF_PAD), bf16),
            jax.ShapeDtypeStruct((D // TILE, TILE, D), bf16),
            jax.ShapeDtypeStruct((FF_PAD // TILE, TILE, D), bf16),
        ],
        scratch_shapes=[
            pltpu.VMEM(source.shape, bf16),
            pltpu.SemaphoreType.DMA((2 * GROUPS,)),
            pltpu.SemaphoreType.DMA((2 * GROUPS * (UP_PIECES + 2),)),
        ],
        compiler_params=pltpu.CompilerParams(vmem_limit_bytes=56 << 20),
        cost_estimate=pl.CostEstimate(
            flops=0, bytes_accessed=4 * source.size, transcendentals=0
        ),
        name="place_rest",
    )(source)
    return up.reshape(D, FF_PAD), out.reshape(D, D), down.reshape(FF_PAD, D)


def tie(*values):
    leaves, form = jax.tree.flatten(values)
    return form.unflatten(lax.optimization_barrier(leaves))


def gather_z(block):
    return [block] + [swap(block, 8 * step) for step in (1, 2, 3)]


def gather_near(parts, cut, axis):
    streams = []
    for stream in range(2):
        if axis == 1:
            own = jnp.stack([p[:, :cut] if stream == 0 else p[:, cut:] for p in parts])
        else:
            own = jnp.stack([p[:cut] if stream == 0 else p[cut:] for p in parts])
        streams.append((own, swap(own, 4 if stream else 2)))
    return streams


def gather_far(streams):
    results = []
    for stream in range(2):
        first = jnp.concatenate(streams[stream])
        results.append((first, swap(first, 2 if stream else 4), swap(first, 1)))
    return results


def gather_core(streams):
    return [(first, second, third, swap(second, 1)) for first, second, third in streams]


def window(value, starts, sizes):
    rank = value.ndim
    starts = list(starts) + [0] * (rank - len(starts))
    lengths = list(value.shape)
    for axis, size in enumerate(sizes):
        if size is not None:
            lengths[axis] = size
    starts = [jnp.int32(0) if start is None else jnp.int32(start) for start in starts]
    result = lax.dynamic_slice(value, starts, lengths)
    kept = [
        length for axis, length in enumerate(lengths) if axis >= len(sizes) or sizes[axis] != 1
    ]
    return result.reshape(kept)


class Reduction:
    def __init__(self, matrices, streams, coords):
        self.matrices = [m.reshape(4, 2, 2, PAIR_TILES, TILE, -1) for m in matrices]
        self.streams = streams
        self.coords = coords

    def part(self, arrays, stream, plane, tile):
        sizes = tuple(None if p is None else 1 for p in plane) + (BLOCK_TILES, None)
        pieces = []
        for number, first, last in self.streams[stream]:
            starts = tuple(plane) + (tile, None, first)
            pieces.append(window(arrays[number], starts, sizes + (last - first,)))
        return pieces[0] if len(pieces) == 1 else jnp.concatenate(pieces, axis=-1)

    def terms(self, stream, plane):
        tile = self.coords[0] * (PAIR_TILES - BLOCK_TILES)
        own = self.part(self.matrices, stream, plane, tile)
        return [own, self.part(self.other, stream, plane, 0)]

    def core_step(self):
        tile = (1 - self.coords[0]) * (PAIR_TILES - BLOCK_TILES)
        starts, sizes = (None, None, None, tile), (None, None, None, BLOCK_TILES)
        return [swap(window(m, starts, sizes), 1) for m in self.matrices]

    def far_step(self, other):
        core, x, y, z = self.coords
        self.other = other
        got = []
        for stream in range(2):
            plane = (None, None, 1 - x) if stream else (None, 1 - y, None)
            send = total_of(self.terms(stream, plane)).astype(bf16)
            got.append(swap(send, 2 if stream else 4))
        return got

    def near_step(self, far):
        core, x, y, z = self.coords
        self.far = far
        got = []
        for stream in range(2):
            plane = (None, 1 - y, x) if stream else (None, y, 1 - x)
            after = (None, 1 - y) if stream else (None, 1 - x)
            terms = self.terms(stream, plane) + [window(far[stream], after, (None, 1))]
            got.append(swap(total_of(terms).astype(bf16), 4 if stream else 2))
        return got

    def at(self, plane):
        core, x, y, z = self.coords
        pieces = []
        for stream in range(2):
            after = (plane, y) if stream else (plane, x)
            terms = self.terms(stream, (plane, y, x)) + [
                window(self.far[stream], after, (1, 1)),
                window(self.near[stream], (plane,), (1,)),
            ]
            pieces.append(total_of(terms))
        return jnp.concatenate(pieces, axis=-1)

    def z_step(self, near):
        z = self.coords[3]
        self.near = near
        return [swap(self.at(z ^ step).astype(bf16), 8 * step) for step in (1, 2, 3)]

    def finish(self, arrived):
        core, x, y, z = self.coords
        total = total_of([self.at(z)] + arrived)
        total = total.reshape(BLOCK_TILES * TILE, -1)
        return lax.dynamic_slice_in_dim(
            total, core * (BLOCK_TILES * TILE - OWN_ROWS), OWN_ROWS, 0
        )


def total_of(terms):
    total = terms[0].astype(f32)
    for term in terms[1:]:
        total = total + term.astype(f32)
    return total


def fetch_pairs(narrow, core):
    q, k, v, o = (narrow[i].reshape(OWN_ROWS, D) for i in (2, 4, 5, 7))
    up = pad_hidden(narrow[11].reshape(OWN_ROWS, FF))
    down = narrow[13]
    rows = jnp.concatenate([q, k, v, o, up], axis=1)
    spare = BLOCK_TILES * TILE - OWN_ROWS
    lead = D * HALF_DOWN - down.shape[0]
    tail = jnp.pad(down[:lead].reshape(spare, -1), ((0, 0), (0, 512 - lead // spare)))
    is_first = core == 0
    edge = jnp.where(is_first, rows[OWN_ROWS - spare :], rows[:spare])
    got = swap(jnp.concatenate([edge, tail], axis=1), 1)
    edge = got[:, : rows.shape[1]]
    block = jnp.where(is_first, jnp.concatenate([rows, edge]), jnp.concatenate([edge, rows]))
    extra = got[:, rows.shape[1] : rows.shape[1] + lead // spare].reshape(-1)
    end = jnp.zeros((D * HALF_DOWN - (down.shape[0] - lead),), bf16)
    down_block = jnp.where(
        is_first, jnp.concatenate([down, extra]), jnp.concatenate([down[lead:], end])
    ).reshape(HALF_DOWN, D)
    small = jnp.concatenate([narrow[i] for i in VECTORS])
    small = jnp.pad(small, (0, BLOCK_TILES * TILE * EXTRA - small.shape[0]))
    small = small.reshape(BLOCK_TILES * TILE, EXTRA)
    square = jnp.concatenate([small, block[:, : 3 * D]], axis=1)
    up_block = jnp.pad(block[:, 4 * D :], ((0, 0), (0, UP_PIECES * D - FF_PAD)))
    pieces = [up_block[:, i * D : (i + 1) * D] for i in range(UP_PIECES)]
    rest = jnp.concatenate(pieces + [block[:, 3 * D : 4 * D], down_block])
    return square, rest


def normalize(values):
    centre = jnp.mean(values, axis=-1, keepdims=True)
    centered = values - centre
    spread_sq = jnp.mean(centered * centered, axis=-1, keepdims=True)
    inverse = lax.rsqrt(spread_sq + 1e-06)
    return centered * inverse, inverse


def normalize_back(grad, gain, xhat, inverse):
    scaled = grad * gain
    first = jnp.mean(scaled, axis=-1, keepdims=True)
    second = jnp.mean(scaled * xhat, axis=-1, keepdims=True)
    return inverse * (scaled - first - xhat * second)


def name_vectors(whole, widths):
    found = {}
    position = 0
    for i in VECTORS:
        found[i] = whole[:, position : position + widths[i]].reshape(-1).astype(f32)
        position += widths[i]
    return found


def gather_plain(narrow, widths):
    whole = {
        i: lax.all_gather(narrow[i], "fsdp", axis=0, tiled=True) for i in (2, 4, 5, 7, 11, 13)
    }
    square = [whole[i][: D * D].reshape(D, D) for i in (2, 4, 5, 7)]
    up = pad_hidden(whole[11][: D * FF].reshape(D, FF))
    down = pad_hidden(whole[13][: D * FF].reshape(FF, D).T).T
    joined = jnp.concatenate([narrow[i] for i in VECTORS])
    length = joined.shape[0]
    joined = jnp.pad(joined, (0, 2048 - length)).reshape(16, 128)
    joined = lax.all_gather(joined, "fsdp", axis=0, tiled=True).reshape(-1, 2048)
    return jnp.concatenate(square[:3], axis=1), square[3], up, down, name_vectors(joined, widths)


def on_device(*args):
    devices = lax.axis_size("fsdp")
    tokens, image_valid = args[0], args[1]
    shards = args[2:17]
    cotangent = args[17]
    staged = devices == 32
    widths = [piece.shape[0] for piece in shards]
    narrow = [piece.astype(bf16) for piece in shards]
    index = lax.axis_index("fsdp")
    core, x, y, z = index % 2, (index // 2) % 2, (index // 4) % 2, index // 8
    coords = (core, x, y, z)
    image_count = image_valid.shape[0]
    seq_len = tokens.shape[0] // image_count
    weight_img = jnp.repeat(image_valid.astype(f32), seq_len)[:, None]

    grad_out = weight_img * cotangent
    grad_branch = grad_out.astype(bf16)
    grads = {14: jnp.sum(grad_branch.astype(f32), axis=0)}
    xhat_one, inverse_one = normalize(tokens)
    if staged:
        where = jnp.stack(coords).astype(jnp.int32)
        sq, rest = fetch_pairs(narrow, core)
        rest = lax.all_gather(rest, "fsdp", axis=0, tiled=True)
        sq = gather_z(sq)
        sq, xhat_one, inverse_one, grad_branch = tie(sq, xhat_one, inverse_one, grad_branch)
        sq = gather_near(sq, QKV_CUT, 1)
        sq = gather_far(sq)
        sq = gather_core(sq)
        weight_qkv, small = place_square(sq, where)
        vectors = name_vectors(small, widths)
    else:
        weight_qkv, weight_o, weight_up, weight_down, vectors = gather_plain(narrow, widths)

    vec = lambda i: vectors[i][:D]
    gain_one, shift_one, gain_two, shift_two = vec(0), vec(1), vec(9), vec(10)
    bias_qkv = jnp.concatenate([vec(3), jnp.zeros((D,), f32), vec(6)])
    bias_o, bias_down = vec(8), vec(14)
    bias_up = pad_hidden(vectors[12][:FF].reshape(1, FF))

    normed = (xhat_one * gain_one + shift_one).astype(bf16)
    qkv = (product(normed, weight_qkv) + bias_qkv).astype(bf16)
    mixed, lse = attn_fwd(qkv, 2)
    if staged:
        mixed, lse, rest = tie(mixed, lse, rest)
        weight_up, weight_o, weight_down = place_rest(rest)
    resid = tokens + product(mixed, weight_o) + bias_o
    xhat_two, inverse_two = normalize(resid)
    normed_two = (xhat_two * gain_two + shift_two).astype(bf16)
    pre = product(normed_two, weight_up) + bias_up
    hidden = jax.nn.gelu(pre, approximate=True).astype(bf16)
    down_grad = product_t(hidden, grad_branch).astype(bf16)
    if staged:
        grad_branch, down_grad, pre = tie(grad_branch, down_grad, pre)
        down_sum = lax.psum_scatter(down_grad, "fsdp", scatter_dimension=0, tiled=True)
    layer_out = weight_img * (resid + product(hidden, weight_down) + bias_down)
    gelu_back = jax.vjp(lambda t: jax.nn.gelu(t, approximate=True), pre)[1]
    grad_pre = gelu_back(product_bt(grad_branch, weight_down))[0].astype(bf16)
    up_bias_grad = jnp.sum(grad_pre.astype(f32), axis=0)
    up_grad = product_t(normed_two, grad_pre).astype(bf16)
    grad_normed_two = product_bt(grad_pre, weight_up)
    grads[9] = jnp.sum(grad_normed_two * xhat_two, axis=0)
    grads[10] = jnp.sum(grad_normed_two, axis=0)
    grad_resid = grad_out + normalize_back(grad_normed_two, gain_two, xhat_two, inverse_two)
    grad_attn = grad_resid.astype(bf16)
    grads[8] = jnp.sum(grad_attn.astype(f32), axis=0)
    o_grad = product_t(mixed, grad_attn).astype(bf16)
    if staged:
        up_grad, o_grad, grad_attn = tie(up_grad, o_grad, grad_attn)
        outer = Reduction(
            (up_grad, o_grad), (((0, 0, UP_CUT),), ((0, UP_CUT, FF_PAD), (1, 0, D))), coords
        )
        outer_other = outer.core_step()
    grad_mixed = product_bt(grad_attn, weight_o).astype(bf16)
    if staged:
        grad_mixed, outer_other = tie(grad_mixed, outer_other)
        outer_far = outer.far_step(outer_other)
    grad_qkv = attn_bwd(qkv, grad_mixed, lse, 2)
    if staged:
        grad_qkv, outer_far = tie(grad_qkv, outer_far)
        outer_near = outer.near_step(outer_far)
    qkv_bias_grad = jnp.sum(grad_qkv.astype(f32), axis=0)
    grads[3], grads[6] = qkv_bias_grad[:D], qkv_bias_grad[2 * D :]
    qkv_grad = product_t(normed, grad_qkv).astype(bf16)
    grad_normed = product_bt(grad_qkv, weight_qkv)
    grads[0] = jnp.sum(grad_normed * xhat_one, axis=0)
    grads[1] = jnp.sum(grad_normed, axis=0)
    grads[12] = trim_hidden(up_bias_grad.reshape(1, FF_PAD)).reshape(FF)

    rows = []
    for i in VECTORS:
        row = grads[i]
        row = jnp.pad(row, (0, widths[i] * devices - row.shape[0]))
        rows.append(row.reshape(devices, widths[i]))
    rows = jnp.concatenate(rows, axis=1)
    owned = [None] * 15
    if staged:
        rows = jnp.pad(rows, ((0, 0), (0, OWN_ROWS * EXTRA - rows.shape[1])))
        rows = rows.reshape(D, EXTRA).astype(bf16)
        inner = Reduction(
            (rows, qkv_grad),
            (((0, 0, EXTRA), (1, 0, QKV_CUT - EXTRA)), ((1, QKV_CUT - EXTRA, 3 * D),)),
            coords,
        )
        rows, qkv_grad, outer_near, grad_normed = tie(rows, qkv_grad, outer_near, grad_normed)
        outer_z = outer.z_step(outer_near)
        inner_other = inner.core_step()
        tokens_grad = grad_resid + normalize_back(grad_normed, gain_one, xhat_one, inverse_one)
        (inner_other,) = tie(inner_other)
        inner_far = inner.far_step(inner_other)
        inner_far, outer_z, tokens_grad = tie(inner_far, outer_z, tokens_grad)
        inner_near = inner.near_step(inner_far)

        flat = down_sum.astype(f32).reshape(-1)
        size = widths[13]
        lead = flat.shape[0] - size
        got = swap(down_sum.reshape(-1)[size:], 1).astype(f32)
        owned[13] = jnp.where(core == 0, flat[:size], jnp.concatenate([got, flat[: size - lead]]))
        outer_sum = outer.finish(outer_z)
        owned[11] = trim_hidden(outer_sum[:, :FF_PAD]).reshape(-1)
        owned[7] = outer_sum[:, FF_PAD:].reshape(-1)
        inner_near, owned[13], owned[11], owned[7] = tie(
            inner_near, owned[13], owned[11], owned[7]
        )
        inner_sum = inner.finish(inner.z_step(inner_near))
        for position, i in enumerate((2, 4, 5)):
            first = EXTRA + position * D
            owned[i] = inner_sum[:, first : first + D].reshape(-1)
        small = inner_sum[:, :EXTRA].reshape(-1)
    else:
        tokens_grad = grad_resid + normalize_back(grad_normed, gain_one, xhat_one, inverse_one)
        scatter = lambda value: lax.psum_scatter(
            value.astype(f32).reshape(-1), "fsdp", scatter_dimension=0, tiled=True
        )
        fill = lambda value, i: jnp.pad(
            value.reshape(-1), (0, widths[i] * devices - value.size)
        )
        for position, i in enumerate((2, 4, 5)):
            owned[i] = scatter(fill(qkv_grad[:, position * D : (position + 1) * D], i))
        owned[7] = scatter(fill(o_grad, 7))
        owned[11] = scatter(fill(trim_hidden(up_grad), 11))
        owned[13] = scatter(fill(trim_hidden(down_grad.T).T, 13))
        small = scatter(rows)
    position = 0
    for i in VECTORS:
        owned[i] = small[position : position + widths[i]]
        position += widths[i]
    return (layer_out, tokens_grad, *owned)


def solution(mesh):
    row, flat = P("fsdp", None), P("fsdp")
    in_specs = (row, flat) + (flat,) * 15 + (row,)
    out_specs = (row, row) + (flat,) * 15
    return jax.shard_map(
        on_device, mesh=mesh, in_specs=in_specs, out_specs=out_specs, check_vma=False
    )
```

time: 689 us -> 581 us (0.84)
  local copies, waits for them, and re-layouts: 112 us -> 67.9 us
  waiting for transfers between devices: 197 us -> 164 us
  other arithmetic: 84.3 us -> 55.1 us
  starting transfers between devices: 46.2 us -> 27 us
  between operations: 3.53 us -> 16.7 us
  matrix products: 135 us -> 142 us
    ppermute x61 -> x31, waiting for transfers between devices: 197 us -> 134 us  [swap(): return lax.ppermute(value, 'fsdp', [(i, i ^ mask) for i in range(devices)])]
    slice x28 -> x10, local copies, waits for them, and re-layouts: 39.2 us -> 0.54 us  [the longest x1 0.22 us: on_device(): owned[i] = inner_sum[:, first:first + D].reshape(-1)]
    all_gather x0 -> x1, waiting for transfers between devices: none -> 30.4 us  [on_device(): rest = lax.all_gather(rest, 'fsdp', axis=0, tiled=True)]
    ppermute x61 -> x31, starting transfers between devices: 46.2 us -> 27 us  [swap(): return lax.ppermute(value, 'fsdp', [(i, i ^ mask) for i in range(devices)])]
    unnamed x192 -> x160, local copies, waits for them, and re-layouts: 23.7 us -> 4.54 us
    reshape x13 -> x38, local copies, waits for them, and re-layouts: 11.7 us -> 29 us  [the longest x24 23.9 us: window(): return result.reshape(kept)]
    select_n x6 -> x2, other arithmetic: 12.8 us -> 1.86 us  [the longest x1 1.82 us: fetch_pairs(): jnp.where(is_first, jnp.concatenate([rows, edge]), jnp.concatenate([edge,...]
    add x7 -> x3, other arithmetic: 13.3 us -> 4.45 us  [total_of(): total = total + term.astype(f32)]
  transfers between devices with their start and end apart: 61 -> 33, of which waited for: 25 -> 14; matrix products, arithmetic and copies ran while one was open for 31% -> 26% of each run, Pallas kernels for 15% -> 14%
where the time goes in v3:
time: 581 us; the launch traced here: 570 us
  waiting for transfers between devices  164 us (28%)
  matrix products  142 us (24%)
  Pallas kernels  96.7 us (17%)
  local copies, waits for them, and re-layouts  67.9 us (12%)
  other arithmetic  55.1 us (9%)
  starting transfers between devices  27 us (5%)
  between operations  16.7 us (3%)
    ppermute x31, waiting for transfers between devices, swap(): return lax.ppermute(value, 'fsdp', [(i, i ^ mask) for i in range(devices)])  134 us
    dot_general x4, matrix products, product_bt(): lax.dot_general(left, right, (((1,), (1,)), ((), ())), preferred_element_...  52.8 us
    dot_general x4, matrix products, product(): return jnp.dot(left, right, preferred_element_type=f32)  48.3 us
    pallas_call x1, Pallas kernels, attn_bwd(): pl.pallas_call(functools.partial(bwd_kernel, tokens, krows, qrows, per),...  44.2 us
    dot_general x4, matrix products, product_t(): lax.dot_general(left, right, (((0,), (0,)), ((), ())), preferred_element_...  41 us
    all_gather x1, waiting for transfers between devices, on_device(): rest = lax.all_gather(rest, 'fsdp', axis=0, tiled=True)  30.4 us
    pallas_call x1, Pallas kernels, attn_fwd(): pl.pallas_call(functools.partial(fwd_kernel, tokens, krows, qrows, per),...  27.7 us
    ppermute x31, starting transfers between devices, swap(): return lax.ppermute(value, 'fsdp', [(i, i ^ mask) for i in range(devices)])  27 us
  transfers between devices with their start and end apart: 33, of which 14 were waited for; matrix products, arithmetic and copies ran while one was open for 26% of the time, Pallas kernels for 14%

profile of v3, /device:TPU:8, one launch (start us, length us, event | category | flops | bytes accessed | tf_op | source)
XLA Modules:
  0.0 569.6 jit_solution(3766834614112247579)
XLA Ops:
  35.9 12.3 %collective-permute-done.1 = bf16[40,3584]{1,0:T(8,128)(2,1)S(1)} collective-permute-done((bf16[40,3584]{1,0:T(8,128)(2,1)S(1)}, bf16[40,3584]{1,0:T(8,128)(2,1)S(1)}, u32[]{:S(2)}, u32[]{:S(2)}) %collective-permute-start.1) | collective-permute-done | bytes 286752 | tf_op jit(solution)/shard_map/ppermute | solution.py:155
  48.2 14.1 %collective-permute-done.2 = bf16[40,3584]{1,0:T(8,128)(2,1)S(1)} collective-permute-done((bf16[40,3584]{1,0:T(8,128)(2,1)S(1)}, bf16[40,3584]{1,0:T(8,128)(2,1)S(1)}, u32[]{:S(2)}, u32[]{:S(2)}) %collective-permute-start.2) | collective-permute-done | bytes 286752 | tf_op jit(solution)/shard_map/ppermute | solution.py:155
  62.3 13.3 %collective-permute-done.3 = bf16[40,3584]{1,0:T(8,128)(2,1)S(1)} collective-permute-done((bf16[40,3584]{1,0:T(8,128)(2,1)S(1)}, bf16[40,3584]{1,0:T(8,128)(2,1)S(1)}, u32[]{:S(2)}, u32[]{:S(2)}) %collective-permute-start.3) | collective-permute-done | bytes 286752 | tf_op jit(solution)/shard_map/ppermute | solution.py:155
  79.2 16.8 %collective-permute-done.4 = bf16[4,40,1792]{2,1,0:T(8,128)(2,1)S(1)} collective-permute-done((bf16[4,40,1792]{2,1,0:T(8,128)(2,1)S(1)}, bf16[4,40,1792]{2,1,0:T(8,128)(2,1)S(1)}, u32[]{:S(2)}, u32[]{:S(2)}) %collective-permute-start.4) | collective-permute-done | bytes 573472 | tf_op jit(solution)/shard_map/ppermute | solution.py:155
  102.8 21.0 %collective-permute-done.5 = bf16[8,40,1792]{2,1,0:T(8,128)(2,1)S(1)} collective-permute-done((bf16[8,40,1792]{2,1,0:T(8,128)(2,1)S(1)}, bf16[8,40,1792]{2,1,0:T(8,128)(2,1)S(1)}, u32[]{:S(2)}, u32[]{:S(2)}) %collective-permute-start.5) | collective-permute-done | bytes 1146912 | tf_op jit(solution)/shard_map/ppermute | solution.py:155
  123.8 9.7 %collective-permute-done.9 = bf16[8,40,1792]{2,1,0:T(8,128)(2,1)S(1)} collective-permute-done((bf16[8,40,1792]{2,1,0:T(8,128)(2,1)S(1)}, bf16[8,40,1792]{2,1,0:T(8,128)(2,1)S(1)}, u32[]{:S(2)}, u32[]{:S(2)}) %collective-permute-start.9) | collective-permute-done | bytes 1146912 | tf_op jit(solution)/shard_map/ppermute | solution.py:155
  136.3 6.8 %place_square.1 = (bf16[144,8,3456]{2,1,0:T(8,128)(2,1)}, bf16[32,5,8,128]{3,2,1,0:T(8,128)(2,1)S(1)}) custom-call(s32[4]{0:T(128)S(1)} %pad_add_fusion.coords, bf16[8,5,8,1792]{3,2,1,0:T(8,128)(2,1)S(1)} %bitcast_dynamic-update-slice_fusion.1.refs_0_, bf16[8,5,8,1792]{3,2,1,0:T(8,128)(2,1)S(1)} %bitcast.359, bf16[8,5,8,1792]{3,2,1,0:T(8,128)(2,1)S(1)} %bitcast.361, ...), custom_call_target="tpu_custom_call" | custom-call | bytes 18350080 | tf_op jit(solution)/shard_map/place_square/pallas_call | solution.py:220
  144.5 15.0 %add_convert_fusion.qkv_ref = bf16[729,3456]{1,0:T(8,128)(2,1)} fusion(bf16[144,8,3456]{2,1,0:T(8,128)(2,1)} %get-tuple-element.68, f32[3456]{0:T(1024)S(1)} %pad_maximum_fusion.9, f32[729,1152]{1,0:T(8,128)} %subtract_multiply_fusion.1, f32[1152]{0:T(1024)S(1)} %reshape.733, f32[1152]{0:T(1024)S(1)} %reshape.732), kind=kOutput, calls=%fused_computation.21 | convolution fusion | flops 5812311552 | bytes 16383744 | tf_op jit(solution)/shard_map/dot_general | solution.py:142
  159.5 27.7 %attention_forward.1 = (bf16[729,1152]{1,0:T(8,128)(2,1)}, f32[16,1,768]{2,1,0:T(1,128)}) custom-call(bf16[729,3456]{1,0:T(8,128)(2,1)} %add_convert_fusion.qkv_ref), custom_call_target="tpu_custom_call" | custom-call | flops 4630511616 | bytes 6718464 | tf_op jit(solution)/shard_map/attention_forward/pallas_call | solution.py:63
  187.2 30.4 %all-gather.2.cloned.1.call-done = bf16[10752,1152]{1,0:T(8,128)(2,1)} async-done(((bf16[336,1152]{1,0:T(8,128)(2,1)}), bf16[10752,1152]{1,0:T(8,128)(2,1)}) %all-gather.2.cloned.1.call-update) | async-done | bytes 24772624 | tf_op jit(solution)/shard_map/all_gather | solution.py:509
  217.6 18.0 %place_rest.1 = (bf16[144,8,4352]{2,1,0:T(8,128)(2,1)}, bf16[144,8,1152]{2,1,0:T(8,128)(2,1)}, bf16[544,8,1152]{2,1,0:T(8,128)(2,1)}) custom-call(bf16[32,42,8,1152]{3,2,1,0:T(8,128)(2,1)} %bitcast.366), custom_call_target="tpu_custom_call" | custom-call | bytes 49545216 | tf_op jit(solution)/shard_map/place_rest/pallas_call | solution.py:273
  235.6 4.6 fusion.89
  242.0 12.1 %fusion.25 = f32[729,4352]{1,0:T(8,128)} fusion(bf16[144,8,4352]{2,1,0:T(8,128)(2,1)S(1)} %bitcast.393, f32[4352]{0:T(1024)S(1)} %reshape.739, f32[729,1152]{1,0:T(8,128)S(1)} %get-tuple-element.212, f32[1152]{0:T(1024)S(1)} %reshape.738, f32[1152]{0:T(1024)S(1)} %reshape.737, f32[729]{0:T(1024)S(1)} %add_rsqrt_fusion, f32[729]{0:T(1024)S(1)} %broadcast_multiply_fusion.4), kind=kOutput, calls=%fused_computation.30 | convolution fusion | flops 7317060608 | bytes 26109128 | tf_op jit(solution)/shard_map/dot_general | solution.py:142
  254.1 15.1 %convolution_convert_fusion.1 = bf16[4352,1152]{1,0:T(8,128)(2,1)} fusion(bf16[729,1152]{1,0:T(8,128)(2,1)S(1)} %copy-done.19, f32[729,4352]{1,0:T(8,128)} %fusion.25), kind=kOutput, calls=%fused_computation.2 | convolution fusion | flops 7343255552 | bytes 24397056 | tf_op jit(solution)/shard_map/dot_general | solution.py:146
  269.2 19.5 %fusion.90 = (bf16[4352]{0:T(1024)(128)(2,1)S(1)}, bf16[729,4352]{1,0:T(8,128)(2,1)}) fusion(f32[729,4352]{1,0:T(8,128)} %fusion.25, bf16[729,1152]{1,0:T(8,128)(2,1)S(1)} %copy-done.19, bf16[544,8,1152]{2,1,0:T(8,128)(2,1)} %get-tuple-element.75), kind=kOutput, calls=%fused_computation.271 | convolution fusion | flops 7376304128 | bytes 30750976 | tf_op jit(solution)/shard_map/dot_general | solution.py:150
  288.7 13.7 %convolution_convert_fusion = bf16[1152,4352]{1,0:T(8,128)(2,1)} fusion(bf16[729,4352]{1,0:T(8,128)(2,1)} %get-tuple-element.215, f32[729,1152]{1,0:T(8,128)S(1)} %copy-done.3, f32[1152]{0:T(1024)S(1)} %reshape.738, f32[1152]{0:T(1024)S(1)} %reshape.737, f32[729]{0:T(1024)S(1)} %add_rsqrt_fusion, f32[729]{0:T(1024)S(1)} %broadcast_multiply_fusion.4), kind=kOutput, calls=%fused_computation.1 | convolution fusion | flops 7318901248 | bytes 19746504 | tf_op jit(solution)/shard_map/dot_general | solution.py:146
  302.4 15.8 %multiply_reduce_fusion.1 = (bf16[1152]{0:T(1024)(128)(2,1)S(1)}, f32[729]{0:T(1024)S(1)}, f32[729]{0:T(1024)S(1)}, bf16[1152]{0:T(1024)(128)(2,1)S(1)}, f32[729,1152]{1,0:T(8,128)}) fusion(f32[729,1152]{1,0:T(8,128)S(1)} %copy-done.3, f32[729]{0:T(1024)S(1)} %add_rsqrt_fusion, f32[729]{0:T(1024)S(1)} %broadcast_multiply_fusion.4, f32[1152]{0:T(1024)S(1)} %reshape.737, ...), kind=kOutput, calls=%fused_computation.45 | convolution fusion | flops 7317242880 | bytes 23111568 | tf_op jit(solution)/shard_map/dot_general | solution.py:150
  358.6 44.2 %attention_backward.1 = bf16[729,3456]{1,0:T(8,128)(2,1)} custom-call(bf16[729,3456]{1,0:T(8,128)(2,1)} %add_convert_fusion.qkv_ref, bf16[729,1152]{1,0:T(8,128)(2,1)} %convolution_convert_fusion.4.go_ref, f32[16,1,768]{2,1,0:T(1,128)} %get-tuple-element.83.lse_ref), custom_call_target="tpu_custom_call" | custom-call | flops 11576279040 | bytes 11757312 | tf_op jit(solution)/shard_map/attention_backward/pallas_call | solution.py:107
  414.9 9.6 %convolution_convert_fusion.2 = bf16[1152,3456]{1,0:T(8,128)(2,1)S(1)} fusion(bf16[729,3456]{1,0:T(8,128)(2,1)} %attention_backward.1, f32[729,1152]{1,0:T(8,128)S(1)} %copy-done.1, f32[1152]{0:T(1024)S(1)} %copy-done.52, f32[1152]{0:T(1024)S(1)} %copy-done.43), kind=kOutput, calls=%fused_computation.5 | convolution fusion | flops 5811253760 | bytes 16369920 | tf_op jit(solution)/shard_map/dot_general | solution.py:146
  427.3 13.7 %fusion.28 = f32[729,1152]{1,0:T(8,128)} fusion(bf16[729,3456]{1,0:T(8,128)(2,1)} %attention_backward.1, bf16[144,8,3456]{2,1,0:T(8,128)(2,1)} %get-tuple-element.68), kind=kOutput, calls=%fused_computation.31 | convolution fusion | flops 5804752896 | bytes 16360704 | tf_op jit(solution)/shard_map/dot_general | solution.py:150
  483.4 7.1 %collective-permute-done.22 = bf16[5,8,5504]{2,1,0:T(8,128)(2,1)S(1)} collective-permute-done((bf16[5,8,5504]{2,1,0:T(8,128)(2,1)S(1)}, bf16[5,8,5504]{2,1,0:T(8,128)(2,1)S(1)}, u32[]{:S(2)}, u32[]{:S(2)}) %collective-permute-start.22) | collective-permute-done | bytes 440352 | tf_op jit(solution)/shard_map/ppermute | solution.py:155
  490.5 13.6 %collective-permute-done.23 = bf16[5,8,5504]{2,1,0:T(8,128)(2,1)S(1)} collective-permute-done((bf16[5,8,5504]{2,1,0:T(8,128)(2,1)S(1)}, bf16[5,8,5504]{2,1,0:T(8,128)(2,1)S(1)}, u32[]{:S(2)}, u32[]{:S(2)}) %collective-permute-start.23) | collective-permute-done | bytes 440352 | tf_op jit(solution)/shard_map/ppermute | solution.py:155
  504.1 10.9 %collective-permute-done.24 = bf16[5,8,5504]{2,1,0:T(8,128)(2,1)S(1)} collective-permute-done((bf16[5,8,5504]{2,1,0:T(8,128)(2,1)S(1)}, bf16[5,8,5504]{2,1,0:T(8,128)(2,1)S(1)}, u32[]{:S(2)}, u32[]{:S(2)}) %collective-permute-start.24) | collective-permute-done | bytes 440352 | tf_op jit(solution)/shard_map/ppermute | solution.py:155
  542.2 16.6 %fusion.40 = f32[729,1152]{1,0:T(8,128)} fusion(f32[729,1152]{1,0:T(8,128)S(1)} %copy-done.4, bf16[544,8,1152]{2,1,0:T(8,128)(2,1)} %get-tuple-element.75, f32[1152]{0:T(1024)S(1)} %copy-done.50, f32[]{:T(128)} %bitcast, f32[729,4352]{1,0:T(8,128)} %fusion.25), kind=kOutput, calls=%fused_computation.38 | convolution fusion | flops 7340761088 | bytes 29440516 | tf_op jit(solution)/shard_map/dot_general | solution.py:142
  (392 shorter events, 171.1 us)
Async XLA Ops:
  7.2 210.4 %all-gather.2.cloned.1.call-start = ((), (), s32[]{:S(2)}) async-start(), calls=%async_computation.1 | async-start | bytes 25546752 | tf_op jit(solution)/shard_map/all_gather | solution.py:509
  26.7 494.4 %reduce-scatter.4.cloned.1.call-start = ((), (), s32[]{:S(2)}) async-start(), calls=%async_computation.2 | async-start | bytes 10340352
  30.8 17.4 %collective-permute-start.1 = (bf16[40,3584]{1,0:T(8,128)(2,1)S(1)}, bf16[40,3584]{1,0:T(8,128)(2,1)S(1)}, u32[]{:S(2)}, u32[]{:S(2)}) collective-permute-start(bf16[40,3584]{1,0:T(8,128)(2,1)S(1)} %pad_maximum_fusion.5), channel_id=1, source_target_pairs={{0,8},{1,9},{2,10},{3,11},{4,12},{5,13},{6,14},{7,15},{8,0},{9,1},... | collective-permute-start | bytes 860168 | tf_op jit(solution)/shard_map/ppermute | solution.py:155
  30.8 31.5 %collective-permute-start.2 = (bf16[40,3584]{1,0:T(8,128)(2,1)S(1)}, bf16[40,3584]{1,0:T(8,128)(2,1)S(1)}, u32[]{:S(2)}, u32[]{:S(2)}) collective-permute-start(bf16[40,3584]{1,0:T(8,128)(2,1)S(1)} %pad_maximum_fusion.5), channel_id=1, source_target_pairs={{0,16},{1,17},{2,18},{3,19},{4,20},{5,21},{6,22},{7,23},{8,24},{9,... | collective-permute-start | bytes 860168 | tf_op jit(solution)/shard_map/ppermute | solution.py:155
  33.9 41.8 %collective-permute-start.3 = (bf16[40,3584]{1,0:T(8,128)(2,1)S(1)}, bf16[40,3584]{1,0:T(8,128)(2,1)S(1)}, u32[]{:S(2)}, u32[]{:S(2)}) collective-permute-start(bf16[40,3584]{1,0:T(8,128)(2,1)S(1)} %pad_maximum_fusion.5), channel_id=1, source_target_pairs={{0,24},{1,25},{2,26},{3,27},{4,28},{5,29},{6,30},{7,31},{8,16},{9,... | collective-permute-start | bytes 860168 | tf_op jit(solution)/shard_map/ppermute | solution.py:155
  75.8 20.1 %collective-permute-start.4 = (bf16[4,40,1792]{2,1,0:T(8,128)(2,1)S(1)}, bf16[4,40,1792]{2,1,0:T(8,128)(2,1)S(1)}, u32[]{:S(2)}, u32[]{:S(2)}) collective-permute-start(bf16[4,40,1792]{2,1,0:T(8,128)(2,1)S(1)} %pad_maximum_fusion), channel_id=1, source_target_pairs={{0,2},{1,3},{2,0},{3,1},{4,6},{5,7},{6,4},{7,5},{8,10},{9,11},{10,... | collective-permute-start | bytes 1720328 | tf_op jit(solution)/shard_map/ppermute | solution.py:155
  77.5 24.5 %collective-permute-start.8 = (bf16[4,40,1792]{2,1,0:T(8,128)(2,1)S(1)}, bf16[4,40,1792]{2,1,0:T(8,128)(2,1)S(1)}, u32[]{:S(2)}, u32[]{:S(2)}) collective-permute-start(bf16[4,40,1792]{2,1,0:T(8,128)(2,1)S(1)} %pad_maximum_fusion.1), channel_id=1, source_target_pairs={{0,4},{1,5},{2,6},{3,7},{4,0},{5,1},{6,2},{7,3},{8,12},{9,13},{10,... | collective-permute-start | bytes 1720328 | tf_op jit(solution)/shard_map/ppermute | solution.py:155
  96.0 27.8 %collective-permute-start.5 = (bf16[8,40,1792]{2,1,0:T(8,128)(2,1)S(1)}, bf16[8,40,1792]{2,1,0:T(8,128)(2,1)S(1)}, u32[]{:S(2)}, u32[]{:S(2)}) collective-permute-start(bf16[8,40,1792]{2,1,0:T(8,128)(2,1)S(1)} %constant_dynamic-update-slice_fusion.5), channel_id=1, source_target_pairs={{0,4},{1,5},{2,6},{3,7},{4,0},{5,1},{6,2},{7,3},{8,12},{9,13},{10,... | collective-permute-start | bytes 3440648 | tf_op jit(solution)/shard_map/ppermute | solution.py:155
  102.0 31.5 %collective-permute-start.9 = (bf16[8,40,1792]{2,1,0:T(8,128)(2,1)S(1)}, bf16[8,40,1792]{2,1,0:T(8,128)(2,1)S(1)}, u32[]{:S(2)}, u32[]{:S(2)}) collective-permute-start(bf16[8,40,1792]{2,1,0:T(8,128)(2,1)S(1)} %constant_dynamic-update-slice_fusion.10), channel_id=1, source_target_pairs={{0,2},{1,3},{2,0},{3,1},{4,6},{5,7},{6,4},{7,5},{8,10},{9,11},{10,... | collective-permute-start | bytes 3440648 | tf_op jit(solution)/shard_map/ppermute | solution.py:155
  102.2 31.4 %collective-permute-start.6 = (bf16[8,40,1792]{2,1,0:T(8,128)(2,1)S(1)}, bf16[8,40,1792]{2,1,0:T(8,128)(2,1)S(1)}, u32[]{:S(2)}, u32[]{:S(2)}) collective-permute-start(bf16[8,40,1792]{2,1,0:T(8,128)(2,1)S(1)} %constant_dynamic-update-slice_fusion.5), channel_id=1, source_target_pairs={{0,1},{1,0},{2,3},{3,2},{4,5},{5,4},{6,7},{7,6},{8,9},{9,8},{10,11... | collective-permute-start | bytes 3440648 | tf_op jit(solution)/shard_map/ppermute | solution.py:155
  102.3 31.4 %collective-permute-start.10 = (bf16[8,40,1792]{2,1,0:T(8,128)(2,1)S(1)}, bf16[8,40,1792]{2,1,0:T(8,128)(2,1)S(1)}, u32[]{:S(2)}, u32[]{:S(2)}) collective-permute-start(bf16[8,40,1792]{2,1,0:T(8,128)(2,1)S(1)} %constant_dynamic-update-slice_fusion.10), channel_id=1, source_target_pairs={{0,1},{1,0},{2,3},{3,2},{4,5},{5,4},{6,7},{7,6},{8,9},{9,8},{10,11... | collective-permute-start | bytes 3440648 | tf_op jit(solution)/shard_map/ppermute | solution.py:155
  351.4 51.5 %collective-permute-start.14 = (bf16[4,2,5,8,2816]{4,3,2,1,0:T(8,128)(2,1)S(1)}, bf16[4,2,5,8,2816]{4,3,2,1,0:T(8,128)(2,1)S(1)}, u32[]{:S(2)}, u32[]{:S(2)}) collective-permute-start(bf16[4,2,5,8,2816]{4,3,2,1,0:T(8,128)(2,1)S(1)} %fusion.46), channel_id=1, source_target_pairs={{0,4},{1,5},{2,6},{3,7},{4,0},{5,1},{6,2},{7,3},{8,12},{9,13},{10,... | collective-permute-start | bytes 5406728 | tf_op jit(solution)/shard_map/ppermute | solution.py:155
  353.2 49.6 %collective-permute-start.15 = (bf16[4,2,5,8,2688]{4,3,2,1,0:T(8,128)(2,1)S(1)}, bf16[4,2,5,8,2688]{4,3,2,1,0:T(8,128)(2,1)S(1)}, u32[]{:S(2)}, u32[]{:S(2)}) collective-permute-start(bf16[4,2,5,8,2688]{4,3,2,1,0:T(8,128)(2,1)S(1)} %add_convert_fusion.2), channel_id=1, source_target_pairs={{0,2},{1,3},{2,0},{3,1},{4,6},{5,7},{6,4},{7,5},{8,10},{9,11},{10,... | collective-permute-start | bytes 5160968 | tf_op jit(solution)/shard_map/ppermute | solution.py:155
  407.0 40.0 %collective-permute-start.20 = (bf16[4,5,8,2816]{3,2,1,0:T(8,128)(2,1)}, bf16[4,5,8,2816]{3,2,1,0:T(8,128)(2,1)}, u32[]{:S(2)}, u32[]{:S(2)}) collective-permute-start(bf16[4,5,8,2816]{3,2,1,0:T(8,128)(2,1)} %fusion.47), channel_id=1, source_target_pairs={{0,2},{1,3},{2,0},{3,1},{4,6},{5,7},{6,4},{7,5},{8,10},{9,11},{10,... | collective-permute-start | bytes 2703368 | tf_op jit(solution)/shard_map/ppermute | solution.py:155
  409.9 37.2 %collective-permute-start.21 = (bf16[4,5,8,2688]{3,2,1,0:T(8,128)(2,1)}, bf16[4,5,8,2688]{3,2,1,0:T(8,128)(2,1)}, u32[]{:S(2)}, u32[]{:S(2)}) collective-permute-start(bf16[4,5,8,2688]{3,2,1,0:T(8,128)(2,1)} %fusion.48), channel_id=1, source_target_pairs={{0,4},{1,5},{2,6},{3,7},{4,0},{5,1},{6,2},{7,3},{8,12},{9,13},{10,... | collective-permute-start | bytes 2580488 | tf_op jit(solution)/shard_map/ppermute | solution.py:155
  427.3 42.8 %collective-permute-start.17 = (bf16[4,2,2,5,8,3456]{5,4,3,2,1,0:T(8,128)(2,1)}, bf16[4,2,2,5,8,3456]{5,4,3,2,1,0:T(8,128)(2,1)}, u32[]{:S(2)}, u32[]{:S(2)}) collective-permute-start(bf16[4,2,2,5,8,3456]{5,4,3,2,1,0:T(8,128)(2,1)} %constant_dynamic-slice_fusion.10), channel_id=1, source_target_pairs={{0,1},{1,0},{2,3},{3,2},{4,5},{5,4},{6,7},{7,6},{8,9},{9,8},{10,11... | collective-permute-start | bytes 13271048 | tf_op jit(solution)/shard_map/ppermute | solution.py:155
  463.9 26.6 %collective-permute-start.22 = (bf16[5,8,5504]{2,1,0:T(8,128)(2,1)S(1)}, bf16[5,8,5504]{2,1,0:T(8,128)(2,1)S(1)}, u32[]{:S(2)}, u32[]{:S(2)}) collective-permute-start(bf16[5,8,5504]{2,1,0:T(8,128)(2,1)S(1)} %pad_maximum_fusion.2), channel_id=1, source_target_pairs={{0,8},{1,9},{2,10},{3,11},{4,12},{5,13},{6,14},{7,15},{8,0},{9,1},... | collective-permute-start | bytes 1320968 | tf_op jit(solution)/shard_map/ppermute | solution.py:155
  468.4 35.7 %collective-permute-start.23 = (bf16[5,8,5504]{2,1,0:T(8,128)(2,1)S(1)}, bf16[5,8,5504]{2,1,0:T(8,128)(2,1)S(1)}, u32[]{:S(2)}, u32[]{:S(2)}) collective-permute-start(bf16[5,8,5504]{2,1,0:T(8,128)(2,1)S(1)} %pad_maximum_fusion.3), channel_id=1, source_target_pairs={{0,16},{1,17},{2,18},{3,19},{4,20},{5,21},{6,22},{7,23},{8,24},{9,... | collective-permute-start | bytes 1320968 | tf_op jit(solution)/shard_map/ppermute | solution.py:155
  469.9 45.1 %collective-permute-start.24 = (bf16[5,8,5504]{2,1,0:T(8,128)(2,1)S(1)}, bf16[5,8,5504]{2,1,0:T(8,128)(2,1)S(1)}, u32[]{:S(2)}, u32[]{:S(2)}) collective-permute-start(bf16[5,8,5504]{2,1,0:T(8,128)(2,1)S(1)} %pad_maximum_fusion.4), channel_id=1, source_target_pairs={{0,24},{1,25},{2,26},{3,27},{4,28},{5,29},{6,30},{7,31},{8,16},{9,... | collective-permute-start | bytes 1320968 | tf_op jit(solution)/shard_map/ppermute | solution.py:155
  471.8 43.2 %collective-permute-start.18 = (bf16[4,2,5,8,1792]{4,3,2,1,0:T(8,128)(2,1)S(1)}, bf16[4,2,5,8,1792]{4,3,2,1,0:T(8,128)(2,1)S(1)}, u32[]{:S(2)}, u32[]{:S(2)}) collective-permute-start(bf16[4,2,5,8,1792]{4,3,2,1,0:T(8,128)(2,1)S(1)} %add_convert_fusion.6), channel_id=1, source_target_pairs={{0,4},{1,5},{2,6},{3,7},{4,0},{5,1},{6,2},{7,3},{8,12},{9,13},{10,... | collective-permute-start | bytes 3440648 | tf_op jit(solution)/shard_map/ppermute | solution.py:155
  475.4 39.7 %collective-permute-start.19 = (bf16[4,2,5,8,1792]{4,3,2,1,0:T(8,128)(2,1)S(1)}, bf16[4,2,5,8,1792]{4,3,2,1,0:T(8,128)(2,1)S(1)}, u32[]{:S(2)}, u32[]{:S(2)}) collective-permute-start(bf16[4,2,5,8,1792]{4,3,2,1,0:T(8,128)(2,1)S(1)} %fusion.49), channel_id=1, source_target_pairs={{0,2},{1,3},{2,0},{3,1},{4,6},{5,7},{6,4},{7,5},{8,10},{9,11},{10,... | collective-permute-start | bytes 3440648 | tf_op jit(solution)/shard_map/ppermute | solution.py:155
  538.4 20.4 %collective-permute-start.30 = (bf16[5,8,3584]{2,1,0:T(8,128)(2,1)S(1)}, bf16[5,8,3584]{2,1,0:T(8,128)(2,1)S(1)}, u32[]{:S(2)}, u32[]{:S(2)}) collective-permute-start(bf16[5,8,3584]{2,1,0:T(8,128)(2,1)S(1)} %pad_maximum_fusion.8), channel_id=1, source_target_pairs={{0,24},{1,25},{2,26},{3,27},{4,28},{5,29},{6,30},{7,31},{8,16},{9,... | collective-permute-start | bytes 860168 | tf_op jit(solution)/shard_map/ppermute | solution.py:155
  538.7 20.1 %collective-permute-start.29 = (bf16[5,8,3584]{2,1,0:T(8,128)(2,1)S(1)}, bf16[5,8,3584]{2,1,0:T(8,128)(2,1)S(1)}, u32[]{:S(2)}, u32[]{:S(2)}) collective-permute-start(bf16[5,8,3584]{2,1,0:T(8,128)(2,1)S(1)} %pad_maximum_fusion.7), channel_id=1, source_target_pairs={{0,16},{1,17},{2,18},{3,19},{4,20},{5,21},{6,22},{7,23},{8,24},{9,... | collective-permute-start | bytes 860168 | tf_op jit(solution)/shard_map/ppermute | solution.py:155
  538.9 20.0 %collective-permute-start.28 = (bf16[5,8,3584]{2,1,0:T(8,128)(2,1)S(1)}, bf16[5,8,3584]{2,1,0:T(8,128)(2,1)S(1)}, u32[]{:S(2)}, u32[]{:S(2)}) collective-permute-start(bf16[5,8,3584]{2,1,0:T(8,128)(2,1)S(1)} %pad_maximum_fusion.6), channel_id=1, source_target_pairs={{0,8},{1,9},{2,10},{3,11},{4,12},{5,13},{6,14},{7,15},{8,0},{9,1},... | collective-permute-start | bytes 860168 | tf_op jit(solution)/shard_map/ppermute | solution.py:155
  (81 other events, 719.8 us)
Sparse Core Ops, SparseCore 0:
  26.8 190.7 all-gather.1
  334.1 169.8 reduce-scatter.3

commit v4 on v3

--- a/solution.py
+++ b/solution.py
@@ -113,8 +113,157 @@
         scratch_shapes=[pltpu.VMEM((HEADS,qrows,LANES),jnp.bfloat16),pltpu.VMEM((HEADS,krows,LANES),jnp.bfloat16),
                         pltpu.VMEM((HEADS,krows,LANES),jnp.bfloat16),pltpu.VMEM((HEADS,qrows,LANES),jnp.bfloat16)],
         compiler_params=pltpu.CompilerParams(vmem_limit_bytes=56<<20,dimension_semantics=("arbitrary",)),
-        cost_estimate=pl.CostEstimate(flops=10*HEADS*qrows*krows*LANES,bytes_accessed=7*tokens*D*2,transcendentals=HEADS*qrows*krows),
+        cost_estimate=pl.CostEstimate(flops=1000000,bytes_accessed=1000000,transcendentals=0),
         name="attention_backward")(qkv,gmixed,lse)
+
+
+GELU_A = 0.7978845608028654
+GELU_B = 0.044715
+
+
+def mlp_kernel(normed_ref, grad_ref, up_ref, bias_ref, down_ref, out_ref, back_ref,
+               up_grad_ref, bias_grad_ref, down_grad_ref, normed, normed_t, grad, out, back):
+    step = pl.program_id(0)
+    tokens = normed_ref.shape[0]
+
+    @pl.when(step == 0)
+    def _():
+        for held, source in ((normed, normed_ref), (grad, grad_ref)):
+            held[...] = jnp.zeros_like(held)
+            held[0:tokens] = source[...]
+        normed_t[...] = normed[...].T
+        out[...] = jnp.zeros_like(out)
+        back[...] = jnp.zeros_like(back)
+
+    pre = nn(normed[...], up_ref[...]) + bias_ref[...]
+    square = pre * pre
+    bend = jnp.tanh(pre * (GELU_A + GELU_A * GELU_B * square))
+    hidden = (0.5 * pre * (1.0 + bend)).astype(jnp.bfloat16)
+    slope = 0.5 * (1.0 + bend) + 0.5 * pre * (1.0 - bend * bend) * (
+        GELU_A + 3.0 * GELU_A * GELU_B * square
+    )
+    grad_pre = (nt(grad[...], down_ref[...]) * slope).astype(jnp.bfloat16)
+    out[...] += nn(hidden, down_ref[...])
+    back[...] += nt(grad_pre, up_ref[...])
+    down_grad_ref[...] = nn(hidden.T, grad[...]).astype(jnp.bfloat16)
+    up_grad_ref[...] = nn(normed_t[...], grad_pre).astype(jnp.bfloat16)
+    bias_grad_ref[...] = jnp.sum(grad_pre.astype(jnp.float32), axis=0, keepdims=True)
+
+    @pl.when(step == pl.num_programs(0) - 1)
+    def _():
+        out_ref[...] = out[0:tokens]
+        back_ref[...] = back[0:tokens]
+
+
+def mlp(normed, grad, up, bias, down):
+    tokens, hidden = normed.shape[0], up.shape[1]
+    rows = -(-tokens // 16) * 16
+    tile = 256
+    whole = lambda shape: pl.BlockSpec(shape, lambda i: (0, 0), pipeline_mode=pl.Buffered(1))
+    return pl.pallas_call(
+        mlp_kernel,
+        grid=(hidden // tile,),
+        in_specs=[
+            whole((tokens, D)),
+            whole((tokens, D)),
+            pl.BlockSpec((D, tile), lambda i: (0, i)),
+            pl.BlockSpec((1, tile), lambda i: (0, i)),
+            pl.BlockSpec((tile, D), lambda i: (i, 0)),
+        ],
+        out_specs=[
+            whole((tokens, D)),
+            whole((tokens, D)),
+            pl.BlockSpec((D, tile), lambda i: (0, i)),
+            pl.BlockSpec((1, tile), lambda i: (0, i)),
+            pl.BlockSpec((tile, D), lambda i: (i, 0)),
+        ],
+        out_shape=[
+            jax.ShapeDtypeStruct((tokens, D), jnp.float32),
+            jax.ShapeDtypeStruct((tokens, D), jnp.float32),
+            jax.ShapeDtypeStruct((D, hidden), jnp.bfloat16),
+            jax.ShapeDtypeStruct((1, hidden), jnp.float32),
+            jax.ShapeDtypeStruct((hidden, D), jnp.bfloat16),
+        ],
+        scratch_shapes=[
+            pltpu.VMEM((rows, D), jnp.bfloat16),
+            pltpu.VMEM((D, rows), jnp.bfloat16),
+            pltpu.VMEM((rows, D), jnp.bfloat16),
+            pltpu.VMEM((rows, D), jnp.float32),
+            pltpu.VMEM((rows, D), jnp.float32),
+        ],
+        compiler_params=pltpu.CompilerParams(
+            vmem_limit_bytes=56 << 20, dimension_semantics=("arbitrary",)
+        ),
+        cost_estimate=pl.CostEstimate(flops=1000000, bytes_accessed=1000000, transcendentals=0),
+        name="mlp_forward_backward",
+    )(normed, grad, up, bias, down)
+
+
+def qkv_back_kernel(grad_ref, normed_ref, weight_ref, xhat_ref, inverse_ref, gain_ref, resid_ref,
+                    weight_grad_ref, bias_grad_ref, sums_ref, tokens_ref, grad, normed_t, total):
+    step = pl.program_id(0)
+    tokens = normed_ref.shape[0]
+
+    @pl.when(step == 0)
+    def _():
+        grad[...] = jnp.zeros_like(grad)
+        grad[0:tokens] = normed_ref[...]
+        normed_t[...] = grad[...].T
+        grad[...] = jnp.zeros_like(grad)
+        total[...] = jnp.zeros_like(total)
+
+    grad[0:tokens] = grad_ref[...]
+    weight_grad_ref[...] = nn(normed_t[...], grad[...]).astype(jnp.bfloat16)
+    bias_grad_ref[...] = jnp.sum(grad[...].astype(jnp.float32), axis=0, keepdims=True)
+    total[...] += nt(grad[...], weight_ref[...])
+
+    @pl.when(step == pl.num_programs(0) - 1)
+    def _():
+        back = total[0:tokens]
+        xhat = xhat_ref[...]
+        sums_ref[0:1] = jnp.sum(back * xhat, axis=0, keepdims=True)
+        sums_ref[1:2] = jnp.sum(back, axis=0, keepdims=True)
+        scaled = back * gain_ref[...]
+        first = jnp.mean(scaled, axis=-1, keepdims=True)
+        second = jnp.mean(scaled * xhat, axis=-1, keepdims=True)
+        tokens_ref[...] = resid_ref[...] + inverse_ref[...] * (scaled - first - xhat * second)
+
+
+def qkv_back(grad, normed, weight, xhat, inverse, gain, resid):
+    tokens = normed.shape[0]
+    rows = -(-tokens // 16) * 16
+    whole = lambda shape: pl.BlockSpec(shape, lambda i: (0, 0), pipeline_mode=pl.Buffered(1))
+    part = lambda shape: pl.BlockSpec(shape, lambda i: (0, i))
+    return pl.pallas_call(
+        qkv_back_kernel,
+        grid=(3,),
+        in_specs=[
+            part((tokens, D)),
+            whole((tokens, D)),
+            part((D, D)),
+            whole((tokens, D)),
+            whole((tokens, 1)),
+            whole((1, D)),
+            whole((tokens, D)),
+        ],
+        out_specs=[part((D, D)), part((1, D)), whole((8, D)), whole((tokens, D))],
+        out_shape=[
+            jax.ShapeDtypeStruct((D, 3 * D), jnp.bfloat16),
+            jax.ShapeDtypeStruct((1, 3 * D), jnp.float32),
+            jax.ShapeDtypeStruct((8, D), jnp.float32),
+            jax.ShapeDtypeStruct((tokens, D), jnp.float32),
+        ],
+        scratch_shapes=[
+            pltpu.VMEM((rows, D), jnp.bfloat16),
+            pltpu.VMEM((D, rows), jnp.bfloat16),
+            pltpu.VMEM((rows, D), jnp.float32),
+        ],
+        compiler_params=pltpu.CompilerParams(
+            vmem_limit_bytes=56 << 20, dimension_semantics=("arbitrary",)
+        ),
+        cost_estimate=pl.CostEstimate(flops=1000000, bytes_accessed=1000000, transcendentals=0),
+        name="qkv_backward",
+    )(grad, normed, weight, xhat, inverse, gain, resid)
 
 
 FF = 4304
@@ -364,14 +513,17 @@
         starts, sizes = (None, None, None, tile), (None, None, None, BLOCK_TILES)
         return [swap(window(m, starts, sizes), 1) for m in self.matrices]
 
-    def far_step(self, other):
+    def far_step(self, other, streams=(0, 1), pieces=slice(None)):
         core, x, y, z = self.coords
         self.other = other
         got = []
-        for stream in range(2):
+        every = self.streams
+        for stream in streams:
             plane = (None, None, 1 - x) if stream else (None, 1 - y, None)
+            self.streams = {stream: every[stream][pieces]}
             send = total_of(self.terms(stream, plane)).astype(bf16)
             got.append(swap(send, 2 if stream else 4))
+        self.streams = every
         return got
 
     def near_step(self, far):
@@ -532,18 +684,13 @@
     resid = tokens + product(mixed, weight_o) + bias_o
     xhat_two, inverse_two = normalize(resid)
     normed_two = (xhat_two * gain_two + shift_two).astype(bf16)
-    pre = product(normed_two, weight_up) + bias_up
-    hidden = jax.nn.gelu(pre, approximate=True).astype(bf16)
-    down_grad = product_t(hidden, grad_branch).astype(bf16)
+    branch, grad_normed_two, up_grad, up_bias_grad, down_grad = mlp(
+        normed_two, grad_branch, weight_up, bias_up, weight_down
+    )
+    up_bias_grad = up_bias_grad.reshape(FF_PAD)
+    layer_out = weight_img * (resid + branch + bias_down)
     if staged:
-        grad_branch, down_grad, pre = tie(grad_branch, down_grad, pre)
         down_sum = lax.psum_scatter(down_grad, "fsdp", scatter_dimension=0, tiled=True)
-    layer_out = weight_img * (resid + product(hidden, weight_down) + bias_down)
-    gelu_back = jax.vjp(lambda t: jax.nn.gelu(t, approximate=True), pre)[1]
-    grad_pre = gelu_back(product_bt(grad_branch, weight_down))[0].astype(bf16)
-    up_bias_grad = jnp.sum(grad_pre.astype(f32), axis=0)
-    up_grad = product_t(normed_two, grad_pre).astype(bf16)
-    grad_normed_two = product_bt(grad_pre, weight_up)
     grads[9] = jnp.sum(grad_normed_two * xhat_two, axis=0)
     grads[10] = jnp.sum(grad_normed_two, axis=0)
     grad_resid = grad_out + normalize_back(grad_normed_two, gain_two, xhat_two, inverse_two)
@@ -564,12 +711,24 @@
     if staged:
         grad_qkv, outer_far = tie(grad_qkv, outer_far)
         outer_near = outer.near_step(outer_far)
-    qkv_bias_grad = jnp.sum(grad_qkv.astype(f32), axis=0)
-    grads[3], grads[6] = qkv_bias_grad[:D], qkv_bias_grad[2 * D :]
-    qkv_grad = product_t(normed, grad_qkv).astype(bf16)
-    grad_normed = product_bt(grad_qkv, weight_qkv)
-    grads[0] = jnp.sum(grad_normed * xhat_one, axis=0)
-    grads[1] = jnp.sum(grad_normed, axis=0)
+    qkv_grad, qkv_bias_grad, norm_sums, tokens_grad = qkv_back(
+        grad_qkv, normed, weight_qkv, xhat_one, inverse_one, gain_one.reshape(1, D), grad_resid
+    )
+    grads[3], grads[6] = qkv_bias_grad[0, :D], qkv_bias_grad[0, 2 * D :]
+    grads[0], grads[1] = norm_sums[0], norm_sums[1]
+    if staged:
+        inner = Reduction((qkv_grad,), (((0, 0, QKV_CUT - EXTRA),),) * 2, coords)
+        inner_other = inner.core_step()
+        inner_other, outer_near, qkv_grad, norm_sums, qkv_bias_grad = tie(
+            inner_other, outer_near, qkv_grad, norm_sums, qkv_bias_grad
+        )
+        inner = Reduction(
+            (qkv_grad, qkv_grad),
+            (((0, 0, QKV_CUT - EXTRA), (1, 0, EXTRA)), ((0, QKV_CUT - EXTRA, 3 * D),)),
+            coords,
+        )
+        inner_far = inner.far_step(inner_other, (0, 1), slice(0, 1))
+        outer_z = outer.z_step(outer_near)
     grads[12] = trim_hidden(up_bias_grad.reshape(1, FF_PAD)).reshape(FF)
 
     rows = []
@@ -582,19 +741,16 @@
     if staged:
         rows = jnp.pad(rows, ((0, 0), (0, OWN_ROWS * EXTRA - rows.shape[1])))
         rows = rows.reshape(D, EXTRA).astype(bf16)
-        inner = Reduction(
-            (rows, qkv_grad),
-            (((0, 0, EXTRA), (1, 0, QKV_CUT - EXTRA)), ((1, QKV_CUT - EXTRA, 3 * D),)),
-            coords,
-        )
-        rows, qkv_grad, outer_near, grad_normed = tie(rows, qkv_grad, outer_near, grad_normed)
-        outer_z = outer.z_step(outer_near)
-        inner_other = inner.core_step()
-        tokens_grad = grad_resid + normalize_back(grad_normed, gain_one, xhat_one, inverse_one)
-        (inner_other,) = tie(inner_other)
-        inner_far = inner.far_step(inner_other)
-        inner_far, outer_z, tokens_grad = tie(inner_far, outer_z, tokens_grad)
+        inner.matrices[1] = rows.reshape(4, 2, 2, PAIR_TILES, TILE, EXTRA)
+        rows_other = Reduction((rows,), None, coords).core_step()
+        inner.other = inner_other + rows_other
+        rows_far = inner.far_step(inner.other, (0,), slice(1, 2))
+        inner_far, rows_far = tie(inner_far, rows_far)
+        inner_far = [jnp.concatenate([inner_far[0], rows_far[0]], axis=-1), inner_far[1]]
         inner_near = inner.near_step(inner_far)
+        inner_near, outer_z = tie(inner_near, outer_z)
+        inner_z = inner.z_step(inner_near)
+        inner_z, down_sum = tie(inner_z, down_sum)
 
         flat = down_sum.astype(f32).reshape(-1)
         size = widths[13]
@@ -604,16 +760,15 @@
         outer_sum = outer.finish(outer_z)
         owned[11] = trim_hidden(outer_sum[:, :FF_PAD]).reshape(-1)
         owned[7] = outer_sum[:, FF_PAD:].reshape(-1)
-        inner_near, owned[13], owned[11], owned[7] = tie(
-            inner_near, owned[13], owned[11], owned[7]
-        )
-        inner_sum = inner.finish(inner.z_step(inner_near))
-        for position, i in enumerate((2, 4, 5)):
-            first = EXTRA + position * D
-            owned[i] = inner_sum[:, first : first + D].reshape(-1)
-        small = inner_sum[:, :EXTRA].reshape(-1)
+        inner_sum = inner.finish(inner_z)
+        first = QKV_CUT - EXTRA
+        owned[2] = inner_sum[:, :D].reshape(-1)
+        owned[4] = jnp.concatenate(
+            [inner_sum[:, D:first], inner_sum[:, QKV_CUT : 2 * D + EXTRA]], axis=1
+        ).reshape(-1)
+        owned[5] = inner_sum[:, 2 * D + EXTRA :].reshape(-1)
+        small = inner_sum[:, first:QKV_CUT].reshape(-1)
     else:
-        tokens_grad = grad_resid + normalize_back(grad_normed, gain_one, xhat_one, inverse_one)
         scatter = lambda value: lax.psum_scatter(
             value.astype(f32).reshape(-1), "fsdp", scatter_dimension=0, tiled=True
         )

time: 581 us -> 627 us (1.079)
  matrix products: 142 us -> 24.9 us
  Pallas kernels: 96.7 us -> 188 us
  waiting for transfers between devices: 164 us -> 242 us
  local copies, waits for them, and re-layouts: 67.9 us -> 58.5 us
    pallas_call x0 -> x2, Pallas kernels: none -> 91.7 us  [the longest x1 66.7 us: mlp(): pl.pallas_call(mlp_kernel, grid=(hidden // tile,), in_specs=[whole((token...]
    dot_general x4 -> x1, matrix products: 52.8 us -> 5.53 us  [product_bt(): lax.dot_general(left, right, (((1,), (1,)), ((), ())), preferred_element_...]
    optimization_barrier x0 -> x1, waiting for transfers between devices: none -> 46.3 us  [tie(): return form.unflatten(lax.optimization_barrier(leaves))]
    dot_general x4 -> x1, matrix products: 41 us -> 2.52 us  [product_t(): lax.dot_general(left, right, (((0,), (0,)), ((), ())), preferred_element_...]
    ppermute x31 -> x32, waiting for transfers between devices: 134 us -> 170 us  [swap(): return lax.ppermute(value, 'fsdp', [(i, i ^ mask) for i in range(devices)])]
    dot_general x4 -> x2, matrix products: 48.3 us -> 16.9 us  [product(): return jnp.dot(left, right, preferred_element_type=f32)]
    reshape x24 -> x20, local copies, waits for them, and re-layouts: 23.9 us -> 18 us  [window(): return result.reshape(kept)]
    ppermute x31 -> x32, starting transfers between devices: 27 us -> 31.7 us  [swap(): return lax.ppermute(value, 'fsdp', [(i, i ^ mask) for i in range(devices)])]
  transfers between devices with their start and end apart: 33 -> 34, of which waited for: 14 -> 20; matrix products, arithmetic and copies ran while one was open for 26% -> 14% of each run, Pallas kernels for 14% -> 13%
where the time goes in v4:
time: 627 us; the launch traced here: 616 us
  waiting for transfers between devices  242 us (39%)
  Pallas kernels  188 us (30%)
  local copies, waits for them, and re-layouts  58.5 us (9%)
  other arithmetic  54.3 us (9%)
  starting transfers between devices  31.7 us (5%)
  matrix products  24.9 us (4%)
  between operations  16.5 us (3%)
    ppermute x32, waiting for transfers between devices, swap(): return lax.ppermute(value, 'fsdp', [(i, i ^ mask) for i in range(devices)])  170 us
    pallas_call x1, Pallas kernels, mlp(): pl.pallas_call(mlp_kernel, grid=(hidden // tile,), in_specs=[whole((token...  66.7 us
    optimization_barrier x1, waiting for transfers between devices, tie(): return form.unflatten(lax.optimization_barrier(leaves))  46.3 us
    pallas_call x1, Pallas kernels, attn_bwd(): pl.pallas_call(functools.partial(bwd_kernel, tokens, krows, qrows, per),...  43.6 us
    ppermute x32, starting transfers between devices, swap(): return lax.ppermute(value, 'fsdp', [(i, i ^ mask) for i in range(devices)])  31.7 us
    pallas_call x1, Pallas kernels, attn_fwd(): pl.pallas_call(functools.partial(fwd_kernel, tokens, krows, qrows, per),...  28.1 us
    all_gather x1, waiting for transfers between devices, on_device(): rest = lax.all_gather(rest, 'fsdp', axis=0, tiled=True)  25.5 us
    pallas_call x1, Pallas kernels, qkv_back(): pl.pallas_call(qkv_back_kernel, grid=(3,), in_specs=[part((tokens, D)), w...  25 us
  transfers between devices with their start and end apart: 34, of which 20 were waited for; matrix products, arithmetic and copies ran while one was open for 14% of the time, Pallas kernels for 13%

profile of v4, /device:TPU:8, one launch (start us, length us, event | category | flops | bytes accessed | tf_op | source)
XLA Modules:
  0.0 615.6 jit_solution(7257252270529985241)
XLA Ops:
  33.0 12.4 %collective-permute-done.1 = bf16[40,3584]{1,0:T(8,128)(2,1)S(1)} collective-permute-done((bf16[40,3584]{1,0:T(8,128)(2,1)S(1)}, bf16[40,3584]{1,0:T(8,128)(2,1)S(1)}, u32[]{:S(2)}, u32[]{:S(2)}) %collective-permute-start.1) | collective-permute-done | bytes 286752 | tf_op jit(solution)/shard_map/ppermute | solution.py:304
  45.4 12.7 %collective-permute-done.2 = bf16[40,3584]{1,0:T(8,128)(2,1)S(1)} collective-permute-done((bf16[40,3584]{1,0:T(8,128)(2,1)S(1)}, bf16[40,3584]{1,0:T(8,128)(2,1)S(1)}, u32[]{:S(2)}, u32[]{:S(2)}) %collective-permute-start.2) | collective-permute-done | bytes 286752 | tf_op jit(solution)/shard_map/ppermute | solution.py:304
  58.0 14.4 %collective-permute-done.3 = bf16[40,3584]{1,0:T(8,128)(2,1)S(1)} collective-permute-done((bf16[40,3584]{1,0:T(8,128)(2,1)S(1)}, bf16[40,3584]{1,0:T(8,128)(2,1)S(1)}, u32[]{:S(2)}, u32[]{:S(2)}) %collective-permute-start.3) | collective-permute-done | bytes 286752 | tf_op jit(solution)/shard_map/ppermute | solution.py:304
  76.0 18.9 %collective-permute-done.8 = bf16[4,40,1792]{2,1,0:T(8,128)(2,1)S(1)} collective-permute-done((bf16[4,40,1792]{2,1,0:T(8,128)(2,1)S(1)}, bf16[4,40,1792]{2,1,0:T(8,128)(2,1)S(1)}, u32[]{:S(2)}, u32[]{:S(2)}) %collective-permute-start.8) | collective-permute-done | bytes 573472 | tf_op jit(solution)/shard_map/ppermute | solution.py:304
  100.3 32.7 %collective-permute-done.9 = bf16[8,40,1792]{2,1,0:T(8,128)(2,1)S(1)} collective-permute-done((bf16[8,40,1792]{2,1,0:T(8,128)(2,1)S(1)}, bf16[8,40,1792]{2,1,0:T(8,128)(2,1)S(1)}, u32[]{:S(2)}, u32[]{:S(2)}) %collective-permute-start.9) | collective-permute-done | bytes 1146912 | tf_op jit(solution)/shard_map/ppermute | solution.py:304
  137.5 6.9 %place_square.1 = (bf16[144,8,3456]{2,1,0:T(8,128)(2,1)}, bf16[32,5,8,128]{3,2,1,0:T(8,128)(2,1)S(1)}) custom-call(s32[4]{0:T(128)S(1)} %pad_add_fusion.coords, bf16[8,5,8,1792]{3,2,1,0:T(8,128)(2,1)S(1)} %bitcast_dynamic-update-slice_fusion.1.refs_0_, bf16[8,5,8,1792]{3,2,1,0:T(8,128)(2,1)S(1)} %bitcast.328, bf16[8,5,8,1792]{3,2,1,0:T(8,128)(2,1)S(1)} %bitcast.330, ...), custom_call_target="tpu_custom_call" | custom-call | bytes 18350080 | tf_op jit(solution)/shard_map/place_square/pallas_call | solution.py:369
  151.2 12.0 %add_convert_fusion.qkv_ref = bf16[729,3456]{1,0:T(8,128)(2,1)} fusion(bf16[729,1152]{1,0:T(8,128)(2,1)S(1)} %add_convert_fusion.4.normed_ref, f32[3456]{0:T(1024)S(1)} %pad_maximum_fusion.10, bf16[144,8,3456]{2,1,0:T(8,128)(2,1)} %get-tuple-element.74), kind=kOutput, calls=%fused_computation | convolution fusion | flops 5809792000 | bytes 14694912 | tf_op jit(solution)/shard_map/dot_general | solution.py:291
  163.2 28.1 %attention_forward.1 = (bf16[729,1152]{1,0:T(8,128)(2,1)}, f32[16,1,768]{2,1,0:T(1,128)}) custom-call(bf16[729,3456]{1,0:T(8,128)(2,1)} %add_convert_fusion.qkv_ref), custom_call_target="tpu_custom_call" | custom-call | flops 4630511616 | bytes 6718464 | tf_op jit(solution)/shard_map/attention_forward/pallas_call | solution.py:63
  191.3 25.5 %all-gather.2.cloned.1.call-done = bf16[10752,1152]{1,0:T(8,128)(2,1)} async-done(((bf16[336,1152]{1,0:T(8,128)(2,1)}), bf16[10752,1152]{1,0:T(8,128)(2,1)}) %all-gather.2.cloned.1.call-update) | async-done | bytes 24772624 | tf_op jit(solution)/shard_map/all_gather | solution.py:661
  216.8 17.6 %place_rest.1 = (bf16[144,8,4352]{2,1,0:T(8,128)(2,1)}, bf16[144,8,1152]{2,1,0:T(8,128)(2,1)}, bf16[544,8,1152]{2,1,0:T(8,128)(2,1)}) custom-call(bf16[32,42,8,1152]{3,2,1,0:T(8,128)(2,1)} %bitcast.334), custom_call_target="tpu_custom_call" | custom-call | bytes 49545216 | tf_op jit(solution)/shard_map/place_rest/pallas_call | solution.py:422
  234.4 4.9 fusion.45
  241.6 66.7 %mlp_forward_backward.1 = (f32[729,1152]{1,0:T(8,128)}, f32[729,1152]{1,0:T(8,128)}, bf16[1152,4352]{1,0:T(8,128)(2,1)}, f32[1,4352]{1,0:T(1,128)}, bf16[4352,1152]{1,0:T(8,128)(2,1)}) custom-call(bf16[729,1152]{1,0:T(8,128)(2,1)} %add_convert_fusion.3.normed_ref, bf16[729,1152]{1,0:T(8,128)(2,1)} %get-tuple-element.80.grad_ref, ...), custom_call_target="tpu_custom_call" | custom-call | flops 1000000 | bytes 1000000 | tf_op jit(solution)/shard_map/mlp_forward_backward/pallas_call | solution.py:163
  308.4 5.5 multiply_reduce_fusion
  327.3 5.5 convolution_convert_fusion.1.go_ref
  337.8 3.7 fusion.3
  346.8 43.6 %attention_backward.1.grad_ref = bf16[729,3456]{1,0:T(8,128)(2,1)} custom-call(bf16[729,3456]{1,0:T(8,128)(2,1)} %add_convert_fusion.qkv_ref, bf16[729,1152]{1,0:T(8,128)(2,1)} %convolution_convert_fusion.1.go_ref, f32[16,1,768]{2,1,0:T(1,128)} %get-tuple-element.90.lse_ref), custom_call_target="tpu_custom_call" | custom-call | flops 1000000 | bytes 1000000 | tf_op jit(solution)/shard_map/attention_backward/pallas_call | solution.py:107
  390.4 25.0 %qkv_backward.1 = (bf16[1152,3456]{1,0:T(8,128)(2,1)}, f32[1,3456]{1,0:T(1,128)}, f32[8,1152]{1,0:T(8,128)}, f32[729,1152]{1,0:T(8,128)}) custom-call(bf16[729,3456]{1,0:T(8,128)(2,1)} %attention_backward.1.grad_ref, bf16[729,1152]{1,0:T(8,128)(2,1)} %copy-done.4, bf16[1152,3456]{1,0:T(8,128)(2,1)} %bitcast.353, ...), custom_call_target="tpu_custom_call" | custom-call | flops 1000000 | bytes 1000000 | tf_op jit(solution)/shard_map/qkv_backward/pallas_call | solution.py:237
  415.4 4.6 constant_dynamic-slice_fusion.11
  444.1 13.1 %collective-permute-done.18 = bf16[4,5,8,2688]{3,2,1,0:T(8,128)(2,1)} collective-permute-done((bf16[4,5,8,2688]{3,2,1,0:T(8,128)(2,1)}, bf16[4,5,8,2688]{3,2,1,0:T(8,128)(2,1)}, u32[]{:S(2)}, u32[]{:S(2)}) %collective-permute-start.18) | collective-permute-done | bytes 860192 | tf_op jit(solution)/shard_map/ppermute | solution.py:304
  479.8 24.1 %collective-permute-done.20 = bf16[4,2,5,8,1664]{4,3,2,1,0:T(8,128)(2,1)S(1)} collective-permute-done((bf16[4,2,5,8,1664]{4,3,2,1,0:T(8,128)(2,1)S(1)}, bf16[4,2,5,8,1664]{4,3,2,1,0:T(8,128)(2,1)S(1)}, u32[]{:S(2)}, u32[]{:S(2)}) %collective-permute-start.20) | collective-permute-done | bytes 1064992 | tf_op jit(solution)/shard_map/ppermute | solution.py:304
  512.6 3.9 collective-permute-done.27
  516.5 15.2 %collective-permute-done.26 = bf16[5,8,5504]{2,1,0:T(8,128)(2,1)S(1)} collective-permute-done((bf16[5,8,5504]{2,1,0:T(8,128)(2,1)S(1)}, bf16[5,8,5504]{2,1,0:T(8,128)(2,1)S(1)}, u32[]{:S(2)}, u32[]{:S(2)}) %collective-permute-start.26) | collective-permute-done | bytes 440352 | tf_op jit(solution)/shard_map/ppermute | solution.py:304
  531.7 7.3 %collective-permute-done.25 = bf16[5,8,5504]{2,1,0:T(8,128)(2,1)S(1)} collective-permute-done((bf16[5,8,5504]{2,1,0:T(8,128)(2,1)S(1)}, bf16[5,8,5504]{2,1,0:T(8,128)(2,1)S(1)}, u32[]{:S(2)}, u32[]{:S(2)}) %collective-permute-start.25) | collective-permute-done | bytes 440352 | tf_op jit(solution)/shard_map/ppermute | solution.py:304
  554.2 46.3 %reduce-scatter.4.cloned.1.call-done = bf16[136,1152]{1,0:T(8,128)(2,1)} async-done(((bf16[4352,1152]{1,0:T(8,128)(2,1)}), bf16[136,1152]{1,0:T(8,128)(2,1)}) %reduce-scatter.4.cloned.1.call-update) | async-done | bytes 313360 | tf_op jit(solution)/shard_map/optimization_barrier | solution.py:447
  (330 shorter events, 148.4 us)
Async XLA Ops:
  7.2 209.6 %all-gather.2.cloned.1.call-start = ((), (), s32[]{:S(2)}) async-start(), calls=%async_computation.1 | async-start | bytes 25546752 | tf_op jit(solution)/shard_map/all_gather | solution.py:661
  22.6 577.8 %reduce-scatter.4.cloned.1.call-start = ((), (), s32[]{:S(2)}) async-start(), calls=%async_computation.2 | async-start | bytes 10340352
  27.3 30.7 %collective-permute-start.2 = (bf16[40,3584]{1,0:T(8,128)(2,1)S(1)}, bf16[40,3584]{1,0:T(8,128)(2,1)S(1)}, u32[]{:S(2)}, u32[]{:S(2)}) collective-permute-start(bf16[40,3584]{1,0:T(8,128)(2,1)S(1)} %pad_maximum_fusion.5), channel_id=1, source_target_pairs={{0,16},{1,17},{2,18},{3,19},{4,20},{5,21},{6,22},{7,23},{8,24},{9,... | collective-permute-start | bytes 860168 | tf_op jit(solution)/shard_map/ppermute | solution.py:304
  30.3 42.1 %collective-permute-start.3 = (bf16[40,3584]{1,0:T(8,128)(2,1)S(1)}, bf16[40,3584]{1,0:T(8,128)(2,1)S(1)}, u32[]{:S(2)}, u32[]{:S(2)}) collective-permute-start(bf16[40,3584]{1,0:T(8,128)(2,1)S(1)} %pad_maximum_fusion.5), channel_id=1, source_target_pairs={{0,24},{1,25},{2,26},{3,27},{4,28},{5,29},{6,30},{7,31},{8,16},{9,... | collective-permute-start | bytes 860168 | tf_op jit(solution)/shard_map/ppermute | solution.py:304
  74.3 25.2 %collective-permute-start.4 = (bf16[4,40,1792]{2,1,0:T(8,128)(2,1)S(1)}, bf16[4,40,1792]{2,1,0:T(8,128)(2,1)S(1)}, u32[]{:S(2)}, u32[]{:S(2)}) collective-permute-start(bf16[4,40,1792]{2,1,0:T(8,128)(2,1)S(1)} %pad_maximum_fusion), channel_id=1, source_target_pairs={{0,2},{1,3},{2,0},{3,1},{4,6},{5,7},{6,4},{7,5},{8,10},{9,11},{10,... | collective-permute-start | bytes 1720328 | tf_op jit(solution)/shard_map/ppermute | solution.py:304
  94.9 38.1 %collective-permute-start.9 = (bf16[8,40,1792]{2,1,0:T(8,128)(2,1)S(1)}, bf16[8,40,1792]{2,1,0:T(8,128)(2,1)S(1)}, u32[]{:S(2)}, u32[]{:S(2)}) collective-permute-start(bf16[8,40,1792]{2,1,0:T(8,128)(2,1)S(1)} %constant_dynamic-update-slice_fusion.10), channel_id=1, source_target_pairs={{0,2},{1,3},{2,0},{3,1},{4,6},{5,7},{6,4},{7,5},{8,10},{9,11},{10,... | collective-permute-start | bytes 3440648 | tf_op jit(solution)/shard_map/ppermute | solution.py:304
  99.6 33.4 %collective-permute-start.5 = (bf16[8,40,1792]{2,1,0:T(8,128)(2,1)S(1)}, bf16[8,40,1792]{2,1,0:T(8,128)(2,1)S(1)}, u32[]{:S(2)}, u32[]{:S(2)}) collective-permute-start(bf16[8,40,1792]{2,1,0:T(8,128)(2,1)S(1)} %constant_dynamic-update-slice_fusion.5), channel_id=1, source_target_pairs={{0,4},{1,5},{2,6},{3,7},{4,0},{5,1},{6,2},{7,3},{8,12},{9,13},{10,... | collective-permute-start | bytes 3440648 | tf_op jit(solution)/shard_map/ppermute | solution.py:304
  99.8 33.9 %collective-permute-start.10 = (bf16[8,40,1792]{2,1,0:T(8,128)(2,1)S(1)}, bf16[8,40,1792]{2,1,0:T(8,128)(2,1)S(1)}, u32[]{:S(2)}, u32[]{:S(2)}) collective-permute-start(bf16[8,40,1792]{2,1,0:T(8,128)(2,1)S(1)} %constant_dynamic-update-slice_fusion.10), channel_id=1, source_target_pairs={{0,1},{1,0},{2,3},{3,2},{4,5},{5,4},{6,7},{7,6},{8,9},{9,8},{10,11... | collective-permute-start | bytes 3440648 | tf_op jit(solution)/shard_map/ppermute | solution.py:304
  99.8 33.8 %collective-permute-start.6 = (bf16[8,40,1792]{2,1,0:T(8,128)(2,1)S(1)}, bf16[8,40,1792]{2,1,0:T(8,128)(2,1)S(1)}, u32[]{:S(2)}, u32[]{:S(2)}) collective-permute-start(bf16[8,40,1792]{2,1,0:T(8,128)(2,1)S(1)} %constant_dynamic-update-slice_fusion.5), channel_id=1, source_target_pairs={{0,1},{1,0},{2,3},{3,2},{4,5},{5,4},{6,7},{7,6},{8,9},{9,8},{10,11... | collective-permute-start | bytes 3440648 | tf_op jit(solution)/shard_map/ppermute | solution.py:304
  341.5 48.9 %collective-permute-start.14 = (bf16[4,2,5,8,2816]{4,3,2,1,0:T(8,128)(2,1)}, bf16[4,2,5,8,2816]{4,3,2,1,0:T(8,128)(2,1)}, u32[]{:S(2)}, u32[]{:S(2)}) collective-permute-start(bf16[4,2,5,8,2816]{4,3,2,1,0:T(8,128)(2,1)} %fusion.3), channel_id=1, source_target_pairs={{0,4},{1,5},{2,6},{3,7},{4,0},{5,1},{6,2},{7,3},{8,12},{9,13},{10,... | collective-permute-start | bytes 5406728 | tf_op jit(solution)/shard_map/ppermute | solution.py:304
  344.6 45.8 %collective-permute-start.15 = (bf16[4,2,5,8,2688]{4,3,2,1,0:T(8,128)(2,1)}, bf16[4,2,5,8,2688]{4,3,2,1,0:T(8,128)(2,1)}, u32[]{:S(2)}, u32[]{:S(2)}) collective-permute-start(bf16[4,2,5,8,2688]{4,3,2,1,0:T(8,128)(2,1)} %add_convert_fusion.2), channel_id=1, source_target_pairs={{0,2},{1,3},{2,0},{3,1},{4,6},{5,7},{6,4},{7,5},{8,10},{9,11},{10,... | collective-permute-start | bytes 5160968 | tf_op jit(solution)/shard_map/ppermute | solution.py:304
  420.1 40.6 %collective-permute-start.16 = (bf16[4,2,2,5,8,3456]{5,4,3,2,1,0:T(8,128)(2,1)}, bf16[4,2,2,5,8,3456]{5,4,3,2,1,0:T(8,128)(2,1)}, u32[]{:S(2)}, u32[]{:S(2)}) collective-permute-start(bf16[4,2,2,5,8,3456]{5,4,3,2,1,0:T(8,128)(2,1)} %constant_dynamic-slice_fusion.11), channel_id=1, source_target_pairs={{0,1},{1,0},{2,3},{3,2},{4,5},{5,4},{6,7},{7,6},{8,9},{9,8},{10,11... | collective-permute-start | bytes 13271048 | tf_op jit(solution)/shard_map/ppermute | solution.py:304
  434.9 22.3 %collective-permute-start.18 = (bf16[4,5,8,2688]{3,2,1,0:T(8,128)(2,1)}, bf16[4,5,8,2688]{3,2,1,0:T(8,128)(2,1)}, u32[]{:S(2)}, u32[]{:S(2)}) collective-permute-start(bf16[4,5,8,2688]{3,2,1,0:T(8,128)(2,1)} %fusion.5), channel_id=1, source_target_pairs={{0,4},{1,5},{2,6},{3,7},{4,0},{5,1},{6,2},{7,3},{8,12},{9,13},{10,... | collective-permute-start | bytes 2580488 | tf_op jit(solution)/shard_map/ppermute | solution.py:304
  441.8 38.0 %collective-permute-start.22 = (bf16[4,2,5,8,128]{4,3,2,1,0:T(8,128)(2,1)S(1)}, bf16[4,2,5,8,128]{4,3,2,1,0:T(8,128)(2,1)S(1)}, u32[]{:S(2)}, u32[]{:S(2)}) collective-permute-start(bf16[4,2,5,8,128]{4,3,2,1,0:T(8,128)(2,1)S(1)} %fusion.30), channel_id=1, source_target_pairs={{0,4},{1,5},{2,6},{3,7},{4,0},{5,1},{6,2},{7,3},{8,12},{9,13},{10,... | collective-permute-start | bytes 245768 | tf_op jit(solution)/shard_map/ppermute | solution.py:304
  465.0 51.5 %collective-permute-start.27 = (bf16[5,8,5504]{2,1,0:T(8,128)(2,1)S(1)}, bf16[5,8,5504]{2,1,0:T(8,128)(2,1)S(1)}, u32[]{:S(2)}, u32[]{:S(2)}) collective-permute-start(bf16[5,8,5504]{2,1,0:T(8,128)(2,1)S(1)} %pad_maximum_fusion.4), channel_id=1, source_target_pairs={{0,24},{1,25},{2,26},{3,27},{4,28},{5,29},{6,30},{7,31},{8,16},{9,... | collective-permute-start | bytes 1320968 | tf_op jit(solution)/shard_map/ppermute | solution.py:304
  469.3 35.4 %collective-permute-start.21 = (bf16[4,2,5,8,1792]{4,3,2,1,0:T(8,128)(2,1)S(1)}, bf16[4,2,5,8,1792]{4,3,2,1,0:T(8,128)(2,1)S(1)}, u32[]{:S(2)}, u32[]{:S(2)}) collective-permute-start(bf16[4,2,5,8,1792]{4,3,2,1,0:T(8,128)(2,1)S(1)} %fusion.6), channel_id=1, source_target_pairs={{0,2},{1,3},{2,0},{3,1},{4,6},{5,7},{6,4},{7,5},{8,10},{9,11},{10,... | collective-permute-start | bytes 3440648 | tf_op jit(solution)/shard_map/ppermute | solution.py:304
  472.3 31.6 %collective-permute-start.20 = (bf16[4,2,5,8,1664]{4,3,2,1,0:T(8,128)(2,1)S(1)}, bf16[4,2,5,8,1664]{4,3,2,1,0:T(8,128)(2,1)S(1)}, u32[]{:S(2)}, u32[]{:S(2)}) collective-permute-start(bf16[4,2,5,8,1664]{4,3,2,1,0:T(8,128)(2,1)S(1)} %fusion.9), channel_id=1, source_target_pairs={{0,4},{1,5},{2,6},{3,7},{4,0},{5,1},{6,2},{7,3},{8,12},{9,13},{10,... | collective-permute-start | bytes 3194888 | tf_op jit(solution)/shard_map/ppermute | solution.py:304
  473.9 57.8 %collective-permute-start.26 = (bf16[5,8,5504]{2,1,0:T(8,128)(2,1)S(1)}, bf16[5,8,5504]{2,1,0:T(8,128)(2,1)S(1)}, u32[]{:S(2)}, u32[]{:S(2)}) collective-permute-start(bf16[5,8,5504]{2,1,0:T(8,128)(2,1)S(1)} %pad_maximum_fusion.3), channel_id=1, source_target_pairs={{0,16},{1,17},{2,18},{3,19},{4,20},{5,21},{6,22},{7,23},{8,24},{9,... | collective-permute-start | bytes 1320968 | tf_op jit(solution)/shard_map/ppermute | solution.py:304
  506.2 32.8 %collective-permute-start.24 = (bf16[4,5,8,1792]{3,2,1,0:T(8,128)(2,1)S(1)}, bf16[4,5,8,1792]{3,2,1,0:T(8,128)(2,1)S(1)}, u32[]{:S(2)}, u32[]{:S(2)}) collective-permute-start(bf16[4,5,8,1792]{3,2,1,0:T(8,128)(2,1)S(1)} %fusion.7), channel_id=1, source_target_pairs={{0,4},{1,5},{2,6},{3,7},{4,0},{5,1},{6,2},{7,3},{8,12},{9,13},{10,... | collective-permute-start | bytes 1720328 | tf_op jit(solution)/shard_map/ppermute | solution.py:304
  507.3 31.7 %collective-permute-start.23 = (bf16[4,5,8,1792]{3,2,1,0:T(8,128)(2,1)S(1)}, bf16[4,5,8,1792]{3,2,1,0:T(8,128)(2,1)S(1)}, u32[]{:S(2)}, u32[]{:S(2)}) collective-permute-start(bf16[4,5,8,1792]{3,2,1,0:T(8,128)(2,1)S(1)} %fusion.8), channel_id=1, source_target_pairs={{0,2},{1,3},{2,0},{3,1},{4,6},{5,7},{6,4},{7,5},{8,10},{9,11},{10,... | collective-permute-start | bytes 1720328 | tf_op jit(solution)/shard_map/ppermute | solution.py:304
  508.9 30.1 %collective-permute-start.25 = (bf16[5,8,5504]{2,1,0:T(8,128)(2,1)S(1)}, bf16[5,8,5504]{2,1,0:T(8,128)(2,1)S(1)}, u32[]{:S(2)}, u32[]{:S(2)}) collective-permute-start(bf16[5,8,5504]{2,1,0:T(8,128)(2,1)S(1)} %pad_maximum_fusion.2), channel_id=1, source_target_pairs={{0,8},{1,9},{2,10},{3,11},{4,12},{5,13},{6,14},{7,15},{8,0},{9,1},... | collective-permute-start | bytes 1320968 | tf_op jit(solution)/shard_map/ppermute | solution.py:304
  541.7 58.8 %collective-permute-start.30 = (bf16[5,8,3584]{2,1,0:T(8,128)(2,1)}, bf16[5,8,3584]{2,1,0:T(8,128)(2,1)}, u32[]{:S(2)}, u32[]{:S(2)}) collective-permute-start(bf16[5,8,3584]{2,1,0:T(8,128)(2,1)} %pad_maximum_fusion.8), channel_id=1, source_target_pairs={{0,24},{1,25},{2,26},{3,27},{4,28},{5,29},{6,30},{7,31},{8,16},{9,... | collective-permute-start | bytes 860168 | tf_op jit(solution)/shard_map/ppermute | solution.py:304
  544.0 56.5 %collective-permute-start.29 = (bf16[5,8,3584]{2,1,0:T(8,128)(2,1)}, bf16[5,8,3584]{2,1,0:T(8,128)(2,1)}, u32[]{:S(2)}, u32[]{:S(2)}) collective-permute-start(bf16[5,8,3584]{2,1,0:T(8,128)(2,1)} %pad_maximum_fusion.7), channel_id=1, source_target_pairs={{0,16},{1,17},{2,18},{3,19},{4,20},{5,21},{6,22},{7,23},{8,24},{9,... | collective-permute-start | bytes 860168 | tf_op jit(solution)/shard_map/ppermute | solution.py:304
  548.0 52.4 %collective-permute-start.28 = (bf16[5,8,3584]{2,1,0:T(8,128)(2,1)}, bf16[5,8,3584]{2,1,0:T(8,128)(2,1)}, u32[]{:S(2)}, u32[]{:S(2)}) collective-permute-start(bf16[5,8,3584]{2,1,0:T(8,128)(2,1)} %pad_maximum_fusion.6), channel_id=1, source_target_pairs={{0,8},{1,9},{2,10},{3,11},{4,12},{5,13},{6,14},{7,15},{8,0},{9,1},... | collective-permute-start | bytes 860168 | tf_op jit(solution)/shard_map/ppermute | solution.py:304
  (51 other events, 318.0 us)
Sparse Core Ops, SparseCore 0:
  22.7 193.9 all-gather.1
  423.5 176.8 reduce-scatter.3

commit v5 on v4

--- a/solution.py
+++ b/solution.py
@@ -121,8 +121,10 @@
 GELU_B = 0.044715
 
 
-def mlp_kernel(normed_ref, grad_ref, up_ref, bias_ref, down_ref, out_ref, back_ref,
-               up_grad_ref, bias_grad_ref, down_grad_ref, normed, normed_t, grad, out, back):
+def mlp_kernel(normed_ref, grad_ref, up_ref, bias_ref, down_ref, xhat_ref, inverse_ref, gain_ref,
+               grad_out_ref, mixed_ref, output_ref, out_ref, up_grad_ref, bias_grad_ref,
+               down_grad_ref, sums_ref, resid_grad_ref, output_grad_ref, mixed_grad_ref,
+               normed, normed_t, grad, out, back):
     step = pl.program_id(0)
     tokens = normed_ref.shape[0]
 
@@ -152,37 +154,52 @@
     @pl.when(step == pl.num_programs(0) - 1)
     def _():
         out_ref[...] = out[0:tokens]
-        back_ref[...] = back[0:tokens]
-
-
-def mlp(normed, grad, up, bias, down):
+        total = back[0:tokens]
+        xhat = xhat_ref[...]
+        sums_ref[0:1] = jnp.sum(total * xhat, axis=0, keepdims=True)
+        sums_ref[1:2] = jnp.sum(total, axis=0, keepdims=True)
+        scaled = total * gain_ref[...]
+        first = jnp.mean(scaled, axis=-1, keepdims=True)
+        second = jnp.mean(scaled * xhat, axis=-1, keepdims=True)
+        resid_grad = grad_out_ref[...] + inverse_ref[...] * (scaled - first - xhat * second)
+        resid_grad_ref[...] = resid_grad
+        grad[0:tokens] = resid_grad.astype(jnp.bfloat16)
+        low = grad[...]
+        sums_ref[2:3] = jnp.sum(low.astype(jnp.float32), axis=0, keepdims=True)
+        mixed_grad_ref[...] = nt(low, output_ref[...]).astype(jnp.bfloat16)[0:tokens]
+        normed[0:tokens] = mixed_ref[...]
+        normed_t[...] = normed[...].T
+        output_grad_ref[...] = nn(normed_t[...], low).astype(jnp.bfloat16)
+
+
+def whole_block(shape):
+    return pl.BlockSpec(shape, lambda i: (0, 0), pipeline_mode=pl.Buffered(1))
+
+
+def mlp(normed, grad, up, bias, down, xhat, inverse, gain, grad_out, mixed, output):
     tokens, hidden = normed.shape[0], up.shape[1]
     rows = -(-tokens // 16) * 16
     tile = 256
-    whole = lambda shape: pl.BlockSpec(shape, lambda i: (0, 0), pipeline_mode=pl.Buffered(1))
+    full = whole_block((tokens, D))
+    columns = pl.BlockSpec((D, tile), lambda i: (0, i))
+    line = pl.BlockSpec((1, tile), lambda i: (0, i))
+    band = pl.BlockSpec((tile, D), lambda i: (i, 0))
+    square = whole_block((D, D))
     return pl.pallas_call(
         mlp_kernel,
         grid=(hidden // tile,),
-        in_specs=[
-            whole((tokens, D)),
-            whole((tokens, D)),
-            pl.BlockSpec((D, tile), lambda i: (0, i)),
-            pl.BlockSpec((1, tile), lambda i: (0, i)),
-            pl.BlockSpec((tile, D), lambda i: (i, 0)),
-        ],
-        out_specs=[
-            whole((tokens, D)),
-            whole((tokens, D)),
-            pl.BlockSpec((D, tile), lambda i: (0, i)),
-            pl.BlockSpec((1, tile), lambda i: (0, i)),
-            pl.BlockSpec((tile, D), lambda i: (i, 0)),
-        ],
+        in_specs=[full, full, columns, line, band, full, whole_block((tokens, 1)),
+                  whole_block((1, D)), full, full, square],
+        out_specs=[full, columns, line, band, whole_block((8, D)), full, square, full],
         out_shape=[
-            jax.ShapeDtypeStruct((tokens, D), jnp.float32),
             jax.ShapeDtypeStruct((tokens, D), jnp.float32),
             jax.ShapeDtypeStruct((D, hidden), jnp.bfloat16),
             jax.ShapeDtypeStruct((1, hidden), jnp.float32),
             jax.ShapeDtypeStruct((hidden, D), jnp.bfloat16),
+            jax.ShapeDtypeStruct((8, D), jnp.float32),
+            jax.ShapeDtypeStruct((tokens, D), jnp.float32),
+            jax.ShapeDtypeStruct((D, D), jnp.bfloat16),
+            jax.ShapeDtypeStruct((tokens, D), jnp.bfloat16),
         ],
         scratch_shapes=[
             pltpu.VMEM((rows, D), jnp.bfloat16),
@@ -196,7 +213,7 @@
         ),
         cost_estimate=pl.CostEstimate(flops=1000000, bytes_accessed=1000000, transcendentals=0),
         name="mlp_forward_backward",
-    )(normed, grad, up, bias, down)
+    )(normed, grad, up, bias, down, xhat, inverse, gain, grad_out, mixed, output)
 
 
 def qkv_back_kernel(grad_ref, normed_ref, weight_ref, xhat_ref, inverse_ref, gain_ref, resid_ref,
@@ -281,7 +298,8 @@
 QKV_CUT = 14 * 128
 UP_CUT = 22 * 128
 UP_PIECES = 4
-REST_ROWS = UP_PIECES * BLOCK_TILES * TILE + BLOCK_TILES * TILE + HALF_DOWN
+DOWN_CUT = 72
+REST_ROWS = UP_PIECES * BLOCK_TILES * TILE + BLOCK_TILES * TILE
 VECTORS = (0, 1, 3, 6, 8, 9, 10, 12, 14)
 bf16 = jnp.bfloat16
 f32 = jnp.float32
@@ -384,7 +402,7 @@
     return whole.reshape(D, 3 * D), small.reshape(2 * GROUPS, -1)
 
 
-def place_rest_kernel(source, up, out, down, held, in_sems, out_sems):
+def place_rest_kernel(source, up, out, held, in_sems, out_sems):
     arrivals = [
         pltpu.make_async_copy(source.at[i], held.at[i], in_sems.at[i]) for i in range(2 * GROUPS)
     ]
@@ -408,8 +426,6 @@
             )
         base = UP_PIECES * BLOCK_TILES
         jobs.append((src.at[pl.ds(base + owner, count)], out.at[pl.ds(first, count)]))
-        rows = HALF_DOWN // TILE
-        jobs.append((src.at[pl.ds(base + BLOCK_TILES, rows)], down.at[pl.ds(device * rows, rows)]))
         for one, other in jobs:
             copies.append(pltpu.make_async_copy(one, other, out_sems.at[len(copies)]))
             copies[-1].start()
@@ -419,19 +435,18 @@
 
 def place_rest(gathered):
     source = gathered.reshape(2 * GROUPS, REST_ROWS // TILE, TILE, D)
-    up, out, down = pl.pallas_call(
+    up, out = pl.pallas_call(
         place_rest_kernel,
         in_specs=[pl.BlockSpec(memory_space=pltpu.HBM)],
-        out_specs=[pl.BlockSpec(memory_space=pltpu.HBM)] * 3,
+        out_specs=[pl.BlockSpec(memory_space=pltpu.HBM)] * 2,
         out_shape=[
             jax.ShapeDtypeStruct((D // TILE, TILE, FF_PAD), bf16),
             jax.ShapeDtypeStruct((D // TILE, TILE, D), bf16),
-            jax.ShapeDtypeStruct((FF_PAD // TILE, TILE, D), bf16),
         ],
         scratch_shapes=[
             pltpu.VMEM(source.shape, bf16),
             pltpu.SemaphoreType.DMA((2 * GROUPS,)),
-            pltpu.SemaphoreType.DMA((2 * GROUPS * (UP_PIECES + 2),)),
+            pltpu.SemaphoreType.DMA((2 * GROUPS * (UP_PIECES + 1),)),
         ],
         compiler_params=pltpu.CompilerParams(vmem_limit_bytes=56 << 20),
         cost_estimate=pl.CostEstimate(
@@ -439,7 +454,48 @@
         ),
         name="place_rest",
     )(source)
-    return up.reshape(D, FF_PAD), out.reshape(D, D), down.reshape(FF_PAD, D)
+    return up.reshape(D, FF_PAD), out.reshape(D, D)
+
+
+def place_down_kernel(coords, *refs):
+    sources, whole = refs[:8], refs[8]
+    held, in_sems, out_sems = refs[9:17], refs[17], refs[18]
+    core, x, y, z = coords[0], coords[1], coords[2], coords[3]
+    arrivals = [pltpu.make_async_copy(sources[i], held[i], in_sems.at[i]) for i in range(8)]
+    for arrival in arrivals:
+        arrival.start()
+    copies = []
+    for part, stream in itertools.product(range(4), range(2)):
+        arrivals[4 * stream + part].wait()
+        for near, dz in itertools.product(range(2), range(4)):
+            src = held[4 * stream + part].at[near * 4 + dz]
+            owner = core if part < 2 else 1 - core
+            far = part % 2
+            dx, dy = (near, far) if stream == 0 else (far, near)
+            chip = ((z ^ dz) * 2 + (y ^ dy)) * 2 + (x ^ dx)
+            first = DOWN_CUT // TILE if stream else 0
+            dst = whole.at[chip * 2 + owner, first : first + src.shape[0]]
+            copies.append(pltpu.make_async_copy(src, dst, out_sems.at[len(copies)]))
+            copies[-1].start()
+    for copy in copies:
+        copy.wait()
+
+
+def place_down(streams, coords):
+    sources = [s.reshape(8, -1, TILE, D) for s in (*streams[0], *streams[1])]
+    size = sum(s.size for s in sources) * 2
+    return pl.pallas_call(
+        place_down_kernel,
+        in_specs=[pl.BlockSpec(memory_space=pltpu.SMEM)]
+        + [pl.BlockSpec(memory_space=pltpu.HBM)] * 8,
+        out_specs=pl.BlockSpec(memory_space=pltpu.HBM),
+        out_shape=jax.ShapeDtypeStruct((2 * GROUPS, HALF_DOWN // TILE, TILE, D), bf16),
+        scratch_shapes=[pltpu.VMEM(s.shape, bf16) for s in sources]
+        + [pltpu.SemaphoreType.DMA((8,)), pltpu.SemaphoreType.DMA((64,))],
+        compiler_params=pltpu.CompilerParams(vmem_limit_bytes=40 << 20),
+        cost_estimate=pl.CostEstimate(flops=0, bytes_accessed=2 * size, transcendentals=0),
+        name="place_down",
+    )(coords, *sources).reshape(FF_PAD, D)
 
 
 def tie(*values):
@@ -466,12 +522,12 @@
     results = []
     for stream in range(2):
         first = jnp.concatenate(streams[stream])
-        results.append((first, swap(first, 2 if stream else 4), swap(first, 1)))
+        results.append((first, swap(first, 2 if stream else 4)))
     return results
 
 
 def gather_core(streams):
-    return [(first, second, third, swap(second, 1)) for first, second, third in streams]
+    return [(first, second, swap(first, 1), swap(second, 1)) for first, second in streams]
 
 
 def window(value, starts, sizes):
@@ -594,8 +650,8 @@
     square = jnp.concatenate([small, block[:, : 3 * D]], axis=1)
     up_block = jnp.pad(block[:, 4 * D :], ((0, 0), (0, UP_PIECES * D - FF_PAD)))
     pieces = [up_block[:, i * D : (i + 1) * D] for i in range(UP_PIECES)]
-    rest = jnp.concatenate(pieces + [block[:, 3 * D : 4 * D], down_block])
-    return square, rest
+    rest = jnp.concatenate(pieces + [block[:, 3 * D : 4 * D]])
+    return square, rest, down_block
 
 
 def normalize(values):
@@ -657,13 +713,18 @@
     xhat_one, inverse_one = normalize(tokens)
     if staged:
         where = jnp.stack(coords).astype(jnp.int32)
-        sq, rest = fetch_pairs(narrow, core)
+        sq, rest, down = fetch_pairs(narrow, core)
         rest = lax.all_gather(rest, "fsdp", axis=0, tiled=True)
         sq = gather_z(sq)
-        sq, xhat_one, inverse_one, grad_branch = tie(sq, xhat_one, inverse_one, grad_branch)
+        sq, down, xhat_one, inverse_one, grad_branch = tie(
+            sq, down, xhat_one, inverse_one, grad_branch
+        )
         sq = gather_near(sq, QKV_CUT, 1)
+        down = gather_z(down)
         sq = gather_far(sq)
+        sq, down = tie(sq, down)
         sq = gather_core(sq)
+        down = gather_near(down, DOWN_CUT, 0)
         weight_qkv, small = place_square(sq, where)
         vectors = name_vectors(small, widths)
     else:
@@ -677,33 +738,43 @@
 
     normed = (xhat_one * gain_one + shift_one).astype(bf16)
     qkv = (product(normed, weight_qkv) + bias_qkv).astype(bf16)
+    if staged:
+        qkv, down = tie(qkv, down)
+        down = gather_far(down)
     mixed, lse = attn_fwd(qkv, 2)
     if staged:
-        mixed, lse, rest = tie(mixed, lse, rest)
-        weight_up, weight_o, weight_down = place_rest(rest)
+        mixed, lse, rest, down = tie(mixed, lse, rest, down)
+        down = gather_core(down)
+        weight_up, weight_o = place_rest(rest)
     resid = tokens + product(mixed, weight_o) + bias_o
     xhat_two, inverse_two = normalize(resid)
     normed_two = (xhat_two * gain_two + shift_two).astype(bf16)
-    branch, grad_normed_two, up_grad, up_bias_grad, down_grad = mlp(
-        normed_two, grad_branch, weight_up, bias_up, weight_down
+    if staged:
+        normed_two, down = tie(normed_two, down)
+        weight_down = place_down(down, where)
+    branch, up_grad, up_bias_grad, down_grad, sums_two, grad_resid, o_grad, grad_mixed = mlp(
+        normed_two,
+        grad_branch,
+        weight_up,
+        bias_up,
+        weight_down,
+        xhat_two,
+        inverse_two,
+        gain_two.reshape(1, D),
+        grad_out,
+        mixed,
+        weight_o,
     )
     up_bias_grad = up_bias_grad.reshape(FF_PAD)
     layer_out = weight_img * (resid + branch + bias_down)
+    grads[9], grads[10], grads[8] = sums_two[0], sums_two[1], sums_two[2]
     if staged:
         down_sum = lax.psum_scatter(down_grad, "fsdp", scatter_dimension=0, tiled=True)
-    grads[9] = jnp.sum(grad_normed_two * xhat_two, axis=0)
-    grads[10] = jnp.sum(grad_normed_two, axis=0)
-    grad_resid = grad_out + normalize_back(grad_normed_two, gain_two, xhat_two, inverse_two)
-    grad_attn = grad_resid.astype(bf16)
-    grads[8] = jnp.sum(grad_attn.astype(f32), axis=0)
-    o_grad = product_t(mixed, grad_attn).astype(bf16)
-    if staged:
-        up_grad, o_grad, grad_attn = tie(up_grad, o_grad, grad_attn)
+    if staged:
         outer = Reduction(
             (up_grad, o_grad), (((0, 0, UP_CUT),), ((0, UP_CUT, FF_PAD), (1, 0, D))), coords
         )
         outer_other = outer.core_step()
-    grad_mixed = product_bt(grad_attn, weight_o).astype(bf16)
     if staged:
         grad_mixed, outer_other = tie(grad_mixed, outer_other)
         outer_far = outer.far_step(outer_other)
@@ -750,7 +821,7 @@
         inner_near = inner.near_step(inner_far)
         inner_near, outer_z = tie(inner_near, outer_z)
         inner_z = inner.z_step(inner_near)
-        inner_z, down_sum = tie(inner_z, down_sum)
+        inner_near, down_sum = tie(inner_near, down_sum)
 
         flat = down_sum.astype(f32).reshape(-1)
         size = widths[13]

time: 627 us -> 593 us (0.946)
  waiting for transfers between devices: 242 us -> 176 us
  local copies, waits for them, and re-layouts: 58.5 us -> 76.6 us
  starting transfers between devices: 31.7 us -> 43.9 us
  Pallas kernels: 188 us -> 200 us
  matrix products: 24.9 us -> 17.5 us
    optimization_barrier x1, waiting for transfers between devices: 46.3 us -> 0.01 us  [tie(): return form.unflatten(lax.optimization_barrier(leaves))]
    all_gather x1, waiting for transfers between devices: 25.5 us -> 0.02 us  [on_device(): rest = lax.all_gather(rest, 'fsdp', axis=0, tiled=True)]
    pallas_call x1 -> x2, Pallas kernels: 66.7 us -> 84.8 us  [the longest x1 78.8 us: mlp(): pl.pallas_call(mlp_kernel, grid=(hidden // tile,), in_specs=[full, full,...]
    ppermute x32 -> x43, starting transfers between devices: 31.7 us -> 43.6 us  [swap(): return lax.ppermute(value, 'fsdp', [(i, i ^ mask) for i in range(devices)])]
    reduce_sum x2 -> x0, other arithmetic: 8.35 us -> none  [the longest x1 5.53 us: on_device(): grads[9] = jnp.sum(grad_normed_two * xhat_two, axis=0)]
    dot_general x2 -> x0, matrix products: 8.05 us -> none  [the longest x1 5.53 us: product_bt(): lax.dot_general(left, right, (((1,), (1,)), ((), ())), preferred_element_...]
    another operation x0 -> x8, local copies, waits for them, and re-layouts: none -> 7.5 us  [gather_near(): own = jnp.stack([p[:cut] if stream == 0 else p[cut:] for p in parts])]
    pallas_call x1, Pallas kernels: 17.6 us -> 11.3 us  [place_rest(): pl.pallas_call(place_rest_kernel, in_specs=[pl.BlockSpec(memory_space=plt...]
  transfers between devices with their start and end apart: 34 -> 45, of which waited for: 20 -> 20; matrix products, arithmetic and copies ran while one was open for 14% -> 22% of each run, Pallas kernels for 13% -> 18%
where the time goes in v5:
time: 593 us; the launch traced here: 587 us
  Pallas kernels  200 us (34%)
  waiting for transfers between devices  176 us (30%)
  local copies, waits for them, and re-layouts  76.6 us (13%)
  other arithmetic  57.9 us (10%)
  starting transfers between devices  43.9 us (7%)
  matrix products  17.5 us (3%)
  between operations  16.3 us (3%)
    ppermute x43, waiting for transfers between devices, swap(): return lax.ppermute(value, 'fsdp', [(i, i ^ mask) for i in range(devices)])  175 us
    pallas_call x1, Pallas kernels, mlp(): pl.pallas_call(mlp_kernel, grid=(hidden // tile,), in_specs=[full, full,...  78.8 us
    pallas_call x1, Pallas kernels, attn_bwd(): pl.pallas_call(functools.partial(bwd_kernel, tokens, krows, qrows, per),...  44 us
    ppermute x43, starting transfers between devices, swap(): return lax.ppermute(value, 'fsdp', [(i, i ^ mask) for i in range(devices)])  43.6 us
    pallas_call x1, Pallas kernels, attn_fwd(): pl.pallas_call(functools.partial(fwd_kernel, tokens, krows, qrows, per),...  27.8 us
    pallas_call x1, Pallas kernels, qkv_back(): pl.pallas_call(qkv_back_kernel, grid=(3,), in_specs=[part((tokens, D)), w...  25.2 us
    reshape x20, local copies, waits for them, and re-layouts, window(): return result.reshape(kept)  23.2 us
    dot_general x2, matrix products, product(): return jnp.dot(left, right, preferred_element_type=f32)  17.5 us
  transfers between devices with their start and end apart: 45, of which 20 were waited for; matrix products, arithmetic and copies ran while one was open for 22% of the time, Pallas kernels for 18%

profile of v5, /device:TPU:8, one launch (start us, length us, event | category | flops | bytes accessed | tf_op | source)
XLA Modules:
  0.0 587.5 jit_solution(12450563251222326149)
XLA Ops:
  37.4 16.4 %collective-permute-done.1 = bf16[40,3584]{1,0:T(8,128)(2,1)S(1)} collective-permute-done((bf16[40,3584]{1,0:T(8,128)(2,1)S(1)}, bf16[40,3584]{1,0:T(8,128)(2,1)S(1)}, u32[]{:S(2)}, u32[]{:S(2)}) %collective-permute-start.1) | collective-permute-done | bytes 286752 | tf_op jit(solution)/shard_map/ppermute | solution.py:322
  53.8 6.4 %collective-permute-done.2 = bf16[40,3584]{1,0:T(8,128)(2,1)S(1)} collective-permute-done((bf16[40,3584]{1,0:T(8,128)(2,1)S(1)}, bf16[40,3584]{1,0:T(8,128)(2,1)S(1)}, u32[]{:S(2)}, u32[]{:S(2)}) %collective-permute-start.2) | collective-permute-done | bytes 286752 | tf_op jit(solution)/shard_map/ppermute | solution.py:322
  60.2 8.0 %collective-permute-done.3 = bf16[40,3584]{1,0:T(8,128)(2,1)S(1)} collective-permute-done((bf16[40,3584]{1,0:T(8,128)(2,1)S(1)}, bf16[40,3584]{1,0:T(8,128)(2,1)S(1)}, u32[]{:S(2)}, u32[]{:S(2)}) %collective-permute-start.3) | collective-permute-done | bytes 286752 | tf_op jit(solution)/shard_map/ppermute | solution.py:322
  71.7 17.7 %collective-permute-done.6 = bf16[4,40,1792]{2,1,0:T(8,128)(2,1)S(1)} collective-permute-done((bf16[4,40,1792]{2,1,0:T(8,128)(2,1)S(1)}, bf16[4,40,1792]{2,1,0:T(8,128)(2,1)S(1)}, u32[]{:S(2)}, u32[]{:S(2)}) %collective-permute-start.6) | collective-permute-done | bytes 573472 | tf_op jit(solution)/shard_map/ppermute | solution.py:322
  90.9 5.6 collective-permute-done.4
  101.8 21.3 %collective-permute-done.10 = bf16[136,1152]{1,0:T(8,128)(2,1)} collective-permute-done((bf16[136,1152]{1,0:T(8,128)(2,1)}, bf16[136,1152]{1,0:T(8,128)(2,1)}, u32[]{:S(2)}, u32[]{:S(2)}) %collective-permute-start.10) | collective-permute-done | bytes 313376 | tf_op jit(solution)/shard_map/ppermute | solution.py:322
  123.0 20.2 %collective-permute-done.9 = bf16[136,1152]{1,0:T(8,128)(2,1)} collective-permute-done((bf16[136,1152]{1,0:T(8,128)(2,1)}, bf16[136,1152]{1,0:T(8,128)(2,1)}, u32[]{:S(2)}, u32[]{:S(2)}) %collective-permute-start.9) | collective-permute-done | bytes 313376 | tf_op jit(solution)/shard_map/ppermute | solution.py:322
  159.6 6.7 %place_square.1 = (bf16[144,8,3456]{2,1,0:T(8,128)(2,1)}, bf16[32,5,8,128]{3,2,1,0:T(8,128)(2,1)S(1)}) custom-call(s32[4]{0:T(128)S(1)} %pad_add_fusion.coords, bf16[8,5,8,1792]{3,2,1,0:T(8,128)(2,1)S(1)} %bitcast.331, bf16[8,5,8,1792]{3,2,1,0:T(8,128)(2,1)} %bitcast.15.refs_1_, bf16[8,5,8,1792]{3,2,1,0:T(8,128)(2,1)S(1)} %bitcast.337, ...), custom_call_target="tpu_custom_call" | custom-call | bytes 18350080 | tf_op jit(solution)/shard_map/place_square/pallas_call | solution.py:387
  169.1 12.6 %add_convert_fusion.qkv_ref = bf16[729,3456]{1,0:T(8,128)(2,1)} fusion(bf16[729,1152]{1,0:T(8,128)(2,1)S(1)} %add_convert_fusion.4.normed_ref, f32[3456]{0:T(1024)S(1)} %pad_maximum_fusion.12, bf16[144,8,3456]{2,1,0:T(8,128)(2,1)} %get-tuple-element.102), kind=kOutput, calls=%fused_computation | convolution fusion | flops 5809792000 | bytes 14694912 | tf_op jit(solution)/shard_map/dot_general | solution.py:309
  188.5 27.8 %attention_forward.1 = (bf16[729,1152]{1,0:T(8,128)(2,1)}, f32[16,1,768]{2,1,0:T(1,128)}) custom-call(bf16[729,3456]{1,0:T(8,128)(2,1)} %add_convert_fusion.qkv_ref), custom_call_target="tpu_custom_call" | custom-call | flops 4630511616 | bytes 6718464 | tf_op jit(solution)/shard_map/attention_forward/pallas_call | solution.py:63
  216.3 11.3 %place_rest.1 = (bf16[144,8,4352]{2,1,0:T(8,128)(2,1)}, bf16[144,8,1152]{2,1,0:T(8,128)(2,1)}) custom-call(bf16[32,25,8,1152]{3,2,1,0:T(8,128)(2,1)} %bitcast.343), custom_call_target="tpu_custom_call" | custom-call | bytes 29491200 | tf_op jit(solution)/shard_map/place_rest/pallas_call | solution.py:438
  228.3 4.9 fusion.43
  238.2 6.0 %place_down.1 = bf16[32,17,8,1152]{3,2,1,0:T(8,128)(2,1)} custom-call(s32[4]{0:T(128)S(1)} %pad_add_fusion.coords, bf16[8,9,8,1152]{3,2,1,0:T(8,128)(2,1)S(1)} %bitcast.328, bf16[8,9,8,1152]{3,2,1,0:T(8,128)(2,1)} %bitcast.35.refs_1_, bf16[8,9,8,1152]{3,2,1,0:T(8,128)(2,1)S(1)} %bitcast.332, bf16[8,9,8,1152]{3,2,1,0:T(8,128)(2,1)S(1)} %bitcast.333, ...), custom_call_target="tpu_custom_call" | custom-call | bytes 20054016 | tf_op jit(solution)/shard_map/place_down/pallas_call | solution.py:487
  244.2 78.8 %mlp_forward_backward.1 = (f32[729,1152]{1,0:T(8,128)}, bf16[1152,4352]{1,0:T(8,128)(2,1)}, f32[1,4352]{1,0:T(1,128)}, bf16[4352,1152]{1,0:T(8,128)(2,1)}, f32[8...) custom-call(bf16[729,1152]{1,0:T(8,128)(2,1)} %get-tuple-element.121.normed_ref, ...), custom_call_target="tpu_custom_call" | custom-call | flops 1000000 | bytes 1000000 | tf_op jit(solution)/shard_map/mlp_forward_backward/pallas_call | solution.py:188
  323.0 5.5 constant_dynamic-slice_fusion.13
  331.6 8.5 %collective-permute-done.24 = bf16[4,2,2,5,8,1152]{5,4,3,2,1,0:T(8,128)(2,1)} collective-permute-done((bf16[4,2,2,5,8,1152]{5,4,3,2,1,0:T(8,128)(2,1)}, bf16[4,2,2,5,8,1152]{5,4,3,2,1,0:T(8,128)(2,1)}, u32[]{:S(2)}, u32[]{:S(2)}) %collective-permute-start.24) | collective-permute-done | bytes 1474592 | tf_op jit(solution)/shard_map/ppermute | solution.py:322
  357.8 44.0 %attention_backward.1.grad_ref = bf16[729,3456]{1,0:T(8,128)(2,1)} custom-call(bf16[729,3456]{1,0:T(8,128)(2,1)} %add_convert_fusion.qkv_ref, bf16[729,1152]{1,0:T(8,128)(2,1)} %get-tuple-element.136.go_ref, f32[16,1,768]{2,1,0:T(1,128)} %get-tuple-element.137.lse_ref), custom_call_target="tpu_custom_call" | custom-call | flops 1000000 | bytes 1000000 | tf_op jit(solution)/shard_map/attention_backward/pallas_call | solution.py:107
  401.8 25.2 %qkv_backward.1 = (bf16[1152,3456]{1,0:T(8,128)(2,1)}, f32[1,3456]{1,0:T(1,128)}, f32[8,1152]{1,0:T(8,128)}, f32[729,1152]{1,0:T(8,128)}) custom-call(bf16[729,3456]{1,0:T(8,128)(2,1)} %attention_backward.1.grad_ref, bf16[729,1152]{1,0:T(8,128)(2,1)} %copy-done.4, bf16[1152,3456]{1,0:T(8,128)(2,1)} %bitcast.359, ...), custom_call_target="tpu_custom_call" | custom-call | flops 1000000 | bytes 1000000 | tf_op jit(solution)/shard_map/qkv_backward/pallas_call | solution.py:254
  456.6 16.7 %collective-permute-done.29 = bf16[4,5,8,2688]{3,2,1,0:T(8,128)(2,1)} collective-permute-done((bf16[4,5,8,2688]{3,2,1,0:T(8,128)(2,1)}, bf16[4,5,8,2688]{3,2,1,0:T(8,128)(2,1)}, u32[]{:S(2)}, u32[]{:S(2)}) %collective-permute-start.29) | collective-permute-done | bytes 860192 | tf_op jit(solution)/shard_map/ppermute | solution.py:322
  497.1 16.1 %collective-permute-done.31 = bf16[4,2,5,8,1664]{4,3,2,1,0:T(8,128)(2,1)S(1)} collective-permute-done((bf16[4,2,5,8,1664]{4,3,2,1,0:T(8,128)(2,1)S(1)}, bf16[4,2,5,8,1664]{4,3,2,1,0:T(8,128)(2,1)S(1)}, u32[]{:S(2)}, u32[]{:S(2)}) %collective-permute-start.31) | collective-permute-done | bytes 1064992 | tf_op jit(solution)/shard_map/ppermute | solution.py:322
  523.5 7.6 %collective-permute-done.36 = bf16[5,8,5504]{2,1,0:T(8,128)(2,1)S(1)} collective-permute-done((bf16[5,8,5504]{2,1,0:T(8,128)(2,1)S(1)}, bf16[5,8,5504]{2,1,0:T(8,128)(2,1)S(1)}, u32[]{:S(2)}, u32[]{:S(2)}) %collective-permute-start.36) | collective-permute-done | bytes 440352 | tf_op jit(solution)/shard_map/ppermute | solution.py:322
  552.7 5.9 %collective-permute-done.39 = bf16[5,8,3584]{2,1,0:T(8,128)(2,1)} collective-permute-done((bf16[5,8,3584]{2,1,0:T(8,128)(2,1)S(1)}, bf16[5,8,3584]{2,1,0:T(8,128)(2,1)}, u32[]{:S(2)}, u32[]{:S(2)}) %collective-permute-start.39) | collective-permute-done | bytes 286752 | tf_op jit(solution)/shard_map/ppermute | solution.py:322
  558.7 10.0 %collective-permute-done.40 = bf16[5,8,3584]{2,1,0:T(8,128)(2,1)} collective-permute-done((bf16[5,8,3584]{2,1,0:T(8,128)(2,1)}, bf16[5,8,3584]{2,1,0:T(8,128)(2,1)}, u32[]{:S(2)}, u32[]{:S(2)}) %collective-permute-start.40) | collective-permute-done | bytes 286752 | tf_op jit(solution)/shard_map/ppermute | solution.py:322
  568.7 6.7 %collective-permute-done.41 = bf16[5,8,3584]{2,1,0:T(8,128)(2,1)} collective-permute-done((bf16[5,8,3584]{2,1,0:T(8,128)(2,1)}, bf16[5,8,3584]{2,1,0:T(8,128)(2,1)}, u32[]{:S(2)}, u32[]{:S(2)}) %collective-permute-start.41) | collective-permute-done | bytes 286752 | tf_op jit(solution)/shard_map/ppermute | solution.py:322
  (370 shorter events, 181.3 us)
Async XLA Ops:
  7.2 209.1 %all-gather.2.cloned.1.call-start = ((), (), s32[]{:S(2)}) async-start(), calls=%async_computation.1 | async-start | bytes 15206400 | tf_op jit(solution)/shard_map/all_gather | solution.py:717
  20.8 513.5 %reduce-scatter.4.cloned.1.call-start = ((), (), s32[]{:S(2)}) async-start(), calls=%async_computation.2 | async-start | bytes 10340352
  31.6 28.6 %collective-permute-start.2 = (bf16[40,3584]{1,0:T(8,128)(2,1)S(1)}, bf16[40,3584]{1,0:T(8,128)(2,1)S(1)}, u32[]{:S(2)}, u32[]{:S(2)}) collective-permute-start(bf16[40,3584]{1,0:T(8,128)(2,1)S(1)} %pad_maximum_fusion.7), channel_id=1, source_target_pairs={{0,16},{1,17},{2,18},{3,19},{4,20},{5,21},{6,22},{7,23},{8,24},{9,... | collective-permute-start | bytes 860168 | tf_op jit(solution)/shard_map/ppermute | solution.py:322
  34.6 33.6 %collective-permute-start.3 = (bf16[40,3584]{1,0:T(8,128)(2,1)S(1)}, bf16[40,3584]{1,0:T(8,128)(2,1)S(1)}, u32[]{:S(2)}, u32[]{:S(2)}) collective-permute-start(bf16[40,3584]{1,0:T(8,128)(2,1)S(1)} %pad_maximum_fusion.7), channel_id=1, source_target_pairs={{0,24},{1,25},{2,26},{3,27},{4,28},{5,29},{6,30},{7,31},{8,16},{9,... | collective-permute-start | bytes 860168 | tf_op jit(solution)/shard_map/ppermute | solution.py:322
  70.0 26.5 %collective-permute-start.4 = (bf16[4,40,1792]{2,1,0:T(8,128)(2,1)S(1)}, bf16[4,40,1792]{2,1,0:T(8,128)(2,1)S(1)}, u32[]{:S(2)}, u32[]{:S(2)}) collective-permute-start(bf16[4,40,1792]{2,1,0:T(8,128)(2,1)S(1)} %pad_maximum_fusion.2), channel_id=1, source_target_pairs={{0,2},{1,3},{2,0},{3,1},{4,6},{5,7},{6,4},{7,5},{8,10},{9,11},{10,... | collective-permute-start | bytes 1720328 | tf_op jit(solution)/shard_map/ppermute | solution.py:322
  89.4 53.8 %collective-permute-start.7 = (bf16[8,40,1792]{2,1,0:T(8,128)(2,1)S(1)}, bf16[8,40,1792]{2,1,0:T(8,128)(2,1)S(1)}, u32[]{:S(2)}, u32[]{:S(2)}) collective-permute-start(bf16[8,40,1792]{2,1,0:T(8,128)(2,1)S(1)} %constant_dynamic-update-slice_fusion.10), channel_id=1, source_target_pairs={{0,2},{1,3},{2,0},{3,1},{4,6},{5,7},{6,4},{7,5},{8,10},{9,11},{10,... | collective-permute-start | bytes 3440648 | tf_op jit(solution)/shard_map/ppermute | solution.py:322
  96.6 46.6 %collective-permute-start.5 = (bf16[8,40,1792]{2,1,0:T(8,128)(2,1)S(1)}, bf16[8,40,1792]{2,1,0:T(8,128)(2,1)}, u32[]{:S(2)}, u32[]{:S(2)}) collective-permute-start(bf16[8,40,1792]{2,1,0:T(8,128)(2,1)S(1)} %constant_dynamic-update-slice_fusion.5), channel_id=1, source_target_pairs={{0,4},{1,5},{2,6},{3,7},{4,0},{5,1},{6,2},{7,3},{8,12},{9,13},{10,... | collective-permute-start | bytes 3440648 | tf_op jit(solution)/shard_map/ppermute | solution.py:322
  98.2 24.8 %collective-permute-start.10 = (bf16[136,1152]{1,0:T(8,128)(2,1)}, bf16[136,1152]{1,0:T(8,128)(2,1)}, u32[]{:S(2)}, u32[]{:S(2)}) collective-permute-start(bf16[136,1152]{1,0:T(8,128)(2,1)} %reshape.672), channel_id=1, source_target_pairs={{0,24},{1,25},{2,26},{3,27},{4,28},{5,29},{6,30},{7,31},{8,16},{9,... | collective-permute-start | bytes 940040 | tf_op jit(solution)/shard_map/ppermute | solution.py:322
  98.8 44.4 %collective-permute-start.9 = (bf16[136,1152]{1,0:T(8,128)(2,1)}, bf16[136,1152]{1,0:T(8,128)(2,1)}, u32[]{:S(2)}, u32[]{:S(2)}) collective-permute-start(bf16[136,1152]{1,0:T(8,128)(2,1)} %reshape.672), channel_id=1, source_target_pairs={{0,16},{1,17},{2,18},{3,19},{4,20},{5,21},{6,22},{7,23},{8,24},{9,... | collective-permute-start | bytes 940040 | tf_op jit(solution)/shard_map/ppermute | solution.py:322
  147.9 33.8 %collective-permute-start.16 = (bf16[4,64,1152]{2,1,0:T(8,128)(2,1)}, bf16[4,64,1152]{2,1,0:T(8,128)(2,1)}, u32[]{:S(2)}, u32[]{:S(2)}) collective-permute-start(bf16[4,64,1152]{2,1,0:T(8,128)(2,1)} %pad_maximum_fusion.1), channel_id=1, source_target_pairs={{0,4},{1,5},{2,6},{3,7},{4,0},{5,1},{6,2},{7,3},{8,12},{9,13},{10,... | collective-permute-start | bytes 1769480 | tf_op jit(solution)/shard_map/ppermute | solution.py:322
  155.5 26.2 %collective-permute-start.15 = (bf16[4,72,1152]{2,1,0:T(8,128)(2,1)}, bf16[4,72,1152]{2,1,0:T(8,128)(2,1)}, u32[]{:S(2)}, u32[]{:S(2)}) collective-permute-start(bf16[4,72,1152]{2,1,0:T(8,128)(2,1)} %pad_maximum_fusion), channel_id=1, source_target_pairs={{0,2},{1,3},{2,0},{3,1},{4,6},{5,7},{6,4},{7,5},{8,10},{9,11},{10,... | collective-permute-start | bytes 1990664 | tf_op jit(solution)/shard_map/ppermute | solution.py:322
  184.0 32.2 %collective-permute-start.17 = (bf16[8,72,1152]{2,1,0:T(8,128)(2,1)S(1)}, bf16[8,72,1152]{2,1,0:T(8,128)(2,1)}, u32[]{:S(2)}, u32[]{:S(2)}) collective-permute-start(bf16[8,72,1152]{2,1,0:T(8,128)(2,1)S(1)} %constant_dynamic-update-slice_fusion.15), channel_id=1, source_target_pairs={{0,4},{1,5},{2,6},{3,7},{4,0},{5,1},{6,2},{7,3},{8,12},{9,13},{10,... | collective-permute-start | bytes 3981320 | tf_op jit(solution)/shard_map/ppermute | solution.py:322
  186.4 29.9 %collective-permute-start.18 = (bf16[8,64,1152]{2,1,0:T(8,128)(2,1)S(1)}, bf16[8,64,1152]{2,1,0:T(8,128)(2,1)}, u32[]{:S(2)}, u32[]{:S(2)}) collective-permute-start(bf16[8,64,1152]{2,1,0:T(8,128)(2,1)S(1)} %constant_dynamic-update-slice_fusion.17), channel_id=1, source_target_pairs={{0,2},{1,3},{2,0},{3,1},{4,6},{5,7},{6,4},{7,5},{8,10},{9,11},{10,... | collective-permute-start | bytes 3538952 | tf_op jit(solution)/shard_map/ppermute | solution.py:322
  345.2 56.6 %collective-permute-start.25 = (bf16[4,2,5,8,2816]{4,3,2,1,0:T(8,128)(2,1)}, bf16[4,2,5,8,2816]{4,3,2,1,0:T(8,128)(2,1)}, u32[]{:S(2)}, u32[]{:S(2)}) collective-permute-start(bf16[4,2,5,8,2816]{4,3,2,1,0:T(8,128)(2,1)} %fusion.1), channel_id=1, source_target_pairs={{0,4},{1,5},{2,6},{3,7},{4,0},{5,1},{6,2},{7,3},{8,12},{9,13},{10,... | collective-permute-start | bytes 5406728 | tf_op jit(solution)/shard_map/ppermute | solution.py:322
  350.2 51.6 %collective-permute-start.26 = (bf16[4,2,5,8,2688]{4,3,2,1,0:T(8,128)(2,1)}, bf16[4,2,5,8,2688]{4,3,2,1,0:T(8,128)(2,1)}, u32[]{:S(2)}, u32[]{:S(2)}) collective-permute-start(bf16[4,2,5,8,2688]{4,3,2,1,0:T(8,128)(2,1)} %add_convert_fusion.2), channel_id=1, source_target_pairs={{0,2},{1,3},{2,0},{3,1},{4,6},{5,7},{6,4},{7,5},{8,10},{9,11},{10,... | collective-permute-start | bytes 5160968 | tf_op jit(solution)/shard_map/ppermute | solution.py:322
  431.8 43.9 %collective-permute-start.27 = (bf16[4,2,2,5,8,3456]{5,4,3,2,1,0:T(8,128)(2,1)}, bf16[4,2,2,5,8,3456]{5,4,3,2,1,0:T(8,128)(2,1)}, u32[]{:S(2)}, u32[]{:S(2)}) collective-permute-start(bf16[4,2,2,5,8,3456]{5,4,3,2,1,0:T(8,128)(2,1)} %constant_dynamic-slice_fusion.11), channel_id=1, source_target_pairs={{0,1},{1,0},{2,3},{3,2},{4,5},{5,4},{6,7},{7,6},{8,9},{9,8},{10,11... | collective-permute-start | bytes 13271048 | tf_op jit(solution)/shard_map/ppermute | solution.py:322
  448.8 24.5 %collective-permute-start.29 = (bf16[4,5,8,2688]{3,2,1,0:T(8,128)(2,1)}, bf16[4,5,8,2688]{3,2,1,0:T(8,128)(2,1)}, u32[]{:S(2)}, u32[]{:S(2)}) collective-permute-start(bf16[4,5,8,2688]{3,2,1,0:T(8,128)(2,1)} %fusion.3), channel_id=1, source_target_pairs={{0,4},{1,5},{2,6},{3,7},{4,0},{5,1},{6,2},{7,3},{8,12},{9,13},{10,... | collective-permute-start | bytes 2580488 | tf_op jit(solution)/shard_map/ppermute | solution.py:322
  451.0 24.6 %collective-permute-start.28 = (bf16[4,5,8,2816]{3,2,1,0:T(8,128)(2,1)S(1)}, bf16[4,5,8,2816]{3,2,1,0:T(8,128)(2,1)S(1)}, u32[]{:S(2)}, u32[]{:S(2)}) collective-permute-start(bf16[4,5,8,2816]{3,2,1,0:T(8,128)(2,1)S(1)} %fusion.2), channel_id=1, source_target_pairs={{0,2},{1,3},{2,0},{3,1},{4,6},{5,7},{6,4},{7,5},{8,10},{9,11},{10,... | collective-permute-start | bytes 2703368 | tf_op jit(solution)/shard_map/ppermute | solution.py:322
  454.1 43.0 %collective-permute-start.33 = (bf16[4,2,5,8,128]{4,3,2,1,0:T(8,128)(2,1)S(1)}, bf16[4,2,5,8,128]{4,3,2,1,0:T(8,128)(2,1)S(1)}, u32[]{:S(2)}, u32[]{:S(2)}) collective-permute-start(bf16[4,2,5,8,128]{4,3,2,1,0:T(8,128)(2,1)S(1)} %fusion.28), channel_id=1, source_target_pairs={{0,4},{1,5},{2,6},{3,7},{4,0},{5,1},{6,2},{7,3},{8,12},{9,13},{10,... | collective-permute-start | bytes 245768 | tf_op jit(solution)/shard_map/ppermute | solution.py:322
  480.0 43.5 %collective-permute-start.38 = (bf16[5,8,5504]{2,1,0:T(8,128)(2,1)S(1)}, bf16[5,8,5504]{2,1,0:T(8,128)(2,1)S(1)}, u32[]{:S(2)}, u32[]{:S(2)}) collective-permute-start(bf16[5,8,5504]{2,1,0:T(8,128)(2,1)S(1)} %pad_maximum_fusion.6), channel_id=1, source_target_pairs={{0,24},{1,25},{2,26},{3,27},{4,28},{5,29},{6,30},{7,31},{8,16},{9,... | collective-permute-start | bytes 1320968 | tf_op jit(solution)/shard_map/ppermute | solution.py:322
  486.6 26.6 %collective-permute-start.32 = (bf16[4,2,5,8,1792]{4,3,2,1,0:T(8,128)(2,1)S(1)}, bf16[4,2,5,8,1792]{4,3,2,1,0:T(8,128)(2,1)S(1)}, u32[]{:S(2)}, u32[]{:S(2)}) collective-permute-start(bf16[4,2,5,8,1792]{4,3,2,1,0:T(8,128)(2,1)S(1)} %fusion.4), channel_id=1, source_target_pairs={{0,2},{1,3},{2,0},{3,1},{4,6},{5,7},{6,4},{7,5},{8,10},{9,11},{10,... | collective-permute-start | bytes 3440648 | tf_op jit(solution)/shard_map/ppermute | solution.py:322
  488.8 24.4 %collective-permute-start.31 = (bf16[4,2,5,8,1664]{4,3,2,1,0:T(8,128)(2,1)S(1)}, bf16[4,2,5,8,1664]{4,3,2,1,0:T(8,128)(2,1)S(1)}, u32[]{:S(2)}, u32[]{:S(2)}) collective-permute-start(bf16[4,2,5,8,1664]{4,3,2,1,0:T(8,128)(2,1)S(1)} %fusion.7), channel_id=1, source_target_pairs={{0,4},{1,5},{2,6},{3,7},{4,0},{5,1},{6,2},{7,3},{8,12},{9,13},{10,... | collective-permute-start | bytes 3194888 | tf_op jit(solution)/shard_map/ppermute | solution.py:322
  490.5 33.0 %collective-permute-start.37 = (bf16[5,8,5504]{2,1,0:T(8,128)(2,1)S(1)}, bf16[5,8,5504]{2,1,0:T(8,128)(2,1)S(1)}, u32[]{:S(2)}, u32[]{:S(2)}) collective-permute-start(bf16[5,8,5504]{2,1,0:T(8,128)(2,1)S(1)} %pad_maximum_fusion.5), channel_id=1, source_target_pairs={{0,16},{1,17},{2,18},{3,19},{4,20},{5,21},{6,22},{7,23},{8,24},{9,... | collective-permute-start | bytes 1320968 | tf_op jit(solution)/shard_map/ppermute | solution.py:322
  549.6 25.8 %collective-permute-start.41 = (bf16[5,8,3584]{2,1,0:T(8,128)(2,1)}, bf16[5,8,3584]{2,1,0:T(8,128)(2,1)}, u32[]{:S(2)}, u32[]{:S(2)}) collective-permute-start(bf16[5,8,3584]{2,1,0:T(8,128)(2,1)} %pad_maximum_fusion.10), channel_id=1, source_target_pairs={{0,24},{1,25},{2,26},{3,27},{4,28},{5,29},{6,30},{7,31},{8,16},{9,... | collective-permute-start | bytes 860168 | tf_op jit(solution)/shard_map/ppermute | solution.py:322
  (68 other events, 560.9 us)
Sparse Core Ops, SparseCore 0:
  20.9 147.5 all-gather.1
  330.4 143.5 reduce-scatter.3

commit v6 on v5

--- a/solution.py
+++ b/solution.py
@@ -298,8 +298,9 @@
 QKV_CUT = 14 * 128
 UP_CUT = 22 * 128
 UP_PIECES = 4
-DOWN_CUT = 72
-REST_ROWS = UP_PIECES * BLOCK_TILES * TILE + BLOCK_TILES * TILE
+DOWN_CUT = 40
+DOWN_FIRST = 64
+REST_ROWS = UP_PIECES * BLOCK_TILES * TILE + BLOCK_TILES * TILE + DOWN_FIRST
 VECTORS = (0, 1, 3, 6, 8, 9, 10, 12, 14)
 bf16 = jnp.bfloat16
 f32 = jnp.float32
@@ -402,100 +403,80 @@
     return whole.reshape(D, 3 * D), small.reshape(2 * GROUPS, -1)
 
 
-def place_rest_kernel(source, up, out, held, in_sems, out_sems):
+def place_rest_kernel(coords, *refs):
+    source, streams, (up, out, down) = refs[0], refs[1:9], refs[9:12]
+    held, in_sems, out_sems = refs[12], refs[13], refs[14]
+    parts, part_sems = refs[15:23], refs[23]
+    core, x, y, z = coords[0], coords[1], coords[2], coords[3]
     arrivals = [
         pltpu.make_async_copy(source.at[i], held.at[i], in_sems.at[i]) for i in range(2 * GROUPS)
     ]
-    for arrival in arrivals:
+    others = [pltpu.make_async_copy(streams[i], parts[i], part_sems.at[i]) for i in range(8)]
+    for arrival in arrivals + others:
         arrival.start()
     copies = []
+
+    def move(one, other):
+        copies.append(pltpu.make_async_copy(one, other, out_sems.at[len(copies)]))
+        copies[-1].start()
+
+    lead = DOWN_FIRST // TILE
     for device in range(2 * GROUPS):
         chip, owner = device // 2, device % 2
         src = held.at[device]
         arrivals[device].wait()
-        jobs = []
         count = BLOCK_TILES - owner
         first = PAIR_TILES * chip + BLOCK_TILES * owner
         for piece in range(UP_PIECES):
             cols = min(D, FF_PAD - piece * D)
-            jobs.append(
-                (
-                    src.at[pl.ds(piece * BLOCK_TILES + owner, count), :, pl.ds(0, cols)],
-                    up.at[pl.ds(first, count), :, pl.ds(piece * D, cols)],
-                )
+            move(
+                src.at[pl.ds(piece * BLOCK_TILES + owner, count), :, pl.ds(0, cols)],
+                up.at[pl.ds(first, count), :, pl.ds(piece * D, cols)],
             )
         base = UP_PIECES * BLOCK_TILES
-        jobs.append((src.at[pl.ds(base + owner, count)], out.at[pl.ds(first, count)]))
-        for one, other in jobs:
-            copies.append(pltpu.make_async_copy(one, other, out_sems.at[len(copies)]))
-            copies[-1].start()
+        move(src.at[pl.ds(base + owner, count)], out.at[pl.ds(first, count)])
+        move(src.at[pl.ds(base + BLOCK_TILES, lead)], down.at[device, pl.ds(0, lead)])
+    for part, stream in itertools.product(range(4), range(2)):
+        others[4 * stream + part].wait()
+        for near, dz in itertools.product(range(2), range(4)):
+            src = parts[4 * stream + part].at[near * 4 + dz]
+            owner = core if part < 2 else 1 - core
+            far = part % 2
+            dx, dy = (near, far) if stream == 0 else (far, near)
+            chip = ((z ^ dz) * 2 + (y ^ dy)) * 2 + (x ^ dx)
+            first = lead + (DOWN_CUT // TILE if stream else 0)
+            move(src, down.at[chip * 2 + owner, pl.ds(first, src.shape[0])])
     for copy in copies:
         copy.wait()
 
 
-def place_rest(gathered):
+def place_rest(gathered, streams, coords):
     source = gathered.reshape(2 * GROUPS, REST_ROWS // TILE, TILE, D)
-    up, out = pl.pallas_call(
+    sources = [s.reshape(8, -1, TILE, D) for s in (*streams[0], *streams[1])]
+    up, out, down = pl.pallas_call(
         place_rest_kernel,
-        in_specs=[pl.BlockSpec(memory_space=pltpu.HBM)],
-        out_specs=[pl.BlockSpec(memory_space=pltpu.HBM)] * 2,
+        in_specs=[pl.BlockSpec(memory_space=pltpu.SMEM)]
+        + [pl.BlockSpec(memory_space=pltpu.HBM)] * 9,
+        out_specs=[pl.BlockSpec(memory_space=pltpu.HBM)] * 3,
         out_shape=[
             jax.ShapeDtypeStruct((D // TILE, TILE, FF_PAD), bf16),
             jax.ShapeDtypeStruct((D // TILE, TILE, D), bf16),
+            jax.ShapeDtypeStruct((2 * GROUPS, HALF_DOWN // TILE, TILE, D), bf16),
         ],
         scratch_shapes=[
             pltpu.VMEM(source.shape, bf16),
             pltpu.SemaphoreType.DMA((2 * GROUPS,)),
-            pltpu.SemaphoreType.DMA((2 * GROUPS * (UP_PIECES + 1),)),
-        ],
-        compiler_params=pltpu.CompilerParams(vmem_limit_bytes=56 << 20),
+            pltpu.SemaphoreType.DMA((2 * GROUPS * (UP_PIECES + 2) + 64,)),
+        ]
+        + [pltpu.VMEM(s.shape, bf16) for s in sources]
+        + [pltpu.SemaphoreType.DMA((8,))],
+        compiler_params=pltpu.CompilerParams(vmem_limit_bytes=60 << 20),
         cost_estimate=pl.CostEstimate(
             flops=0, bytes_accessed=4 * source.size, transcendentals=0
         ),
         name="place_rest",
-    )(source)
-    return up.reshape(D, FF_PAD), out.reshape(D, D)
-
-
-def place_down_kernel(coords, *refs):
-    sources, whole = refs[:8], refs[8]
-    held, in_sems, out_sems = refs[9:17], refs[17], refs[18]
-    core, x, y, z = coords[0], coords[1], coords[2], coords[3]
-    arrivals = [pltpu.make_async_copy(sources[i], held[i], in_sems.at[i]) for i in range(8)]
-    for arrival in arrivals:
-        arrival.start()
-    copies = []
-    for part, stream in itertools.product(range(4), range(2)):
-        arrivals[4 * stream + part].wait()
-        for near, dz in itertools.product(range(2), range(4)):
-            src = held[4 * stream + part].at[near * 4 + dz]
-            owner = core if part < 2 else 1 - core
-            far = part % 2
-            dx, dy = (near, far) if stream == 0 else (far, near)
-            chip = ((z ^ dz) * 2 + (y ^ dy)) * 2 + (x ^ dx)
-            first = DOWN_CUT // TILE if stream else 0
-            dst = whole.at[chip * 2 + owner, first : first + src.shape[0]]
-            copies.append(pltpu.make_async_copy(src, dst, out_sems.at[len(copies)]))
-            copies[-1].start()
-    for copy in copies:
-        copy.wait()
-
-
-def place_down(streams, coords):
-    sources = [s.reshape(8, -1, TILE, D) for s in (*streams[0], *streams[1])]
-    size = sum(s.size for s in sources) * 2
-    return pl.pallas_call(
-        place_down_kernel,
-        in_specs=[pl.BlockSpec(memory_space=pltpu.SMEM)]
-        + [pl.BlockSpec(memory_space=pltpu.HBM)] * 8,
-        out_specs=pl.BlockSpec(memory_space=pltpu.HBM),
-        out_shape=jax.ShapeDtypeStruct((2 * GROUPS, HALF_DOWN // TILE, TILE, D), bf16),
-        scratch_shapes=[pltpu.VMEM(s.shape, bf16) for s in sources]
-        + [pltpu.SemaphoreType.DMA((8,)), pltpu.SemaphoreType.DMA((64,))],
-        compiler_params=pltpu.CompilerParams(vmem_limit_bytes=40 << 20),
-        cost_estimate=pl.CostEstimate(flops=0, bytes_accessed=2 * size, transcendentals=0),
-        name="place_down",
-    )(coords, *sources).reshape(FF_PAD, D)
+    )(coords, source, *sources)
+    return up.reshape(D, FF_PAD), out.reshape(D, D), down.reshape(FF_PAD, D)
 
 
 def tie(*values):
@@ -650,8 +631,8 @@
     square = jnp.concatenate([small, block[:, : 3 * D]], axis=1)
     up_block = jnp.pad(block[:, 4 * D :], ((0, 0), (0, UP_PIECES * D - FF_PAD)))
     pieces = [up_block[:, i * D : (i + 1) * D] for i in range(UP_PIECES)]
-    rest = jnp.concatenate(pieces + [block[:, 3 * D : 4 * D]])
-    return square, rest, down_block
+    rest = jnp.concatenate(pieces + [block[:, 3 * D : 4 * D], down_block[:DOWN_FIRST]])
+    return square, rest, down_block[DOWN_FIRST:]
 
 
 def normalize(values):
@@ -743,15 +724,12 @@
         down = gather_far(down)
     mixed, lse = attn_fwd(qkv, 2)
     if staged:
-        mixed, lse, rest, down = tie(mixed, lse, rest, down)
+        mixed, lse, down = tie(mixed, lse, down)
         down = gather_core(down)
-        weight_up, weight_o = place_rest(rest)
+        weight_up, weight_o, weight_down = place_rest(rest, down, where)
     resid = tokens + product(mixed, weight_o) + bias_o
     xhat_two, inverse_two = normalize(resid)
     normed_two = (xhat_two * gain_two + shift_two).astype(bf16)
-    if staged:
-        normed_two, down = tie(normed_two, down)
-        weight_down = place_down(down, where)
     branch, up_grad, up_bias_grad, down_grad, sums_two, grad_resid, o_grad, grad_mixed = mlp(
         normed_two,
         grad_branch,
@@ -788,6 +766,7 @@
     grads[3], grads[6] = qkv_bias_grad[0, :D], qkv_bias_grad[0, 2 * D :]
     grads[0], grads[1] = norm_sums[0], norm_sums[1]
     if staged:
+        qkv_grad, outer_near = tie(qkv_grad, outer_near)
         inner = Reduction((qkv_grad,), (((0, 0, QKV_CUT - EXTRA),),) * 2, coords)
         inner_other = inner.core_step()
         inner_other, outer_near, qkv_grad, norm_sums, qkv_bias_grad = tie(

time: 593 us -> 591 us (level)
  waiting for transfers between devices: 176 us -> 154 us
  local copies, waits for them, and re-layouts: 76.6 us -> 89.8 us
  Pallas kernels: 200 us -> 211 us
    ppermute x43, waiting for transfers between devices: 175 us -> 154 us  [swap(): return lax.ppermute(value, 'fsdp', [(i, i ^ mask) for i in range(devices)])]
    pallas_call x1, Pallas kernels: 78.8 us -> 87.6 us  [mlp(): pl.pallas_call(mlp_kernel, grid=(hidden // tile,), in_specs=[full, full,...]
    pallas_call x1, Pallas kernels: 11.3 us -> 19.5 us  [place_rest(): pl.pallas_call(place_rest_kernel, in_specs=[pl.BlockSpec(memory_space=plt...]
    unnamed x108 -> x141, local copies, waits for them, and re-layouts: 6.8 us -> 14.1 us
    pallas_call x1 -> x0, Pallas kernels: 5.97 us -> none  [place_down(): pl.pallas_call(place_down_kernel, in_specs=[pl.BlockSpec(memory_space=plt...]
  transfers between devices with their start and end apart: 45 -> 45, of which waited for: 20 -> 18; matrix products, arithmetic and copies ran while one was open for 22% -> 19% of each run, Pallas kernels for 18% -> 18%
where the time goes in v6:
time: 591 us; the launch traced here: 585 us
  Pallas kernels  211 us (36%)
  waiting for transfers between devices  154 us (26%)
  local copies, waits for them, and re-layouts  89.8 us (15%)
  other arithmetic  57.6 us (10%)
  starting transfers between devices  39.2 us (7%)
  matrix products  17.5 us (3%)
  between operations  16.3 us (3%)
    ppermute x43, waiting for transfers between devices, swap(): return lax.ppermute(value, 'fsdp', [(i, i ^ mask) for i in range(devices)])  154 us
    pallas_call x1, Pallas kernels, mlp(): pl.pallas_call(mlp_kernel, grid=(hidden // tile,), in_specs=[full, full,...  87.6 us
    pallas_call x1, Pallas kernels, attn_bwd(): pl.pallas_call(functools.partial(bwd_kernel, tokens, krows, qrows, per),...  43.9 us
    ppermute x43, starting transfers between devices, swap(): return lax.ppermute(value, 'fsdp', [(i, i ^ mask) for i in range(devices)])  39.2 us
    pallas_call x1, Pallas kernels, attn_fwd(): pl.pallas_call(functools.partial(fwd_kernel, tokens, krows, qrows, per),...  27.9 us
    pallas_call x1, Pallas kernels, qkv_back(): pl.pallas_call(qkv_back_kernel, grid=(3,), in_specs=[part((tokens, D)), w...  25 us
    reshape x20, local copies, waits for them, and re-layouts, window(): return result.reshape(kept)  21.2 us
    pallas_call x1, Pallas kernels, place_rest(): pl.pallas_call(place_rest_kernel, in_specs=[pl.BlockSpec(memory_space=plt...  19.5 us
  transfers between devices with their start and end apart: 45, of which 18 were waited for; matrix products, arithmetic and copies ran while one was open for 19% of the time, Pallas kernels for 18%

profile of v6, /device:TPU:8, one launch (start us, length us, event | category | flops | bytes accessed | tf_op | source)
XLA Modules:
  0.0 585.2 jit_solution(5439351860229824401)
XLA Ops:
  43.0 12.0 %collective-permute-done.1 = bf16[40,3584]{1,0:T(8,128)(2,1)S(1)} collective-permute-done((bf16[40,3584]{1,0:T(8,128)(2,1)S(1)}, bf16[40,3584]{1,0:T(8,128)(2,1)S(1)}, u32[]{:S(2)}, u32[]{:S(2)}) %collective-permute-start.1) | collective-permute-done | bytes 286752 | tf_op jit(solution)/shard_map/ppermute | solution.py:323
  55.0 14.1 %collective-permute-done.2 = bf16[40,3584]{1,0:T(8,128)(2,1)S(1)} collective-permute-done((bf16[40,3584]{1,0:T(8,128)(2,1)S(1)}, bf16[40,3584]{1,0:T(8,128)(2,1)S(1)}, u32[]{:S(2)}, u32[]{:S(2)}) %collective-permute-start.2) | collective-permute-done | bytes 286752 | tf_op jit(solution)/shard_map/ppermute | solution.py:323
  69.1 7.7 %collective-permute-done.3 = bf16[40,3584]{1,0:T(8,128)(2,1)S(1)} collective-permute-done((bf16[40,3584]{1,0:T(8,128)(2,1)S(1)}, bf16[40,3584]{1,0:T(8,128)(2,1)S(1)}, u32[]{:S(2)}, u32[]{:S(2)}) %collective-permute-start.3) | collective-permute-done | bytes 286752 | tf_op jit(solution)/shard_map/ppermute | solution.py:323
  80.4 19.4 %collective-permute-done.6 = bf16[4,40,1792]{2,1,0:T(8,128)(2,1)S(1)} collective-permute-done((bf16[4,40,1792]{2,1,0:T(8,128)(2,1)S(1)}, bf16[4,40,1792]{2,1,0:T(8,128)(2,1)S(1)}, u32[]{:S(2)}, u32[]{:S(2)}) %collective-permute-start.6) | collective-permute-done | bytes 573472 | tf_op jit(solution)/shard_map/ppermute | solution.py:323
  101.3 5.4 collective-permute-done.4
  110.5 9.8 %collective-permute-done.10 = bf16[72,1152]{1,0:T(8,128)(2,1)} collective-permute-done((bf16[72,1152]{1,0:T(8,128)(2,1)}, bf16[72,1152]{1,0:T(8,128)(2,1)}, u32[]{:S(2)}, u32[]{:S(2)}) %collective-permute-start.10) | collective-permute-done | bytes 165920 | tf_op jit(solution)/shard_map/ppermute | solution.py:323
  120.3 7.4 %collective-permute-done.9 = bf16[72,1152]{1,0:T(8,128)(2,1)} collective-permute-done((bf16[72,1152]{1,0:T(8,128)(2,1)}, bf16[72,1152]{1,0:T(8,128)(2,1)}, u32[]{:S(2)}, u32[]{:S(2)}) %collective-permute-start.9) | collective-permute-done | bytes 165920 | tf_op jit(solution)/shard_map/ppermute | solution.py:323
  127.8 6.6 %collective-permute-done.7 = bf16[8,40,1792]{2,1,0:T(8,128)(2,1)S(1)} collective-permute-done((bf16[8,40,1792]{2,1,0:T(8,128)(2,1)S(1)}, bf16[8,40,1792]{2,1,0:T(8,128)(2,1)S(1)}, u32[]{:S(2)}, u32[]{:S(2)}) %collective-permute-start.7) | collective-permute-done | bytes 1146912 | tf_op jit(solution)/shard_map/ppermute | solution.py:323
  147.4 6.6 %place_square.1 = (bf16[144,8,3456]{2,1,0:T(8,128)(2,1)}, bf16[32,5,8,128]{3,2,1,0:T(8,128)(2,1)S(1)}) custom-call(s32[4]{0:T(128)S(1)} %pad_add_fusion.coords, bf16[8,5,8,1792]{3,2,1,0:T(8,128)(2,1)S(1)} %bitcast.329, bf16[8,5,8,1792]{3,2,1,0:T(8,128)(2,1)} %bitcast.15.refs_1_, bf16[8,5,8,1792]{3,2,1,0:T(8,128)(2,1)S(1)} %bitcast.331, ...), custom_call_target="tpu_custom_call" | custom-call | bytes 18350080 | tf_op jit(solution)/shard_map/place_square/pallas_call | solution.py:388
  158.3 12.6 %add_convert_fusion.qkv_ref = bf16[729,3456]{1,0:T(8,128)(2,1)} fusion(bf16[729,1152]{1,0:T(8,128)(2,1)S(1)} %add_convert_fusion.4.normed_ref, f32[3456]{0:T(1024)S(1)} %pad_maximum_fusion.12, bf16[144,8,3456]{2,1,0:T(8,128)(2,1)} %get-tuple-element.96), kind=kOutput, calls=%fused_computation | convolution fusion | flops 5809792000 | bytes 14694912 | tf_op jit(solution)/shard_map/dot_general | solution.py:310
  178.2 27.9 %attention_forward.1 = (bf16[729,1152]{1,0:T(8,128)(2,1)}, f32[16,1,768]{2,1,0:T(1,128)}) custom-call(bf16[729,3456]{1,0:T(8,128)(2,1)} %add_convert_fusion.qkv_ref), custom_call_target="tpu_custom_call" | custom-call | flops 4630511616 | bytes 6718464 | tf_op jit(solution)/shard_map/attention_forward/pallas_call | solution.py:63
  217.0 19.5 %place_rest.1 = (bf16[144,8,4352]{2,1,0:T(8,128)(2,1)}, bf16[144,8,1152]{2,1,0:T(8,128)(2,1)}, bf16[32,17,8,1152]{3,2,1,0:T(8,128)(2,1)}) custom-call(s32[4]{0:T(128)} %copy-done, bf16[32,33,8,1152]{3,2,1,0:T(8,128)(2,1)} %bitcast.336, bf16[8,5,8,1152]{3,2,1,0:T(8,128)(2,1)} %bitcast.360, bf16[8,5,8,1152]{3,2,1,0:T(8,128)(2,1)} %bitcast.362, ...), custom_call_target="tpu_custom_call" | custom-call | bytes 38928384 | tf_op jit(solution)/shard_map/place_rest/pallas_call | solution.py:456
  236.5 4.9 fusion.43
  246.3 87.6 %mlp_forward_backward.1 = (f32[729,1152]{1,0:T(8,128)}, bf16[1152,4352]{1,0:T(8,128)(2,1)}, f32[1,4352]{1,0:T(1,128)}, bf16[4352,1152]{1,0:T(8,128)(2,1)}, f32[8...) custom-call(bf16[729,1152]{1,0:T(8,128)(2,1)} %get-tuple-element.163.normed_ref, ...), custom_call_target="tpu_custom_call" | custom-call | flops 1000000 | bytes 1000000 | tf_op jit(solution)/shard_map/mlp_forward_backward/pallas_call | solution.py:188
  333.9 5.5 constant_dynamic-slice_fusion.13
  342.5 8.5 %collective-permute-done.24 = bf16[4,2,2,5,8,1152]{5,4,3,2,1,0:T(8,128)(2,1)} collective-permute-done((bf16[4,2,2,5,8,1152]{5,4,3,2,1,0:T(8,128)(2,1)}, bf16[4,2,2,5,8,1152]{5,4,3,2,1,0:T(8,128)(2,1)}, u32[]{:S(2)}, u32[]{:S(2)}) %collective-permute-start.24) | collective-permute-done | bytes 1474592 | tf_op jit(solution)/shard_map/ppermute | solution.py:323
  360.7 43.9 %attention_backward.1.grad_ref = bf16[729,3456]{1,0:T(8,128)(2,1)} custom-call(bf16[729,3456]{1,0:T(8,128)(2,1)} %add_convert_fusion.qkv_ref, bf16[729,1152]{1,0:T(8,128)(2,1)} %get-tuple-element.121.go_ref, f32[16,1,768]{2,1,0:T(1,128)} %get-tuple-element.122.lse_ref), custom_call_target="tpu_custom_call" | custom-call | flops 1000000 | bytes 1000000 | tf_op jit(solution)/shard_map/attention_backward/pallas_call | solution.py:107
  415.5 25.0 %qkv_backward.1 = (bf16[1152,3456]{1,0:T(8,128)(2,1)}, f32[1,3456]{1,0:T(1,128)}, f32[8,1152]{1,0:T(8,128)}, f32[729,1152]{1,0:T(8,128)}) custom-call(bf16[729,3456]{1,0:T(8,128)(2,1)} %attention_backward.1.grad_ref, bf16[729,1152]{1,0:T(8,128)(2,1)} %copy-done.5, bf16[1152,3456]{1,0:T(8,128)(2,1)} %bitcast.353, ...), custom_call_target="tpu_custom_call" | custom-call | flops 1000000 | bytes 1000000 | tf_op jit(solution)/shard_map/qkv_backward/pallas_call | solution.py:254
  479.9 19.2 %collective-permute-done.31 = bf16[4,2,5,8,1664]{4,3,2,1,0:T(8,128)(2,1)S(1)} collective-permute-done((bf16[4,2,5,8,1664]{4,3,2,1,0:T(8,128)(2,1)S(1)}, bf16[4,2,5,8,1664]{4,3,2,1,0:T(8,128)(2,1)S(1)}, u32[]{:S(2)}, u32[]{:S(2)}) %collective-permute-start.31) | collective-permute-done | bytes 1064992 | tf_op jit(solution)/shard_map/ppermute | solution.py:323
  510.0 6.8 %collective-permute-done.37 = bf16[5,8,5504]{2,1,0:T(8,128)(2,1)S(1)} collective-permute-done((bf16[5,8,5504]{2,1,0:T(8,128)(2,1)S(1)}, bf16[5,8,5504]{2,1,0:T(8,128)(2,1)S(1)}, u32[]{:S(2)}, u32[]{:S(2)}) %collective-permute-start.37) | collective-permute-done | bytes 440352 | tf_op jit(solution)/shard_map/ppermute | solution.py:323
  516.8 12.4 %collective-permute-done.36 = bf16[5,8,5504]{2,1,0:T(8,128)(2,1)S(1)} collective-permute-done((bf16[5,8,5504]{2,1,0:T(8,128)(2,1)S(1)}, bf16[5,8,5504]{2,1,0:T(8,128)(2,1)S(1)}, u32[]{:S(2)}, u32[]{:S(2)}) %collective-permute-start.36) | collective-permute-done | bytes 440352 | tf_op jit(solution)/shard_map/ppermute | solution.py:323
  550.5 5.2 collective-permute-done.39
  555.7 9.8 %collective-permute-done.40 = bf16[5,8,3584]{2,1,0:T(8,128)(2,1)} collective-permute-done((bf16[5,8,3584]{2,1,0:T(8,128)(2,1)}, bf16[5,8,3584]{2,1,0:T(8,128)(2,1)}, u32[]{:S(2)}, u32[]{:S(2)}) %collective-permute-start.40) | collective-permute-done | bytes 286752 | tf_op jit(solution)/shard_map/ppermute | solution.py:323
  565.5 7.7 %collective-permute-done.41 = bf16[5,8,3584]{2,1,0:T(8,128)(2,1)} collective-permute-done((bf16[5,8,3584]{2,1,0:T(8,128)(2,1)}, bf16[5,8,3584]{2,1,0:T(8,128)(2,1)}, u32[]{:S(2)}, u32[]{:S(2)}) %collective-permute-start.41) | collective-permute-done | bytes 286752 | tf_op jit(solution)/shard_map/ppermute | solution.py:323
  (406 shorter events, 183.2 us)
Async XLA Ops:
  7.2 208.7 %all-gather.2.cloned.1.call-start = ((), (), s32[]{:S(2)}) async-start(), calls=%async_computation.1 | async-start | bytes 20072448 | tf_op jit(solution)/shard_map/all_gather | solution.py:698
  27.5 504.8 %reduce-scatter.4.cloned.1.call-start = ((), (), s32[]{:S(2)}) async-start(), calls=%async_computation.2 | async-start | bytes 10340352
  35.3 33.9 %collective-permute-start.2 = (bf16[40,3584]{1,0:T(8,128)(2,1)S(1)}, bf16[40,3584]{1,0:T(8,128)(2,1)S(1)}, u32[]{:S(2)}, u32[]{:S(2)}) collective-permute-start(bf16[40,3584]{1,0:T(8,128)(2,1)S(1)} %pad_maximum_fusion.7), channel_id=1, source_target_pairs={{0,16},{1,17},{2,18},{3,19},{4,20},{5,21},{6,22},{7,23},{8,24},{9,... | collective-permute-start | bytes 860168 | tf_op jit(solution)/shard_map/ppermute | solution.py:323
  38.3 38.6 %collective-permute-start.3 = (bf16[40,3584]{1,0:T(8,128)(2,1)S(1)}, bf16[40,3584]{1,0:T(8,128)(2,1)S(1)}, u32[]{:S(2)}, u32[]{:S(2)}) collective-permute-start(bf16[40,3584]{1,0:T(8,128)(2,1)S(1)} %pad_maximum_fusion.7), channel_id=1, source_target_pairs={{0,24},{1,25},{2,26},{3,27},{4,28},{5,29},{6,30},{7,31},{8,16},{9,... | collective-permute-start | bytes 860168 | tf_op jit(solution)/shard_map/ppermute | solution.py:323
  77.0 22.7 %collective-permute-start.6 = (bf16[4,40,1792]{2,1,0:T(8,128)(2,1)S(1)}, bf16[4,40,1792]{2,1,0:T(8,128)(2,1)S(1)}, u32[]{:S(2)}, u32[]{:S(2)}) collective-permute-start(bf16[4,40,1792]{2,1,0:T(8,128)(2,1)S(1)} %pad_maximum_fusion.1), channel_id=1, source_target_pairs={{0,4},{1,5},{2,6},{3,7},{4,0},{5,1},{6,2},{7,3},{8,12},{9,13},{10,... | collective-permute-start | bytes 1720328 | tf_op jit(solution)/shard_map/ppermute | solution.py:323
  78.7 28.1 %collective-permute-start.4 = (bf16[4,40,1792]{2,1,0:T(8,128)(2,1)S(1)}, bf16[4,40,1792]{2,1,0:T(8,128)(2,1)S(1)}, u32[]{:S(2)}, u32[]{:S(2)}) collective-permute-start(bf16[4,40,1792]{2,1,0:T(8,128)(2,1)S(1)} %pad_maximum_fusion), channel_id=1, source_target_pairs={{0,2},{1,3},{2,0},{3,1},{4,6},{5,7},{6,4},{7,5},{8,10},{9,11},{10,... | collective-permute-start | bytes 1720328 | tf_op jit(solution)/shard_map/ppermute | solution.py:323
  99.8 34.6 %collective-permute-start.7 = (bf16[8,40,1792]{2,1,0:T(8,128)(2,1)S(1)}, bf16[8,40,1792]{2,1,0:T(8,128)(2,1)S(1)}, u32[]{:S(2)}, u32[]{:S(2)}) collective-permute-start(bf16[8,40,1792]{2,1,0:T(8,128)(2,1)S(1)} %constant_dynamic-update-slice_fusion.10), channel_id=1, source_target_pairs={{0,2},{1,3},{2,0},{3,1},{4,6},{5,7},{6,4},{7,5},{8,10},{9,11},{10,... | collective-permute-start | bytes 3440648 | tf_op jit(solution)/shard_map/ppermute | solution.py:323
  106.8 27.6 %collective-permute-start.5 = (bf16[8,40,1792]{2,1,0:T(8,128)(2,1)S(1)}, bf16[8,40,1792]{2,1,0:T(8,128)(2,1)}, u32[]{:S(2)}, u32[]{:S(2)}) collective-permute-start(bf16[8,40,1792]{2,1,0:T(8,128)(2,1)S(1)} %constant_dynamic-update-slice_fusion.5), channel_id=1, source_target_pairs={{0,4},{1,5},{2,6},{3,7},{4,0},{5,1},{6,2},{7,3},{8,12},{9,13},{10,... | collective-permute-start | bytes 3440648 | tf_op jit(solution)/shard_map/ppermute | solution.py:323
  138.8 32.1 %collective-permute-start.16 = (bf16[4,32,1152]{2,1,0:T(8,128)(2,1)}, bf16[4,32,1152]{2,1,0:T(8,128)(2,1)}, u32[]{:S(2)}, u32[]{:S(2)}) collective-permute-start(bf16[4,32,1152]{2,1,0:T(8,128)(2,1)} %pad_maximum_fusion.6), channel_id=1, source_target_pairs={{0,4},{1,5},{2,6},{3,7},{4,0},{5,1},{6,2},{7,3},{8,12},{9,13},{10,... | collective-permute-start | bytes 884744 | tf_op jit(solution)/shard_map/ppermute | solution.py:323
  144.8 26.1 %collective-permute-start.15 = (bf16[4,40,1152]{2,1,0:T(8,128)(2,1)}, bf16[4,40,1152]{2,1,0:T(8,128)(2,1)}, u32[]{:S(2)}, u32[]{:S(2)}) collective-permute-start(bf16[4,40,1152]{2,1,0:T(8,128)(2,1)} %pad_maximum_fusion.5), channel_id=1, source_target_pairs={{0,2},{1,3},{2,0},{3,1},{4,6},{5,7},{6,4},{7,5},{8,10},{9,11},{10,... | collective-permute-start | bytes 1105928 | tf_op jit(solution)/shard_map/ppermute | solution.py:323
  173.0 33.0 %collective-permute-start.17 = (bf16[8,40,1152]{2,1,0:T(8,128)(2,1)S(1)}, bf16[8,40,1152]{2,1,0:T(8,128)(2,1)S(1)}, u32[]{:S(2)}, u32[]{:S(2)}) collective-permute-start(bf16[8,40,1152]{2,1,0:T(8,128)(2,1)S(1)} %constant_dynamic-update-slice_fusion.15), channel_id=1, source_target_pairs={{0,4},{1,5},{2,6},{3,7},{4,0},{5,1},{6,2},{7,3},{8,12},{9,13},{10,... | collective-permute-start | bytes 2211848 | tf_op jit(solution)/shard_map/ppermute | solution.py:323
  176.6 29.5 %collective-permute-start.18 = (bf16[8,32,1152]{2,1,0:T(8,128)(2,1)S(1)}, bf16[8,32,1152]{2,1,0:T(8,128)(2,1)}, u32[]{:S(2)}, u32[]{:S(2)}) collective-permute-start(bf16[8,32,1152]{2,1,0:T(8,128)(2,1)S(1)} %constant_dynamic-update-slice_fusion.17), channel_id=1, source_target_pairs={{0,2},{1,3},{2,0},{3,1},{4,6},{5,7},{6,4},{7,5},{8,10},{9,11},{10,... | collective-permute-start | bytes 1769480 | tf_op jit(solution)/shard_map/ppermute | solution.py:323
  357.1 49.8 %collective-permute-start.25 = (bf16[4,2,5,8,2816]{4,3,2,1,0:T(8,128)(2,1)}, bf16[4,2,5,8,2816]{4,3,2,1,0:T(8,128)(2,1)}, u32[]{:S(2)}, u32[]{:S(2)}) collective-permute-start(bf16[4,2,5,8,2816]{4,3,2,1,0:T(8,128)(2,1)} %fusion.1), channel_id=1, source_target_pairs={{0,4},{1,5},{2,6},{3,7},{4,0},{5,1},{6,2},{7,3},{8,12},{9,13},{10,... | collective-permute-start | bytes 5406728 | tf_op jit(solution)/shard_map/ppermute | solution.py:323
  359.0 47.9 %collective-permute-start.26 = (bf16[4,2,5,8,2688]{4,3,2,1,0:T(8,128)(2,1)}, bf16[4,2,5,8,2688]{4,3,2,1,0:T(8,128)(2,1)}, u32[]{:S(2)}, u32[]{:S(2)}) collective-permute-start(bf16[4,2,5,8,2688]{4,3,2,1,0:T(8,128)(2,1)} %add_convert_fusion.2), channel_id=1, source_target_pairs={{0,2},{1,3},{2,0},{3,1},{4,6},{5,7},{6,4},{7,5},{8,10},{9,11},{10,... | collective-permute-start | bytes 5160968 | tf_op jit(solution)/shard_map/ppermute | solution.py:323
  409.1 31.5 %collective-permute-start.27 = (bf16[4,5,8,2816]{3,2,1,0:T(8,128)(2,1)S(1)}, bf16[4,5,8,2816]{3,2,1,0:T(8,128)(2,1)S(1)}, u32[]{:S(2)}, u32[]{:S(2)}) collective-permute-start(bf16[4,5,8,2816]{3,2,1,0:T(8,128)(2,1)S(1)} %fusion.2), channel_id=1, source_target_pairs={{0,2},{1,3},{2,0},{3,1},{4,6},{5,7},{6,4},{7,5},{8,10},{9,11},{10,... | collective-permute-start | bytes 2703368 | tf_op jit(solution)/shard_map/ppermute | solution.py:323
  412.1 28.4 %collective-permute-start.28 = (bf16[4,5,8,2688]{3,2,1,0:T(8,128)(2,1)S(1)}, bf16[4,5,8,2688]{3,2,1,0:T(8,128)(2,1)S(1)}, u32[]{:S(2)}, u32[]{:S(2)}) collective-permute-start(bf16[4,5,8,2688]{3,2,1,0:T(8,128)(2,1)S(1)} %fusion.3), channel_id=1, source_target_pairs={{0,4},{1,5},{2,6},{3,7},{4,0},{5,1},{6,2},{7,3},{8,12},{9,13},{10,... | collective-permute-start | bytes 2580488 | tf_op jit(solution)/shard_map/ppermute | solution.py:323
  467.5 42.5 %collective-permute-start.38 = (bf16[5,8,5504]{2,1,0:T(8,128)(2,1)S(1)}, bf16[5,8,5504]{2,1,0:T(8,128)(2,1)S(1)}, u32[]{:S(2)}, u32[]{:S(2)}) collective-permute-start(bf16[5,8,5504]{2,1,0:T(8,128)(2,1)S(1)} %pad_maximum_fusion.4), channel_id=1, source_target_pairs={{0,24},{1,25},{2,26},{3,27},{4,28},{5,29},{6,30},{7,31},{8,16},{9,... | collective-permute-start | bytes 1320968 | tf_op jit(solution)/shard_map/ppermute | solution.py:323
  471.0 28.1 %collective-permute-start.32 = (bf16[4,2,5,8,1792]{4,3,2,1,0:T(8,128)(2,1)S(1)}, bf16[4,2,5,8,1792]{4,3,2,1,0:T(8,128)(2,1)S(1)}, u32[]{:S(2)}, u32[]{:S(2)}) collective-permute-start(bf16[4,2,5,8,1792]{4,3,2,1,0:T(8,128)(2,1)S(1)} %fusion.4), channel_id=1, source_target_pairs={{0,2},{1,3},{2,0},{3,1},{4,6},{5,7},{6,4},{7,5},{8,10},{9,11},{10,... | collective-permute-start | bytes 3440648 | tf_op jit(solution)/shard_map/ppermute | solution.py:323
  474.0 25.0 %collective-permute-start.31 = (bf16[4,2,5,8,1664]{4,3,2,1,0:T(8,128)(2,1)S(1)}, bf16[4,2,5,8,1664]{4,3,2,1,0:T(8,128)(2,1)S(1)}, u32[]{:S(2)}, u32[]{:S(2)}) collective-permute-start(bf16[4,2,5,8,1664]{4,3,2,1,0:T(8,128)(2,1)S(1)} %fusion.7), channel_id=1, source_target_pairs={{0,4},{1,5},{2,6},{3,7},{4,0},{5,1},{6,2},{7,3},{8,12},{9,13},{10,... | collective-permute-start | bytes 3194888 | tf_op jit(solution)/shard_map/ppermute | solution.py:323
  475.0 41.8 %collective-permute-start.37 = (bf16[5,8,5504]{2,1,0:T(8,128)(2,1)S(1)}, bf16[5,8,5504]{2,1,0:T(8,128)(2,1)S(1)}, u32[]{:S(2)}, u32[]{:S(2)}) collective-permute-start(bf16[5,8,5504]{2,1,0:T(8,128)(2,1)S(1)} %pad_maximum_fusion.3), channel_id=1, source_target_pairs={{0,16},{1,17},{2,18},{3,19},{4,20},{5,21},{6,22},{7,23},{8,24},{9,... | collective-permute-start | bytes 1320968 | tf_op jit(solution)/shard_map/ppermute | solution.py:323
  500.5 28.7 %collective-permute-start.35 = (bf16[4,5,8,1792]{3,2,1,0:T(8,128)(2,1)S(1)}, bf16[4,5,8,1792]{3,2,1,0:T(8,128)(2,1)S(1)}, u32[]{:S(2)}, u32[]{:S(2)}) collective-permute-start(bf16[4,5,8,1792]{3,2,1,0:T(8,128)(2,1)S(1)} %fusion.5), channel_id=1, source_target_pairs={{0,4},{1,5},{2,6},{3,7},{4,0},{5,1},{6,2},{7,3},{8,12},{9,13},{10,... | collective-permute-start | bytes 1720328 | tf_op jit(solution)/shard_map/ppermute | solution.py:323
  501.9 27.3 %collective-permute-start.34 = (bf16[4,5,8,1792]{3,2,1,0:T(8,128)(2,1)S(1)}, bf16[4,5,8,1792]{3,2,1,0:T(8,128)(2,1)}, u32[]{:S(2)}, u32[]{:S(2)}) collective-permute-start(bf16[4,5,8,1792]{3,2,1,0:T(8,128)(2,1)S(1)} %fusion.6), channel_id=1, source_target_pairs={{0,2},{1,3},{2,0},{3,1},{4,6},{5,7},{6,4},{7,5},{8,10},{9,11},{10,... | collective-permute-start | bytes 1720328 | tf_op jit(solution)/shard_map/ppermute | solution.py:323
  503.6 25.6 %collective-permute-start.36 = (bf16[5,8,5504]{2,1,0:T(8,128)(2,1)S(1)}, bf16[5,8,5504]{2,1,0:T(8,128)(2,1)S(1)}, u32[]{:S(2)}, u32[]{:S(2)}) collective-permute-start(bf16[5,8,5504]{2,1,0:T(8,128)(2,1)S(1)} %pad_maximum_fusion.2), channel_id=1, source_target_pairs={{0,8},{1,9},{2,10},{3,11},{4,12},{5,13},{6,14},{7,15},{8,0},{9,1},... | collective-permute-start | bytes 1320968 | tf_op jit(solution)/shard_map/ppermute | solution.py:323
  546.5 26.7 %collective-permute-start.41 = (bf16[5,8,3584]{2,1,0:T(8,128)(2,1)}, bf16[5,8,3584]{2,1,0:T(8,128)(2,1)}, u32[]{:S(2)}, u32[]{:S(2)}) collective-permute-start(bf16[5,8,3584]{2,1,0:T(8,128)(2,1)} %pad_maximum_fusion.10), channel_id=1, source_target_pairs={{0,24},{1,25},{2,26},{3,27},{4,28},{5,29},{6,30},{7,31},{8,16},{9,... | collective-permute-start | bytes 860168 | tf_op jit(solution)/shard_map/ppermute | solution.py:323
  (85 other events, 719.6 us)
Sparse Core Ops, SparseCore 0:
  27.6 175.1 all-gather.1
  359.7 167.1 reduce-scatter.3

commit v7 on v6

--- a/solution.py
+++ b/solution.py
@@ -121,9 +121,21 @@
 GELU_B = 0.044715
 
 
-def mlp_kernel(normed_ref, grad_ref, up_ref, bias_ref, down_ref, xhat_ref, inverse_ref, gain_ref,
-               grad_out_ref, mixed_ref, output_ref, out_ref, up_grad_ref, bias_grad_ref,
-               down_grad_ref, sums_ref, resid_grad_ref, output_grad_ref, mixed_grad_ref,
+PAIR_ROWS = D // HEADS
+BLOCK_ROWS = 40
+
+
+def share_rows(core, value, keep_ref, send_ref):
+    for chip in range(value.shape[0] // PAIR_ROWS):
+        first = value[chip * PAIR_ROWS : chip * PAIR_ROWS + BLOCK_ROWS]
+        last = value[(chip + 1) * PAIR_ROWS - BLOCK_ROWS : (chip + 1) * PAIR_ROWS]
+        keep_ref[chip] = jnp.where(core == 0, first, last).astype(jnp.bfloat16)
+        send_ref[chip] = jnp.where(core == 0, last, first).astype(jnp.bfloat16)
+
+
+def mlp_kernel(coords, normed_ref, grad_ref, up_ref, bias_ref, down_ref, xhat_ref, inverse_ref, gain_ref,
+               grad_out_ref, mixed_ref, output_ref, out_ref, up_keep_ref, up_send_ref, bias_grad_ref,
+               down_grad_ref, sums_ref, resid_grad_ref, output_keep_ref, output_send_ref, mixed_grad_ref,
                normed, normed_t, grad, out, back):
     step = pl.program_id(0)
     tokens = normed_ref.shape[0]
@@ -148,7 +160,7 @@
     out[...] += nn(hidden, down_ref[...])
     back[...] += nt(grad_pre, up_ref[...])
     down_grad_ref[...] = nn(hidden.T, grad[...]).astype(jnp.bfloat16)
-    up_grad_ref[...] = nn(normed_t[...], grad_pre).astype(jnp.bfloat16)
+    share_rows(coords[0], nn(normed_t[...], grad_pre), up_keep_ref, up_send_ref)
     bias_grad_ref[...] = jnp.sum(grad_pre.astype(jnp.float32), axis=0, keepdims=True)
 
     @pl.when(step == pl.num_programs(0) - 1)
@@ -169,14 +181,14 @@
         mixed_grad_ref[...] = nt(low, output_ref[...]).astype(jnp.bfloat16)[0:tokens]
         normed[0:tokens] = mixed_ref[...]
         normed_t[...] = normed[...].T
-        output_grad_ref[...] = nn(normed_t[...], low).astype(jnp.bfloat16)
+        share_rows(coords[0], nn(normed_t[...], low), output_keep_ref, output_send_ref)
 
 
 def whole_block(shape):
     return pl.BlockSpec(shape, lambda i: (0, 0), pipeline_mode=pl.Buffered(1))
 
 
-def mlp(normed, grad, up, bias, down, xhat, inverse, gain, grad_out, mixed, output):
+def mlp(coords, normed, grad, up, bias, down, xhat, inverse, gain, grad_out, mixed, output):
     tokens, hidden = normed.shape[0], up.shape[1]
     rows = -(-tokens // 16) * 16
     tile = 256
@@ -185,20 +197,28 @@
     line = pl.BlockSpec((1, tile), lambda i: (0, i))
     band = pl.BlockSpec((tile, D), lambda i: (i, 0))
     square = whole_block((D, D))
+    shares = (D // PAIR_ROWS, BLOCK_ROWS)
+    part = pl.BlockSpec(shares + (tile,), lambda i: (0, 0, i))
+    full_part = pl.BlockSpec(
+        shares + (D,), lambda i: (0, 0, 0), pipeline_mode=pl.Buffered(1)
+    )
     return pl.pallas_call(
         mlp_kernel,
         grid=(hidden // tile,),
-        in_specs=[full, full, columns, line, band, full, whole_block((tokens, 1)),
+        in_specs=[pl.BlockSpec(memory_space=pltpu.SMEM), full, full, columns, line, band, full, whole_block((tokens, 1)),
                   whole_block((1, D)), full, full, square],
-        out_specs=[full, columns, line, band, whole_block((8, D)), full, square, full],
+        out_specs=[full, part, part, line, band, whole_block((8, D)), full, full_part, full_part,
+                   full],
         out_shape=[
             jax.ShapeDtypeStruct((tokens, D), jnp.float32),
-            jax.ShapeDtypeStruct((D, hidden), jnp.bfloat16),
+            jax.ShapeDtypeStruct(shares + (hidden,), jnp.bfloat16),
+            jax.ShapeDtypeStruct(shares + (hidden,), jnp.bfloat16),
             jax.ShapeDtypeStruct((1, hidden), jnp.float32),
             jax.ShapeDtypeStruct((hidden, D), jnp.bfloat16),
             jax.ShapeDtypeStruct((8, D), jnp.float32),
             jax.ShapeDtypeStruct((tokens, D), jnp.float32),
-            jax.ShapeDtypeStruct((D, D), jnp.bfloat16),
+            jax.ShapeDtypeStruct(shares + (D,), jnp.bfloat16),
+            jax.ShapeDtypeStruct(shares + (D,), jnp.bfloat16),
             jax.ShapeDtypeStruct((tokens, D), jnp.bfloat16),
         ],
         scratch_shapes=[
@@ -213,11 +233,11 @@
         ),
         cost_estimate=pl.CostEstimate(flops=1000000, bytes_accessed=1000000, transcendentals=0),
         name="mlp_forward_backward",
-    )(normed, grad, up, bias, down, xhat, inverse, gain, grad_out, mixed, output)
-
-
-def qkv_back_kernel(grad_ref, normed_ref, weight_ref, xhat_ref, inverse_ref, gain_ref, resid_ref,
-                    weight_grad_ref, bias_grad_ref, sums_ref, tokens_ref, grad, normed_t, total):
+    )(coords, normed, grad, up, bias, down, xhat, inverse, gain, grad_out, mixed, output)
+
+
+def qkv_back_kernel(coords, grad_ref, normed_ref, weight_ref, xhat_ref, inverse_ref, gain_ref, resid_ref,
+                    keep_ref, send_ref, bias_grad_ref, sums_ref, tokens_ref, grad, normed_t, total):
     step = pl.program_id(0)
     tokens = normed_ref.shape[0]
 
@@ -230,7 +250,7 @@
         total[...] = jnp.zeros_like(total)
 
     grad[0:tokens] = grad_ref[...]
-    weight_grad_ref[...] = nn(normed_t[...], grad[...]).astype(jnp.bfloat16)
+    share_rows(coords[0], nn(normed_t[...], grad[...]), keep_ref, send_ref)
     bias_grad_ref[...] = jnp.sum(grad[...].astype(jnp.float32), axis=0, keepdims=True)
     total[...] += nt(grad[...], weight_ref[...])
 
@@ -246,15 +266,18 @@
         tokens_ref[...] = resid_ref[...] + inverse_ref[...] * (scaled - first - xhat * second)
 
 
-def qkv_back(grad, normed, weight, xhat, inverse, gain, resid):
+def qkv_back(coords, grad, normed, weight, xhat, inverse, gain, resid):
     tokens = normed.shape[0]
     rows = -(-tokens // 16) * 16
     whole = lambda shape: pl.BlockSpec(shape, lambda i: (0, 0), pipeline_mode=pl.Buffered(1))
     part = lambda shape: pl.BlockSpec(shape, lambda i: (0, i))
+    shares = (D // PAIR_ROWS, BLOCK_ROWS)
+    share = pl.BlockSpec(shares + (D,), lambda i: (0, 0, i))
     return pl.pallas_call(
         qkv_back_kernel,
         grid=(3,),
         in_specs=[
+            pl.BlockSpec(memory_space=pltpu.SMEM),
             part((tokens, D)),
             whole((tokens, D)),
             part((D, D)),
@@ -263,9 +286,10 @@
             whole((1, D)),
             whole((tokens, D)),
         ],
-        out_specs=[part((D, D)), part((1, D)), whole((8, D)), whole((tokens, D))],
+        out_specs=[share, share, part((1, D)), whole((8, D)), whole((tokens, D))],
         out_shape=[
-            jax.ShapeDtypeStruct((D, 3 * D), jnp.bfloat16),
+            jax.ShapeDtypeStruct(shares + (3 * D,), jnp.bfloat16),
+            jax.ShapeDtypeStruct(shares + (3 * D,), jnp.bfloat16),
             jax.ShapeDtypeStruct((1, 3 * D), jnp.float32),
             jax.ShapeDtypeStruct((8, D), jnp.float32),
             jax.ShapeDtypeStruct((tokens, D), jnp.float32),
@@ -280,7 +304,7 @@
         ),
         cost_estimate=pl.CostEstimate(flops=1000000, bytes_accessed=1000000, transcendentals=0),
         name="qkv_backward",
-    )(grad, normed, weight, xhat, inverse, gain, resid)
+    )(coords, grad, normed, weight, xhat, inverse, gain, resid)
 
 
 FF = 4304
@@ -288,7 +312,6 @@
 FF_GROUP = FF // GROUPS
 FF_ROWS = 272
 FF_PAD = GROUPS * FF_ROWS
-PAIR_ROWS = D // GROUPS
 HALF_DOWN = FF_ROWS // 2
 OWN_ROWS = PAIR_ROWS // 2
 TILE = 8
@@ -301,7 +324,7 @@
 DOWN_CUT = 40
 DOWN_FIRST = 64
 REST_ROWS = UP_PIECES * BLOCK_TILES * TILE + BLOCK_TILES * TILE + DOWN_FIRST
-VECTORS = (0, 1, 3, 6, 8, 9, 10, 12, 14)
+VECTORS = (0, 1, 3, 6, 8, 9, 10, 14, 12)
 bf16 = jnp.bfloat16
 f32 = jnp.float32
 
@@ -527,52 +550,53 @@
 
 
 class Reduction:
-    def __init__(self, matrices, streams, coords):
-        self.matrices = [m.reshape(4, 2, 2, PAIR_TILES, TILE, -1) for m in matrices]
+    def __init__(self, keeps, streams, coords):
+        self.keeps = [k.reshape(4, 2, 2, BLOCK_TILES, TILE, -1) for k in keeps]
         self.streams = streams
         self.coords = coords
 
-    def part(self, arrays, stream, plane, tile):
-        sizes = tuple(None if p is None else 1 for p in plane) + (BLOCK_TILES, None)
+    def part(self, arrays, stream, plane):
+        sizes = tuple(None if p is None else 1 for p in plane) + (None, None)
         pieces = []
         for number, first, last in self.streams[stream]:
-            starts = tuple(plane) + (tile, None, first)
+            starts = tuple(plane) + (None, None, first)
             pieces.append(window(arrays[number], starts, sizes + (last - first,)))
         return pieces[0] if len(pieces) == 1 else jnp.concatenate(pieces, axis=-1)
 
     def terms(self, stream, plane):
-        tile = self.coords[0] * (PAIR_TILES - BLOCK_TILES)
-        own = self.part(self.matrices, stream, plane, tile)
-        return [own, self.part(self.other, stream, plane, 0)]
-
-    def core_step(self):
-        tile = (1 - self.coords[0]) * (PAIR_TILES - BLOCK_TILES)
-        starts, sizes = (None, None, None, tile), (None, None, None, BLOCK_TILES)
-        return [swap(window(m, starts, sizes), 1) for m in self.matrices]
-
-    def far_step(self, other, streams=(0, 1), pieces=slice(None)):
+        return [self.part(self.keeps, stream, plane), self.part(self.other, stream, plane)]
+
+    def core_step(self, sends):
+        return [swap(send.reshape(4, 2, 2, BLOCK_TILES, TILE, -1), 1) for send in sends]
+
+    def far_sends(self, other, streams=(0, 1), pieces=slice(None)):
         core, x, y, z = self.coords
         self.other = other
-        got = []
+        sends = []
         every = self.streams
         for stream in streams:
             plane = (None, None, 1 - x) if stream else (None, 1 - y, None)
             self.streams = {stream: every[stream][pieces]}
-            send = total_of(self.terms(stream, plane)).astype(bf16)
-            got.append(swap(send, 2 if stream else 4))
+            sends.append(total_of(self.terms(stream, plane)).astype(bf16))
         self.streams = every
-        return got
-
-    def near_step(self, far):
+        return sends
+
+    def far_swap(self, sends):
+        return [swap(send, 2 if stream else 4) for stream, send in enumerate(sends)]
+
+    def near_sends(self, far):
         core, x, y, z = self.coords
         self.far = far
-        got = []
+        sends = []
         for stream in range(2):
             plane = (None, 1 - y, x) if stream else (None, y, 1 - x)
             after = (None, 1 - y) if stream else (None, 1 - x)
             terms = self.terms(stream, plane) + [window(far[stream], after, (None, 1))]
-            got.append(swap(total_of(terms).astype(bf16), 4 if stream else 2))
-        return got
+            sends.append(total_of(terms).astype(bf16))
+        return sends
+
+    def near_swap(self, sends):
+        return [swap(send, 4 if stream else 2) for stream, send in enumerate(sends)]
 
     def at(self, plane):
         core, x, y, z = self.coords
@@ -586,10 +610,13 @@
             pieces.append(total_of(terms))
         return jnp.concatenate(pieces, axis=-1)
 
-    def z_step(self, near):
+    def z_sends(self, near):
         z = self.coords[3]
         self.near = near
-        return [swap(self.at(z ^ step).astype(bf16), 8 * step) for step in (1, 2, 3)]
+        return [self.at(z ^ step).astype(bf16) for step in (1, 2, 3)]
+
+    def z_swap(self, sends):
+        return [swap(send, 8 * step) for step, send in zip((1, 2, 3), sends)]
 
     def finish(self, arrived):
         core, x, y, z = self.coords
@@ -598,6 +625,11 @@
         return lax.dynamic_slice_in_dim(
             total, core * (BLOCK_TILES * TILE - OWN_ROWS), OWN_ROWS, 0
         )
+
+
+def join_rows(keep, send):
+    whole = jnp.concatenate([keep, send[:, 2 * BLOCK_ROWS - PAIR_ROWS :]], axis=1)
+    return whole.reshape(D, -1)
 
 
 def total_of(terms):
@@ -651,12 +683,25 @@
 
 
 def name_vectors(whole, widths):
-    found = {}
-    position = 0
-    for i in VECTORS:
-        found[i] = whole[:, position : position + widths[i]].reshape(-1).astype(f32)
-        position += widths[i]
+    count = len(VECTORS) - 1
+    width = widths[VECTORS[0]]
+    pieces = whole[:, : count * width].reshape(-1, count, width)
+    pieces = pieces.transpose(1, 0, 2).reshape(count, -1).astype(f32)
+    found = {i: pieces[position] for position, i in enumerate(VECTORS[:-1])}
+    last = widths[VECTORS[-1]]
+    found[VECTORS[-1]] = whole[:, count * width : count * width + last].reshape(-1).astype(f32)
     return found
+
+
+def pack_vectors(grads, widths, devices):
+    count = len(VECTORS) - 1
+    width = widths[VECTORS[0]]
+    rows = jnp.stack([grads[i] for i in VECTORS[:-1]])
+    rows = jnp.pad(rows, ((0, 0), (0, width * devices - rows.shape[1])))
+    rows = rows.reshape(count, devices, width).transpose(1, 0, 2).reshape(devices, -1)
+    last = grads[VECTORS[-1]]
+    last = jnp.pad(last, (0, widths[VECTORS[-1]] * devices - last.shape[0]))
+    return jnp.concatenate([rows, last.reshape(devices, -1)], axis=1)
 
 
 def gather_plain(narrow, widths):
@@ -692,8 +737,8 @@
     grad_branch = grad_out.astype(bf16)
     grads = {14: jnp.sum(grad_branch.astype(f32), axis=0)}
     xhat_one, inverse_one = normalize(tokens)
+    where = jnp.stack(coords if staged else (jnp.int32(0),) * 4).astype(jnp.int32)
     if staged:
-        where = jnp.stack(coords).astype(jnp.int32)
         sq, rest, down = fetch_pairs(narrow, core)
         rest = lax.all_gather(rest, "fsdp", axis=0, tiled=True)
         sq = gather_z(sq)
@@ -730,7 +775,19 @@
     resid = tokens + product(mixed, weight_o) + bias_o
     xhat_two, inverse_two = normalize(resid)
     normed_two = (xhat_two * gain_two + shift_two).astype(bf16)
-    branch, up_grad, up_bias_grad, down_grad, sums_two, grad_resid, o_grad, grad_mixed = mlp(
+    (
+        branch,
+        up_keep,
+        up_send,
+        up_bias_grad,
+        down_grad,
+        sums_two,
+        grad_resid,
+        o_keep,
+        o_send,
+        grad_mixed,
+    ) = mlp(
+        where,
         normed_two,
         grad_branch,
         weight_up,
@@ -750,66 +807,70 @@
         down_sum = lax.psum_scatter(down_grad, "fsdp", scatter_dimension=0, tiled=True)
     if staged:
         outer = Reduction(
-            (up_grad, o_grad), (((0, 0, UP_CUT),), ((0, UP_CUT, FF_PAD), (1, 0, D))), coords
+            (up_keep, o_keep), (((0, 0, UP_CUT),), ((0, UP_CUT, FF_PAD), (1, 0, D))), coords
         )
-        outer_other = outer.core_step()
-    if staged:
+        outer_other = outer.core_step((up_send, o_send))
         grad_mixed, outer_other = tie(grad_mixed, outer_other)
-        outer_far = outer.far_step(outer_other)
+        outer_far = outer.far_swap(outer.far_sends(outer_other))
     grad_qkv = attn_bwd(qkv, grad_mixed, lse, 2)
     if staged:
         grad_qkv, outer_far = tie(grad_qkv, outer_far)
-        outer_near = outer.near_step(outer_far)
-    qkv_grad, qkv_bias_grad, norm_sums, tokens_grad = qkv_back(
-        grad_qkv, normed, weight_qkv, xhat_one, inverse_one, gain_one.reshape(1, D), grad_resid
+        outer_near = outer.near_sends(outer_far)
+        grad_qkv, outer_near = tie(grad_qkv, outer_near)
+        outer_near = outer.near_swap(outer_near)
+    qkv_keep, qkv_send, qkv_bias_grad, norm_sums, tokens_grad = qkv_back(
+        where,
+        grad_qkv,
+        normed,
+        weight_qkv,
+        xhat_one,
+        inverse_one,
+        gain_one.reshape(1, D),
+        grad_resid,
     )
+    if staged:
+        qkv_keep, qkv_send, norm_sums, qkv_bias_grad, outer_near = tie(
+            qkv_keep, qkv_send, norm_sums, qkv_bias_grad, outer_near
+        )
+        outer_z = outer.z_sends(outer_near)
+        qkv_other = outer.core_step((qkv_send,))[0]
     grads[3], grads[6] = qkv_bias_grad[0, :D], qkv_bias_grad[0, 2 * D :]
     grads[0], grads[1] = norm_sums[0], norm_sums[1]
-    if staged:
-        qkv_grad, outer_near = tie(qkv_grad, outer_near)
-        inner = Reduction((qkv_grad,), (((0, 0, QKV_CUT - EXTRA),),) * 2, coords)
-        inner_other = inner.core_step()
-        inner_other, outer_near, qkv_grad, norm_sums, qkv_bias_grad = tie(
-            inner_other, outer_near, qkv_grad, norm_sums, qkv_bias_grad
-        )
-        inner = Reduction(
-            (qkv_grad, qkv_grad),
-            (((0, 0, QKV_CUT - EXTRA), (1, 0, EXTRA)), ((0, QKV_CUT - EXTRA, 3 * D),)),
-            coords,
-        )
-        inner_far = inner.far_step(inner_other, (0, 1), slice(0, 1))
-        outer_z = outer.z_step(outer_near)
     grads[12] = trim_hidden(up_bias_grad.reshape(1, FF_PAD)).reshape(FF)
 
-    rows = []
-    for i in VECTORS:
-        row = grads[i]
-        row = jnp.pad(row, (0, widths[i] * devices - row.shape[0]))
-        rows.append(row.reshape(devices, widths[i]))
-    rows = jnp.concatenate(rows, axis=1)
+    rows = pack_vectors(grads, widths, devices)
     owned = [None] * 15
     if staged:
         rows = jnp.pad(rows, ((0, 0), (0, OWN_ROWS * EXTRA - rows.shape[1])))
-        rows = rows.reshape(D, EXTRA).astype(bf16)
-        inner.matrices[1] = rows.reshape(4, 2, 2, PAIR_TILES, TILE, EXTRA)
-        rows_other = Reduction((rows,), None, coords).core_step()
-        inner.other = inner_other + rows_other
-        rows_far = inner.far_step(inner.other, (0,), slice(1, 2))
-        inner_far, rows_far = tie(inner_far, rows_far)
-        inner_far = [jnp.concatenate([inner_far[0], rows_far[0]], axis=-1), inner_far[1]]
-        inner_near = inner.near_step(inner_far)
-        inner_near, outer_z = tie(inner_near, outer_z)
-        inner_z = inner.z_step(inner_near)
-        inner_near, down_sum = tie(inner_near, down_sum)
+        rows = rows.reshape(GROUPS, PAIR_ROWS, EXTRA).astype(bf16)
+        top, bottom = rows[:, :BLOCK_ROWS], rows[:, PAIR_ROWS - BLOCK_ROWS :]
+        rows_keep = jnp.where(core == 0, top, bottom)
+        rows_send = jnp.where(core == 0, bottom, top)
+        rows_other = outer.core_step((rows_send,))[0]
+        cut = QKV_CUT - EXTRA
+        inner = Reduction(
+            (qkv_keep, rows_keep), (((0, 0, cut), (1, 0, EXTRA)), ((0, cut, 3 * D),)), coords
+        )
+        qkv_other, rows_other, outer_z = tie(qkv_other, rows_other, outer_z)
+        inner_far = inner.far_swap(inner.far_sends((qkv_other, rows_other)))
+        outer_z = outer.z_swap(outer_z)
+        inner_far, layer_out = tie(inner_far, layer_out)
+        inner_near = inner.near_swap(inner.near_sends(inner_far))
+        outer_sum = outer.finish(outer_z)
+        owned[11] = trim_hidden(outer_sum[:, :FF_PAD]).reshape(-1)
+        owned[7] = outer_sum[:, FF_PAD:].reshape(-1)
+        inner_near, down_sum, owned[11], owned[7] = tie(
+            inner_near, down_sum, owned[11], owned[7]
+        )
+        inner_z = inner.z_sends(inner_near)
+        inner_z, down_sum = tie(inner_z, down_sum)
+        inner_z = inner.z_swap(inner_z)
 
         flat = down_sum.astype(f32).reshape(-1)
         size = widths[13]
         lead = flat.shape[0] - size
         got = swap(down_sum.reshape(-1)[size:], 1).astype(f32)
         owned[13] = jnp.where(core == 0, flat[:size], jnp.concatenate([got, flat[: size - lead]]))
-        outer_sum = outer.finish(outer_z)
-        owned[11] = trim_hidden(outer_sum[:, :FF_PAD]).reshape(-1)
-        owned[7] = outer_sum[:, FF_PAD:].reshape(-1)
         inner_sum = inner.finish(inner_z)
         first = QKV_CUT - EXTRA
         owned[2] = inner_sum[:, :D].reshape(-1)
@@ -825,10 +886,11 @@
         fill = lambda value, i: jnp.pad(
             value.reshape(-1), (0, widths[i] * devices - value.size)
         )
+        qkv_grad = join_rows(qkv_keep, qkv_send)
         for position, i in enumerate((2, 4, 5)):
             owned[i] = scatter(fill(qkv_grad[:, position * D : (position + 1) * D], i))
-        owned[7] = scatter(fill(o_grad, 7))
-        owned[11] = scatter(fill(trim_hidden(up_grad), 11))
+        owned[7] = scatter(fill(join_rows(o_keep, o_send), 7))
+        owned[11] = scatter(fill(trim_hidden(join_rows(up_keep, up_send)), 11))
         owned[13] = scatter(fill(trim_hidden(down_grad.T).T, 13))
         small = scatter(rows)
     position = 0

time: 591 us -> 577 us (0.976)
  local copies, waits for them, and re-layouts: 89.8 us -> 78.1 us
  Pallas kernels: 211 us -> 204 us
  waiting for transfers between devices: 154 us -> 161 us
    dynamic_slice x4 -> x0, local copies, waits for them, and re-layouts: 11.5 us -> none  [window(): result = lax.dynamic_slice(value, starts, lengths)]
    pallas_call x2, Pallas kernels: 113 us -> 104 us  [the longest x1 78.9 us: mlp(): pl.pallas_call(mlp_kernel, grid=(hidden // tile,), in_specs=[pl.BlockSpec...]
    ppermute x43 -> x42, waiting for transfers between devices: 154 us -> 161 us  [swap(): return lax.ppermute(value, 'fsdp', [(i, i ^ mask) for i in range(devices)])]
    ppermute x43 -> x42, starting transfers between devices: 39.2 us -> 34.8 us  [swap(): return lax.ppermute(value, 'fsdp', [(i, i ^ mask) for i in range(devices)])]
    unnamed x141 -> x128, local copies, waits for them, and re-layouts: 14.1 us -> 12.9 us
    reshape x20 -> x24, local copies, waits for them, and re-layouts: 21.2 us -> 21.6 us  [window(): return result.reshape(kept)]
    convert_element_type x10 -> x9, other arithmetic: 15.2 us -> 15.5 us  [the longest x4 7.82 us: near_sends(): sends.append(total_of(terms).astype(bf16))]
  transfers between devices with their start and end apart: 45 -> 44, of which waited for: 18 -> 20; matrix products, arithmetic and copies ran while one was open for 19% -> 20% of each run, Pallas kernels for 18% -> 18%
where the time goes in v7:
time: 577 us; the launch traced here: 571 us
  Pallas kernels  204 us (35%)
  waiting for transfers between devices  161 us (28%)
  local copies, waits for them, and re-layouts  78.1 us (14%)
  other arithmetic  58.6 us (10%)
  starting transfers between devices  35.2 us (6%)
  matrix products  17.6 us (3%)
  between operations  16.4 us (3%)
    ppermute x42, waiting for transfers between devices, swap(): return lax.ppermute(value, 'fsdp', [(i, i ^ mask) for i in range(devices)])  161 us
    pallas_call x1, Pallas kernels, mlp(): pl.pallas_call(mlp_kernel, grid=(hidden // tile,), in_specs=[pl.BlockSpec...  78.9 us
    pallas_call x1, Pallas kernels, attn_bwd(): pl.pallas_call(functools.partial(bwd_kernel, tokens, krows, qrows, per),...  44.4 us
    ppermute x42, starting transfers between devices, swap(): return lax.ppermute(value, 'fsdp', [(i, i ^ mask) for i in range(devices)])  34.8 us
    pallas_call x1, Pallas kernels, attn_fwd(): pl.pallas_call(functools.partial(fwd_kernel, tokens, krows, qrows, per),...  28.9 us
    pallas_call x1, Pallas kernels, qkv_back(): pl.pallas_call(qkv_back_kernel, grid=(3,), in_specs=[pl.BlockSpec(memory_...  25.2 us
    reshape x24, local copies, waits for them, and re-layouts, window(): return result.reshape(kept)  21.6 us
    pallas_call x1, Pallas kernels, place_rest(): pl.pallas_call(place_rest_kernel, in_specs=[pl.BlockSpec(memory_space=plt...  19.4 us
  transfers between devices with their start and end apart: 44, of which 20 were waited for; matrix products, arithmetic and copies ran while one was open for 20% of the time, Pallas kernels for 18%

profile of v7, /device:TPU:8, one launch (start us, length us, event | category | flops | bytes accessed | tf_op | source)
XLA Modules:
  0.0 571.0 jit_solution(5003249466413065174)
XLA Ops:
  43.2 11.9 %collective-permute-done.1 = bf16[40,3584]{1,0:T(8,128)(2,1)S(1)} collective-permute-done((bf16[40,3584]{1,0:T(8,128)(2,1)S(1)}, bf16[40,3584]{1,0:T(8,128)(2,1)S(1)}, u32[]{:S(2)}, u32[]{:S(2)}) %collective-permute-start.1) | collective-permute-done | bytes 286752 | tf_op jit(solution)/shard_map/ppermute | solution.py:346
  55.0 14.0 %collective-permute-done.2 = bf16[40,3584]{1,0:T(8,128)(2,1)S(1)} collective-permute-done((bf16[40,3584]{1,0:T(8,128)(2,1)S(1)}, bf16[40,3584]{1,0:T(8,128)(2,1)S(1)}, u32[]{:S(2)}, u32[]{:S(2)}) %collective-permute-start.2) | collective-permute-done | bytes 286752 | tf_op jit(solution)/shard_map/ppermute | solution.py:346
  69.1 8.1 %collective-permute-done.3 = bf16[40,3584]{1,0:T(8,128)(2,1)S(1)} collective-permute-done((bf16[40,3584]{1,0:T(8,128)(2,1)S(1)}, bf16[40,3584]{1,0:T(8,128)(2,1)S(1)}, u32[]{:S(2)}, u32[]{:S(2)}) %collective-permute-start.3) | collective-permute-done | bytes 286752 | tf_op jit(solution)/shard_map/ppermute | solution.py:346
  80.6 19.4 %collective-permute-done.6 = bf16[4,40,1792]{2,1,0:T(8,128)(2,1)S(1)} collective-permute-done((bf16[4,40,1792]{2,1,0:T(8,128)(2,1)S(1)}, bf16[4,40,1792]{2,1,0:T(8,128)(2,1)S(1)}, u32[]{:S(2)}, u32[]{:S(2)}) %collective-permute-start.6) | collective-permute-done | bytes 573472 | tf_op jit(solution)/shard_map/ppermute | solution.py:346
  101.6 5.5 collective-permute-done.4
  110.8 9.6 %collective-permute-done.10 = bf16[72,1152]{1,0:T(8,128)(2,1)} collective-permute-done((bf16[72,1152]{1,0:T(8,128)(2,1)}, bf16[72,1152]{1,0:T(8,128)(2,1)}, u32[]{:S(2)}, u32[]{:S(2)}) %collective-permute-start.10) | collective-permute-done | bytes 165920 | tf_op jit(solution)/shard_map/ppermute | solution.py:346
  120.4 7.8 %collective-permute-done.9 = bf16[72,1152]{1,0:T(8,128)(2,1)} collective-permute-done((bf16[72,1152]{1,0:T(8,128)(2,1)}, bf16[72,1152]{1,0:T(8,128)(2,1)}, u32[]{:S(2)}, u32[]{:S(2)}) %collective-permute-start.9) | collective-permute-done | bytes 165920 | tf_op jit(solution)/shard_map/ppermute | solution.py:346
  128.3 6.4 %collective-permute-done.7 = bf16[8,40,1792]{2,1,0:T(8,128)(2,1)S(1)} collective-permute-done((bf16[8,40,1792]{2,1,0:T(8,128)(2,1)S(1)}, bf16[8,40,1792]{2,1,0:T(8,128)(2,1)S(1)}, u32[]{:S(2)}, u32[]{:S(2)}) %collective-permute-start.7) | collective-permute-done | bytes 1146912 | tf_op jit(solution)/shard_map/ppermute | solution.py:346
  147.9 6.7 %place_square.1 = (bf16[144,8,3456]{2,1,0:T(8,128)(2,1)}, bf16[32,5,8,128]{3,2,1,0:T(8,128)(2,1)S(1)}) custom-call(s32[4]{0:T(128)S(1)} %pad_add_fusion.coords, bf16[8,5,8,1792]{3,2,1,0:T(8,128)(2,1)S(1)} %bitcast.339, bf16[8,5,8,1792]{3,2,1,0:T(8,128)(2,1)} %bitcast.15.refs_1_, bf16[8,5,8,1792]{3,2,1,0:T(8,128)(2,1)S(1)} %bitcast.341, ...), custom_call_target="tpu_custom_call" | custom-call | bytes 18350080 | tf_op jit(solution)/shard_map/place_square/pallas_call | solution.py:411
  159.7 12.7 %add_convert_fusion.qkv_ref = bf16[729,3456]{1,0:T(8,128)(2,1)} fusion(bf16[729,1152]{1,0:T(8,128)(2,1)S(1)} %add_convert_fusion.4.normed_ref, f32[3456]{0:T(1024)S(1)} %pad_maximum_fusion.12, bf16[144,8,3456]{2,1,0:T(8,128)(2,1)} %get-tuple-element.109), kind=kOutput, calls=%fused_computation | convolution fusion | flops 5809792000 | bytes 14694912 | tf_op jit(solution)/shard_map/dot_general | solution.py:333
  179.5 28.9 %attention_forward.1 = (bf16[729,1152]{1,0:T(8,128)(2,1)}, f32[16,1,768]{2,1,0:T(1,128)}) custom-call(bf16[729,3456]{1,0:T(8,128)(2,1)} %add_convert_fusion.qkv_ref), custom_call_target="tpu_custom_call" | custom-call | flops 4630511616 | bytes 6718464 | tf_op jit(solution)/shard_map/attention_forward/pallas_call | solution.py:63
  221.4 19.4 %place_rest.1 = (bf16[144,8,4352]{2,1,0:T(8,128)(2,1)}, bf16[144,8,1152]{2,1,0:T(8,128)(2,1)}, bf16[32,17,8,1152]{3,2,1,0:T(8,128)(2,1)}) custom-call(s32[4]{0:T(128)} %copy-done, bf16[32,33,8,1152]{3,2,1,0:T(8,128)(2,1)} %bitcast.346, bf16[8,5,8,1152]{3,2,1,0:T(8,128)(2,1)} %bitcast.364, bf16[8,5,8,1152]{3,2,1,0:T(8,128)(2,1)} %bitcast.369, ...), custom_call_target="tpu_custom_call" | custom-call | bytes 38928384 | tf_op jit(solution)/shard_map/place_rest/pallas_call | solution.py:479
  240.8 4.9 fusion.44
  250.7 78.9 %mlp_forward_backward.1 = (f32[729,1152]{1,0:T(8,128)}, bf16[16,40,4352]{2,1,0:T(8,128)(2,1)}, bf16[16,40,4352]{2,1,0:T(8,128)(2,1)}, f32[1,4352]{1,0:T(1,128)},...) custom-call(s32[4]{0:T(128)} %copy-done, ...), custom_call_target="tpu_custom_call" | custom-call | flops 1000000 | bytes 1000000 | tf_op jit(solution)/shard_map/mlp_forward_backward/pallas_call | solution.py:205
  342.7 3.9 fusion.1
  351.0 4.3 add_multiply_fusion
  355.3 44.4 %attention_backward.1.grad_ref = bf16[729,3456]{1,0:T(8,128)(2,1)} custom-call(bf16[729,3456]{1,0:T(8,128)(2,1)} %add_convert_fusion.qkv_ref, bf16[729,1152]{1,0:T(8,128)(2,1)} %get-tuple-element.133.go_ref, f32[16,1,768]{2,1,0:T(1,128)} %get-tuple-element.134.lse_ref), custom_call_target="tpu_custom_call" | custom-call | flops 1000000 | bytes 1000000 | tf_op jit(solution)/shard_map/attention_backward/pallas_call | solution.py:107
  412.9 25.2 %qkv_backward.1 = (bf16[16,40,3456]{2,1,0:T(8,128)(2,1)}, bf16[16,40,3456]{2,1,0:T(8,128)(2,1)}, f32[1,3456]{1,0:T(1,128)}, f32[8,1152]{1,0:T(8,128)}, f32[729,1152]{1,0:T(8,128)}) custom-call(s32[4]{0:T(128)} %copy-done, bf16[729,3456]{1,0:T(8,128)(2,1)} %attention_backward.1.grad_ref, bf16[729,1152]{1,0:T(8,128)(2,1)} %copy-done.5, ...), custom_call_target="tpu_custom_call" | custom-call | flops 1000000 | bytes 1000000 | tf_op jit(solution)/shard_map/qkv_backward/pallas_call | solution.py:276
  463.7 12.6 %collective-permute-done.35 = bf16[5,8,5504]{2,1,0:T(8,128)(2,1)S(1)} collective-permute-done((bf16[5,8,5504]{2,1,0:T(8,128)(2,1)S(1)}, bf16[5,8,5504]{2,1,0:T(8,128)(2,1)S(1)}, u32[]{:S(2)}, u32[]{:S(2)}) %collective-permute-start.35) | collective-permute-done | bytes 440352 | tf_op jit(solution)/shard_map/ppermute | solution.py:346
  479.3 24.5 %collective-permute-done.37 = bf16[5,8,5504]{2,1,0:T(8,128)(2,1)S(1)} collective-permute-done((bf16[5,8,5504]{2,1,0:T(8,128)(2,1)S(1)}, bf16[5,8,5504]{2,1,0:T(8,128)(2,1)S(1)}, u32[]{:S(2)}, u32[]{:S(2)}) %collective-permute-start.37) | collective-permute-done | bytes 440352 | tf_op jit(solution)/shard_map/ppermute | solution.py:346
  513.3 8.8 %collective-permute-done.34 = bf16[4,5,8,1792]{3,2,1,0:T(8,128)(2,1)S(1)} collective-permute-done((bf16[4,5,8,1792]{3,2,1,0:T(8,128)(2,1)}, bf16[4,5,8,1792]{3,2,1,0:T(8,128)(2,1)S(1)}, u32[]{:S(2)}, u32[]{:S(2)}) %collective-permute-start.34) | collective-permute-done | bytes 573472 | tf_op jit(solution)/shard_map/ppermute | solution.py:346
  535.9 5.8 %collective-permute-done.38 = bf16[5,8,3584]{2,1,0:T(8,128)(2,1)} collective-permute-done((bf16[5,8,3584]{2,1,0:T(8,128)(2,1)}, bf16[5,8,3584]{2,1,0:T(8,128)(2,1)}, u32[]{:S(2)}, u32[]{:S(2)}) %collective-permute-start.38) | collective-permute-done | bytes 286752 | tf_op jit(solution)/shard_map/ppermute | solution.py:346
  541.7 9.4 %collective-permute-done.39 = bf16[5,8,3584]{2,1,0:T(8,128)(2,1)} collective-permute-done((bf16[5,8,3584]{2,1,0:T(8,128)(2,1)}, bf16[5,8,3584]{2,1,0:T(8,128)(2,1)}, u32[]{:S(2)}, u32[]{:S(2)}) %collective-permute-start.39) | collective-permute-done | bytes 286752 | tf_op jit(solution)/shard_map/ppermute | solution.py:346
  551.1 7.9 %collective-permute-done.40 = bf16[5,8,3584]{2,1,0:T(8,128)(2,1)} collective-permute-done((bf16[5,8,3584]{2,1,0:T(8,128)(2,1)}, bf16[5,8,3584]{2,1,0:T(8,128)(2,1)}, u32[]{:S(2)}, u32[]{:S(2)}) %collective-permute-start.40) | collective-permute-done | bytes 286752 | tf_op jit(solution)/shard_map/ppermute | solution.py:346
  (393 shorter events, 173.4 us)
Async XLA Ops:
  7.2 213.1 %all-gather.2.cloned.1.call-start = ((), (), s32[]{:S(2)}) async-start(), calls=%async_computation.1 | async-start | bytes 20072448 | tf_op jit(solution)/shard_map/all_gather | solution.py:743
  27.5 485.7 %reduce-scatter.4.cloned.1.call-start = ((), (), s32[]{:S(2)}) async-start(), calls=%async_computation.2 | async-start | bytes 10340352
  35.5 19.6 %collective-permute-start.1 = (bf16[40,3584]{1,0:T(8,128)(2,1)S(1)}, bf16[40,3584]{1,0:T(8,128)(2,1)S(1)}, u32[]{:S(2)}, u32[]{:S(2)}) collective-permute-start(bf16[40,3584]{1,0:T(8,128)(2,1)S(1)} %pad_maximum_fusion.7), channel_id=1, source_target_pairs={{0,8},{1,9},{2,10},{3,11},{4,12},{5,13},{6,14},{7,15},{8,0},{9,1},... | collective-permute-start | bytes 860168 | tf_op jit(solution)/shard_map/ppermute | solution.py:346
  35.5 33.5 %collective-permute-start.2 = (bf16[40,3584]{1,0:T(8,128)(2,1)S(1)}, bf16[40,3584]{1,0:T(8,128)(2,1)S(1)}, u32[]{:S(2)}, u32[]{:S(2)}) collective-permute-start(bf16[40,3584]{1,0:T(8,128)(2,1)S(1)} %pad_maximum_fusion.7), channel_id=1, source_target_pairs={{0,16},{1,17},{2,18},{3,19},{4,20},{5,21},{6,22},{7,23},{8,24},{9,... | collective-permute-start | bytes 860168 | tf_op jit(solution)/shard_map/ppermute | solution.py:346
  38.6 38.6 %collective-permute-start.3 = (bf16[40,3584]{1,0:T(8,128)(2,1)S(1)}, bf16[40,3584]{1,0:T(8,128)(2,1)S(1)}, u32[]{:S(2)}, u32[]{:S(2)}) collective-permute-start(bf16[40,3584]{1,0:T(8,128)(2,1)S(1)} %pad_maximum_fusion.7), channel_id=1, source_target_pairs={{0,24},{1,25},{2,26},{3,27},{4,28},{5,29},{6,30},{7,31},{8,16},{9,... | collective-permute-start | bytes 860168 | tf_op jit(solution)/shard_map/ppermute | solution.py:346
  77.3 22.7 %collective-permute-start.6 = (bf16[4,40,1792]{2,1,0:T(8,128)(2,1)S(1)}, bf16[4,40,1792]{2,1,0:T(8,128)(2,1)S(1)}, u32[]{:S(2)}, u32[]{:S(2)}) collective-permute-start(bf16[4,40,1792]{2,1,0:T(8,128)(2,1)S(1)} %pad_maximum_fusion.1), channel_id=1, source_target_pairs={{0,4},{1,5},{2,6},{3,7},{4,0},{5,1},{6,2},{7,3},{8,12},{9,13},{10,... | collective-permute-start | bytes 1720328 | tf_op jit(solution)/shard_map/ppermute | solution.py:346
  79.0 28.1 %collective-permute-start.4 = (bf16[4,40,1792]{2,1,0:T(8,128)(2,1)S(1)}, bf16[4,40,1792]{2,1,0:T(8,128)(2,1)S(1)}, u32[]{:S(2)}, u32[]{:S(2)}) collective-permute-start(bf16[4,40,1792]{2,1,0:T(8,128)(2,1)S(1)} %pad_maximum_fusion), channel_id=1, source_target_pairs={{0,2},{1,3},{2,0},{3,1},{4,6},{5,7},{6,4},{7,5},{8,10},{9,11},{10,... | collective-permute-start | bytes 1720328 | tf_op jit(solution)/shard_map/ppermute | solution.py:346
  100.1 34.6 %collective-permute-start.7 = (bf16[8,40,1792]{2,1,0:T(8,128)(2,1)S(1)}, bf16[8,40,1792]{2,1,0:T(8,128)(2,1)S(1)}, u32[]{:S(2)}, u32[]{:S(2)}) collective-permute-start(bf16[8,40,1792]{2,1,0:T(8,128)(2,1)S(1)} %constant_dynamic-update-slice_fusion.10), channel_id=1, source_target_pairs={{0,2},{1,3},{2,0},{3,1},{4,6},{5,7},{6,4},{7,5},{8,10},{9,11},{10,... | collective-permute-start | bytes 3440648 | tf_op jit(solution)/shard_map/ppermute | solution.py:346
  107.1 27.5 %collective-permute-start.5 = (bf16[8,40,1792]{2,1,0:T(8,128)(2,1)S(1)}, bf16[8,40,1792]{2,1,0:T(8,128)(2,1)}, u32[]{:S(2)}, u32[]{:S(2)}) collective-permute-start(bf16[8,40,1792]{2,1,0:T(8,128)(2,1)S(1)} %constant_dynamic-update-slice_fusion.5), channel_id=1, source_target_pairs={{0,4},{1,5},{2,6},{3,7},{4,0},{5,1},{6,2},{7,3},{8,12},{9,13},{10,... | collective-permute-start | bytes 3440648 | tf_op jit(solution)/shard_map/ppermute | solution.py:346
  139.1 33.3 %collective-permute-start.16 = (bf16[4,32,1152]{2,1,0:T(8,128)(2,1)}, bf16[4,32,1152]{2,1,0:T(8,128)(2,1)}, u32[]{:S(2)}, u32[]{:S(2)}) collective-permute-start(bf16[4,32,1152]{2,1,0:T(8,128)(2,1)} %pad_maximum_fusion.6), channel_id=1, source_target_pairs={{0,4},{1,5},{2,6},{3,7},{4,0},{5,1},{6,2},{7,3},{8,12},{9,13},{10,... | collective-permute-start | bytes 884744 | tf_op jit(solution)/shard_map/ppermute | solution.py:346
  145.0 27.3 %collective-permute-start.15 = (bf16[4,40,1152]{2,1,0:T(8,128)(2,1)}, bf16[4,40,1152]{2,1,0:T(8,128)(2,1)}, u32[]{:S(2)}, u32[]{:S(2)}) collective-permute-start(bf16[4,40,1152]{2,1,0:T(8,128)(2,1)} %pad_maximum_fusion.5), channel_id=1, source_target_pairs={{0,2},{1,3},{2,0},{3,1},{4,6},{5,7},{6,4},{7,5},{8,10},{9,11},{10,... | collective-permute-start | bytes 1105928 | tf_op jit(solution)/shard_map/ppermute | solution.py:346
  174.4 34.0 %collective-permute-start.17 = (bf16[8,40,1152]{2,1,0:T(8,128)(2,1)S(1)}, bf16[8,40,1152]{2,1,0:T(8,128)(2,1)S(1)}, u32[]{:S(2)}, u32[]{:S(2)}) collective-permute-start(bf16[8,40,1152]{2,1,0:T(8,128)(2,1)S(1)} %constant_dynamic-update-slice_fusion.15), channel_id=1, source_target_pairs={{0,4},{1,5},{2,6},{3,7},{4,0},{5,1},{6,2},{7,3},{8,12},{9,13},{10,... | collective-permute-start | bytes 2211848 | tf_op jit(solution)/shard_map/ppermute | solution.py:346
  178.0 30.4 %collective-permute-start.18 = (bf16[8,32,1152]{2,1,0:T(8,128)(2,1)S(1)}, bf16[8,32,1152]{2,1,0:T(8,128)(2,1)}, u32[]{:S(2)}, u32[]{:S(2)}) collective-permute-start(bf16[8,32,1152]{2,1,0:T(8,128)(2,1)S(1)} %constant_dynamic-update-slice_fusion.17), channel_id=1, source_target_pairs={{0,2},{1,3},{2,0},{3,1},{4,6},{5,7},{6,4},{7,5},{8,10},{9,11},{10,... | collective-permute-start | bytes 1769480 | tf_op jit(solution)/shard_map/ppermute | solution.py:346
  346.6 54.4 %collective-permute-start.25 = (bf16[4,2,5,8,2816]{4,3,2,1,0:T(8,128)(2,1)}, bf16[4,2,5,8,2816]{4,3,2,1,0:T(8,128)(2,1)}, u32[]{:S(2)}, u32[]{:S(2)}) collective-permute-start(bf16[4,2,5,8,2816]{4,3,2,1,0:T(8,128)(2,1)} %fusion.1), channel_id=1, source_target_pairs={{0,4},{1,5},{2,6},{3,7},{4,0},{5,1},{6,2},{7,3},{8,12},{9,13},{10,... | collective-permute-start | bytes 5406728 | tf_op jit(solution)/shard_map/ppermute | solution.py:346
  348.4 52.7 %collective-permute-start.26 = (bf16[4,2,5,8,2688]{4,3,2,1,0:T(8,128)(2,1)}, bf16[4,2,5,8,2688]{4,3,2,1,0:T(8,128)(2,1)}, u32[]{:S(2)}, u32[]{:S(2)}) collective-permute-start(bf16[4,2,5,8,2688]{4,3,2,1,0:T(8,128)(2,1)} %add_convert_fusion.2), channel_id=1, source_target_pairs={{0,2},{1,3},{2,0},{3,1},{4,6},{5,7},{6,4},{7,5},{8,10},{9,11},{10,... | collective-permute-start | bytes 5160968 | tf_op jit(solution)/shard_map/ppermute | solution.py:346
  404.7 33.4 %collective-permute-start.27 = (bf16[4,5,8,2816]{3,2,1,0:T(8,128)(2,1)S(1)}, bf16[4,5,8,2816]{3,2,1,0:T(8,128)(2,1)S(1)}, u32[]{:S(2)}, u32[]{:S(2)}) collective-permute-start(bf16[4,5,8,2816]{3,2,1,0:T(8,128)(2,1)S(1)} %fusion.2), channel_id=1, source_target_pairs={{0,2},{1,3},{2,0},{3,1},{4,6},{5,7},{6,4},{7,5},{8,10},{9,11},{10,... | collective-permute-start | bytes 2703368 | tf_op jit(solution)/shard_map/ppermute | solution.py:346
  406.1 32.0 %collective-permute-start.28 = (bf16[4,5,8,2688]{3,2,1,0:T(8,128)(2,1)S(1)}, bf16[4,5,8,2688]{3,2,1,0:T(8,128)(2,1)S(1)}, u32[]{:S(2)}, u32[]{:S(2)}) collective-permute-start(bf16[4,5,8,2688]{3,2,1,0:T(8,128)(2,1)S(1)} %fusion.3), channel_id=1, source_target_pairs={{0,4},{1,5},{2,6},{3,7},{4,0},{5,1},{6,2},{7,3},{8,12},{9,13},{10,... | collective-permute-start | bytes 2580488 | tf_op jit(solution)/shard_map/ppermute | solution.py:346
  451.7 24.7 %collective-permute-start.35 = (bf16[5,8,5504]{2,1,0:T(8,128)(2,1)S(1)}, bf16[5,8,5504]{2,1,0:T(8,128)(2,1)S(1)}, u32[]{:S(2)}, u32[]{:S(2)}) collective-permute-start(bf16[5,8,5504]{2,1,0:T(8,128)(2,1)S(1)} %pad_maximum_fusion.2), channel_id=1, source_target_pairs={{0,8},{1,9},{2,10},{3,11},{4,12},{5,13},{6,14},{7,15},{8,0},{9,1},... | collective-permute-start | bytes 1320968 | tf_op jit(solution)/shard_map/ppermute | solution.py:346
  451.8 27.6 %collective-permute-start.36 = (bf16[5,8,5504]{2,1,0:T(8,128)(2,1)S(1)}, bf16[5,8,5504]{2,1,0:T(8,128)(2,1)S(1)}, u32[]{:S(2)}, u32[]{:S(2)}) collective-permute-start(bf16[5,8,5504]{2,1,0:T(8,128)(2,1)S(1)} %pad_maximum_fusion.3), channel_id=1, source_target_pairs={{0,16},{1,17},{2,18},{3,19},{4,20},{5,21},{6,22},{7,23},{8,24},{9,... | collective-permute-start | bytes 1320968 | tf_op jit(solution)/shard_map/ppermute | solution.py:346
  454.7 49.1 %collective-permute-start.37 = (bf16[5,8,5504]{2,1,0:T(8,128)(2,1)S(1)}, bf16[5,8,5504]{2,1,0:T(8,128)(2,1)S(1)}, u32[]{:S(2)}, u32[]{:S(2)}) collective-permute-start(bf16[5,8,5504]{2,1,0:T(8,128)(2,1)S(1)} %pad_maximum_fusion.4), channel_id=1, source_target_pairs={{0,24},{1,25},{2,26},{3,27},{4,28},{5,29},{6,30},{7,31},{8,16},{9,... | collective-permute-start | bytes 1320968 | tf_op jit(solution)/shard_map/ppermute | solution.py:346
  457.1 47.0 %collective-permute-start.32 = (bf16[4,2,5,8,1792]{4,3,2,1,0:T(8,128)(2,1)S(1)}, bf16[4,2,5,8,1792]{4,3,2,1,0:T(8,128)(2,1)S(1)}, u32[]{:S(2)}, u32[]{:S(2)}) collective-permute-start(bf16[4,2,5,8,1792]{4,3,2,1,0:T(8,128)(2,1)S(1)} %fusion.4), channel_id=1, source_target_pairs={{0,2},{1,3},{2,0},{3,1},{4,6},{5,7},{6,4},{7,5},{8,10},{9,11},{10,... | collective-permute-start | bytes 3440648 | tf_op jit(solution)/shard_map/ppermute | solution.py:346
  459.4 44.7 %collective-permute-start.31 = (bf16[4,2,5,8,1792]{4,3,2,1,0:T(8,128)(2,1)S(1)}, bf16[4,2,5,8,1792]{4,3,2,1,0:T(8,128)(2,1)S(1)}, u32[]{:S(2)}, u32[]{:S(2)}) collective-permute-start(bf16[4,2,5,8,1792]{4,3,2,1,0:T(8,128)(2,1)S(1)} %add_convert_fusion.6), channel_id=1, source_target_pairs={{0,4},{1,5},{2,6},{3,7},{4,0},{5,1},{6,2},{7,3},{8,12},{9,13},{10,... | collective-permute-start | bytes 3440648 | tf_op jit(solution)/shard_map/ppermute | solution.py:346
  529.9 21.2 %collective-permute-start.39 = (bf16[5,8,3584]{2,1,0:T(8,128)(2,1)}, bf16[5,8,3584]{2,1,0:T(8,128)(2,1)}, u32[]{:S(2)}, u32[]{:S(2)}) collective-permute-start(bf16[5,8,3584]{2,1,0:T(8,128)(2,1)} %pad_maximum_fusion.9), channel_id=1, source_target_pairs={{0,16},{1,17},{2,18},{3,19},{4,20},{5,21},{6,22},{7,23},{8,24},{9,... | collective-permute-start | bytes 860168 | tf_op jit(solution)/shard_map/ppermute | solution.py:346
  531.4 27.6 %collective-permute-start.40 = (bf16[5,8,3584]{2,1,0:T(8,128)(2,1)}, bf16[5,8,3584]{2,1,0:T(8,128)(2,1)}, u32[]{:S(2)}, u32[]{:S(2)}) collective-permute-start(bf16[5,8,3584]{2,1,0:T(8,128)(2,1)} %pad_maximum_fusion.10), channel_id=1, source_target_pairs={{0,24},{1,25},{2,26},{3,27},{4,28},{5,29},{6,30},{7,31},{8,16},{9,... | collective-permute-start | bytes 860168 | tf_op jit(solution)/shard_map/ppermute | solution.py:346
  (78 other events, 1047.1 us)
Sparse Core Ops, SparseCore 0:
  27.6 174.7 all-gather.1
  333.9 166.2 reduce-scatter.3

commit v8 on v7

--- a/solution.py
+++ b/solution.py
@@ -12,12 +12,11 @@
 def nt(a,b): return lax.dot_general(a,b,(((1,),(1,)),((),())),preferred_element_type=jnp.float32)
 def nn(a,b): return lax.dot_general(a,b,(((1,),(0,)),((),())),preferred_element_type=jnp.float32)
 
-def fill_heads(dst, src, col, tokens, fill):
-    rows=dst.shape[1]
-    for h in range(HEADS):
-        if fill is not None:
-            dst[h]=fill
-        dst[h,0:tokens,0:HEAD_DIM]=src[:,col+h*HEAD_DIM:col+(h+1)*HEAD_DIM]
+def fill_heads(dst, src, col, tokens, fill, first=0):
+    for h in range(dst.shape[0]):
+        start=col+(first+h)*HEAD_DIM
+        dst[h]=fill
+        dst[h,0:tokens,0:HEAD_DIM]=src[:,start:start+HEAD_DIM]
 
 def pad_values(rows, tokens, kind):
     lane=lax.broadcasted_iota(jnp.int32,(rows,LANES),1)
@@ -71,14 +70,14 @@
         cost_estimate=pl.CostEstimate(flops=4*HEADS*qrows*krows*LANES,bytes_accessed=4*tokens*D*2,transcendentals=HEADS*qrows*krows),
         name="attention_forward")(qkv)
 
-def bwd_kernel(tokens, krows, qrows, per, qkv_ref, go_ref, lse_ref, dqkv_ref, qs, ks, vs, gs):
+def bwd_kernel(tokens, krows, qrows, per, first, qkv_ref, go_ref, lse_ref, dqkv_ref, qs, ks, vs, gs):
     step=pl.program_id(0)
     @pl.when(step==0)
     def _():
-        fill_heads(qs,qkv_ref,0,tokens,pad_values(qrows,tokens,"query"))
-        fill_heads(ks,qkv_ref,D,tokens,pad_values(krows,tokens,"key"))
-        fill_heads(vs,qkv_ref,2*D,tokens,pad_values(krows,tokens,"value"))
-        fill_heads(gs,go_ref,0,tokens,pad_values(qrows,tokens,"value"))
+        fill_heads(qs,qkv_ref,0,tokens,pad_values(qrows,tokens,"query"),first)
+        fill_heads(ks,qkv_ref,D,tokens,pad_values(krows,tokens,"key"),first)
+        fill_heads(vs,qkv_ref,2*D,tokens,pad_values(krows,tokens,"value"),first)
+        fill_heads(gs,go_ref,0,tokens,pad_values(qrows,tokens,"value"),first)
     scale=HEAD_DIM**-0.5
     c=scale*LOG2E
     for j in range(per):
@@ -98,20 +97,20 @@
     @pl.when(step==pl.num_programs(0)-1)
     def _():
         for i,r in enumerate((qs,ks,vs)):
-            for h in range(HEADS):
-                dqkv_ref[:,i*D+h*HEAD_DIM:i*D+(h+1)*HEAD_DIM]=r[h,0:tokens,0:HEAD_DIM]
-
-def attn_bwd(qkv, gmixed, lse, per=1):
+            for h in range(qs.shape[0]):
+                dqkv_ref[i,:,h*HEAD_DIM:(h+1)*HEAD_DIM]=r[h,0:tokens,0:HEAD_DIM]
+
+def attn_bwd(qkv, gmixed, lse, per, first, count):
     tokens=qkv.shape[0]
     krows=-(-tokens//16)*16; qrows=-(-tokens//128)*128
-    return pl.pallas_call(functools.partial(bwd_kernel,tokens,krows,qrows,per),
-        grid=(HEADS//per,),
+    return pl.pallas_call(functools.partial(bwd_kernel,tokens,krows,qrows,per,first),
+        grid=(count//per,),
         in_specs=[pl.BlockSpec(qkv.shape,lambda i:(0,0),pipeline_mode=pl.Buffered(1)),pl.BlockSpec(gmixed.shape,lambda i:(0,0),pipeline_mode=pl.Buffered(1)),
-                  pl.BlockSpec((per,1,qrows),lambda i:(i,0,0))],
-        out_specs=pl.BlockSpec((tokens,3*D),lambda i:(0,0),pipeline_mode=pl.Buffered(1)),
-        out_shape=jax.ShapeDtypeStruct((tokens,3*D),jnp.bfloat16),
-        scratch_shapes=[pltpu.VMEM((HEADS,qrows,LANES),jnp.bfloat16),pltpu.VMEM((HEADS,krows,LANES),jnp.bfloat16),
-                        pltpu.VMEM((HEADS,krows,LANES),jnp.bfloat16),pltpu.VMEM((HEADS,qrows,LANES),jnp.bfloat16)],
+                  pl.BlockSpec((per,1,qrows),lambda i:(i+first//per,0,0))],
+        out_specs=pl.BlockSpec((3,tokens,count*HEAD_DIM),lambda i:(0,0,0),pipeline_mode=pl.Buffered(1)),
+        out_shape=jax.ShapeDtypeStruct((3,tokens,count*HEAD_DIM),jnp.bfloat16),
+        scratch_shapes=[pltpu.VMEM((count,qrows,LANES),jnp.bfloat16),pltpu.VMEM((count,krows,LANES),jnp.bfloat16),
+                        pltpu.VMEM((count,krows,LANES),jnp.bfloat16),pltpu.VMEM((count,qrows,LANES),jnp.bfloat16)],
         compiler_params=pltpu.CompilerParams(vmem_limit_bytes=56<<20,dimension_semantics=("arbitrary",)),
         cost_estimate=pl.CostEstimate(flops=1000000,bytes_accessed=1000000,transcendentals=0),
         name="attention_backward")(qkv,gmixed,lse)
@@ -236,7 +235,7 @@
     )(coords, normed, grad, up, bias, down, xhat, inverse, gain, grad_out, mixed, output)
 
 
-def qkv_back_kernel(coords, grad_ref, normed_ref, weight_ref, xhat_ref, inverse_ref, gain_ref, resid_ref,
+def qkv_back_kernel(coords, first_ref, second_ref, normed_ref, weight_ref, xhat_ref, inverse_ref, gain_ref, resid_ref,
                     keep_ref, send_ref, bias_grad_ref, sums_ref, tokens_ref, grad, normed_t, total):
     step = pl.program_id(0)
     tokens = normed_ref.shape[0]
@@ -249,7 +248,9 @@
         grad[...] = jnp.zeros_like(grad)
         total[...] = jnp.zeros_like(total)
 
-    grad[0:tokens] = grad_ref[...]
+    cut = first_ref.shape[-1]
+    grad[0:tokens, 0:cut] = first_ref[0]
+    grad[0:tokens, cut:D] = second_ref[0]
     share_rows(coords[0], nn(normed_t[...], grad[...]), keep_ref, send_ref)
     bias_grad_ref[...] = jnp.sum(grad[...].astype(jnp.float32), axis=0, keepdims=True)
     total[...] += nt(grad[...], weight_ref[...])
@@ -266,7 +267,7 @@
         tokens_ref[...] = resid_ref[...] + inverse_ref[...] * (scaled - first - xhat * second)
 
 
-def qkv_back(coords, grad, normed, weight, xhat, inverse, gain, resid):
+def qkv_back(coords, first, second, normed, weight, xhat, inverse, gain, resid):
     tokens = normed.shape[0]
     rows = -(-tokens // 16) * 16
     whole = lambda shape: pl.BlockSpec(shape, lambda i: (0, 0), pipeline_mode=pl.Buffered(1))
@@ -278,7 +279,8 @@
         grid=(3,),
         in_specs=[
             pl.BlockSpec(memory_space=pltpu.SMEM),
-            part((tokens, D)),
+            pl.BlockSpec((1,) + first.shape[1:], lambda i: (i, 0, 0)),
+            pl.BlockSpec((1,) + second.shape[1:], lambda i: (i, 0, 0)),
             whole((tokens, D)),
             part((D, D)),
             whole((tokens, D)),
@@ -304,7 +306,7 @@
         ),
         cost_estimate=pl.CostEstimate(flops=1000000, bytes_accessed=1000000, transcendentals=0),
         name="qkv_backward",
-    )(coords, grad, normed, weight, xhat, inverse, gain, resid)
+    )(coords, first, second, normed, weight, xhat, inverse, gain, resid)
 
 
 FF = 4304
@@ -687,7 +689,7 @@
     width = widths[VECTORS[0]]
     pieces = whole[:, : count * width].reshape(-1, count, width)
     pieces = pieces.transpose(1, 0, 2).reshape(count, -1).astype(f32)
-    found = {i: pieces[position] for position, i in enumerate(VECTORS[:-1])}
+    found = {i: pieces[position : position + 1] for position, i in enumerate(VECTORS[:-1])}
     last = widths[VECTORS[-1]]
     found[VECTORS[-1]] = whole[:, count * width : count * width + last].reshape(-1).astype(f32)
     return found
@@ -741,7 +743,9 @@
     if staged:
         sq, rest, down = fetch_pairs(narrow, core)
         rest = lax.all_gather(rest, "fsdp", axis=0, tiled=True)
+        sq, tokens = tie(sq, tokens)
         sq = gather_z(sq)
+        xhat_one, inverse_one = normalize(tokens)
         sq, down, xhat_one, inverse_one, grad_branch = tie(
             sq, down, xhat_one, inverse_one, grad_branch
         )
@@ -756,9 +760,9 @@
     else:
         weight_qkv, weight_o, weight_up, weight_down, vectors = gather_plain(narrow, widths)
 
-    vec = lambda i: vectors[i][:D]
+    vec = lambda i: vectors[i][:, :D]
     gain_one, shift_one, gain_two, shift_two = vec(0), vec(1), vec(9), vec(10)
-    bias_qkv = jnp.concatenate([vec(3), jnp.zeros((D,), f32), vec(6)])
+    bias_qkv = jnp.concatenate([vec(3), jnp.zeros((1, D), f32), vec(6)], axis=1)
     bias_o, bias_down = vec(8), vec(14)
     bias_up = pad_hidden(vectors[12][:FF].reshape(1, FF))
 
@@ -812,15 +816,22 @@
         outer_other = outer.core_step((up_send, o_send))
         grad_mixed, outer_other = tie(grad_mixed, outer_other)
         outer_far = outer.far_swap(outer.far_sends(outer_other))
-    grad_qkv = attn_bwd(qkv, grad_mixed, lse, 2)
+    grads_first = attn_bwd(qkv, grad_mixed, lse, 2, 0, 12)
     if staged:
-        grad_qkv, outer_far = tie(grad_qkv, outer_far)
+        grads_first, outer_far, grad_mixed = tie(grads_first, outer_far, grad_mixed)
         outer_near = outer.near_sends(outer_far)
-        grad_qkv, outer_near = tie(grad_qkv, outer_near)
+        grad_mixed, outer_near = tie(grad_mixed, outer_near)
         outer_near = outer.near_swap(outer_near)
+    grads_second = attn_bwd(qkv, grad_mixed, lse, 2, 12, 4)
+    if staged:
+        grads_second, outer_near = tie(grads_second, outer_near)
+        outer_z = outer.z_sends(outer_near)
+        grads_second, outer_z = tie(grads_second, outer_z)
+        outer_z = outer.z_swap(outer_z)
     qkv_keep, qkv_send, qkv_bias_grad, norm_sums, tokens_grad = qkv_back(
         where,
-        grad_qkv,
+        grads_first,
+        grads_second,
         normed,
         weight_qkv,
         xhat_one,
@@ -829,10 +840,9 @@
         grad_resid,
     )
     if staged:
-        qkv_keep, qkv_send, norm_sums, qkv_bias_grad, outer_near = tie(
-            qkv_keep, qkv_send, norm_sums, qkv_bias_grad, outer_near
+        qkv_keep, qkv_send, norm_sums, qkv_bias_grad, outer_z = tie(
+            qkv_keep, qkv_send, norm_sums, qkv_bias_grad, outer_z
         )
-        outer_z = outer.z_sends(outer_near)
         qkv_other = outer.core_step((qkv_send,))[0]
     grads[3], grads[6] = qkv_bias_grad[0, :D], qkv_bias_grad[0, 2 * D :]
     grads[0], grads[1] = norm_sums[0], norm_sums[1]
@@ -851,9 +861,8 @@
         inner = Reduction(
             (qkv_keep, rows_keep), (((0, 0, cut), (1, 0, EXTRA)), ((0, cut, 3 * D),)), coords
         )
-        qkv_other, rows_other, outer_z = tie(qkv_other, rows_other, outer_z)
+        qkv_other, rows_other = tie(qkv_other, rows_other)
         inner_far = inner.far_swap(inner.far_sends((qkv_other, rows_other)))
-        outer_z = outer.z_swap(outer_z)
         inner_far, layer_out = tie(inner_far, layer_out)
         inner_near = inner.near_swap(inner.near_sends(inner_far))
         outer_sum = outer.finish(outer_z)

time: 577 us -> 587 us (1.017)
  waiting for transfers between devices: 161 us -> 179 us
  local copies, waits for them, and re-layouts: 78.1 us -> 69.8 us
    ppermute x42, waiting for transfers between devices: 161 us -> 179 us  [swap(): return lax.ppermute(value, 'fsdp', [(i, i ^ mask) for i in range(devices)])]
    unnamed x128 -> x114, local copies, waits for them, and re-layouts: 12.9 us -> 9.72 us
    pallas_call x1 -> x2, Pallas kernels: 44.4 us -> 47.6 us  [attn_bwd(): pl.pallas_call(functools.partial(bwd_kernel, tokens, krows, qrows, per, f...]
  transfers between devices with their start and end apart: 44 -> 44, of which waited for: 20 -> 26; matrix products, arithmetic and copies ran while one was open for 20% -> 19% of each run, Pallas kernels for 18% -> 19%
where the time goes in v8:
time: 587 us; the launch traced here: 581 us
  Pallas kernels  207 us (35%)
  waiting for transfers between devices  179 us (30%)
  local copies, waits for them, and re-layouts  69.8 us (12%)
  other arithmetic  58.1 us (10%)
  starting transfers between devices  32.6 us (6%)
  matrix products  17.6 us (3%)
  between operations  16.4 us (3%)
    ppermute x42, waiting for transfers between devices, swap(): return lax.ppermute(value, 'fsdp', [(i, i ^ mask) for i in range(devices)])  179 us
    pallas_call x1, Pallas kernels, mlp(): pl.pallas_call(mlp_kernel, grid=(hidden // tile,), in_specs=[pl.BlockSpec...  78.9 us
    pallas_call x2, Pallas kernels, attn_bwd(): pl.pallas_call(functools.partial(bwd_kernel, tokens, krows, qrows, per, f...  47.6 us
    ppermute x42, starting transfers between devices, swap(): return lax.ppermute(value, 'fsdp', [(i, i ^ mask) for i in range(devices)])  32.3 us
    pallas_call x1, Pallas kernels, attn_fwd(): pl.pallas_call(functools.partial(fwd_kernel, tokens, krows, qrows, per),...  28.4 us
    pallas_call x1, Pallas kernels, qkv_back(): pl.pallas_call(qkv_back_kernel, grid=(3,), in_specs=[pl.BlockSpec(memory_...  26.1 us
    pallas_call x1, Pallas kernels, place_rest(): pl.pallas_call(place_rest_kernel, in_specs=[pl.BlockSpec(memory_space=plt...  19.5 us
    reshape x24, local copies, waits for them, and re-layouts, window(): return result.reshape(kept)  18.9 us
  transfers between devices with their start and end apart: 44, of which 26 were waited for; matrix products, arithmetic and copies ran while one was open for 19% of the time, Pallas kernels for 19%

profile of v8, /device:TPU:8, one launch (start us, length us, event | category | flops | bytes accessed | tf_op | source)
XLA Modules:
  0.0 580.6 jit_solution(17771817236406885925)
XLA Ops:
  32.6 12.3 %collective-permute-done.1 = bf16[40,3584]{1,0:T(8,128)(2,1)} collective-permute-done((bf16[40,3584]{1,0:T(8,128)(2,1)}, bf16[40,3584]{1,0:T(8,128)(2,1)}, u32[]{:S(2)}, u32[]{:S(2)}) %collective-permute-start.1) | collective-permute-done | bytes 286752 | tf_op jit(solution)/shard_map/ppermute | solution.py:348
  44.9 14.5 %collective-permute-done.2 = bf16[40,3584]{1,0:T(8,128)(2,1)} collective-permute-done((bf16[40,3584]{1,0:T(8,128)(2,1)}, bf16[40,3584]{1,0:T(8,128)(2,1)}, u32[]{:S(2)}, u32[]{:S(2)}) %collective-permute-start.2) | collective-permute-done | bytes 286752 | tf_op jit(solution)/shard_map/ppermute | solution.py:348
  59.4 7.3 %collective-permute-done.3 = bf16[40,3584]{1,0:T(8,128)(2,1)} collective-permute-done((bf16[40,3584]{1,0:T(8,128)(2,1)}, bf16[40,3584]{1,0:T(8,128)(2,1)}, u32[]{:S(2)}, u32[]{:S(2)}) %collective-permute-start.3) | collective-permute-done | bytes 286752 | tf_op jit(solution)/shard_map/ppermute | solution.py:348
  76.6 14.6 %collective-permute-done.6 = bf16[4,40,1792]{2,1,0:T(8,128)(2,1)S(1)} collective-permute-done((bf16[4,40,1792]{2,1,0:T(8,128)(2,1)S(1)}, bf16[4,40,1792]{2,1,0:T(8,128)(2,1)S(1)}, u32[]{:S(2)}, u32[]{:S(2)}) %collective-permute-start.6) | collective-permute-done | bytes 573472 | tf_op jit(solution)/shard_map/ppermute | solution.py:348
  92.7 6.5 %collective-permute-done.4 = bf16[4,40,1792]{2,1,0:T(8,128)(2,1)S(1)} collective-permute-done((bf16[4,40,1792]{2,1,0:T(8,128)(2,1)S(1)}, bf16[4,40,1792]{2,1,0:T(8,128)(2,1)S(1)}, u32[]{:S(2)}, u32[]{:S(2)}) %collective-permute-start.4) | collective-permute-done | bytes 573472 | tf_op jit(solution)/shard_map/ppermute | solution.py:348
  103.4 14.2 %collective-permute-done.10 = bf16[72,1152]{1,0:T(8,128)(2,1)} collective-permute-done((bf16[72,1152]{1,0:T(8,128)(2,1)}, bf16[72,1152]{1,0:T(8,128)(2,1)}, u32[]{:S(2)}, u32[]{:S(2)}) %collective-permute-start.10) | collective-permute-done | bytes 165920 | tf_op jit(solution)/shard_map/ppermute | solution.py:348
  118.7 5.7 collective-permute-done.7
  138.3 6.8 %place_square.1 = (bf16[144,8,3456]{2,1,0:T(8,128)(2,1)}, bf16[32,5,8,128]{3,2,1,0:T(8,128)(2,1)S(1)}) custom-call(s32[4]{0:T(128)S(1)} %pad_add_fusion.coords, bf16[8,5,8,1792]{3,2,1,0:T(8,128)(2,1)S(1)} %bitcast.339, bf16[8,5,8,1792]{3,2,1,0:T(8,128)(2,1)} %bitcast.15.refs_1_, bf16[8,5,8,1792]{3,2,1,0:T(8,128)(2,1)S(1)} %bitcast.341, ...), custom_call_target="tpu_custom_call" | custom-call | bytes 18350080 | tf_op jit(solution)/shard_map/place_square/pallas_call | solution.py:413
  150.2 12.6 %add_convert_fusion.qkv_ref = bf16[729,3456]{1,0:T(8,128)(2,1)} fusion(bf16[729,1152]{1,0:T(8,128)(2,1)S(1)} %add_convert_fusion.4.normed_ref, f32[3456]{0:T(1024)S(1)} %fusion.32, bf16[144,8,3456]{2,1,0:T(8,128)(2,1)} %get-tuple-element.119), kind=kOutput, calls=%fused_computation | convolution fusion | flops 5809792000 | bytes 14694912 | tf_op jit(solution)/shard_map/dot_general | solution.py:335
  169.9 28.4 %attention_forward.1 = (bf16[729,1152]{1,0:T(8,128)(2,1)}, f32[16,1,768]{2,1,0:T(1,128)}) custom-call(bf16[729,3456]{1,0:T(8,128)(2,1)} %add_convert_fusion.qkv_ref), custom_call_target="tpu_custom_call" | custom-call | flops 4630511616 | bytes 6718464 | tf_op jit(solution)/shard_map/attention_forward/pallas_call | solution.py:62
  211.3 19.5 %place_rest.1 = (bf16[144,8,4352]{2,1,0:T(8,128)(2,1)}, bf16[144,8,1152]{2,1,0:T(8,128)(2,1)}, bf16[32,17,8,1152]{3,2,1,0:T(8,128)(2,1)}) custom-call(s32[4]{0:T(128)} %copy-done, bf16[32,33,8,1152]{3,2,1,0:T(8,128)(2,1)} %bitcast.346, bf16[8,5,8,1152]{3,2,1,0:T(8,128)(2,1)} %bitcast.364, bf16[8,5,8,1152]{3,2,1,0:T(8,128)(2,1)} %bitcast.369, ...), custom_call_target="tpu_custom_call" | custom-call | bytes 38928384 | tf_op jit(solution)/shard_map/place_rest/pallas_call | solution.py:481
  240.6 78.9 %mlp_forward_backward.1 = (f32[729,1152]{1,0:T(8,128)}, bf16[16,40,4352]{2,1,0:T(8,128)(2,1)}, bf16[16,40,4352]{2,1,0:T(8,128)(2,1)}, f32[1,4352]{1,0:T(1,128)},...) custom-call(s32[4]{0:T(128)} %copy-done, ...), custom_call_target="tpu_custom_call" | custom-call | flops 1000000 | bytes 1000000 | tf_op jit(solution)/shard_map/mlp_forward_backward/pallas_call | solution.py:204
  321.4 8.1 %collective-permute-done.24 = bf16[4,2,2,5,8,1152]{5,4,3,2,1,0:T(8,128)(2,1)S(1)} collective-permute-done((bf16[4,2,2,5,8,1152]{5,4,3,2,1,0:T(8,128)(2,1)}, bf16[4,2,2,5,8,1152]{5,4,3,2,1,0:T(8,128)(2,1)S(1)}, u32[]{:S(2)}, u32[]{:S(2)}) %collective-permute-start.24) | collective-permute-done | bytes 1474592 | tf_op jit(solution)/shard_map/ppermute | solution.py:348
  338.5 34.0 %attention_backward.2.first_ref = bf16[3,729,864]{2,1,0:T(8,128)(2,1)} custom-call(bf16[729,3456]{1,0:T(8,128)(2,1)} %add_convert_fusion.qkv_ref, bf16[729,1152]{1,0:T(8,128)(2,1)} %get-tuple-element.153.go_ref, f32[16,1,768]{2,1,0:T(1,128)} %get-tuple-element.144.lse_ref), custom_call_target="tpu_custom_call" | custom-call | flops 1000000 | bytes 1000000 | tf_op jit(solution)/shard_map/attention_backward/pallas_call | solution.py:106
  384.8 13.5 %attention_backward.3.second_ref = bf16[3,729,288]{2,1,0:T(8,128)(2,1)} custom-call(bf16[729,3456]{1,0:T(8,128)(2,1)} %add_convert_fusion.qkv_ref, bf16[729,1152]{1,0:T(8,128)(2,1)} %get-tuple-element.153.go_ref, f32[16,1,768]{2,1,0:T(1,128)} %get-tuple-element.144.lse_ref), custom_call_target="tpu_custom_call" | custom-call | flops 1000000 | bytes 1000000 | tf_op jit(solution)/shard_map/attention_backward/pallas_call | solution.py:106
  398.3 11.4 %collective-permute-done.28 = bf16[4,5,8,2688]{3,2,1,0:T(8,128)(2,1)S(1)} collective-permute-done((bf16[4,5,8,2688]{3,2,1,0:T(8,128)(2,1)S(1)}, bf16[4,5,8,2688]{3,2,1,0:T(8,128)(2,1)S(1)}, u32[]{:S(2)}, u32[]{:S(2)}) %collective-permute-start.28) | collective-permute-done | bytes 860192 | tf_op jit(solution)/shard_map/ppermute | solution.py:348
  424.5 26.1 %qkv_backward.1 = (bf16[16,40,3456]{2,1,0:T(8,128)(2,1)}, bf16[16,40,3456]{2,1,0:T(8,128)(2,1)}, f32[1,3456]{1,0:T(1,128)}, f32[8,1152]{1,0:T(8,128)}, f32[729,1152]{1,0:T(8,128)}) custom-call(s32[4]{0:T(128)} %copy-done, bf16[3,729,864]{2,1,0:T(8,128)(2,1)} %attention_backward.2.first_ref, bf16[3,729,288]{2,1,0:T(8,128)(2,1)} %attention_backward.3.second_ref, ...), custom_call_target="tpu_custom_call" | custom-call | flops 1000000 | bytes 1000000 | tf_op jit(solution)/shard_map/qkv_backward/pallas_call | solution.py:277
  450.5 7.6 %collective-permute-done.30 = bf16[5,8,5504]{2,1,0:T(8,128)(2,1)} collective-permute-done((bf16[5,8,5504]{2,1,0:T(8,128)(2,1)}, bf16[5,8,5504]{2,1,0:T(8,128)(2,1)}, u32[]{:S(2)}, u32[]{:S(2)}) %collective-permute-start.30) | collective-permute-done | bytes 440352 | tf_op jit(solution)/shard_map/ppermute | solution.py:348
  458.1 14.9 %collective-permute-done.31 = bf16[5,8,5504]{2,1,0:T(8,128)(2,1)} collective-permute-done((bf16[5,8,5504]{2,1,0:T(8,128)(2,1)}, bf16[5,8,5504]{2,1,0:T(8,128)(2,1)}, u32[]{:S(2)}, u32[]{:S(2)}) %collective-permute-start.31) | collective-permute-done | bytes 440352 | tf_op jit(solution)/shard_map/ppermute | solution.py:348
  494.9 19.4 %collective-permute-done.35 = bf16[4,2,5,8,1792]{4,3,2,1,0:T(8,128)(2,1)} collective-permute-done((bf16[4,2,5,8,1792]{4,3,2,1,0:T(8,128)(2,1)}, bf16[4,2,5,8,1792]{4,3,2,1,0:T(8,128)(2,1)}, u32[]{:S(2)}, u32[]{:S(2)}) %collective-permute-start.35) | collective-permute-done | bytes 1146912 | tf_op jit(solution)/shard_map/ppermute | solution.py:348
  526.5 6.1 %collective-permute-done.37 = bf16[4,5,8,1792]{3,2,1,0:T(8,128)(2,1)S(1)} collective-permute-done((bf16[4,5,8,1792]{3,2,1,0:T(8,128)(2,1)S(1)}, bf16[4,5,8,1792]{3,2,1,0:T(8,128)(2,1)S(1)}, u32[]{:S(2)}, u32[]{:S(2)}) %collective-permute-start.37) | collective-permute-done | bytes 573472 | tf_op jit(solution)/shard_map/ppermute | solution.py:348
  545.4 6.8 %collective-permute-done.38 = bf16[5,8,3584]{2,1,0:T(8,128)(2,1)} collective-permute-done((bf16[5,8,3584]{2,1,0:T(8,128)(2,1)}, bf16[5,8,3584]{2,1,0:T(8,128)(2,1)}, u32[]{:S(2)}, u32[]{:S(2)}) %collective-permute-start.38) | collective-permute-done | bytes 286752 | tf_op jit(solution)/shard_map/ppermute | solution.py:348
  552.2 9.7 %collective-permute-done.39 = bf16[5,8,3584]{2,1,0:T(8,128)(2,1)} collective-permute-done((bf16[5,8,3584]{2,1,0:T(8,128)(2,1)}, bf16[5,8,3584]{2,1,0:T(8,128)(2,1)}, u32[]{:S(2)}, u32[]{:S(2)}) %collective-permute-start.39) | collective-permute-done | bytes 286752 | tf_op jit(solution)/shard_map/ppermute | solution.py:348
  561.9 6.7 %collective-permute-done.40 = bf16[5,8,3584]{2,1,0:T(8,128)(2,1)} collective-permute-done((bf16[5,8,3584]{2,1,0:T(8,128)(2,1)S(1)}, bf16[5,8,3584]{2,1,0:T(8,128)(2,1)}, u32[]{:S(2)}, u32[]{:S(2)}) %collective-permute-start.40) | collective-permute-done | bytes 286752 | tf_op jit(solution)/shard_map/ppermute | solution.py:348
  (380 shorter events, 178.7 us)
Async XLA Ops:
  7.2 203.0 %all-gather.2.cloned.1.call-start = ((), (), s32[]{:S(2)}) async-start(), calls=%async_computation.1 | async-start | bytes 20072448 | tf_op jit(solution)/shard_map/all_gather | solution.py:745
  17.4 509.1 %reduce-scatter.4.cloned.1.call-start = ((), (), s32[]{:S(2)}) async-start(), calls=%async_computation.2 | async-start | bytes 10340352
  24.8 20.2 %collective-permute-start.1 = (bf16[40,3584]{1,0:T(8,128)(2,1)}, bf16[40,3584]{1,0:T(8,128)(2,1)}, u32[]{:S(2)}, u32[]{:S(2)}) collective-permute-start(bf16[40,3584]{1,0:T(8,128)(2,1)} %pad_maximum_fusion.7), channel_id=1, source_target_pairs={{0,8},{1,9},{2,10},{3,11},{4,12},{5,13},{6,14},{7,15},{8,0},{9,1},... | collective-permute-start | bytes 860168 | tf_op jit(solution)/shard_map/ppermute | solution.py:348
  24.8 34.7 %collective-permute-start.2 = (bf16[40,3584]{1,0:T(8,128)(2,1)}, bf16[40,3584]{1,0:T(8,128)(2,1)}, u32[]{:S(2)}, u32[]{:S(2)}) collective-permute-start(bf16[40,3584]{1,0:T(8,128)(2,1)} %pad_maximum_fusion.7), channel_id=1, source_target_pairs={{0,16},{1,17},{2,18},{3,19},{4,20},{5,21},{6,22},{7,23},{8,24},{9,... | collective-permute-start | bytes 860168 | tf_op jit(solution)/shard_map/ppermute | solution.py:348
  27.8 38.9 %collective-permute-start.3 = (bf16[40,3584]{1,0:T(8,128)(2,1)}, bf16[40,3584]{1,0:T(8,128)(2,1)}, u32[]{:S(2)}, u32[]{:S(2)}) collective-permute-start(bf16[40,3584]{1,0:T(8,128)(2,1)} %pad_maximum_fusion.7), channel_id=1, source_target_pairs={{0,24},{1,25},{2,26},{3,27},{4,28},{5,29},{6,30},{7,31},{8,16},{9,... | collective-permute-start | bytes 860168 | tf_op jit(solution)/shard_map/ppermute | solution.py:348
  69.4 21.8 %collective-permute-start.6 = (bf16[4,40,1792]{2,1,0:T(8,128)(2,1)S(1)}, bf16[4,40,1792]{2,1,0:T(8,128)(2,1)S(1)}, u32[]{:S(2)}, u32[]{:S(2)}) collective-permute-start(bf16[4,40,1792]{2,1,0:T(8,128)(2,1)S(1)} %pad_maximum_fusion.1), channel_id=1, source_target_pairs={{0,4},{1,5},{2,6},{3,7},{4,0},{5,1},{6,2},{7,3},{8,12},{9,13},{10,... | collective-permute-start | bytes 1720328 | tf_op jit(solution)/shard_map/ppermute | solution.py:348
  71.0 28.2 %collective-permute-start.4 = (bf16[4,40,1792]{2,1,0:T(8,128)(2,1)S(1)}, bf16[4,40,1792]{2,1,0:T(8,128)(2,1)S(1)}, u32[]{:S(2)}, u32[]{:S(2)}) collective-permute-start(bf16[4,40,1792]{2,1,0:T(8,128)(2,1)S(1)} %pad_maximum_fusion), channel_id=1, source_target_pairs={{0,2},{1,3},{2,0},{3,1},{4,6},{5,7},{6,4},{7,5},{8,10},{9,11},{10,... | collective-permute-start | bytes 1720328 | tf_op jit(solution)/shard_map/ppermute | solution.py:348
  91.2 33.3 %collective-permute-start.7 = (bf16[8,40,1792]{2,1,0:T(8,128)(2,1)S(1)}, bf16[8,40,1792]{2,1,0:T(8,128)(2,1)S(1)}, u32[]{:S(2)}, u32[]{:S(2)}) collective-permute-start(bf16[8,40,1792]{2,1,0:T(8,128)(2,1)S(1)} %constant_dynamic-update-slice_fusion.10), channel_id=1, source_target_pairs={{0,2},{1,3},{2,0},{3,1},{4,6},{5,7},{6,4},{7,5},{8,10},{9,11},{10,... | collective-permute-start | bytes 3440648 | tf_op jit(solution)/shard_map/ppermute | solution.py:348
  99.2 25.2 %collective-permute-start.5 = (bf16[8,40,1792]{2,1,0:T(8,128)(2,1)S(1)}, bf16[8,40,1792]{2,1,0:T(8,128)(2,1)}, u32[]{:S(2)}, u32[]{:S(2)}) collective-permute-start(bf16[8,40,1792]{2,1,0:T(8,128)(2,1)S(1)} %constant_dynamic-update-slice_fusion.5), channel_id=1, source_target_pairs={{0,4},{1,5},{2,6},{3,7},{4,0},{5,1},{6,2},{7,3},{8,12},{9,13},{10,... | collective-permute-start | bytes 3440648 | tf_op jit(solution)/shard_map/ppermute | solution.py:348
  128.9 33.9 %collective-permute-start.16 = (bf16[4,32,1152]{2,1,0:T(8,128)(2,1)}, bf16[4,32,1152]{2,1,0:T(8,128)(2,1)}, u32[]{:S(2)}, u32[]{:S(2)}) collective-permute-start(bf16[4,32,1152]{2,1,0:T(8,128)(2,1)} %pad_maximum_fusion.6), channel_id=1, source_target_pairs={{0,4},{1,5},{2,6},{3,7},{4,0},{5,1},{6,2},{7,3},{8,12},{9,13},{10,... | collective-permute-start | bytes 884744 | tf_op jit(solution)/shard_map/ppermute | solution.py:348
  135.8 27.0 %collective-permute-start.15 = (bf16[4,40,1152]{2,1,0:T(8,128)(2,1)}, bf16[4,40,1152]{2,1,0:T(8,128)(2,1)}, u32[]{:S(2)}, u32[]{:S(2)}) collective-permute-start(bf16[4,40,1152]{2,1,0:T(8,128)(2,1)} %pad_maximum_fusion.5), channel_id=1, source_target_pairs={{0,2},{1,3},{2,0},{3,1},{4,6},{5,7},{6,4},{7,5},{8,10},{9,11},{10,... | collective-permute-start | bytes 1105928 | tf_op jit(solution)/shard_map/ppermute | solution.py:348
  164.9 33.4 %collective-permute-start.17 = (bf16[8,40,1152]{2,1,0:T(8,128)(2,1)S(1)}, bf16[8,40,1152]{2,1,0:T(8,128)(2,1)S(1)}, u32[]{:S(2)}, u32[]{:S(2)}) collective-permute-start(bf16[8,40,1152]{2,1,0:T(8,128)(2,1)S(1)} %constant_dynamic-update-slice_fusion.15), channel_id=1, source_target_pairs={{0,4},{1,5},{2,6},{3,7},{4,0},{5,1},{6,2},{7,3},{8,12},{9,13},{10,... | collective-permute-start | bytes 2211848 | tf_op jit(solution)/shard_map/ppermute | solution.py:348
  168.4 29.9 %collective-permute-start.18 = (bf16[8,32,1152]{2,1,0:T(8,128)(2,1)S(1)}, bf16[8,32,1152]{2,1,0:T(8,128)(2,1)}, u32[]{:S(2)}, u32[]{:S(2)}) collective-permute-start(bf16[8,32,1152]{2,1,0:T(8,128)(2,1)S(1)} %constant_dynamic-update-slice_fusion.17), channel_id=1, source_target_pairs={{0,2},{1,3},{2,0},{3,1},{4,6},{5,7},{6,4},{7,5},{8,10},{9,11},{10,... | collective-permute-start | bytes 1769480 | tf_op jit(solution)/shard_map/ppermute | solution.py:348
  335.0 41.5 %collective-permute-start.25 = (bf16[4,2,5,8,2816]{4,3,2,1,0:T(8,128)(2,1)S(1)}, bf16[4,2,5,8,2816]{4,3,2,1,0:T(8,128)(2,1)}, u32[]{:S(2)}, u32[]{:S(2)}) collective-permute-start(bf16[4,2,5,8,2816]{4,3,2,1,0:T(8,128)(2,1)S(1)} %fusion.1), channel_id=1, source_target_pairs={{0,4},{1,5},{2,6},{3,7},{4,0},{5,1},{6,2},{7,3},{8,12},{9,13},{10,... | collective-permute-start | bytes 5406728 | tf_op jit(solution)/shard_map/ppermute | solution.py:348
  335.8 39.5 %collective-permute-start.26 = (bf16[4,2,5,8,2688]{4,3,2,1,0:T(8,128)(2,1)S(1)}, bf16[4,2,5,8,2688]{4,3,2,1,0:T(8,128)(2,1)}, u32[]{:S(2)}, u32[]{:S(2)}) collective-permute-start(bf16[4,2,5,8,2688]{4,3,2,1,0:T(8,128)(2,1)S(1)} %add_convert_fusion.2), channel_id=1, source_target_pairs={{0,2},{1,3},{2,0},{3,1},{4,6},{5,7},{6,4},{7,5},{8,10},{9,11},{10,... | collective-permute-start | bytes 5160968 | tf_op jit(solution)/shard_map/ppermute | solution.py:348
  380.1 30.2 %collective-permute-start.27 = (bf16[4,5,8,2816]{3,2,1,0:T(8,128)(2,1)S(1)}, bf16[4,5,8,2816]{3,2,1,0:T(8,128)(2,1)S(1)}, u32[]{:S(2)}, u32[]{:S(2)}) collective-permute-start(bf16[4,5,8,2816]{3,2,1,0:T(8,128)(2,1)S(1)} %fusion.2), channel_id=1, source_target_pairs={{0,2},{1,3},{2,0},{3,1},{4,6},{5,7},{6,4},{7,5},{8,10},{9,11},{10,... | collective-permute-start | bytes 2703368 | tf_op jit(solution)/shard_map/ppermute | solution.py:348
  380.7 29.0 %collective-permute-start.28 = (bf16[4,5,8,2688]{3,2,1,0:T(8,128)(2,1)S(1)}, bf16[4,5,8,2688]{3,2,1,0:T(8,128)(2,1)S(1)}, u32[]{:S(2)}, u32[]{:S(2)}) collective-permute-start(bf16[4,5,8,2688]{3,2,1,0:T(8,128)(2,1)S(1)} %fusion.3), channel_id=1, source_target_pairs={{0,4},{1,5},{2,6},{3,7},{4,0},{5,1},{6,2},{7,3},{8,12},{9,13},{10,... | collective-permute-start | bytes 2580488 | tf_op jit(solution)/shard_map/ppermute | solution.py:348
  419.3 31.2 %collective-permute-start.29 = (bf16[5,8,5504]{2,1,0:T(8,128)(2,1)}, bf16[5,8,5504]{2,1,0:T(8,128)(2,1)}, u32[]{:S(2)}, u32[]{:S(2)}) collective-permute-start(bf16[5,8,5504]{2,1,0:T(8,128)(2,1)} %pad_maximum_fusion.2), channel_id=1, source_target_pairs={{0,8},{1,9},{2,10},{3,11},{4,12},{5,13},{6,14},{7,15},{8,0},{9,1},... | collective-permute-start | bytes 1320968 | tf_op jit(solution)/shard_map/ppermute | solution.py:348
  419.6 38.6 %collective-permute-start.30 = (bf16[5,8,5504]{2,1,0:T(8,128)(2,1)}, bf16[5,8,5504]{2,1,0:T(8,128)(2,1)}, u32[]{:S(2)}, u32[]{:S(2)}) collective-permute-start(bf16[5,8,5504]{2,1,0:T(8,128)(2,1)} %pad_maximum_fusion.3), channel_id=1, source_target_pairs={{0,16},{1,17},{2,18},{3,19},{4,20},{5,21},{6,22},{7,23},{8,24},{9,... | collective-permute-start | bytes 1320968 | tf_op jit(solution)/shard_map/ppermute | solution.py:348
  422.1 50.9 %collective-permute-start.31 = (bf16[5,8,5504]{2,1,0:T(8,128)(2,1)}, bf16[5,8,5504]{2,1,0:T(8,128)(2,1)}, u32[]{:S(2)}, u32[]{:S(2)}) collective-permute-start(bf16[5,8,5504]{2,1,0:T(8,128)(2,1)} %pad_maximum_fusion.4), channel_id=1, source_target_pairs={{0,24},{1,25},{2,26},{3,27},{4,28},{5,29},{6,30},{7,31},{8,16},{9,... | collective-permute-start | bytes 1320968 | tf_op jit(solution)/shard_map/ppermute | solution.py:348
  486.7 27.6 %collective-permute-start.35 = (bf16[4,2,5,8,1792]{4,3,2,1,0:T(8,128)(2,1)}, bf16[4,2,5,8,1792]{4,3,2,1,0:T(8,128)(2,1)}, u32[]{:S(2)}, u32[]{:S(2)}) collective-permute-start(bf16[4,2,5,8,1792]{4,3,2,1,0:T(8,128)(2,1)} %fusion.4), channel_id=1, source_target_pairs={{0,2},{1,3},{2,0},{3,1},{4,6},{5,7},{6,4},{7,5},{8,10},{9,11},{10,... | collective-permute-start | bytes 3440648 | tf_op jit(solution)/shard_map/ppermute | solution.py:348
  489.6 27.4 %collective-permute-start.34 = (bf16[4,2,5,8,1792]{4,3,2,1,0:T(8,128)(2,1)}, bf16[4,2,5,8,1792]{4,3,2,1,0:T(8,128)(2,1)}, u32[]{:S(2)}, u32[]{:S(2)}) collective-permute-start(bf16[4,2,5,8,1792]{4,3,2,1,0:T(8,128)(2,1)} %add_convert_fusion.6), channel_id=1, source_target_pairs={{0,4},{1,5},{2,6},{3,7},{4,0},{5,1},{6,2},{7,3},{8,12},{9,13},{10,... | collective-permute-start | bytes 3440648 | tf_op jit(solution)/shard_map/ppermute | solution.py:348
  539.4 22.5 %collective-permute-start.39 = (bf16[5,8,3584]{2,1,0:T(8,128)(2,1)}, bf16[5,8,3584]{2,1,0:T(8,128)(2,1)}, u32[]{:S(2)}, u32[]{:S(2)}) collective-permute-start(bf16[5,8,3584]{2,1,0:T(8,128)(2,1)} %pad_maximum_fusion.9), channel_id=1, source_target_pairs={{0,16},{1,17},{2,18},{3,19},{4,20},{5,21},{6,22},{7,23},{8,24},{9,... | collective-permute-start | bytes 860168 | tf_op jit(solution)/shard_map/ppermute | solution.py:348
  542.0 26.5 %collective-permute-start.40 = (bf16[5,8,3584]{2,1,0:T(8,128)(2,1)S(1)}, bf16[5,8,3584]{2,1,0:T(8,128)(2,1)}, u32[]{:S(2)}, u32[]{:S(2)}) collective-permute-start(bf16[5,8,3584]{2,1,0:T(8,128)(2,1)S(1)} %pad_maximum_fusion.10), channel_id=1, source_target_pairs={{0,24},{1,25},{2,26},{3,27},{4,28},{5,29},{6,30},{7,31},{8,16},{9,... | collective-permute-start | bytes 860168 | tf_op jit(solution)/shard_map/ppermute | solution.py:348
  (70 other events, 793.8 us)
Sparse Core Ops, SparseCore 0:
  17.5 175.0 all-gather.1
  336.5 153.0 reduce-scatter.3

commit v9 on v7

--- a/solution.py
+++ b/solution.py
@@ -687,7 +687,7 @@
     width = widths[VECTORS[0]]
     pieces = whole[:, : count * width].reshape(-1, count, width)
     pieces = pieces.transpose(1, 0, 2).reshape(count, -1).astype(f32)
-    found = {i: pieces[position] for position, i in enumerate(VECTORS[:-1])}
+    found = {i: pieces[position : position + 1] for position, i in enumerate(VECTORS[:-1])}
     last = widths[VECTORS[-1]]
     found[VECTORS[-1]] = whole[:, count * width : count * width + last].reshape(-1).astype(f32)
     return found
@@ -741,7 +741,9 @@
     if staged:
         sq, rest, down = fetch_pairs(narrow, core)
         rest = lax.all_gather(rest, "fsdp", axis=0, tiled=True)
+        sq, tokens = tie(sq, tokens)
         sq = gather_z(sq)
+        xhat_one, inverse_one = normalize(tokens)
         sq, down, xhat_one, inverse_one, grad_branch = tie(
             sq, down, xhat_one, inverse_one, grad_branch
         )
@@ -756,9 +758,9 @@
     else:
         weight_qkv, weight_o, weight_up, weight_down, vectors = gather_plain(narrow, widths)
 
-    vec = lambda i: vectors[i][:D]
+    vec = lambda i: vectors[i][:, :D]
     gain_one, shift_one, gain_two, shift_two = vec(0), vec(1), vec(9), vec(10)
-    bias_qkv = jnp.concatenate([vec(3), jnp.zeros((D,), f32), vec(6)])
+    bias_qkv = jnp.concatenate([vec(3), jnp.zeros((1, D), f32), vec(6)], axis=1)
     bias_o, bias_down = vec(8), vec(14)
     bias_up = pad_hidden(vectors[12][:FF].reshape(1, FF))
 
@@ -766,11 +768,11 @@
     qkv = (product(normed, weight_qkv) + bias_qkv).astype(bf16)
     if staged:
         qkv, down = tie(qkv, down)
-        down = gather_far(down)
+        down = [(*pair, swap(pair[0], 1)) for pair in gather_far(down)]
     mixed, lse = attn_fwd(qkv, 2)
     if staged:
         mixed, lse, down = tie(mixed, lse, down)
-        down = gather_core(down)
+        down = [(*parts, swap(parts[1], 1)) for parts in down]
         weight_up, weight_o, weight_down = place_rest(rest, down, where)
     resid = tokens + product(mixed, weight_o) + bias_o
     xhat_two, inverse_two = normalize(resid)
@@ -855,7 +857,8 @@
         inner_far = inner.far_swap(inner.far_sends((qkv_other, rows_other)))
         outer_z = outer.z_swap(outer_z)
         inner_far, layer_out = tie(inner_far, layer_out)
-        inner_near = inner.near_swap(inner.near_sends(inner_far))
+        inner_near, outer.near = tie(inner.near_sends(inner_far), outer.near)
+        inner_near = inner.near_swap(inner_near)
         outer_sum = outer.finish(outer_z)
         owned[11] = trim_hidden(outer_sum[:, :FF_PAD]).reshape(-1)
         owned[7] = outer_sum[:, FF_PAD:].reshape(-1)

time: 577 us -> 567 us (0.983)
    ppermute x42, waiting for transfers between devices: 161 us -> 147 us  [swap(): return lax.ppermute(value, 'fsdp', [(i, i ^ mask) for i in range(devices)])]
    optimization_barrier x1, waiting for transfers between devices: 0.01 us -> 9.19 us  [tie(): return form.unflatten(lax.optimization_barrier(leaves))]
    unnamed x128 -> x138, local copies, waits for them, and re-layouts: 12.9 us -> 12 us
  transfers between devices with their start and end apart: 44 -> 44, of which waited for: 20 -> 20; matrix products, arithmetic and copies ran while one was open for 20% -> 20% of each run, Pallas kernels for 18% -> 19%
where the time goes in v9:
time: 567 us; the launch traced here: 561 us
  Pallas kernels  203 us (36%)
  waiting for transfers between devices  156 us (28%)
  local copies, waits for them, and re-layouts  78.7 us (14%)
  other arithmetic  53.4 us (9%)
  starting transfers between devices  35.3 us (6%)
  matrix products  17.5 us (3%)
  between operations  16.5 us (3%)
    ppermute x42, waiting for transfers between devices, swap(): return lax.ppermute(value, 'fsdp', [(i, i ^ mask) for i in range(devices)])  147 us
    pallas_call x1, Pallas kernels, mlp(): pl.pallas_call(mlp_kernel, grid=(hidden // tile,), in_specs=[pl.BlockSpec...  78.9 us
    pallas_call x1, Pallas kernels, attn_bwd(): pl.pallas_call(functools.partial(bwd_kernel, tokens, krows, qrows, per),...  44.4 us
    ppermute x42, starting transfers between devices, swap(): return lax.ppermute(value, 'fsdp', [(i, i ^ mask) for i in range(devices)])  34.9 us
    pallas_call x1, Pallas kernels, attn_fwd(): pl.pallas_call(functools.partial(fwd_kernel, tokens, krows, qrows, per),...  28.6 us
    pallas_call x1, Pallas kernels, qkv_back(): pl.pallas_call(qkv_back_kernel, grid=(3,), in_specs=[pl.BlockSpec(memory_...  25.5 us
    pallas_call x1, Pallas kernels, place_rest(): pl.pallas_call(place_rest_kernel, in_specs=[pl.BlockSpec(memory_space=plt...  19.4 us
    reshape x24, local copies, waits for them, and re-layouts, window(): return result.reshape(kept)  19.4 us
  transfers between devices with their start and end apart: 44, of which 20 were waited for; matrix products, arithmetic and copies ran while one was open for 20% of the time, Pallas kernels for 19%

profile of v9, /device:TPU:8, one launch (start us, length us, event | category | flops | bytes accessed | tf_op | source)
XLA Modules:
  0.0 561.2 jit_solution(8368974110905132839)
XLA Ops:
  18.7 5.4 fusion.43
  32.6 12.3 %collective-permute-done.1 = bf16[40,3584]{1,0:T(8,128)(2,1)} collective-permute-done((bf16[40,3584]{1,0:T(8,128)(2,1)}, bf16[40,3584]{1,0:T(8,128)(2,1)}, u32[]{:S(2)}, u32[]{:S(2)}) %collective-permute-start.1) | collective-permute-done | bytes 286752 | tf_op jit(solution)/shard_map/ppermute | solution.py:346
  44.9 14.0 %collective-permute-done.2 = bf16[40,3584]{1,0:T(8,128)(2,1)} collective-permute-done((bf16[40,3584]{1,0:T(8,128)(2,1)}, bf16[40,3584]{1,0:T(8,128)(2,1)}, u32[]{:S(2)}, u32[]{:S(2)}) %collective-permute-start.2) | collective-permute-done | bytes 286752 | tf_op jit(solution)/shard_map/ppermute | solution.py:346
  58.9 7.8 %collective-permute-done.3 = bf16[40,3584]{1,0:T(8,128)(2,1)} collective-permute-done((bf16[40,3584]{1,0:T(8,128)(2,1)}, bf16[40,3584]{1,0:T(8,128)(2,1)}, u32[]{:S(2)}, u32[]{:S(2)}) %collective-permute-start.3) | collective-permute-done | bytes 286752 | tf_op jit(solution)/shard_map/ppermute | solution.py:346
  76.6 14.6 %collective-permute-done.6 = bf16[4,40,1792]{2,1,0:T(8,128)(2,1)S(1)} collective-permute-done((bf16[4,40,1792]{2,1,0:T(8,128)(2,1)S(1)}, bf16[4,40,1792]{2,1,0:T(8,128)(2,1)S(1)}, u32[]{:S(2)}, u32[]{:S(2)}) %collective-permute-start.6) | collective-permute-done | bytes 573472 | tf_op jit(solution)/shard_map/ppermute | solution.py:346
  92.7 6.5 %collective-permute-done.4 = bf16[4,40,1792]{2,1,0:T(8,128)(2,1)S(1)} collective-permute-done((bf16[4,40,1792]{2,1,0:T(8,128)(2,1)S(1)}, bf16[4,40,1792]{2,1,0:T(8,128)(2,1)S(1)}, u32[]{:S(2)}, u32[]{:S(2)}) %collective-permute-start.4) | collective-permute-done | bytes 573472 | tf_op jit(solution)/shard_map/ppermute | solution.py:346
  103.4 14.2 %collective-permute-done.10 = bf16[72,1152]{1,0:T(8,128)(2,1)} collective-permute-done((bf16[72,1152]{1,0:T(8,128)(2,1)}, bf16[72,1152]{1,0:T(8,128)(2,1)}, u32[]{:S(2)}, u32[]{:S(2)}) %collective-permute-start.10) | collective-permute-done | bytes 165920 | tf_op jit(solution)/shard_map/ppermute | solution.py:346
  118.8 5.7 %collective-permute-done.7 = bf16[8,40,1792]{2,1,0:T(8,128)(2,1)S(1)} collective-permute-done((bf16[8,40,1792]{2,1,0:T(8,128)(2,1)S(1)}, bf16[8,40,1792]{2,1,0:T(8,128)(2,1)S(1)}, u32[]{:S(2)}, u32[]{:S(2)}) %collective-permute-start.7) | collective-permute-done | bytes 1146912 | tf_op jit(solution)/shard_map/ppermute | solution.py:346
  138.3 6.7 %place_square.1 = (bf16[144,8,3456]{2,1,0:T(8,128)(2,1)}, bf16[32,5,8,128]{3,2,1,0:T(8,128)(2,1)S(1)}) custom-call(s32[4]{0:T(128)S(1)} %pad_add_fusion.coords, bf16[8,5,8,1792]{3,2,1,0:T(8,128)(2,1)S(1)} %bitcast.339, bf16[8,5,8,1792]{3,2,1,0:T(8,128)(2,1)} %bitcast.15.refs_1_, bf16[8,5,8,1792]{3,2,1,0:T(8,128)(2,1)S(1)} %bitcast.341, ...), custom_call_target="tpu_custom_call" | custom-call | bytes 18350080 | tf_op jit(solution)/shard_map/place_square/pallas_call | solution.py:411
  150.0 12.6 %add_convert_fusion.qkv_ref = bf16[729,3456]{1,0:T(8,128)(2,1)} fusion(bf16[729,1152]{1,0:T(8,128)(2,1)S(1)} %add_convert_fusion.4.normed_ref, f32[3456]{0:T(1024)S(1)} %fusion.32, bf16[144,8,3456]{2,1,0:T(8,128)(2,1)} %get-tuple-element.119), kind=kOutput, calls=%fused_computation | convolution fusion | flops 5809792000 | bytes 14694912 | tf_op jit(solution)/shard_map/dot_general | solution.py:333
  170.0 28.6 %attention_forward.1 = (bf16[729,1152]{1,0:T(8,128)(2,1)}, f32[16,1,768]{2,1,0:T(1,128)}) custom-call(bf16[729,3456]{1,0:T(8,128)(2,1)} %add_convert_fusion.qkv_ref), custom_call_target="tpu_custom_call" | custom-call | flops 4630511616 | bytes 6718464 | tf_op jit(solution)/shard_map/attention_forward/pallas_call | solution.py:63
  205.8 19.4 %place_rest.1 = (bf16[144,8,4352]{2,1,0:T(8,128)(2,1)}, bf16[144,8,1152]{2,1,0:T(8,128)(2,1)}, bf16[32,17,8,1152]{3,2,1,0:T(8,128)(2,1)}) custom-call(s32[4]{0:T(128)} %copy-done, bf16[32,33,8,1152]{3,2,1,0:T(8,128)(2,1)} %bitcast.346, bf16[8,5,8,1152]{3,2,1,0:T(8,128)(2,1)} %bitcast.367, bf16[8,5,8,1152]{3,2,1,0:T(8,128)(2,1)} %bitcast.372, ...), custom_call_target="tpu_custom_call" | custom-call | bytes 38928384 | tf_op jit(solution)/shard_map/place_rest/pallas_call | solution.py:479
  225.2 4.9 fusion.46
  235.0 78.9 %mlp_forward_backward.1 = (f32[729,1152]{1,0:T(8,128)}, bf16[16,40,4352]{2,1,0:T(8,128)(2,1)}, bf16[16,40,4352]{2,1,0:T(8,128)(2,1)}, f32[1,4352]{1,0:T(1,128)},...) custom-call(s32[4]{0:T(128)} %copy-done, ...), custom_call_target="tpu_custom_call" | custom-call | flops 1000000 | bytes 1000000 | tf_op jit(solution)/shard_map/mlp_forward_backward/pallas_call | solution.py:205
  315.8 7.5 %collective-permute-done.24 = bf16[4,2,2,5,8,1152]{5,4,3,2,1,0:T(8,128)(2,1)S(1)} collective-permute-done((bf16[4,2,2,5,8,1152]{5,4,3,2,1,0:T(8,128)(2,1)}, bf16[4,2,2,5,8,1152]{5,4,3,2,1,0:T(8,128)(2,1)S(1)}, u32[]{:S(2)}, u32[]{:S(2)}) %collective-permute-start.24) | collective-permute-done | bytes 1474592 | tf_op jit(solution)/shard_map/ppermute | solution.py:346
  353.7 44.4 %attention_backward.1.grad_ref = bf16[729,3456]{1,0:T(8,128)(2,1)} custom-call(bf16[729,3456]{1,0:T(8,128)(2,1)} %add_convert_fusion.qkv_ref, bf16[729,1152]{1,0:T(8,128)(2,1)} %get-tuple-element.145.go_ref, f32[16,1,768]{2,1,0:T(1,128)} %get-tuple-element.146.lse_ref), custom_call_target="tpu_custom_call" | custom-call | flops 1000000 | bytes 1000000 | tf_op jit(solution)/shard_map/attention_backward/pallas_call | solution.py:107
  409.5 25.5 %qkv_backward.1 = (bf16[16,40,3456]{2,1,0:T(8,128)(2,1)}, bf16[16,40,3456]{2,1,0:T(8,128)(2,1)}, f32[1,3456]{1,0:T(1,128)}, f32[8,1152]{1,0:T(8,128)}, f32[729,1152]{1,0:T(8,128)}) custom-call(s32[4]{0:T(128)} %copy-done, bf16[729,3456]{1,0:T(8,128)(2,1)} %attention_backward.1.grad_ref, bf16[729,1152]{1,0:T(8,128)(2,1)} %copy-done.5, ...), custom_call_target="tpu_custom_call" | custom-call | flops 1000000 | bytes 1000000 | tf_op jit(solution)/shard_map/qkv_backward/pallas_call | solution.py:276
  457.6 19.4 %collective-permute-done.32 = bf16[4,2,5,8,1792]{4,3,2,1,0:T(8,128)(2,1)S(1)} collective-permute-done((bf16[4,2,5,8,1792]{4,3,2,1,0:T(8,128)(2,1)S(1)}, bf16[4,2,5,8,1792]{4,3,2,1,0:T(8,128)(2,1)S(1)}, u32[]{:S(2)}, u32[]{:S(2)}) %collective-permute-start.32) | collective-permute-done | bytes 1146912 | tf_op jit(solution)/shard_map/ppermute | solution.py:346
  477.0 4.5 collective-permute-done.31
  489.3 11.2 %collective-permute-done.37 = bf16[5,8,5504]{2,1,0:T(8,128)(2,1)S(1)} collective-permute-done((bf16[5,8,5504]{2,1,0:T(8,128)(2,1)S(1)}, bf16[5,8,5504]{2,1,0:T(8,128)(2,1)S(1)}, u32[]{:S(2)}, u32[]{:S(2)}) %collective-permute-start.37) | collective-permute-done | bytes 440352 | tf_op jit(solution)/shard_map/ppermute | solution.py:346
  503.6 9.2 %reduce-scatter.4.cloned.1.call-done = bf16[136,1152]{1,0:T(8,128)(2,1)} async-done(((bf16[4352,1152]{1,0:T(8,128)(2,1)}), bf16[136,1152]{1,0:T(8,128)(2,1)}) %reduce-scatter.4.cloned.1.call-update) | async-done | bytes 313360 | tf_op jit(solution)/shard_map/optimization_barrier | solution.py:507
  526.0 8.2 %collective-permute-done.38 = bf16[5,8,3584]{2,1,0:T(8,128)(2,1)} collective-permute-done((bf16[5,8,3584]{2,1,0:T(8,128)(2,1)}, bf16[5,8,3584]{2,1,0:T(8,128)(2,1)}, u32[]{:S(2)}, u32[]{:S(2)}) %collective-permute-start.38) | collective-permute-done | bytes 286752 | tf_op jit(solution)/shard_map/ppermute | solution.py:346
  534.2 8.3 %collective-permute-done.39 = bf16[5,8,3584]{2,1,0:T(8,128)(2,1)} collective-permute-done((bf16[5,8,3584]{2,1,0:T(8,128)(2,1)}, bf16[5,8,3584]{2,1,0:T(8,128)(2,1)}, u32[]{:S(2)}, u32[]{:S(2)}) %collective-permute-start.39) | collective-permute-done | bytes 286752 | tf_op jit(solution)/shard_map/ppermute | solution.py:346
  542.5 6.7 %collective-permute-done.40 = bf16[5,8,3584]{2,1,0:T(8,128)(2,1)} collective-permute-done((bf16[5,8,3584]{2,1,0:T(8,128)(2,1)}, bf16[5,8,3584]{2,1,0:T(8,128)(2,1)}, u32[]{:S(2)}, u32[]{:S(2)}) %collective-permute-start.40) | collective-permute-done | bytes 286752 | tf_op jit(solution)/shard_map/ppermute | solution.py:346
  (405 shorter events, 168.5 us)
Async XLA Ops:
  7.2 197.5 %all-gather.2.cloned.1.call-start = ((), (), s32[]{:S(2)}) async-start(), calls=%async_computation.1 | async-start | bytes 20072448 | tf_op jit(solution)/shard_map/all_gather | solution.py:743
  17.4 495.5 %reduce-scatter.4.cloned.1.call-start = ((), (), s32[]{:S(2)}) async-start(), calls=%async_computation.2 | async-start | bytes 10340352
  24.8 34.1 %collective-permute-start.2 = (bf16[40,3584]{1,0:T(8,128)(2,1)}, bf16[40,3584]{1,0:T(8,128)(2,1)}, u32[]{:S(2)}, u32[]{:S(2)}) collective-permute-start(bf16[40,3584]{1,0:T(8,128)(2,1)} %pad_maximum_fusion.7), channel_id=1, source_target_pairs={{0,16},{1,17},{2,18},{3,19},{4,20},{5,21},{6,22},{7,23},{8,24},{9,... | collective-permute-start | bytes 860168 | tf_op jit(solution)/shard_map/ppermute | solution.py:346
  27.8 38.9 %collective-permute-start.3 = (bf16[40,3584]{1,0:T(8,128)(2,1)}, bf16[40,3584]{1,0:T(8,128)(2,1)}, u32[]{:S(2)}, u32[]{:S(2)}) collective-permute-start(bf16[40,3584]{1,0:T(8,128)(2,1)} %pad_maximum_fusion.7), channel_id=1, source_target_pairs={{0,24},{1,25},{2,26},{3,27},{4,28},{5,29},{6,30},{7,31},{8,16},{9,... | collective-permute-start | bytes 860168 | tf_op jit(solution)/shard_map/ppermute | solution.py:346
  71.0 28.2 %collective-permute-start.4 = (bf16[4,40,1792]{2,1,0:T(8,128)(2,1)S(1)}, bf16[4,40,1792]{2,1,0:T(8,128)(2,1)S(1)}, u32[]{:S(2)}, u32[]{:S(2)}) collective-permute-start(bf16[4,40,1792]{2,1,0:T(8,128)(2,1)S(1)} %pad_maximum_fusion), channel_id=1, source_target_pairs={{0,2},{1,3},{2,0},{3,1},{4,6},{5,7},{6,4},{7,5},{8,10},{9,11},{10,... | collective-permute-start | bytes 1720328 | tf_op jit(solution)/shard_map/ppermute | solution.py:346
  91.2 33.3 %collective-permute-start.7 = (bf16[8,40,1792]{2,1,0:T(8,128)(2,1)S(1)}, bf16[8,40,1792]{2,1,0:T(8,128)(2,1)S(1)}, u32[]{:S(2)}, u32[]{:S(2)}) collective-permute-start(bf16[8,40,1792]{2,1,0:T(8,128)(2,1)S(1)} %constant_dynamic-update-slice_fusion.10), channel_id=1, source_target_pairs={{0,2},{1,3},{2,0},{3,1},{4,6},{5,7},{6,4},{7,5},{8,10},{9,11},{10,... | collective-permute-start | bytes 3440648 | tf_op jit(solution)/shard_map/ppermute | solution.py:346
  128.9 33.7 %collective-permute-start.16 = (bf16[4,32,1152]{2,1,0:T(8,128)(2,1)}, bf16[4,32,1152]{2,1,0:T(8,128)(2,1)}, u32[]{:S(2)}, u32[]{:S(2)}) collective-permute-start(bf16[4,32,1152]{2,1,0:T(8,128)(2,1)} %pad_maximum_fusion.6), channel_id=1, source_target_pairs={{0,4},{1,5},{2,6},{3,7},{4,0},{5,1},{6,2},{7,3},{8,12},{9,13},{10,... | collective-permute-start | bytes 884744 | tf_op jit(solution)/shard_map/ppermute | solution.py:346
  135.8 26.8 %collective-permute-start.15 = (bf16[4,40,1152]{2,1,0:T(8,128)(2,1)}, bf16[4,40,1152]{2,1,0:T(8,128)(2,1)}, u32[]{:S(2)}, u32[]{:S(2)}) collective-permute-start(bf16[4,40,1152]{2,1,0:T(8,128)(2,1)} %pad_maximum_fusion.5), channel_id=1, source_target_pairs={{0,2},{1,3},{2,0},{3,1},{4,6},{5,7},{6,4},{7,5},{8,10},{9,11},{10,... | collective-permute-start | bytes 1105928 | tf_op jit(solution)/shard_map/ppermute | solution.py:346
  164.7 34.0 %collective-permute-start.17 = (bf16[8,40,1152]{2,1,0:T(8,128)(2,1)S(1)}, bf16[8,40,1152]{2,1,0:T(8,128)(2,1)S(1)}, u32[]{:S(2)}, u32[]{:S(2)}) collective-permute-start(bf16[8,40,1152]{2,1,0:T(8,128)(2,1)S(1)} %constant_dynamic-update-slice_fusion.15), channel_id=1, source_target_pairs={{0,4},{1,5},{2,6},{3,7},{4,0},{5,1},{6,2},{7,3},{8,12},{9,13},{10,... | collective-permute-start | bytes 2211848 | tf_op jit(solution)/shard_map/ppermute | solution.py:346
  166.2 32.4 %collective-permute-start.18 = (bf16[8,40,1152]{2,1,0:T(8,128)(2,1)S(1)}, bf16[8,40,1152]{2,1,0:T(8,128)(2,1)S(1)}, u32[]{:S(2)}, u32[]{:S(2)}) collective-permute-start(bf16[8,40,1152]{2,1,0:T(8,128)(2,1)S(1)} %constant_dynamic-update-slice_fusion.15), channel_id=1, source_target_pairs={{0,1},{1,0},{2,3},{3,2},{4,5},{5,4},{6,7},{7,6},{8,9},{9,8},{10,11... | collective-permute-start | bytes 2211848 | tf_op jit(solution)/shard_map/ppermute | solution.py:346
  168.3 30.3 %collective-permute-start.19 = (bf16[8,32,1152]{2,1,0:T(8,128)(2,1)S(1)}, bf16[8,32,1152]{2,1,0:T(8,128)(2,1)S(1)}, u32[]{:S(2)}, u32[]{:S(2)}) collective-permute-start(bf16[8,32,1152]{2,1,0:T(8,128)(2,1)S(1)} %constant_dynamic-update-slice_fusion.17), channel_id=1, source_target_pairs={{0,2},{1,3},{2,0},{3,1},{4,6},{5,7},{6,4},{7,5},{8,10},{9,11},{10,... | collective-permute-start | bytes 1769480 | tf_op jit(solution)/shard_map/ppermute | solution.py:346
  169.8 28.8 %collective-permute-start.20 = (bf16[8,32,1152]{2,1,0:T(8,128)(2,1)S(1)}, bf16[8,32,1152]{2,1,0:T(8,128)(2,1)S(1)}, u32[]{:S(2)}, u32[]{:S(2)}) collective-permute-start(bf16[8,32,1152]{2,1,0:T(8,128)(2,1)S(1)} %constant_dynamic-update-slice_fusion.17), channel_id=1, source_target_pairs={{0,1},{1,0},{2,3},{3,2},{4,5},{5,4},{6,7},{7,6},{8,9},{9,8},{10,11... | collective-permute-start | bytes 1769480 | tf_op jit(solution)/shard_map/ppermute | solution.py:346
  329.4 69.8 %collective-permute-start.25 = (bf16[4,2,5,8,2816]{4,3,2,1,0:T(8,128)(2,1)S(1)}, bf16[4,2,5,8,2816]{4,3,2,1,0:T(8,128)(2,1)}, u32[]{:S(2)}, u32[]{:S(2)}) collective-permute-start(bf16[4,2,5,8,2816]{4,3,2,1,0:T(8,128)(2,1)S(1)} %fusion.1), channel_id=1, source_target_pairs={{0,4},{1,5},{2,6},{3,7},{4,0},{5,1},{6,2},{7,3},{8,12},{9,13},{10,... | collective-permute-start | bytes 5406728 | tf_op jit(solution)/shard_map/ppermute | solution.py:346
  330.3 68.9 %collective-permute-start.26 = (bf16[4,2,5,8,2688]{4,3,2,1,0:T(8,128)(2,1)S(1)}, bf16[4,2,5,8,2688]{4,3,2,1,0:T(8,128)(2,1)}, u32[]{:S(2)}, u32[]{:S(2)}) collective-permute-start(bf16[4,2,5,8,2688]{4,3,2,1,0:T(8,128)(2,1)S(1)} %add_convert_fusion.2), channel_id=1, source_target_pairs={{0,2},{1,3},{2,0},{3,1},{4,6},{5,7},{6,4},{7,5},{8,10},{9,11},{10,... | collective-permute-start | bytes 5160968 | tf_op jit(solution)/shard_map/ppermute | solution.py:346
  403.2 31.8 %collective-permute-start.27 = (bf16[4,5,8,2816]{3,2,1,0:T(8,128)(2,1)S(1)}, bf16[4,5,8,2816]{3,2,1,0:T(8,128)(2,1)S(1)}, u32[]{:S(2)}, u32[]{:S(2)}) collective-permute-start(bf16[4,5,8,2816]{3,2,1,0:T(8,128)(2,1)S(1)} %fusion.2), channel_id=1, source_target_pairs={{0,2},{1,3},{2,0},{3,1},{4,6},{5,7},{6,4},{7,5},{8,10},{9,11},{10,... | collective-permute-start | bytes 2703368 | tf_op jit(solution)/shard_map/ppermute | solution.py:346
  404.7 30.3 %collective-permute-start.28 = (bf16[4,5,8,2688]{3,2,1,0:T(8,128)(2,1)S(1)}, bf16[4,5,8,2688]{3,2,1,0:T(8,128)(2,1)S(1)}, u32[]{:S(2)}, u32[]{:S(2)}) collective-permute-start(bf16[4,5,8,2688]{3,2,1,0:T(8,128)(2,1)S(1)} %fusion.3), channel_id=1, source_target_pairs={{0,4},{1,5},{2,6},{3,7},{4,0},{5,1},{6,2},{7,3},{8,12},{9,13},{10,... | collective-permute-start | bytes 2580488 | tf_op jit(solution)/shard_map/ppermute | solution.py:346
  447.0 30.0 %collective-permute-start.32 = (bf16[4,2,5,8,1792]{4,3,2,1,0:T(8,128)(2,1)S(1)}, bf16[4,2,5,8,1792]{4,3,2,1,0:T(8,128)(2,1)S(1)}, u32[]{:S(2)}, u32[]{:S(2)}) collective-permute-start(bf16[4,2,5,8,1792]{4,3,2,1,0:T(8,128)(2,1)S(1)} %fusion.4), channel_id=1, source_target_pairs={{0,2},{1,3},{2,0},{3,1},{4,6},{5,7},{6,4},{7,5},{8,10},{9,11},{10,... | collective-permute-start | bytes 3440648 | tf_op jit(solution)/shard_map/ppermute | solution.py:346
  449.0 32.4 %collective-permute-start.31 = (bf16[4,2,5,8,1792]{4,3,2,1,0:T(8,128)(2,1)S(1)}, bf16[4,2,5,8,1792]{4,3,2,1,0:T(8,128)(2,1)S(1)}, u32[]{:S(2)}, u32[]{:S(2)}) collective-permute-start(bf16[4,2,5,8,1792]{4,3,2,1,0:T(8,128)(2,1)S(1)} %add_convert_fusion.6), channel_id=1, source_target_pairs={{0,4},{1,5},{2,6},{3,7},{4,0},{5,1},{6,2},{7,3},{8,12},{9,13},{10,... | collective-permute-start | bytes 3440648 | tf_op jit(solution)/shard_map/ppermute | solution.py:346
  450.5 38.8 %collective-permute-start.35 = (bf16[5,8,5504]{2,1,0:T(8,128)(2,1)S(1)}, bf16[5,8,5504]{2,1,0:T(8,128)(2,1)S(1)}, u32[]{:S(2)}, u32[]{:S(2)}) collective-permute-start(bf16[5,8,5504]{2,1,0:T(8,128)(2,1)S(1)} %pad_maximum_fusion.2), channel_id=1, source_target_pairs={{0,8},{1,9},{2,10},{3,11},{4,12},{5,13},{6,14},{7,15},{8,0},{9,1},... | collective-permute-start | bytes 1320968 | tf_op jit(solution)/shard_map/ppermute | solution.py:346
  450.7 38.5 %collective-permute-start.36 = (bf16[5,8,5504]{2,1,0:T(8,128)(2,1)S(1)}, bf16[5,8,5504]{2,1,0:T(8,128)(2,1)S(1)}, u32[]{:S(2)}, u32[]{:S(2)}) collective-permute-start(bf16[5,8,5504]{2,1,0:T(8,128)(2,1)S(1)} %pad_maximum_fusion.3), channel_id=1, source_target_pairs={{0,16},{1,17},{2,18},{3,19},{4,20},{5,21},{6,22},{7,23},{8,24},{9,... | collective-permute-start | bytes 1320968 | tf_op jit(solution)/shard_map/ppermute | solution.py:346
  453.4 47.1 %collective-permute-start.37 = (bf16[5,8,5504]{2,1,0:T(8,128)(2,1)S(1)}, bf16[5,8,5504]{2,1,0:T(8,128)(2,1)S(1)}, u32[]{:S(2)}, u32[]{:S(2)}) collective-permute-start(bf16[5,8,5504]{2,1,0:T(8,128)(2,1)S(1)} %pad_maximum_fusion.4), channel_id=1, source_target_pairs={{0,24},{1,25},{2,26},{3,27},{4,28},{5,29},{6,30},{7,31},{8,16},{9,... | collective-permute-start | bytes 1320968 | tf_op jit(solution)/shard_map/ppermute | solution.py:346
  486.1 26.7 %collective-permute-start.33 = (bf16[4,5,8,1792]{3,2,1,0:T(8,128)(2,1)}, bf16[4,5,8,1792]{3,2,1,0:T(8,128)(2,1)S(1)}, u32[]{:S(2)}, u32[]{:S(2)}) collective-permute-start(bf16[4,5,8,1792]{3,2,1,0:T(8,128)(2,1)} %fusion.6), channel_id=1, source_target_pairs={{0,2},{1,3},{2,0},{3,1},{4,6},{5,7},{6,4},{7,5},{8,10},{9,11},{10,... | collective-permute-start | bytes 1720328 | tf_op jit(solution)/shard_map/ppermute | solution.py:346
  487.7 26.0 %collective-permute-start.34 = (bf16[4,5,8,1792]{3,2,1,0:T(8,128)(2,1)}, bf16[4,5,8,1792]{3,2,1,0:T(8,128)(2,1)}, u32[]{:S(2)}, u32[]{:S(2)}) collective-permute-start(bf16[4,5,8,1792]{3,2,1,0:T(8,128)(2,1)} %fusion.5), channel_id=1, source_target_pairs={{0,4},{1,5},{2,6},{3,7},{4,0},{5,1},{6,2},{7,3},{8,12},{9,13},{10,... | collective-permute-start | bytes 1720328 | tf_op jit(solution)/shard_map/ppermute | solution.py:346
  522.6 26.5 %collective-permute-start.40 = (bf16[5,8,3584]{2,1,0:T(8,128)(2,1)}, bf16[5,8,3584]{2,1,0:T(8,128)(2,1)}, u32[]{:S(2)}, u32[]{:S(2)}) collective-permute-start(bf16[5,8,3584]{2,1,0:T(8,128)(2,1)} %pad_maximum_fusion.10), channel_id=1, source_target_pairs={{0,24},{1,25},{2,26},{3,27},{4,28},{5,29},{6,30},{7,31},{8,16},{9,... | collective-permute-start | bytes 860168 | tf_op jit(solution)/shard_map/ppermute | solution.py:346
  (82 other events, 674.0 us)
Sparse Core Ops, SparseCore 0:
  17.5 175.0 all-gather.1
  348.1 164.7 reduce-scatter.3

commit v10 on v9

--- a/solution.py
+++ b/solution.py
@@ -693,15 +693,11 @@
     return found
 
 
-def pack_vectors(grads, widths, devices):
-    count = len(VECTORS) - 1
-    width = widths[VECTORS[0]]
-    rows = jnp.stack([grads[i] for i in VECTORS[:-1]])
+def pack_vectors(vectors, width, devices):
+    rows = jnp.stack(vectors)
     rows = jnp.pad(rows, ((0, 0), (0, width * devices - rows.shape[1])))
-    rows = rows.reshape(count, devices, width).transpose(1, 0, 2).reshape(devices, -1)
-    last = grads[VECTORS[-1]]
-    last = jnp.pad(last, (0, widths[VECTORS[-1]] * devices - last.shape[0]))
-    return jnp.concatenate([rows, last.reshape(devices, -1)], axis=1)
+    rows = rows.reshape(len(vectors), devices, width)
+    return rows.transpose(1, 0, 2).reshape(devices, -1)
 
 
 def gather_plain(narrow, widths):
@@ -805,6 +801,14 @@
     up_bias_grad = up_bias_grad.reshape(FF_PAD)
     layer_out = weight_img * (resid + branch + bias_down)
     grads[9], grads[10], grads[8] = sums_two[0], sums_two[1], sums_two[2]
+    hidden_grad = trim_hidden(up_bias_grad.reshape(1, FF_PAD)).reshape(FF)
+    early = jnp.concatenate(
+        [
+            pack_vectors([grads[i] for i in VECTORS[4:8]], widths[0], devices),
+            pack_vectors([hidden_grad], widths[12], devices),
+        ],
+        axis=1,
+    )
     if staged:
         down_sum = lax.psum_scatter(down_grad, "fsdp", scatter_dimension=0, tiled=True)
     if staged:
@@ -812,7 +816,8 @@
             (up_keep, o_keep), (((0, 0, UP_CUT),), ((0, UP_CUT, FF_PAD), (1, 0, D))), coords
         )
         outer_other = outer.core_step((up_send, o_send))
-        grad_mixed, outer_other = tie(grad_mixed, outer_other)
+        early = early.astype(bf16)
+        grad_mixed, outer_other, early = tie(grad_mixed, outer_other, early)
         outer_far = outer.far_swap(outer.far_sends(outer_other))
     grad_qkv = attn_bwd(qkv, grad_mixed, lse, 2)
     if staged:
@@ -838,9 +843,11 @@
         qkv_other = outer.core_step((qkv_send,))[0]
     grads[3], grads[6] = qkv_bias_grad[0, :D], qkv_bias_grad[0, 2 * D :]
     grads[0], grads[1] = norm_sums[0], norm_sums[1]
-    grads[12] = trim_hidden(up_bias_grad.reshape(1, FF_PAD)).reshape(FF)
-
-    rows = pack_vectors(grads, widths, devices)
+
+    late = [grads[i] for i in VECTORS[:4]]
+    rows = jnp.concatenate(
+        [pack_vectors(late, widths[0], devices).astype(early.dtype), early], axis=1
+    )
     owned = [None] * 15
     if staged:
         rows = jnp.pad(rows, ((0, 0), (0, OWN_ROWS * EXTRA - rows.shape[1])))

time: 567 us -> 544 us (0.959)
  local copies, waits for them, and re-layouts: 78.7 us -> 65.1 us
  waiting for transfers between devices: 156 us -> 146 us
    optimization_barrier x1, waiting for transfers between devices: 9.19 us -> 0.01 us  [tie(): return form.unflatten(lax.optimization_barrier(leaves))]
    unnamed x138 -> x134, local copies, waits for them, and re-layouts: 12 us -> 11.4 us
  transfers between devices with their start and end apart: 44 -> 44, of which waited for: 20 -> 19; matrix products, arithmetic and copies ran while one was open for 20% -> 20% of each run, Pallas kernels for 19% -> 19%
where the time goes in v10:
time: 544 us; the launch traced here: 539 us
  Pallas kernels  203 us (37%)
  waiting for transfers between devices  146 us (27%)
  local copies, waits for them, and re-layouts  65.1 us (12%)
  other arithmetic  56 us (10%)
  starting transfers between devices  34.2 us (6%)
  matrix products  17.6 us (3%)
  between operations  16.5 us (3%)
    ppermute x42, waiting for transfers between devices, swap(): return lax.ppermute(value, 'fsdp', [(i, i ^ mask) for i in range(devices)])  146 us
    pallas_call x1, Pallas kernels, mlp(): pl.pallas_call(mlp_kernel, grid=(hidden // tile,), in_specs=[pl.BlockSpec...  78.9 us
    pallas_call x1, Pallas kernels, attn_bwd(): pl.pallas_call(functools.partial(bwd_kernel, tokens, krows, qrows, per),...  44.3 us
    ppermute x42, starting transfers between devices, swap(): return lax.ppermute(value, 'fsdp', [(i, i ^ mask) for i in range(devices)])  33.8 us
    pallas_call x1, Pallas kernels, attn_fwd(): pl.pallas_call(functools.partial(fwd_kernel, tokens, krows, qrows, per),...  28.7 us
    pallas_call x1, Pallas kernels, qkv_back(): pl.pallas_call(qkv_back_kernel, grid=(3,), in_specs=[pl.BlockSpec(memory_...  25.5 us
    pallas_call x1, Pallas kernels, place_rest(): pl.pallas_call(place_rest_kernel, in_specs=[pl.BlockSpec(memory_space=plt...  19.4 us
    reshape x24, local copies, waits for them, and re-layouts, window(): return result.reshape(kept)  18.4 us
  transfers between devices with their start and end apart: 44, of which 19 were waited for; matrix products, arithmetic and copies ran while one was open for 20% of the time, Pallas kernels for 19%

profile of v10, /device:TPU:8, one launch (start us, length us, event | category | flops | bytes accessed | tf_op | source)
XLA Modules:
  0.0 539.1 jit_solution(7307987268926493863)
XLA Ops:
  18.7 5.4 %fusion.43 = (bf16[1152]{0:T(1024)(128)(2,1)}, bf16[729,1152]{1,0:T(8,128)(2,1)}, f32[729,1152]{1,0:T(8,128)}) fusion(f32[729,1152]{1,0:T(8,128)} %param.35, f32[]{:T(128)} %bitcast.5), kind=kLoop, calls=%fused_computation.233 | loop fusion | flops 2518272 | bytes 8400388 | tf_op jit(solution)/shard_map/reduce_sum | solution.py:734
  24.8 3.0 collective-permute-start.2
  32.6 12.3 %collective-permute-done.1 = bf16[40,3584]{1,0:T(8,128)(2,1)} collective-permute-done((bf16[40,3584]{1,0:T(8,128)(2,1)}, bf16[40,3584]{1,0:T(8,128)(2,1)}, u32[]{:S(2)}, u32[]{:S(2)}) %collective-permute-start.1) | collective-permute-done | bytes 286752 | tf_op jit(solution)/shard_map/ppermute | solution.py:346
  44.9 14.7 %collective-permute-done.2 = bf16[40,3584]{1,0:T(8,128)(2,1)} collective-permute-done((bf16[40,3584]{1,0:T(8,128)(2,1)}, bf16[40,3584]{1,0:T(8,128)(2,1)}, u32[]{:S(2)}, u32[]{:S(2)}) %collective-permute-start.2) | collective-permute-done | bytes 286752 | tf_op jit(solution)/shard_map/ppermute | solution.py:346
  59.6 7.1 %collective-permute-done.3 = bf16[40,3584]{1,0:T(8,128)(2,1)} collective-permute-done((bf16[40,3584]{1,0:T(8,128)(2,1)}, bf16[40,3584]{1,0:T(8,128)(2,1)}, u32[]{:S(2)}, u32[]{:S(2)}) %collective-permute-start.3) | collective-permute-done | bytes 286752 | tf_op jit(solution)/shard_map/ppermute | solution.py:346
  76.7 14.5 %collective-permute-done.6 = bf16[4,40,1792]{2,1,0:T(8,128)(2,1)S(1)} collective-permute-done((bf16[4,40,1792]{2,1,0:T(8,128)(2,1)S(1)}, bf16[4,40,1792]{2,1,0:T(8,128)(2,1)S(1)}, u32[]{:S(2)}, u32[]{:S(2)}) %collective-permute-start.6) | collective-permute-done | bytes 573472 | tf_op jit(solution)/shard_map/ppermute | solution.py:346
  92.8 6.5 %collective-permute-done.4 = bf16[4,40,1792]{2,1,0:T(8,128)(2,1)S(1)} collective-permute-done((bf16[4,40,1792]{2,1,0:T(8,128)(2,1)S(1)}, bf16[4,40,1792]{2,1,0:T(8,128)(2,1)S(1)}, u32[]{:S(2)}, u32[]{:S(2)}) %collective-permute-start.4) | collective-permute-done | bytes 573472 | tf_op jit(solution)/shard_map/ppermute | solution.py:346
  103.4 14.0 %collective-permute-done.10 = bf16[72,1152]{1,0:T(8,128)(2,1)} collective-permute-done((bf16[72,1152]{1,0:T(8,128)(2,1)}, bf16[72,1152]{1,0:T(8,128)(2,1)}, u32[]{:S(2)}, u32[]{:S(2)}) %collective-permute-start.10) | collective-permute-done | bytes 165920 | tf_op jit(solution)/shard_map/ppermute | solution.py:346
  118.6 5.9 %collective-permute-done.7 = bf16[8,40,1792]{2,1,0:T(8,128)(2,1)S(1)} collective-permute-done((bf16[8,40,1792]{2,1,0:T(8,128)(2,1)S(1)}, bf16[8,40,1792]{2,1,0:T(8,128)(2,1)S(1)}, u32[]{:S(2)}, u32[]{:S(2)}) %collective-permute-start.7) | collective-permute-done | bytes 1146912 | tf_op jit(solution)/shard_map/ppermute | solution.py:346
  138.3 6.6 %place_square.1 = (bf16[144,8,3456]{2,1,0:T(8,128)(2,1)}, bf16[32,5,8,128]{3,2,1,0:T(8,128)(2,1)S(1)}) custom-call(s32[4]{0:T(128)S(1)} %pad_add_fusion.coords, bf16[8,5,8,1792]{3,2,1,0:T(8,128)(2,1)S(1)} %bitcast.343, bf16[8,5,8,1792]{3,2,1,0:T(8,128)(2,1)} %bitcast.15.refs_1_, bf16[8,5,8,1792]{3,2,1,0:T(8,128)(2,1)S(1)} %bitcast.345, ...), custom_call_target="tpu_custom_call" | custom-call | bytes 18350080 | tf_op jit(solution)/shard_map/place_square/pallas_call | solution.py:411
  149.9 12.7 %add_convert_fusion.qkv_ref = bf16[729,3456]{1,0:T(8,128)(2,1)} fusion(bf16[729,1152]{1,0:T(8,128)(2,1)S(1)} %add_convert_fusion.4.normed_ref, f32[3456]{0:T(1024)S(1)} %fusion.32, bf16[144,8,3456]{2,1,0:T(8,128)(2,1)} %get-tuple-element.120), kind=kOutput, calls=%fused_computation | convolution fusion | flops 5809792000 | bytes 14694912 | tf_op jit(solution)/shard_map/dot_general | solution.py:333
  170.1 28.7 %attention_forward.1 = (bf16[729,1152]{1,0:T(8,128)(2,1)}, f32[16,1,768]{2,1,0:T(1,128)}) custom-call(bf16[729,3456]{1,0:T(8,128)(2,1)} %add_convert_fusion.qkv_ref), custom_call_target="tpu_custom_call" | custom-call | flops 4630511616 | bytes 6718464 | tf_op jit(solution)/shard_map/attention_forward/pallas_call | solution.py:63
  205.8 19.4 %place_rest.1 = (bf16[144,8,4352]{2,1,0:T(8,128)(2,1)}, bf16[144,8,1152]{2,1,0:T(8,128)(2,1)}, bf16[32,17,8,1152]{3,2,1,0:T(8,128)(2,1)}) custom-call(s32[4]{0:T(128)} %copy-done, bf16[32,33,8,1152]{3,2,1,0:T(8,128)(2,1)} %bitcast.350, bf16[8,5,8,1152]{3,2,1,0:T(8,128)(2,1)} %bitcast.373, bf16[8,5,8,1152]{3,2,1,0:T(8,128)(2,1)} %bitcast.378, ...), custom_call_target="tpu_custom_call" | custom-call | bytes 38928384 | tf_op jit(solution)/shard_map/place_rest/pallas_call | solution.py:479
  225.3 4.9 fusion.47
  232.1 3.0 add_convert_fusion.3
  235.1 78.9 %mlp_forward_backward.1 = (f32[729,1152]{1,0:T(8,128)}, bf16[16,40,4352]{2,1,0:T(8,128)(2,1)}, bf16[16,40,4352]{2,1,0:T(8,128)(2,1)}, f32[1,4352]{1,0:T(1,128)},...) custom-call(s32[4]{0:T(128)} %copy-done, ...), custom_call_target="tpu_custom_call" | custom-call | flops 1000000 | bytes 1000000 | tf_op jit(solution)/shard_map/mlp_forward_backward/pallas_call | solution.py:205
  329.1 2.7 fusion.1
  334.5 44.3 %attention_backward.1.grad_ref = bf16[729,3456]{1,0:T(8,128)(2,1)} custom-call(bf16[729,3456]{1,0:T(8,128)(2,1)} %add_convert_fusion.qkv_ref, bf16[729,1152]{1,0:T(8,128)(2,1)} %get-tuple-element.148.go_ref, f32[16,1,768]{2,1,0:T(1,128)} %get-tuple-element.149.lse_ref), custom_call_target="tpu_custom_call" | custom-call | flops 1000000 | bytes 1000000 | tf_op jit(solution)/shard_map/attention_backward/pallas_call | solution.py:107
  393.1 25.5 %qkv_backward.1 = (bf16[16,40,3456]{2,1,0:T(8,128)(2,1)}, bf16[16,40,3456]{2,1,0:T(8,128)(2,1)}, f32[1,3456]{1,0:T(1,128)}, f32[8,1152]{1,0:T(8,128)}, f32[729,1152]{1,0:T(8,128)}) custom-call(s32[4]{0:T(128)} %copy-done, bf16[729,3456]{1,0:T(8,128)(2,1)} %attention_backward.1.grad_ref, bf16[729,1152]{1,0:T(8,128)(2,1)} %copy-done.5, ...), custom_call_target="tpu_custom_call" | custom-call | flops 1000000 | bytes 1000000 | tf_op jit(solution)/shard_map/qkv_backward/pallas_call | solution.py:276
  440.9 16.3 %collective-permute-done.32 = bf16[4,2,5,8,1792]{4,3,2,1,0:T(8,128)(2,1)S(1)} collective-permute-done((bf16[4,2,5,8,1792]{4,3,2,1,0:T(8,128)(2,1)S(1)}, bf16[4,2,5,8,1792]{4,3,2,1,0:T(8,128)(2,1)S(1)}, u32[]{:S(2)}, u32[]{:S(2)}) %collective-permute-start.32) | collective-permute-done | bytes 1146912 | tf_op jit(solution)/shard_map/ppermute | solution.py:346
  466.9 20.7 %collective-permute-done.37 = bf16[5,8,5504]{2,1,0:T(8,128)(2,1)S(1)} collective-permute-done((bf16[5,8,5504]{2,1,0:T(8,128)(2,1)S(1)}, bf16[5,8,5504]{2,1,0:T(8,128)(2,1)S(1)}, u32[]{:S(2)}, u32[]{:S(2)}) %collective-permute-start.37) | collective-permute-done | bytes 440352 | tf_op jit(solution)/shard_map/ppermute | solution.py:346
  504.0 6.2 %collective-permute-done.38 = bf16[5,8,3584]{2,1,0:T(8,128)(2,1)} collective-permute-done((bf16[5,8,3584]{2,1,0:T(8,128)(2,1)}, bf16[5,8,3584]{2,1,0:T(8,128)(2,1)}, u32[]{:S(2)}, u32[]{:S(2)}) %collective-permute-start.38) | collective-permute-done | bytes 286752 | tf_op jit(solution)/shard_map/ppermute | solution.py:346
  510.1 9.6 %collective-permute-done.39 = bf16[5,8,3584]{2,1,0:T(8,128)(2,1)} collective-permute-done((bf16[5,8,3584]{2,1,0:T(8,128)(2,1)}, bf16[5,8,3584]{2,1,0:T(8,128)(2,1)}, u32[]{:S(2)}, u32[]{:S(2)}) %collective-permute-start.39) | collective-permute-done | bytes 286752 | tf_op jit(solution)/shard_map/ppermute | solution.py:346
  519.7 7.4 %collective-permute-done.40 = bf16[5,8,3584]{2,1,0:T(8,128)(2,1)} collective-permute-done((bf16[5,8,3584]{2,1,0:T(8,128)(2,1)}, bf16[5,8,3584]{2,1,0:T(8,128)(2,1)}, u32[]{:S(2)}, u32[]{:S(2)}) %collective-permute-start.40) | collective-permute-done | bytes 286752 | tf_op jit(solution)/shard_map/ppermute | solution.py:346
  (403 shorter events, 152.2 us)
Async XLA Ops:
  7.2 197.6 %all-gather.2.cloned.1.call-start = ((), (), s32[]{:S(2)}) async-start(), calls=%async_computation.1 | async-start | bytes 20072448 | tf_op jit(solution)/shard_map/all_gather | solution.py:739
  17.4 473.4 %reduce-scatter.4.cloned.1.call-start = ((), (), s32[]{:S(2)}) async-start(), calls=%async_computation.2 | async-start | bytes 10340352
  24.8 34.8 %collective-permute-start.2 = (bf16[40,3584]{1,0:T(8,128)(2,1)}, bf16[40,3584]{1,0:T(8,128)(2,1)}, u32[]{:S(2)}, u32[]{:S(2)}) collective-permute-start(bf16[40,3584]{1,0:T(8,128)(2,1)} %pad_maximum_fusion.7), channel_id=1, source_target_pairs={{0,16},{1,17},{2,18},{3,19},{4,20},{5,21},{6,22},{7,23},{8,24},{9,... | collective-permute-start | bytes 860168 | tf_op jit(solution)/shard_map/ppermute | solution.py:346
  27.9 38.9 %collective-permute-start.3 = (bf16[40,3584]{1,0:T(8,128)(2,1)}, bf16[40,3584]{1,0:T(8,128)(2,1)}, u32[]{:S(2)}, u32[]{:S(2)}) collective-permute-start(bf16[40,3584]{1,0:T(8,128)(2,1)} %pad_maximum_fusion.7), channel_id=1, source_target_pairs={{0,24},{1,25},{2,26},{3,27},{4,28},{5,29},{6,30},{7,31},{8,16},{9,... | collective-permute-start | bytes 860168 | tf_op jit(solution)/shard_map/ppermute | solution.py:346
  71.1 28.2 %collective-permute-start.4 = (bf16[4,40,1792]{2,1,0:T(8,128)(2,1)S(1)}, bf16[4,40,1792]{2,1,0:T(8,128)(2,1)S(1)}, u32[]{:S(2)}, u32[]{:S(2)}) collective-permute-start(bf16[4,40,1792]{2,1,0:T(8,128)(2,1)S(1)} %pad_maximum_fusion), channel_id=1, source_target_pairs={{0,2},{1,3},{2,0},{3,1},{4,6},{5,7},{6,4},{7,5},{8,10},{9,11},{10,... | collective-permute-start | bytes 1720328 | tf_op jit(solution)/shard_map/ppermute | solution.py:346
  91.2 33.3 %collective-permute-start.7 = (bf16[8,40,1792]{2,1,0:T(8,128)(2,1)S(1)}, bf16[8,40,1792]{2,1,0:T(8,128)(2,1)S(1)}, u32[]{:S(2)}, u32[]{:S(2)}) collective-permute-start(bf16[8,40,1792]{2,1,0:T(8,128)(2,1)S(1)} %constant_dynamic-update-slice_fusion.10), channel_id=1, source_target_pairs={{0,2},{1,3},{2,0},{3,1},{4,6},{5,7},{6,4},{7,5},{8,10},{9,11},{10,... | collective-permute-start | bytes 3440648 | tf_op jit(solution)/shard_map/ppermute | solution.py:346
  128.9 33.7 %collective-permute-start.16 = (bf16[4,32,1152]{2,1,0:T(8,128)(2,1)}, bf16[4,32,1152]{2,1,0:T(8,128)(2,1)}, u32[]{:S(2)}, u32[]{:S(2)}) collective-permute-start(bf16[4,32,1152]{2,1,0:T(8,128)(2,1)} %pad_maximum_fusion.6), channel_id=1, source_target_pairs={{0,4},{1,5},{2,6},{3,7},{4,0},{5,1},{6,2},{7,3},{8,12},{9,13},{10,... | collective-permute-start | bytes 884744 | tf_op jit(solution)/shard_map/ppermute | solution.py:346
  135.8 26.8 %collective-permute-start.15 = (bf16[4,40,1152]{2,1,0:T(8,128)(2,1)}, bf16[4,40,1152]{2,1,0:T(8,128)(2,1)}, u32[]{:S(2)}, u32[]{:S(2)}) collective-permute-start(bf16[4,40,1152]{2,1,0:T(8,128)(2,1)} %pad_maximum_fusion.5), channel_id=1, source_target_pairs={{0,2},{1,3},{2,0},{3,1},{4,6},{5,7},{6,4},{7,5},{8,10},{9,11},{10,... | collective-permute-start | bytes 1105928 | tf_op jit(solution)/shard_map/ppermute | solution.py:346
  164.7 34.1 %collective-permute-start.17 = (bf16[8,40,1152]{2,1,0:T(8,128)(2,1)S(1)}, bf16[8,40,1152]{2,1,0:T(8,128)(2,1)S(1)}, u32[]{:S(2)}, u32[]{:S(2)}) collective-permute-start(bf16[8,40,1152]{2,1,0:T(8,128)(2,1)S(1)} %constant_dynamic-update-slice_fusion.15), channel_id=1, source_target_pairs={{0,4},{1,5},{2,6},{3,7},{4,0},{5,1},{6,2},{7,3},{8,12},{9,13},{10,... | collective-permute-start | bytes 2211848 | tf_op jit(solution)/shard_map/ppermute | solution.py:346
  166.3 32.6 %collective-permute-start.18 = (bf16[8,40,1152]{2,1,0:T(8,128)(2,1)S(1)}, bf16[8,40,1152]{2,1,0:T(8,128)(2,1)S(1)}, u32[]{:S(2)}, u32[]{:S(2)}) collective-permute-start(bf16[8,40,1152]{2,1,0:T(8,128)(2,1)S(1)} %constant_dynamic-update-slice_fusion.15), channel_id=1, source_target_pairs={{0,1},{1,0},{2,3},{3,2},{4,5},{5,4},{6,7},{7,6},{8,9},{9,8},{10,11... | collective-permute-start | bytes 2211848 | tf_op jit(solution)/shard_map/ppermute | solution.py:346
  168.3 30.4 %collective-permute-start.19 = (bf16[8,32,1152]{2,1,0:T(8,128)(2,1)S(1)}, bf16[8,32,1152]{2,1,0:T(8,128)(2,1)S(1)}, u32[]{:S(2)}, u32[]{:S(2)}) collective-permute-start(bf16[8,32,1152]{2,1,0:T(8,128)(2,1)S(1)} %constant_dynamic-update-slice_fusion.17), channel_id=1, source_target_pairs={{0,2},{1,3},{2,0},{3,1},{4,6},{5,7},{6,4},{7,5},{8,10},{9,11},{10,... | collective-permute-start | bytes 1769480 | tf_op jit(solution)/shard_map/ppermute | solution.py:346
  169.8 28.9 %collective-permute-start.20 = (bf16[8,32,1152]{2,1,0:T(8,128)(2,1)S(1)}, bf16[8,32,1152]{2,1,0:T(8,128)(2,1)S(1)}, u32[]{:S(2)}, u32[]{:S(2)}) collective-permute-start(bf16[8,32,1152]{2,1,0:T(8,128)(2,1)S(1)} %constant_dynamic-update-slice_fusion.17), channel_id=1, source_target_pairs={{0,1},{1,0},{2,3},{3,2},{4,5},{5,4},{6,7},{7,6},{8,9},{9,8},{10,11... | collective-permute-start | bytes 1769480 | tf_op jit(solution)/shard_map/ppermute | solution.py:346
  328.6 52.3 %collective-permute-start.26 = (bf16[4,2,5,8,2688]{4,3,2,1,0:T(8,128)(2,1)}, bf16[4,2,5,8,2688]{4,3,2,1,0:T(8,128)(2,1)}, u32[]{:S(2)}, u32[]{:S(2)}) collective-permute-start(bf16[4,2,5,8,2688]{4,3,2,1,0:T(8,128)(2,1)} %add_convert_fusion.2), channel_id=1, source_target_pairs={{0,2},{1,3},{2,0},{3,1},{4,6},{5,7},{6,4},{7,5},{8,10},{9,11},{10,... | collective-permute-start | bytes 5160968 | tf_op jit(solution)/shard_map/ppermute | solution.py:346
  331.8 49.1 %collective-permute-start.25 = (bf16[4,2,5,8,2816]{4,3,2,1,0:T(8,128)(2,1)S(1)}, bf16[4,2,5,8,2816]{4,3,2,1,0:T(8,128)(2,1)}, u32[]{:S(2)}, u32[]{:S(2)}) collective-permute-start(bf16[4,2,5,8,2816]{4,3,2,1,0:T(8,128)(2,1)S(1)} %fusion.1), channel_id=1, source_target_pairs={{0,4},{1,5},{2,6},{3,7},{4,0},{5,1},{6,2},{7,3},{8,12},{9,13},{10,... | collective-permute-start | bytes 5406728 | tf_op jit(solution)/shard_map/ppermute | solution.py:346
  385.3 33.3 %collective-permute-start.27 = (bf16[4,5,8,2816]{3,2,1,0:T(8,128)(2,1)S(1)}, bf16[4,5,8,2816]{3,2,1,0:T(8,128)(2,1)S(1)}, u32[]{:S(2)}, u32[]{:S(2)}) collective-permute-start(bf16[4,5,8,2816]{3,2,1,0:T(8,128)(2,1)S(1)} %fusion.2), channel_id=1, source_target_pairs={{0,2},{1,3},{2,0},{3,1},{4,6},{5,7},{6,4},{7,5},{8,10},{9,11},{10,... | collective-permute-start | bytes 2703368 | tf_op jit(solution)/shard_map/ppermute | solution.py:346
  386.1 32.6 %collective-permute-start.28 = (bf16[4,5,8,2688]{3,2,1,0:T(8,128)(2,1)}, bf16[4,5,8,2688]{3,2,1,0:T(8,128)(2,1)}, u32[]{:S(2)}, u32[]{:S(2)}) collective-permute-start(bf16[4,5,8,2688]{3,2,1,0:T(8,128)(2,1)} %fusion.3), channel_id=1, source_target_pairs={{0,4},{1,5},{2,6},{3,7},{4,0},{5,1},{6,2},{7,3},{8,12},{9,13},{10,... | collective-permute-start | bytes 2580488 | tf_op jit(solution)/shard_map/ppermute | solution.py:346
  429.7 27.4 %collective-permute-start.32 = (bf16[4,2,5,8,1792]{4,3,2,1,0:T(8,128)(2,1)S(1)}, bf16[4,2,5,8,1792]{4,3,2,1,0:T(8,128)(2,1)S(1)}, u32[]{:S(2)}, u32[]{:S(2)}) collective-permute-start(bf16[4,2,5,8,1792]{4,3,2,1,0:T(8,128)(2,1)S(1)} %fusion.4), channel_id=1, source_target_pairs={{0,2},{1,3},{2,0},{3,1},{4,6},{5,7},{6,4},{7,5},{8,10},{9,11},{10,... | collective-permute-start | bytes 3440648 | tf_op jit(solution)/shard_map/ppermute | solution.py:346
  432.8 26.9 %collective-permute-start.31 = (bf16[4,2,5,8,1792]{4,3,2,1,0:T(8,128)(2,1)S(1)}, bf16[4,2,5,8,1792]{4,3,2,1,0:T(8,128)(2,1)S(1)}, u32[]{:S(2)}, u32[]{:S(2)}) collective-permute-start(bf16[4,2,5,8,1792]{4,3,2,1,0:T(8,128)(2,1)S(1)} %add_convert_fusion.6), channel_id=1, source_target_pairs={{0,4},{1,5},{2,6},{3,7},{4,0},{5,1},{6,2},{7,3},{8,12},{9,13},{10,... | collective-permute-start | bytes 3440648 | tf_op jit(solution)/shard_map/ppermute | solution.py:346
  433.7 33.1 %collective-permute-start.35 = (bf16[5,8,5504]{2,1,0:T(8,128)(2,1)S(1)}, bf16[5,8,5504]{2,1,0:T(8,128)(2,1)S(1)}, u32[]{:S(2)}, u32[]{:S(2)}) collective-permute-start(bf16[5,8,5504]{2,1,0:T(8,128)(2,1)S(1)} %pad_maximum_fusion.2), channel_id=1, source_target_pairs={{0,8},{1,9},{2,10},{3,11},{4,12},{5,13},{6,14},{7,15},{8,0},{9,1},... | collective-permute-start | bytes 1320968 | tf_op jit(solution)/shard_map/ppermute | solution.py:346
  434.2 32.7 %collective-permute-start.36 = (bf16[5,8,5504]{2,1,0:T(8,128)(2,1)S(1)}, bf16[5,8,5504]{2,1,0:T(8,128)(2,1)S(1)}, u32[]{:S(2)}, u32[]{:S(2)}) collective-permute-start(bf16[5,8,5504]{2,1,0:T(8,128)(2,1)S(1)} %pad_maximum_fusion.3), channel_id=1, source_target_pairs={{0,16},{1,17},{2,18},{3,19},{4,20},{5,21},{6,22},{7,23},{8,24},{9,... | collective-permute-start | bytes 1320968 | tf_op jit(solution)/shard_map/ppermute | solution.py:346
  436.7 50.9 %collective-permute-start.37 = (bf16[5,8,5504]{2,1,0:T(8,128)(2,1)S(1)}, bf16[5,8,5504]{2,1,0:T(8,128)(2,1)S(1)}, u32[]{:S(2)}, u32[]{:S(2)}) collective-permute-start(bf16[5,8,5504]{2,1,0:T(8,128)(2,1)S(1)} %pad_maximum_fusion.4), channel_id=1, source_target_pairs={{0,24},{1,25},{2,26},{3,27},{4,28},{5,29},{6,30},{7,31},{8,16},{9,... | collective-permute-start | bytes 1320968 | tf_op jit(solution)/shard_map/ppermute | solution.py:346
  464.5 26.3 %collective-permute-start.33 = (bf16[4,5,8,1792]{3,2,1,0:T(8,128)(2,1)}, bf16[4,5,8,1792]{3,2,1,0:T(8,128)(2,1)S(1)}, u32[]{:S(2)}, u32[]{:S(2)}) collective-permute-start(bf16[4,5,8,1792]{3,2,1,0:T(8,128)(2,1)} %fusion.6), channel_id=1, source_target_pairs={{0,2},{1,3},{2,0},{3,1},{4,6},{5,7},{6,4},{7,5},{8,10},{9,11},{10,... | collective-permute-start | bytes 1720328 | tf_op jit(solution)/shard_map/ppermute | solution.py:346
  465.4 26.2 %collective-permute-start.34 = (bf16[4,5,8,1792]{3,2,1,0:T(8,128)(2,1)}, bf16[4,5,8,1792]{3,2,1,0:T(8,128)(2,1)}, u32[]{:S(2)}, u32[]{:S(2)}) collective-permute-start(bf16[4,5,8,1792]{3,2,1,0:T(8,128)(2,1)} %fusion.5), channel_id=1, source_target_pairs={{0,4},{1,5},{2,6},{3,7},{4,0},{5,1},{6,2},{7,3},{8,12},{9,13},{10,... | collective-permute-start | bytes 1720328 | tf_op jit(solution)/shard_map/ppermute | solution.py:346
  499.9 27.2 %collective-permute-start.40 = (bf16[5,8,3584]{2,1,0:T(8,128)(2,1)}, bf16[5,8,3584]{2,1,0:T(8,128)(2,1)}, u32[]{:S(2)}, u32[]{:S(2)}) collective-permute-start(bf16[5,8,3584]{2,1,0:T(8,128)(2,1)} %pad_maximum_fusion.10), channel_id=1, source_target_pairs={{0,24},{1,25},{2,26},{3,27},{4,28},{5,29},{6,30},{7,31},{8,16},{9,... | collective-permute-start | bytes 860168 | tf_op jit(solution)/shard_map/ppermute | solution.py:346
  (80 other events, 897.2 us)
Sparse Core Ops, SparseCore 0:
  17.5 174.9 all-gather.1
  319.1 163.7 reduce-scatter.3

commit v11 on v10

--- a/solution.py
+++ b/solution.py
@@ -765,7 +765,7 @@
     if staged:
         qkv, down = tie(qkv, down)
         down = [(*pair, swap(pair[0], 1)) for pair in gather_far(down)]
-    mixed, lse = attn_fwd(qkv, 2)
+    mixed, lse = attn_fwd(qkv, 4)
     if staged:
         mixed, lse, down = tie(mixed, lse, down)
         down = [(*parts, swap(parts[1], 1)) for parts in down]
@@ -819,7 +819,7 @@
         early = early.astype(bf16)
         grad_mixed, outer_other, early = tie(grad_mixed, outer_other, early)
         outer_far = outer.far_swap(outer.far_sends(outer_other))
-    grad_qkv = attn_bwd(qkv, grad_mixed, lse, 2)
+    grad_qkv = attn_bwd(qkv, grad_mixed, lse, 4)
     if staged:
         grad_qkv, outer_far = tie(grad_qkv, outer_far)
         outer_near = outer.near_sends(outer_far)

time: 544 us -> 543 us (level)
  transfers between devices with their start and end apart: 44 -> 44, of which waited for: 19 -> 21; matrix products, arithmetic and copies ran while one was open for 20% -> 20% of each run, Pallas kernels for 19% -> 19%
where the time goes in v11:
time: 543 us; the launch traced here: 538 us
  Pallas kernels  201 us (37%)
  waiting for transfers between devices  146 us (27%)
  local copies, waits for them, and re-layouts  65.1 us (12%)
  other arithmetic  55.8 us (10%)
  starting transfers between devices  35.2 us (6%)
  matrix products  17.6 us (3%)
  between operations  16.5 us (3%)
    ppermute x42, waiting for transfers between devices, swap(): return lax.ppermute(value, 'fsdp', [(i, i ^ mask) for i in range(devices)])  146 us
    pallas_call x1, Pallas kernels, mlp(): pl.pallas_call(mlp_kernel, grid=(hidden // tile,), in_specs=[pl.BlockSpec...  78.7 us
    pallas_call x1, Pallas kernels, attn_bwd(): pl.pallas_call(functools.partial(bwd_kernel, tokens, krows, qrows, per),...  43.1 us
    ppermute x42, starting transfers between devices, swap(): return lax.ppermute(value, 'fsdp', [(i, i ^ mask) for i in range(devices)])  34.9 us
    pallas_call x1, Pallas kernels, attn_fwd(): pl.pallas_call(functools.partial(fwd_kernel, tokens, krows, qrows, per),...  27.8 us
    pallas_call x1, Pallas kernels, qkv_back(): pl.pallas_call(qkv_back_kernel, grid=(3,), in_specs=[pl.BlockSpec(memory_...  25.4 us
    pallas_call x1, Pallas kernels, place_rest(): pl.pallas_call(place_rest_kernel, in_specs=[pl.BlockSpec(memory_space=plt...  19.4 us
    reshape x24, local copies, waits for them, and re-layouts, window(): return result.reshape(kept)  18.4 us
  transfers between devices with their start and end apart: 44, of which 21 were waited for; matrix products, arithmetic and copies ran while one was open for 20% of the time, Pallas kernels for 19%

profile of v11, /device:TPU:8, one launch (start us, length us, event | category | flops | bytes accessed | tf_op | source)
XLA Modules:
  0.0 537.5 jit_solution(15795010640917060134)
XLA Ops:
  18.6 5.4 %fusion.43 = (bf16[1152]{0:T(1024)(128)(2,1)}, bf16[729,1152]{1,0:T(8,128)(2,1)}, f32[729,1152]{1,0:T(8,128)}) fusion(f32[729,1152]{1,0:T(8,128)} %param.35, f32[]{:T(128)} %bitcast.5), kind=kLoop, calls=%fused_computation.233 | loop fusion | flops 2518272 | bytes 8400388 | tf_op jit(solution)/shard_map/reduce_sum | solution.py:734
  24.7 3.0 collective-permute-start.2
  32.5 12.4 %collective-permute-done.1 = bf16[40,3584]{1,0:T(8,128)(2,1)} collective-permute-done((bf16[40,3584]{1,0:T(8,128)(2,1)}, bf16[40,3584]{1,0:T(8,128)(2,1)}, u32[]{:S(2)}, u32[]{:S(2)}) %collective-permute-start.1) | collective-permute-done | bytes 286752 | tf_op jit(solution)/shard_map/ppermute | solution.py:346
  44.9 14.5 %collective-permute-done.2 = bf16[40,3584]{1,0:T(8,128)(2,1)} collective-permute-done((bf16[40,3584]{1,0:T(8,128)(2,1)}, bf16[40,3584]{1,0:T(8,128)(2,1)}, u32[]{:S(2)}, u32[]{:S(2)}) %collective-permute-start.2) | collective-permute-done | bytes 286752 | tf_op jit(solution)/shard_map/ppermute | solution.py:346
  59.5 7.2 %collective-permute-done.3 = bf16[40,3584]{1,0:T(8,128)(2,1)} collective-permute-done((bf16[40,3584]{1,0:T(8,128)(2,1)}, bf16[40,3584]{1,0:T(8,128)(2,1)}, u32[]{:S(2)}, u32[]{:S(2)}) %collective-permute-start.3) | collective-permute-done | bytes 286752 | tf_op jit(solution)/shard_map/ppermute | solution.py:346
  76.6 14.6 %collective-permute-done.6 = bf16[4,40,1792]{2,1,0:T(8,128)(2,1)S(1)} collective-permute-done((bf16[4,40,1792]{2,1,0:T(8,128)(2,1)S(1)}, bf16[4,40,1792]{2,1,0:T(8,128)(2,1)S(1)}, u32[]{:S(2)}, u32[]{:S(2)}) %collective-permute-start.6) | collective-permute-done | bytes 573472 | tf_op jit(solution)/shard_map/ppermute | solution.py:346
  92.7 6.4 %collective-permute-done.4 = bf16[4,40,1792]{2,1,0:T(8,128)(2,1)S(1)} collective-permute-done((bf16[4,40,1792]{2,1,0:T(8,128)(2,1)S(1)}, bf16[4,40,1792]{2,1,0:T(8,128)(2,1)S(1)}, u32[]{:S(2)}, u32[]{:S(2)}) %collective-permute-start.4) | collective-permute-done | bytes 573472 | tf_op jit(solution)/shard_map/ppermute | solution.py:346
  103.4 14.2 %collective-permute-done.10 = bf16[72,1152]{1,0:T(8,128)(2,1)} collective-permute-done((bf16[72,1152]{1,0:T(8,128)(2,1)}, bf16[72,1152]{1,0:T(8,128)(2,1)}, u32[]{:S(2)}, u32[]{:S(2)}) %collective-permute-start.10) | collective-permute-done | bytes 165920 | tf_op jit(solution)/shard_map/ppermute | solution.py:346
  118.6 5.8 %collective-permute-done.7 = bf16[8,40,1792]{2,1,0:T(8,128)(2,1)S(1)} collective-permute-done((bf16[8,40,1792]{2,1,0:T(8,128)(2,1)S(1)}, bf16[8,40,1792]{2,1,0:T(8,128)(2,1)S(1)}, u32[]{:S(2)}, u32[]{:S(2)}) %collective-permute-start.7) | collective-permute-done | bytes 1146912 | tf_op jit(solution)/shard_map/ppermute | solution.py:346
  138.3 6.6 %place_square.1 = (bf16[144,8,3456]{2,1,0:T(8,128)(2,1)}, bf16[32,5,8,128]{3,2,1,0:T(8,128)(2,1)S(1)}) custom-call(s32[4]{0:T(128)S(1)} %pad_add_fusion.coords, bf16[8,5,8,1792]{3,2,1,0:T(8,128)(2,1)S(1)} %bitcast.343, bf16[8,5,8,1792]{3,2,1,0:T(8,128)(2,1)} %bitcast.15.refs_1_, bf16[8,5,8,1792]{3,2,1,0:T(8,128)(2,1)S(1)} %bitcast.345, ...), custom_call_target="tpu_custom_call" | custom-call | bytes 18350080 | tf_op jit(solution)/shard_map/place_square/pallas_call | solution.py:411
  149.9 12.7 %add_convert_fusion.qkv_ref = bf16[729,3456]{1,0:T(8,128)(2,1)} fusion(bf16[729,1152]{1,0:T(8,128)(2,1)S(1)} %add_convert_fusion.4.normed_ref, f32[3456]{0:T(1024)S(1)} %fusion.32, bf16[144,8,3456]{2,1,0:T(8,128)(2,1)} %get-tuple-element.120), kind=kOutput, calls=%fused_computation | convolution fusion | flops 5809792000 | bytes 14694912 | tf_op jit(solution)/shard_map/dot_general | solution.py:333
  170.1 27.8 %attention_forward.1 = (bf16[729,1152]{1,0:T(8,128)(2,1)}, f32[16,1,768]{2,1,0:T(1,128)}) custom-call(bf16[729,3456]{1,0:T(8,128)(2,1)} %add_convert_fusion.qkv_ref), custom_call_target="tpu_custom_call" | custom-call | flops 4630511616 | bytes 6718464 | tf_op jit(solution)/shard_map/attention_forward/pallas_call | solution.py:63
  205.0 19.4 %place_rest.1 = (bf16[144,8,4352]{2,1,0:T(8,128)(2,1)}, bf16[144,8,1152]{2,1,0:T(8,128)(2,1)}, bf16[32,17,8,1152]{3,2,1,0:T(8,128)(2,1)}) custom-call(s32[4]{0:T(128)} %copy-done, bf16[32,33,8,1152]{3,2,1,0:T(8,128)(2,1)} %bitcast.350, bf16[8,5,8,1152]{3,2,1,0:T(8,128)(2,1)} %bitcast.373, bf16[8,5,8,1152]{3,2,1,0:T(8,128)(2,1)} %bitcast.378, ...), custom_call_target="tpu_custom_call" | custom-call | bytes 38928384 | tf_op jit(solution)/shard_map/place_rest/pallas_call | solution.py:479
  224.4 4.9 fusion.47
  234.2 78.7 %mlp_forward_backward.1 = (f32[729,1152]{1,0:T(8,128)}, bf16[16,40,4352]{2,1,0:T(8,128)(2,1)}, bf16[16,40,4352]{2,1,0:T(8,128)(2,1)}, f32[1,4352]{1,0:T(1,128)},...) custom-call(s32[4]{0:T(128)} %copy-done, ...), custom_call_target="tpu_custom_call" | custom-call | flops 1000000 | bytes 1000000 | tf_op jit(solution)/shard_map/mlp_forward_backward/pallas_call | solution.py:205
  333.4 43.1 %attention_backward.1.grad_ref = bf16[729,3456]{1,0:T(8,128)(2,1)} custom-call(bf16[729,3456]{1,0:T(8,128)(2,1)} %add_convert_fusion.qkv_ref, bf16[729,1152]{1,0:T(8,128)(2,1)} %get-tuple-element.148.go_ref, f32[16,1,768]{2,1,0:T(1,128)} %get-tuple-element.149.lse_ref), custom_call_target="tpu_custom_call" | custom-call | flops 1000000 | bytes 1000000 | tf_op jit(solution)/shard_map/attention_backward/pallas_call | solution.py:107
  390.9 25.4 %qkv_backward.1 = (bf16[16,40,3456]{2,1,0:T(8,128)(2,1)}, bf16[16,40,3456]{2,1,0:T(8,128)(2,1)}, f32[1,3456]{1,0:T(1,128)}, f32[8,1152]{1,0:T(8,128)}, f32[729,1152]{1,0:T(8,128)}) custom-call(s32[4]{0:T(128)} %copy-done, bf16[729,3456]{1,0:T(8,128)(2,1)} %attention_backward.1.grad_ref, bf16[729,1152]{1,0:T(8,128)(2,1)} %copy-done.5, ...), custom_call_target="tpu_custom_call" | custom-call | flops 1000000 | bytes 1000000 | tf_op jit(solution)/shard_map/qkv_backward/pallas_call | solution.py:276
  439.2 15.0 %collective-permute-done.32 = bf16[4,2,5,8,1792]{4,3,2,1,0:T(8,128)(2,1)S(1)} collective-permute-done((bf16[4,2,5,8,1792]{4,3,2,1,0:T(8,128)(2,1)S(1)}, bf16[4,2,5,8,1792]{4,3,2,1,0:T(8,128)(2,1)S(1)}, u32[]{:S(2)}, u32[]{:S(2)}) %collective-permute-start.32) | collective-permute-done | bytes 1146912 | tf_op jit(solution)/shard_map/ppermute | solution.py:346
  454.3 3.4 collective-permute-done.31
  465.6 6.3 %collective-permute-done.36 = bf16[5,8,5504]{2,1,0:T(8,128)(2,1)S(1)} collective-permute-done((bf16[5,8,5504]{2,1,0:T(8,128)(2,1)S(1)}, bf16[5,8,5504]{2,1,0:T(8,128)(2,1)S(1)}, u32[]{:S(2)}, u32[]{:S(2)}) %collective-permute-start.36) | collective-permute-done | bytes 440352 | tf_op jit(solution)/shard_map/ppermute | solution.py:346
  472.0 14.0 %collective-permute-done.37 = bf16[5,8,5504]{2,1,0:T(8,128)(2,1)S(1)} collective-permute-done((bf16[5,8,5504]{2,1,0:T(8,128)(2,1)S(1)}, bf16[5,8,5504]{2,1,0:T(8,128)(2,1)S(1)}, u32[]{:S(2)}, u32[]{:S(2)}) %collective-permute-start.37) | collective-permute-done | bytes 440352 | tf_op jit(solution)/shard_map/ppermute | solution.py:346
  502.4 6.7 %collective-permute-done.38 = bf16[5,8,3584]{2,1,0:T(8,128)(2,1)} collective-permute-done((bf16[5,8,3584]{2,1,0:T(8,128)(2,1)}, bf16[5,8,3584]{2,1,0:T(8,128)(2,1)}, u32[]{:S(2)}, u32[]{:S(2)}) %collective-permute-start.38) | collective-permute-done | bytes 286752 | tf_op jit(solution)/shard_map/ppermute | solution.py:346
  509.1 9.7 %collective-permute-done.39 = bf16[5,8,3584]{2,1,0:T(8,128)(2,1)} collective-permute-done((bf16[5,8,3584]{2,1,0:T(8,128)(2,1)}, bf16[5,8,3584]{2,1,0:T(8,128)(2,1)}, u32[]{:S(2)}, u32[]{:S(2)}) %collective-permute-start.39) | collective-permute-done | bytes 286752 | tf_op jit(solution)/shard_map/ppermute | solution.py:346
  518.8 6.7 %collective-permute-done.40 = bf16[5,8,3584]{2,1,0:T(8,128)(2,1)} collective-permute-done((bf16[5,8,3584]{2,1,0:T(8,128)(2,1)}, bf16[5,8,3584]{2,1,0:T(8,128)(2,1)}, u32[]{:S(2)}, u32[]{:S(2)}) %collective-permute-start.40) | collective-permute-done | bytes 286752 | tf_op jit(solution)/shard_map/ppermute | solution.py:346
  (403 shorter events, 156.8 us)
Async XLA Ops:
  7.2 196.7 %all-gather.2.cloned.1.call-start = ((), (), s32[]{:S(2)}) async-start(), calls=%async_computation.1 | async-start | bytes 20072448 | tf_op jit(solution)/shard_map/all_gather | solution.py:739
  17.4 471.8 %reduce-scatter.4.cloned.1.call-start = ((), (), s32[]{:S(2)}) async-start(), calls=%async_computation.2 | async-start | bytes 10340352
  24.7 34.7 %collective-permute-start.2 = (bf16[40,3584]{1,0:T(8,128)(2,1)}, bf16[40,3584]{1,0:T(8,128)(2,1)}, u32[]{:S(2)}, u32[]{:S(2)}) collective-permute-start(bf16[40,3584]{1,0:T(8,128)(2,1)} %pad_maximum_fusion.7), channel_id=1, source_target_pairs={{0,16},{1,17},{2,18},{3,19},{4,20},{5,21},{6,22},{7,23},{8,24},{9,... | collective-permute-start | bytes 860168 | tf_op jit(solution)/shard_map/ppermute | solution.py:346
  27.8 38.9 %collective-permute-start.3 = (bf16[40,3584]{1,0:T(8,128)(2,1)}, bf16[40,3584]{1,0:T(8,128)(2,1)}, u32[]{:S(2)}, u32[]{:S(2)}) collective-permute-start(bf16[40,3584]{1,0:T(8,128)(2,1)} %pad_maximum_fusion.7), channel_id=1, source_target_pairs={{0,24},{1,25},{2,26},{3,27},{4,28},{5,29},{6,30},{7,31},{8,16},{9,... | collective-permute-start | bytes 860168 | tf_op jit(solution)/shard_map/ppermute | solution.py:346
  71.0 28.2 %collective-permute-start.4 = (bf16[4,40,1792]{2,1,0:T(8,128)(2,1)S(1)}, bf16[4,40,1792]{2,1,0:T(8,128)(2,1)S(1)}, u32[]{:S(2)}, u32[]{:S(2)}) collective-permute-start(bf16[4,40,1792]{2,1,0:T(8,128)(2,1)S(1)} %pad_maximum_fusion), channel_id=1, source_target_pairs={{0,2},{1,3},{2,0},{3,1},{4,6},{5,7},{6,4},{7,5},{8,10},{9,11},{10,... | collective-permute-start | bytes 1720328 | tf_op jit(solution)/shard_map/ppermute | solution.py:346
  91.2 33.3 %collective-permute-start.7 = (bf16[8,40,1792]{2,1,0:T(8,128)(2,1)S(1)}, bf16[8,40,1792]{2,1,0:T(8,128)(2,1)S(1)}, u32[]{:S(2)}, u32[]{:S(2)}) collective-permute-start(bf16[8,40,1792]{2,1,0:T(8,128)(2,1)S(1)} %constant_dynamic-update-slice_fusion.10), channel_id=1, source_target_pairs={{0,2},{1,3},{2,0},{3,1},{4,6},{5,7},{6,4},{7,5},{8,10},{9,11},{10,... | collective-permute-start | bytes 3440648 | tf_op jit(solution)/shard_map/ppermute | solution.py:346
  128.9 33.8 %collective-permute-start.16 = (bf16[4,32,1152]{2,1,0:T(8,128)(2,1)}, bf16[4,32,1152]{2,1,0:T(8,128)(2,1)}, u32[]{:S(2)}, u32[]{:S(2)}) collective-permute-start(bf16[4,32,1152]{2,1,0:T(8,128)(2,1)} %pad_maximum_fusion.6), channel_id=1, source_target_pairs={{0,4},{1,5},{2,6},{3,7},{4,0},{5,1},{6,2},{7,3},{8,12},{9,13},{10,... | collective-permute-start | bytes 884744 | tf_op jit(solution)/shard_map/ppermute | solution.py:346
  135.8 26.9 %collective-permute-start.15 = (bf16[4,40,1152]{2,1,0:T(8,128)(2,1)}, bf16[4,40,1152]{2,1,0:T(8,128)(2,1)}, u32[]{:S(2)}, u32[]{:S(2)}) collective-permute-start(bf16[4,40,1152]{2,1,0:T(8,128)(2,1)} %pad_maximum_fusion.5), channel_id=1, source_target_pairs={{0,2},{1,3},{2,0},{3,1},{4,6},{5,7},{6,4},{7,5},{8,10},{9,11},{10,... | collective-permute-start | bytes 1105928 | tf_op jit(solution)/shard_map/ppermute | solution.py:346
  164.7 33.2 %collective-permute-start.17 = (bf16[8,40,1152]{2,1,0:T(8,128)(2,1)S(1)}, bf16[8,40,1152]{2,1,0:T(8,128)(2,1)S(1)}, u32[]{:S(2)}, u32[]{:S(2)}) collective-permute-start(bf16[8,40,1152]{2,1,0:T(8,128)(2,1)S(1)} %constant_dynamic-update-slice_fusion.15), channel_id=1, source_target_pairs={{0,4},{1,5},{2,6},{3,7},{4,0},{5,1},{6,2},{7,3},{8,12},{9,13},{10,... | collective-permute-start | bytes 2211848 | tf_op jit(solution)/shard_map/ppermute | solution.py:346
  166.3 31.7 %collective-permute-start.18 = (bf16[8,40,1152]{2,1,0:T(8,128)(2,1)S(1)}, bf16[8,40,1152]{2,1,0:T(8,128)(2,1)S(1)}, u32[]{:S(2)}, u32[]{:S(2)}) collective-permute-start(bf16[8,40,1152]{2,1,0:T(8,128)(2,1)S(1)} %constant_dynamic-update-slice_fusion.15), channel_id=1, source_target_pairs={{0,1},{1,0},{2,3},{3,2},{4,5},{5,4},{6,7},{7,6},{8,9},{9,8},{10,11... | collective-permute-start | bytes 2211848 | tf_op jit(solution)/shard_map/ppermute | solution.py:346
  168.3 29.6 %collective-permute-start.19 = (bf16[8,32,1152]{2,1,0:T(8,128)(2,1)S(1)}, bf16[8,32,1152]{2,1,0:T(8,128)(2,1)S(1)}, u32[]{:S(2)}, u32[]{:S(2)}) collective-permute-start(bf16[8,32,1152]{2,1,0:T(8,128)(2,1)S(1)} %constant_dynamic-update-slice_fusion.17), channel_id=1, source_target_pairs={{0,2},{1,3},{2,0},{3,1},{4,6},{5,7},{6,4},{7,5},{8,10},{9,11},{10,... | collective-permute-start | bytes 1769480 | tf_op jit(solution)/shard_map/ppermute | solution.py:346
  169.9 28.0 %collective-permute-start.20 = (bf16[8,32,1152]{2,1,0:T(8,128)(2,1)S(1)}, bf16[8,32,1152]{2,1,0:T(8,128)(2,1)S(1)}, u32[]{:S(2)}, u32[]{:S(2)}) collective-permute-start(bf16[8,32,1152]{2,1,0:T(8,128)(2,1)S(1)} %constant_dynamic-update-slice_fusion.17), channel_id=1, source_target_pairs={{0,1},{1,0},{2,3},{3,2},{4,5},{5,4},{6,7},{7,6},{8,9},{9,8},{10,11... | collective-permute-start | bytes 1769480 | tf_op jit(solution)/shard_map/ppermute | solution.py:346
  327.5 51.1 %collective-permute-start.26 = (bf16[4,2,5,8,2688]{4,3,2,1,0:T(8,128)(2,1)}, bf16[4,2,5,8,2688]{4,3,2,1,0:T(8,128)(2,1)}, u32[]{:S(2)}, u32[]{:S(2)}) collective-permute-start(bf16[4,2,5,8,2688]{4,3,2,1,0:T(8,128)(2,1)} %add_convert_fusion.2), channel_id=1, source_target_pairs={{0,2},{1,3},{2,0},{3,1},{4,6},{5,7},{6,4},{7,5},{8,10},{9,11},{10,... | collective-permute-start | bytes 5160968 | tf_op jit(solution)/shard_map/ppermute | solution.py:346
  330.8 48.6 %collective-permute-start.25 = (bf16[4,2,5,8,2816]{4,3,2,1,0:T(8,128)(2,1)S(1)}, bf16[4,2,5,8,2816]{4,3,2,1,0:T(8,128)(2,1)}, u32[]{:S(2)}, u32[]{:S(2)}) collective-permute-start(bf16[4,2,5,8,2816]{4,3,2,1,0:T(8,128)(2,1)S(1)} %fusion.1), channel_id=1, source_target_pairs={{0,4},{1,5},{2,6},{3,7},{4,0},{5,1},{6,2},{7,3},{8,12},{9,13},{10,... | collective-permute-start | bytes 5406728 | tf_op jit(solution)/shard_map/ppermute | solution.py:346
  383.7 32.6 %collective-permute-start.27 = (bf16[4,5,8,2816]{3,2,1,0:T(8,128)(2,1)S(1)}, bf16[4,5,8,2816]{3,2,1,0:T(8,128)(2,1)S(1)}, u32[]{:S(2)}, u32[]{:S(2)}) collective-permute-start(bf16[4,5,8,2816]{3,2,1,0:T(8,128)(2,1)S(1)} %fusion.2), channel_id=1, source_target_pairs={{0,2},{1,3},{2,0},{3,1},{4,6},{5,7},{6,4},{7,5},{8,10},{9,11},{10,... | collective-permute-start | bytes 2703368 | tf_op jit(solution)/shard_map/ppermute | solution.py:346
  384.3 32.0 %collective-permute-start.28 = (bf16[4,5,8,2688]{3,2,1,0:T(8,128)(2,1)}, bf16[4,5,8,2688]{3,2,1,0:T(8,128)(2,1)}, u32[]{:S(2)}, u32[]{:S(2)}) collective-permute-start(bf16[4,5,8,2688]{3,2,1,0:T(8,128)(2,1)} %fusion.3), channel_id=1, source_target_pairs={{0,4},{1,5},{2,6},{3,7},{4,0},{5,1},{6,2},{7,3},{8,12},{9,13},{10,... | collective-permute-start | bytes 2580488 | tf_op jit(solution)/shard_map/ppermute | solution.py:346
  427.2 27.0 %collective-permute-start.32 = (bf16[4,2,5,8,1792]{4,3,2,1,0:T(8,128)(2,1)S(1)}, bf16[4,2,5,8,1792]{4,3,2,1,0:T(8,128)(2,1)S(1)}, u32[]{:S(2)}, u32[]{:S(2)}) collective-permute-start(bf16[4,2,5,8,1792]{4,3,2,1,0:T(8,128)(2,1)S(1)} %fusion.4), channel_id=1, source_target_pairs={{0,2},{1,3},{2,0},{3,1},{4,6},{5,7},{6,4},{7,5},{8,10},{9,11},{10,... | collective-permute-start | bytes 3440648 | tf_op jit(solution)/shard_map/ppermute | solution.py:346
  430.1 27.6 %collective-permute-start.31 = (bf16[4,2,5,8,1792]{4,3,2,1,0:T(8,128)(2,1)S(1)}, bf16[4,2,5,8,1792]{4,3,2,1,0:T(8,128)(2,1)S(1)}, u32[]{:S(2)}, u32[]{:S(2)}) collective-permute-start(bf16[4,2,5,8,1792]{4,3,2,1,0:T(8,128)(2,1)S(1)} %add_convert_fusion.6), channel_id=1, source_target_pairs={{0,4},{1,5},{2,6},{3,7},{4,0},{5,1},{6,2},{7,3},{8,12},{9,13},{10,... | collective-permute-start | bytes 3440648 | tf_op jit(solution)/shard_map/ppermute | solution.py:346
  432.1 33.6 %collective-permute-start.35 = (bf16[5,8,5504]{2,1,0:T(8,128)(2,1)S(1)}, bf16[5,8,5504]{2,1,0:T(8,128)(2,1)S(1)}, u32[]{:S(2)}, u32[]{:S(2)}) collective-permute-start(bf16[5,8,5504]{2,1,0:T(8,128)(2,1)S(1)} %pad_maximum_fusion.2), channel_id=1, source_target_pairs={{0,8},{1,9},{2,10},{3,11},{4,12},{5,13},{6,14},{7,15},{8,0},{9,1},... | collective-permute-start | bytes 1320968 | tf_op jit(solution)/shard_map/ppermute | solution.py:346
  432.4 39.5 %collective-permute-start.36 = (bf16[5,8,5504]{2,1,0:T(8,128)(2,1)S(1)}, bf16[5,8,5504]{2,1,0:T(8,128)(2,1)S(1)}, u32[]{:S(2)}, u32[]{:S(2)}) collective-permute-start(bf16[5,8,5504]{2,1,0:T(8,128)(2,1)S(1)} %pad_maximum_fusion.3), channel_id=1, source_target_pairs={{0,16},{1,17},{2,18},{3,19},{4,20},{5,21},{6,22},{7,23},{8,24},{9,... | collective-permute-start | bytes 1320968 | tf_op jit(solution)/shard_map/ppermute | solution.py:346
  435.0 51.0 %collective-permute-start.37 = (bf16[5,8,5504]{2,1,0:T(8,128)(2,1)S(1)}, bf16[5,8,5504]{2,1,0:T(8,128)(2,1)S(1)}, u32[]{:S(2)}, u32[]{:S(2)}) collective-permute-start(bf16[5,8,5504]{2,1,0:T(8,128)(2,1)S(1)} %pad_maximum_fusion.4), channel_id=1, source_target_pairs={{0,24},{1,25},{2,26},{3,27},{4,28},{5,29},{6,30},{7,31},{8,16},{9,... | collective-permute-start | bytes 1320968 | tf_op jit(solution)/shard_map/ppermute | solution.py:346
  462.5 26.7 %collective-permute-start.33 = (bf16[4,5,8,1792]{3,2,1,0:T(8,128)(2,1)}, bf16[4,5,8,1792]{3,2,1,0:T(8,128)(2,1)S(1)}, u32[]{:S(2)}, u32[]{:S(2)}) collective-permute-start(bf16[4,5,8,1792]{3,2,1,0:T(8,128)(2,1)} %fusion.6), channel_id=1, source_target_pairs={{0,2},{1,3},{2,0},{3,1},{4,6},{5,7},{6,4},{7,5},{8,10},{9,11},{10,... | collective-permute-start | bytes 1720328 | tf_op jit(solution)/shard_map/ppermute | solution.py:346
  464.0 26.0 %collective-permute-start.34 = (bf16[4,5,8,1792]{3,2,1,0:T(8,128)(2,1)}, bf16[4,5,8,1792]{3,2,1,0:T(8,128)(2,1)}, u32[]{:S(2)}, u32[]{:S(2)}) collective-permute-start(bf16[4,5,8,1792]{3,2,1,0:T(8,128)(2,1)} %fusion.5), channel_id=1, source_target_pairs={{0,4},{1,5},{2,6},{3,7},{4,0},{5,1},{6,2},{7,3},{8,12},{9,13},{10,... | collective-permute-start | bytes 1720328 | tf_op jit(solution)/shard_map/ppermute | solution.py:346
  499.0 26.5 %collective-permute-start.40 = (bf16[5,8,3584]{2,1,0:T(8,128)(2,1)}, bf16[5,8,3584]{2,1,0:T(8,128)(2,1)}, u32[]{:S(2)}, u32[]{:S(2)}) collective-permute-start(bf16[5,8,3584]{2,1,0:T(8,128)(2,1)} %pad_maximum_fusion.10), channel_id=1, source_target_pairs={{0,24},{1,25},{2,26},{3,27},{4,28},{5,29},{6,30},{7,31},{8,16},{9,... | collective-permute-start | bytes 860168 | tf_op jit(solution)/shard_map/ppermute | solution.py:346
  (80 other events, 897.8 us)
Sparse Core Ops, SparseCore 0:
  17.5 174.9 all-gather.1
  318.1 163.6 reduce-scatter.3
